TPU v7x, 256 devices: a whole 4x4x8 slice. The times are simulated.
256 devices in a mesh: ka: 32 (over y_hi, z, core), band: 8 (over y_lo, x).
Axes of the slice: x: 4, y: 4 (y_hi: 2, y_lo: 2; y = y_hi * 2 + y_lo), z: 8, core: 2. Of those that a mesh axis runs over, the one named last changes fastest.
Arguments:
- coefficients: bfloat16 [32, 2, 160, 2400], P('ka'), may hold values from -6 to 6
- class_weight: float32 [32], replicated, may hold values from 0.5 to 5
- diff_class: int32 [32, 32], replicated, may hold values from 0 to 31
- frag_cells: int32 [2], replicated, may hold values from 0 to 31
- block_pattern: int32 [2, 30], replicated, may hold values 0 or 1
Outputs:
- cluster: float32 [2, 2, 160, 2400], P(None, None, 'band', 'ka')
All inputs are finite; a program needn't handle non-finite values.
Results may differ from a plain program's by a relative error of at most 0.0017.
Values may be sent and summed in bfloat16 or wider, within the bound.
No kernel may reach another device: no remote copies, remote signals or barrier semaphores. Data moves between devices by JAX's collectives and lax.ppermute only.
A program may use at most 64 MiB of HBM per device.

v0:
```python
import jax
import jax.numpy as jnp
from jax import lax
from jax.sharding import PartitionSpec as P


def shards(coefficients, class_weight, diff_class, frag_cells, block_pattern):
    own_block = coefficients[0]
    occupied = own_block.shape[1]
    functions = own_block.shape[2]
    band_count = lax.axis_size("band")
    group_width = occupied // band_count
    kpoint_count = lax.axis_size("ka")
    kpoint_index = lax.axis_index("ka")
    high = lax.Precision.HIGHEST
    own_flat = own_block.reshape(2 * occupied, functions)
    my_group = lax.dynamic_slice_in_dim(
        own_block, lax.axis_index("band") * group_width, group_width, 1
    )
    diff_row = lax.dynamic_index_in_dim(diff_class, kpoint_index, 0, keepdims=False)
    classes = jnp.arange(class_weight.shape[0], dtype=jnp.int32)
    onehot = (diff_row[:, None] == classes[None, :]).astype(jnp.float32)
    weights = jnp.dot(onehot, class_weight, precision=high) / functions
    piece = lax.all_gather(my_group[None], "ka", axis=0, tiled=True)
    pieces = piece.shape[0]
    blocks = piece.reshape(pieces, 2 * group_width, functions)
    intersection = jnp.einsum("qia,ja->qij", blocks, own_flat, preferred_element_type=jnp.float32)
    m_real = intersection[:, :group_width, :occupied] + intersection[:, group_width:, occupied:]
    m_imag = intersection[:, :group_width, occupied:] - intersection[:, group_width:, :occupied]
    scaling = weights[:, None, None]
    m_real = (scaling * m_real).astype(jnp.bfloat16)
    m_imag = (scaling * m_imag).astype(jnp.bfloat16)
    m_block = jnp.concatenate(
        [jnp.concatenate([m_real, m_imag], 2), jnp.concatenate([-m_imag, m_real], 2)], 1
    )
    exchange = jnp.einsum("qio,qia->oa", m_block, blocks, preferred_element_type=jnp.float32)
    exchange = exchange.reshape(2, occupied, functions)
    phase_index = kpoint_index * frag_cells % kpoint_count
    angles = 2.0 * jnp.pi * phase_index.astype(jnp.float32) / kpoint_count
    cosines = (jnp.cos(angles) / kpoint_count)[:, None, None]
    sines = (jnp.sin(angles) / kpoint_count)[:, None, None]
    w_real = exchange[0][None]
    w_imag = exchange[1][None]
    terms = jnp.stack([cosines * w_real - sines * w_imag, sines * w_real + cosines * w_imag], 1)
    partial_value = lax.psum_scatter(terms, "band", scatter_dimension=2, tiled=True)
    cluster = lax.psum_scatter(partial_value, "ka", scatter_dimension=3, tiled=True)
    columns = cluster.shape[3]
    block_size = functions // block_pattern.shape[1]
    local_ids = (kpoint_index * columns + jnp.arange(columns, dtype=jnp.int32)) // block_size
    block_ids = jnp.arange(block_pattern.shape[1], dtype=jnp.int32)
    block_onehot = (block_ids[:, None] == local_ids[None, :]).astype(jnp.float32)
    block_mask = jnp.dot(block_pattern.astype(jnp.float32), block_onehot, precision=high)
    return cluster * block_mask[:, None, None, :]


def solution(mesh):
    placed = (P("ka", None, None, None), P(), P(), P(), P())
    return jax.shard_map(
        shards, mesh=mesh, in_specs=placed, out_specs=P(None, None, "band", "ka"), check_vma=False
    )
```

profile of v0, /device:TPU:1, one launch (start us, length us, event | category | flops | bytes accessed | tf_op | source)
XLA Modules:
  0.0 558.0 jit_solution(7503871566022568461)
XLA Ops:
  6.5 0.0 copy-start
  6.5 0.0 all-gather.2.cloned.1.call-start
  6.5 1.4 copy-done
  7.9 0.1 constant_dynamic-slice_fusion.1
  8.0 0.8 copy.19
  8.8 0.0 all-gather.2.cloned.1.call-update
  8.8 0.0 all-reduce.5.cloned.1.call-start
  8.9 0.7 dynamic-slice_bitcast_fusion
  9.6 0.7 cosine_multiply_fusion
  10.4 0.8 fusion
  11.2 97.5 %all-gather.2.cloned.1.call-done = bf16[32,2,20,2400]{3,1,2,0:T(2,128)(2,1)} async-done(((bf16[1,2,20,2400]{3,1,2,0:T(2,128)(2,1)}), bf16[32,2,20,2400]{3,1,2,0:T(2,128)(2,1)}) %all-gather.2.cloned.1.call-update) | async-done | bytes 6144016 | tf_op jit(solution)/shard_map/all_gather | solution.py:24
  108.7 3.5 copy.10
  112.2 3.5 fusion.24
  115.7 0.3 fusion.11
  116.0 0.3 fusion.21
  116.2 2.5 convolution_bitcast_fusion
  118.7 0.2 fusion.23
  118.9 6.8 %multiply_subtract_fusion = (f32[2,1,160,2400]{3,1,2,0:T(1,128)S(1)}, f32[2,1,160,2400]{3,1,2,0:T(1,128)}) fusion(f32[160,2400]{1,0:T(8,128)S(1)} %get-tuple-element.12, f32[160,2400]{1,0:T(8,128)S(1)} %get-tuple-element.11, f32[2]{0:T(128)S(1)} %sine_multiply_fusion, f32[2]{0:T(128)S(1)} %get-tuple-element.5), kind=kLoop, calls=%fused_computation.3 | loop fusion | flops 4608000 | bytes 9216016 | tf_op jit(solution)/shard_map/sub | solution.py:44
  125.7 10.2 %pad_maximum_fusion = f32[2,2,160,2400]{3,1,2,0:T(2,128)} fusion(f32[2,1,160,2400]{3,1,2,0:T(1,128)} %get-tuple-element.10, f32[2,1,160,2400]{3,1,2,0:T(1,128)S(1)} %get-tuple-element.9), kind=kLoop, calls=%fused_computation | loop fusion | flops 1536000 | bytes 12288000 | tf_op jit(solution)/shard_map/stack | solution.py:44
  135.9 0.0 all-reduce.5.cloned.1.call-update
  135.9 0.0 all-reduce.7.cloned.1.call-start
  136.0 0.6 copy-done.3
  136.6 0.6 dynamic-slice.1
  137.8 143.1 %all-reduce.5.cloned.1.call-done = f32[2,2,160,2400]{3,1,2,0:T(2,128)} async-done(((f32[2,2,160,2400]{3,1,2,0:T(2,128)}), f32[2,2,160,2400]{3,1,2,0:T(2,128)}) %all-reduce.5.cloned.1.call-update) | async-done | bytes 6144016
  280.9 2.1 constant_dynamic-slice_fusion
  283.0 0.0 all-reduce.7.cloned.1.call-update
  283.0 0.0 copy-done.2
  283.0 0.6 dynamic-slice.3
  284.3 0.0 copy-done.1
  284.3 0.1 convolution_bitcast_fusion.1
  284.4 265.5 %all-reduce.7.cloned.1.call-done = f32[2,2,20,2400]{3,1,2,0:T(2,128)} async-done(((f32[2,2,20,2400]{3,1,2,0:T(2,128)}), f32[2,2,20,2400]{3,1,2,0:T(2,128)}) %all-reduce.7.cloned.1.call-update) | async-done | bytes 768016
  549.9 1.6 dynamic-slice_multiply_fusion
  (5 shorter events, 0.1 us)
Async XLA Ops:
  6.5 1.4 copy-start
  6.5 102.2 %all-gather.2.cloned.1.call-start = ((), (), s32[]{:S(2)}) async-start(), calls=%async_computation | async-start | bytes 6420480 | tf_op jit(solution)/shard_map/all_gather | solution.py:24
  8.8 272.0 %all-reduce.5.cloned.1.call-start = ((), (), s32[]{:S(2)}) async-start(), calls=%async_computation.1 | async-start | bytes 12451840
  135.9 0.7 copy-start.3
  135.9 147.1 %copy-start.2 = (u32[256]{0:T(256)S(1)}, u32[256]{0:T(256)}, u32[]{:S(2)}) copy-start(u32[256]{0:T(256)} %constant.64) | copy-start | bytes 3076
  135.9 148.4 %copy-start.1 = (s32[2,30]{1,0:T(2,128)S(1)}, s32[2,30]{1,0:T(2,128)}, u32[]{:S(2)}) copy-start(s32[2,30]{1,0:T(2,128)} %param.9) | copy-start | bytes 724
  135.9 414.0 %all-reduce.7.cloned.1.call-start = ((), (), s32[]{:S(2)}) async-start(), calls=%async_computation.2 | async-start | bytes 1556480
Sparse Core Ops, SparseCore 0:
  10.1 98.5 all-gather.1
  136.0 144.7 all-reduce.4
  283.7 266.1 all-reduce.6
where the time goes:
time: 558 us
  waiting for transfers between devices  506 us (91%)
  other arithmetic  19.9 us (4%)
  between operations  14.5 us (3%)
  local copies, waits for them, and re-layouts  10.5 us (2%)
  matrix products  6.93 us (1%)
    unnamed x5, waiting for transfers between devices  409 us
    all_gather x1, waiting for transfers between devices, shards(): piece = lax.all_gather(my_group[None], 'ka', axis=0, tiled=True)  97.5 us
  transfers between devices with their start and end apart: 3, of which 3 were waited for; matrix products, arithmetic and copies ran while one was open for 1% of the time, Pallas kernels for 0%

commit v1 on v0

v1 whole, which is shorter than its diff:
```python
import jax
import jax.numpy as jnp
import numpy as np
from jax import lax
from jax.experimental import pallas as pl
from jax.experimental.pallas import tpu as pltpu
from jax.sharding import Mesh
from jax.sharding import PartitionSpec as P

AXES = ("yh", "z", "core", "yl", "x")
KA = ("yh", "z", "core")
BAND = ("yl", "x")
PARTS = (2, 8, 2, 2, 4)
F32 = jnp.float32
BF16 = jnp.bfloat16


def phase_signs(width, blocks):
    rows = np.arange(8 * width)
    cols = np.arange(2 * blocks * width)
    partner, part = (rows // (4 * width))[:, None], (rows // width % 2)[:, None]
    part_m = (cols // width % 2)[None, :]
    same = (rows % width)[:, None] == (cols % width)[None, :]
    real = np.where(partner == 0, part == 0, part == 1)
    sign = np.where((partner == 1) & (part == 0), -1, 1)
    cos_sign = same * sign * np.where(real, part_m == 0, part_m == 1)
    sin_sign = same * sign * np.where(real, -1 * (part_m == 1), part_m == 0)
    return cos_sign.astype(np.float32), sin_sign.astype(np.float32)


def turned(width):
    turn = np.zeros((2 * width, 2 * width), np.float32)
    turn[:width, width:] = np.eye(width)
    turn[width:, :width] = -np.eye(width)
    return turn


def cluster_kernel(core_ref, own, near, far_r, far_i, diag_r, diag_i, *refs):
    blocks, (weights, g_high, g_low, turn, mine, other, b_ref, bt_ref, u_ref) = refs[:8], refs[8:]
    rows = blocks[0].shape[0]
    for step, block in enumerate(blocks):
        value = block[...]
        b_ref[pl.ds(step * rows, rows), :] = value
        swapped = jnp.dot(turn[...], value, preferred_element_type=F32)
        bt_ref[pl.ds(step * rows, rows), :] = swapped.astype(BF16)
    outs = g_high.shape[0] // 2
    contract = (((1,), (1,)), ((), ()))
    for q in range(4):
        real, imag = (
            (own[0], own[1]),
            (near[0], near[1]),
            (far_r[...], far_i[...]),
            (diag_r[...], diag_i[...]),
        )[q]
        m = lax.dot_general(b_ref[...], real, contract, preferred_element_type=F32)
        m = m + lax.dot_general(bt_ref[...], imag, contract, preferred_element_type=F32)
        m = (weights[q] * m).astype(BF16)
        t = jnp.dot(g_high[...], m, preferred_element_type=F32)
        t = t + jnp.dot(g_low[...], m, preferred_element_type=F32)
        t_high = t.astype(BF16)
        t_low = (t - t_high.astype(F32)).astype(BF16)
        u = jnp.dot(t_high[:outs], real, preferred_element_type=F32)
        u = u + jnp.dot(t_high[outs:], imag, preferred_element_type=F32)
        u = u + jnp.dot(t_low[:outs], real, preferred_element_type=F32)
        u = u + jnp.dot(t_low[outs:], imag, preferred_element_type=F32)
        u_ref[...] = u if q == 0 else u_ref[...] + u
    chips, _, columns = mine.shape
    for core in range(2):

        @pl.when(core_ref[0] == core)
        def _():
            for chip in range(chips):
                at = (2 * chip + core) * columns
                mine[chip] = u_ref[:, at : at + columns]
                at = (2 * chip + 1 - core) * columns
                other[chip] = u_ref[:, at : at + columns]


def shards(coefficients, class_weight, diff_class, frag_cells, block_pattern):
    own = coefficients[0]
    _, occupied, functions = own.shape
    yh, z, core = (lax.axis_index(name) for name in KA)
    band = lax.axis_index("yl") * PARTS[4] + lax.axis_index("x")
    width = occupied // (PARTS[3] * PARTS[4])
    kpoint_count = PARTS[0] * PARTS[1] * PARTS[2]
    up = [(i, (i + 1) % PARTS[1]) for i in range(PARTS[1])]
    down = [(j, i) for i, j in up]
    swap = [(0, 1), (1, 0)]

    block = lax.dynamic_slice_in_dim(own, band * width, width, 1).reshape(2 * width, functions)
    near = lax.ppermute(own, "core", swap)
    far_r = lax.ppermute(own[0], "yh", swap)
    far_i = lax.ppermute(own[1], "yh", swap)
    diag_r = lax.ppermute(far_r, "core", swap)
    diag_i = lax.ppermute(far_i, "core", swap)
    blocks, offsets = [block], [0]
    from_below = from_above = block
    for step in range(1, PARTS[1] // 2 + 1):
        from_below = lax.ppermute(from_below, "z", up)
        blocks.append(from_below)
        offsets.append(-step)
        if step < PARTS[1] // 2:
            from_above = lax.ppermute(from_above, "z", down)
            blocks.append(from_above)
            offsets.append(step)

    kpoints = (yh * PARTS[1] + (z + jnp.array(offsets, jnp.int32)) % PARTS[1]) * 2 + core
    q_yh = jnp.stack([yh, yh, 1 - yh, 1 - yh])
    q_core = jnp.stack([core, 1 - core, core, 1 - core])
    q_points = (q_yh * PARTS[1] + z) * 2 + q_core
    picked = jnp.take(jnp.take(diff_class, kpoints, axis=0), q_points, axis=1)
    weights = jnp.take(class_weight, picked.T) / functions
    weights = jnp.repeat(weights, 2 * width, axis=1)[:, :, None]

    phase_index = frag_cells[:, None] * kpoints[None, :] % kpoint_count
    angles = 2.0 * jnp.pi * phase_index.astype(F32) / kpoint_count
    cells = frag_cells.shape[0]
    spread = (1, cells, 2 * width, 2 * width * len(blocks))
    full = (2,) + spread[1:]
    cosines = jnp.repeat(jnp.cos(angles) / kpoint_count, 2 * width, axis=1)[None, :, None, :]
    sines = jnp.repeat(jnp.sin(angles) / kpoint_count, 2 * width, axis=1)[None, :, None, :]
    cos_sign, sin_sign = (jnp.asarray(a.reshape(full)) for a in phase_signs(width, len(blocks)))
    g = (cos_sign * cosines + sin_sign * sines).reshape(8 * width, -1)
    g_high = g.astype(BF16)
    g_low = (g - g_high.astype(F32)).astype(BF16)

    chips = PARTS[0] * PARTS[1]
    columns = functions // kpoint_count
    piece = jax.ShapeDtypeStruct((chips, 4 * width, columns), F32)
    mine, other = pl.pallas_call(
        cluster_kernel,
        out_shape=(piece, piece),
        in_specs=[pl.BlockSpec(memory_space=pltpu.SMEM)] + [pl.BlockSpec(memory_space=pltpu.VMEM)] * 18,
        out_specs=(pl.BlockSpec(memory_space=pltpu.VMEM),) * 2,
        scratch_shapes=[
            pltpu.VMEM((2 * width * len(blocks), functions), BF16),
            pltpu.VMEM((2 * width * len(blocks), functions), BF16),
            pltpu.VMEM((4 * width, functions), F32),
        ],
        compiler_params=pltpu.CompilerParams(vmem_limit_bytes=48 * 2**20),
        cost_estimate=pl.CostEstimate(flops=3 * 10**9, bytes_accessed=10**7, transcendentals=0),
        name="cluster_terms",
    )(core[None], own, near, far_r, far_i, diag_r, diag_i, *blocks, weights, g_high, g_low, jnp.asarray(turned(width), BF16))

    sums = (mine + lax.ppermute(other, "core", swap)).astype(BF16)
    arrived = lax.all_to_all(sums, ("yh", "z"), 0, 0, tiled=True)
    cluster = jnp.sum(arrived.astype(F32), axis=0).reshape(cells, 2, width, columns)
    index = (yh * PARTS[1] + z) * 2 + core
    block_size = functions // block_pattern.shape[1]
    local_ids = (index * columns + jnp.arange(columns, dtype=jnp.int32)) // block_size
    block_ids = jnp.arange(block_pattern.shape[1], dtype=jnp.int32)
    onehot = (block_ids[:, None] == local_ids[None, :]).astype(F32)
    mask = jnp.dot(block_pattern.astype(F32), onehot, precision=lax.Precision.HIGHEST)
    return cluster * mask[:, None, None, :]


def solution(mesh):
    placed = (P(KA, None, None, None), P(), P(), P(), P())
    return jax.shard_map(
        shards,
        mesh=Mesh(mesh.devices.reshape(PARTS), AXES),
        in_specs=placed,
        out_specs=P(None, None, BAND, KA),
        check_vma=False,
    )
```

time: 558 us -> 109 us (0.20)
  waiting for transfers between devices: 506 us -> 52.5 us
  starting transfers between devices: 0.09 us -> 31.5 us
  other arithmetic: 19.9 us -> 2.45 us
  Pallas kernels: 0 us -> 14.3 us
  between operations: 14.5 us -> 0.22 us
  matrix products: 6.93 us -> 0.13 us
    unnamed x5 -> x0, waiting for transfers between devices: 409 us -> none
    all_gather x1 -> x0, waiting for transfers between devices: 97.5 us -> none  [shards(): piece = lax.all_gather(my_group[None], 'ka', axis=0, tiled=True)]
    ppermute x0 -> x13, waiting for transfers between devices: none -> 41.2 us  [the longest x1 13.5 us: shards(): far_r = lax.ppermute(own[0], 'yh', swap)]
    ppermute x0 -> x13, starting transfers between devices: none -> 24.7 us  [the longest x3 12 us: shards(): from_above = lax.ppermute(from_above, 'z', down)]
    pallas_call x0 -> x1, Pallas kernels: none -> 14.3 us  [shards(): pl.pallas_call(cluster_kernel, out_shape=(piece, piece), in_specs=[pl.Blo...]
    all_to_all x0 -> x1, waiting for transfers between devices: none -> 11.2 us  [shards(): arrived = lax.all_to_all(sums, ('yh', 'z'), 0, 0, tiled=True)]
    another operation x1 -> x0, other arithmetic: 10.2 us -> none  [shards(): jnp.stack([cosines * w_real - sines * w_imag, sines * w_real + cosines *...]
    all_to_all x0 -> x1, starting transfers between devices: none -> 6.81 us  [shards(): arrived = lax.all_to_all(sums, ('yh', 'z'), 0, 0, tiled=True)]
  transfers between devices with their start and end apart: 3 -> 14, of which waited for: 3 -> 7; matrix products, arithmetic and copies ran while one was open for 1% -> 5% of each run, Pallas kernels for 0% -> 0%
where the time goes in v1:
time: 109 us; the launch traced here: 108 us
  waiting for transfers between devices  52.5 us (48%)
  starting transfers between devices  31.5 us (29%)
  Pallas kernels  14.3 us (13%)
  local copies, waits for them, and re-layouts  7.28 us (7%)
  other arithmetic  2.45 us (2%)
    pallas_call x1, Pallas kernels, shards(): pl.pallas_call(cluster_kernel, out_shape=(piece, piece), in_specs=[pl.Blo...  14.3 us
    ppermute x1, waiting for transfers between devices, shards(): far_r = lax.ppermute(own[0], 'yh', swap)  13.5 us
    ppermute x4, waiting for transfers between devices, shards(): from_below = lax.ppermute(from_below, 'z', up)  13.3 us
    ppermute x1, waiting for transfers between devices, shards(): far_i = lax.ppermute(own[1], 'yh', swap)  12.8 us
    ppermute x3, starting transfers between devices, shards(): from_above = lax.ppermute(from_above, 'z', down)  12 us
    all_to_all x1, waiting for transfers between devices, shards(): arrived = lax.all_to_all(sums, ('yh', 'z'), 0, 0, tiled=True)  11.2 us
    all_to_all x1, starting transfers between devices, shards(): arrived = lax.all_to_all(sums, ('yh', 'z'), 0, 0, tiled=True)  6.81 us
    ppermute x1, starting transfers between devices, shards(): diag_i = lax.ppermute(far_i, 'core', swap)  3.33 us
  transfers between devices with their start and end apart: 14, of which 7 were waited for; matrix products, arithmetic and copies ran while one was open for 5% of the time, Pallas kernels for 0%

profile of v1, /device:TPU:1, one launch (start us, length us, event | category | flops | bytes accessed | tf_op | source)
XLA Modules:
  0.0 108.3 jit_solution(14596785971679402765)
XLA Ops:
  0.0 1.0 constant_dynamic-slice_fusion
  1.1 6.5 %collective-permute-start.6 = (bf16[40,2400]{1,0:T(8,128)(2,1)S(1)}, bf16[40,2400]{1,0:T(8,128)(2,1)S(1)}, u32[]{:S(2)}, u32[]{:S(2)}) collective-permute-start(bf16[40,2400]{1,0:T(8,128)(2,1)S(1)} %reshape.211.refs_0_), channel_id=1, source_target_pairs={{16,0},{32,16},{48,32},{64,48},{80,64},{96,80},{112,96},{0,112},{1... | collective-permute-start | bytes 576008 | tf_op jit(solution)/shard_map/ppermute | solution.py:103
  7.6 1.5 %slice_bitcast_fusion = (bf16[160,2400]{1,0:T(8,128)(2,1)S(1)}, bf16[160,2400]{1,0:T(8,128)(2,1)S(1)}) fusion(bf16[1,2,160,2400]{3,2,1,0:T(8,128)(2,1)} %param.9), kind=kLoop, calls=%fused_computation.4 | loop fusion | bytes 3072000 | tf_op jit(solution)/shard_map/squeeze | solution.py:93
  9.1 3.0 %collective-permute-start.2 = (bf16[160,2400]{1,0:T(8,128)(2,1)S(1)}, bf16[160,2400]{1,0:T(8,128)(2,1)S(1)}, u32[]{:S(2)}, u32[]{:S(2)}) collective-permute-start(bf16[160,2400]{1,0:T(8,128)(2,1)S(1)} %get-tuple-element.13), channel_id=1, source_target_pairs={{0,128},{128,0},{1,129},{129,1},{2,130},{130,2},{3,131},{131,3},{4... | collective-permute-start | bytes 2304008 | tf_op jit(solution)/shard_map/ppermute | solution.py:93
  12.1 0.1 collective-permute-start.1
  12.2 1.5 %collective-permute-start = (bf16[2,160,2400]{2,1,0:T(8,128)(2,1)}, bf16[2,160,2400]{2,1,0:T(8,128)(2,1)}, u32[]{:S(2)}, u32[]{:S(2)}) collective-permute-start(bf16[2,160,2400]{2,1,0:T(8,128)(2,1)} %bitcast.1.own), channel_id=1, source_target_pairs={{0,8},{8,0},{1,9},{9,1},{2,10},{10,2},{3,11},{11,3},{4,12},{12,4},... | collective-permute-start | bytes 4608008 | tf_op jit(solution)/shard_map/ppermute | solution.py:91
  13.7 0.6 gather_fusion
  14.5 0.6 gather_fusion.1
  15.3 0.1 cosine_multiply_fusion
  15.8 12.8 %collective-permute-done.2.far_i = bf16[160,2400]{1,0:T(8,128)(2,1)S(1)} collective-permute-done((bf16[160,2400]{1,0:T(8,128)(2,1)S(1)}, bf16[160,2400]{1,0:T(8,128)(2,1)S(1)}, u32[]{:S(2)}, u32[]{:S(2)}) %collective-permute-start.2) | collective-permute-done | bytes 768032 | tf_op jit(solution)/shard_map/ppermute | solution.py:93
  28.6 3.3 %collective-permute-start.4 = (bf16[160,2400]{1,0:T(8,128)(2,1)S(1)}, bf16[160,2400]{1,0:T(8,128)(2,1)}, u32[]{:S(2)}, u32[]{:S(2)}) collective-permute-start(bf16[160,2400]{1,0:T(8,128)(2,1)S(1)} %collective-permute-done.2.far_i), channel_id=1, source_target_pairs={{0,8},{8,0},{1,9},{9,1},{2,10},{10,2},{3,11},{11,3},{4,12},{12,4},... | collective-permute-start | bytes 2304008 | tf_op jit(solution)/shard_map/ppermute | solution.py:95
  32.0 13.5 %collective-permute-done.1.far_r = bf16[160,2400]{1,0:T(8,128)(2,1)} collective-permute-done((bf16[160,2400]{1,0:T(8,128)(2,1)S(1)}, bf16[160,2400]{1,0:T(8,128)(2,1)}, u32[]{:S(2)}, u32[]{:S(2)}) %collective-permute-start.1) | collective-permute-done | bytes 768032 | tf_op jit(solution)/shard_map/ppermute | solution.py:92
  45.4 1.9 %collective-permute-start.3 = (bf16[160,2400]{1,0:T(8,128)(2,1)}, bf16[160,2400]{1,0:T(8,128)(2,1)}, u32[]{:S(2)}, u32[]{:S(2)}) collective-permute-start(bf16[160,2400]{1,0:T(8,128)(2,1)} %collective-permute-done.1.far_r), channel_id=1, source_target_pairs={{0,8},{8,0},{1,9},{9,1},{2,10},{10,2},{3,11},{11,3},{4,12},{12,4},... | collective-permute-start | bytes 2304008 | tf_op jit(solution)/shard_map/ppermute | solution.py:94
  47.3 0.7 gather_fusion.2
  48.2 0.2 broadcast_in_dim_reshape.6.refs_8_
  48.5 2.7 %collective-permute-start.8 = (bf16[40,2400]{1,0:T(8,128)(2,1)S(1)}, bf16[40,2400]{1,0:T(8,128)(2,1)S(1)}, u32[]{:S(2)}, u32[]{:S(2)}) collective-permute-start(bf16[40,2400]{1,0:T(8,128)(2,1)S(1)} %collective-permute-done.6.refs_2_), channel_id=1, source_target_pairs={{16,0},{32,16},{48,32},{64,48},{80,64},{96,80},{112,96},{0,112},{1... | collective-permute-start | bytes 576008 | tf_op jit(solution)/shard_map/ppermute | solution.py:103
  51.2 4.5 %collective-permute-done.7.refs_3_ = bf16[40,2400]{1,0:T(8,128)(2,1)S(1)} collective-permute-done((bf16[40,2400]{1,0:T(8,128)(2,1)S(1)}, bf16[40,2400]{1,0:T(8,128)(2,1)S(1)}, u32[]{:S(2)}, u32[]{:S(2)}) %collective-permute-start.7) | collective-permute-done | bytes 192032 | tf_op jit(solution)/shard_map/ppermute | solution.py:99
  55.8 1.0 multiply_add_fusion
  56.8 2.7 %collective-permute-start.10 = (bf16[40,2400]{1,0:T(8,128)(2,1)S(1)}, bf16[40,2400]{1,0:T(8,128)(2,1)S(1)}, u32[]{:S(2)}, u32[]{:S(2)}) collective-permute-start(bf16[40,2400]{1,0:T(8,128)(2,1)S(1)} %collective-permute-done.8.refs_4_), channel_id=1, source_target_pairs={{16,0},{32,16},{48,32},{64,48},{80,64},{96,80},{112,96},{0,112},{1... | collective-permute-start | bytes 576008 | tf_op jit(solution)/shard_map/ppermute | solution.py:103
  59.5 3.1 %collective-permute-done.9.refs_5_ = bf16[40,2400]{1,0:T(8,128)(2,1)S(1)} collective-permute-done((bf16[40,2400]{1,0:T(8,128)(2,1)S(1)}, bf16[40,2400]{1,0:T(8,128)(2,1)S(1)}, u32[]{:S(2)}, u32[]{:S(2)}) %collective-permute-start.9) | collective-permute-done | bytes 192032 | tf_op jit(solution)/shard_map/ppermute | solution.py:99
  62.6 5.7 %collective-permute-done.11.refs_7_ = bf16[40,2400]{1,0:T(8,128)(2,1)S(1)} collective-permute-done((bf16[40,2400]{1,0:T(8,128)(2,1)S(1)}, bf16[40,2400]{1,0:T(8,128)(2,1)S(1)}, u32[]{:S(2)}, u32[]{:S(2)}) %collective-permute-start.11) | collective-permute-done | bytes 192032 | tf_op jit(solution)/shard_map/ppermute | solution.py:99
  68.3 0.7 copy-done.1
  69.0 14.3 %cluster_terms.1 = (f32[16,80,75]{2,1,0:T(8,128)S(1)}, f32[16,80,75]{2,1,0:T(8,128)S(1)}) custom-call(s32[1]{0:T(128)} %bitcast.core_ref, bf16[2,160,2400]{2,1,0:T(8,128)(2,1)} %bitcast.1.own, bf16[2,160,2400]{2,1,0:T(8,128)(2,1)} %collective-permute-done.near, bf16[160,2400]{1,0:T(8,128)(2,1)} %collective-permute-done.1.far_r, ...), custom_call_target="tpu_custom_call" | custom-call | flops 3000000000 | bytes 10000000 | tf_op jit(solution)/shard_map/cluster_terms/pallas_call | solution.py:130
  83.3 0.3 copy.16
  83.6 2.9 %collective-permute-start.12 = (f32[16,80,75]{1,0,2:T(8,128)S(1)}, f32[16,80,75]{1,0,2:T(8,128)S(1)}, u32[]{:S(2)}, u32[]{:S(2)}) collective-permute-start(f32[16,80,75]{1,0,2:T(8,128)S(1)} %copy.16), channel_id=1, source_target_pairs={{0,8},{8,0},{1,9},{9,1},{2,10},{10,2},{3,11},{11,3},{4,12},{12,4},... | collective-permute-start | bytes 1152008 | tf_op jit(solution)/shard_map/ppermute | solution.py:145
  86.5 1.7 %collective-permute-done.12 = f32[16,80,75]{1,0,2:T(8,128)S(1)} collective-permute-done((f32[16,80,75]{1,0,2:T(8,128)S(1)}, f32[16,80,75]{1,0,2:T(8,128)S(1)}, u32[]{:S(2)}, u32[]{:S(2)}) %collective-permute-start.12) | collective-permute-done | bytes 384032 | tf_op jit(solution)/shard_map/ppermute | solution.py:145
  88.2 0.3 copy.17
  88.5 0.8 add_convert_fusion
  89.3 6.8 %all-to-all-start = ((bf16[16,80,75]{2,1,0:T(8,128)(2,1)}), bf16[16,80,75]{2,1,0:T(8,128)(2,1)S(1)}, u32[]{:S(2)}, u32[]{:S(2)}) async-start(bf16[16,80,75]{2,1,0:T(8,128)(2,1)} %add_convert_fusion), calls=%async_computation | async-start | bytes 655360 | tf_op jit(solution)/shard_map/all_to_all | solution.py:146
  96.2 0.1 convolution_bitcast_fusion
  96.3 11.2 %all-to-all-done = bf16[16,80,75]{2,1,0:T(8,128)(2,1)S(1)} async-done(((bf16[16,80,75]{2,1,0:T(8,128)(2,1)}), bf16[16,80,75]{2,1,0:T(8,128)(2,1)S(1)}, u32[]{:S(2)}, u32[]{:S(2)}) %all-to-all-start) | async-done | bytes 192032 | tf_op jit(solution)/shard_map/all_to_all | solution.py:146
  107.6 0.6 copy.18
  (48 shorter events, 1.3 us)
Async XLA Ops:
  0.0 13.7 %copy-start = (s32[32,32]{1,0:T(8,128)S(1)}, s32[32,32]{1,0:T(8,128)}, u32[]{:S(2)}) copy-start(s32[32,32]{1,0:T(8,128)} %param.11) | copy-start | bytes 12292
  1.1 12.6 %copy-start.5 = (s32[8]{0:T(128)S(1)}, s32[8]{0:T(128)}, u32[]{:S(2)}) copy-start(s32[8]{0:T(128)} %constant.134.clone) | copy-start | bytes 100
  1.1 14.2 %copy-start.4 = (s32[2]{0:T(128)S(1)}, s32[2]{0:T(128)}, u32[]{:S(2)}) copy-start(s32[2]{0:T(128)} %param.12) | copy-start | bytes 28
  1.1 46.2 %copy-start.2 = (f32[32]{0:T(128)S(1)}, f32[32]{0:T(128)}, u32[]{:S(2)}) copy-start(f32[32]{0:T(128)} %param.10) | copy-start | bytes 388
  1.1 47.4 %collective-permute-start.6 = (bf16[40,2400]{1,0:T(8,128)(2,1)S(1)}, bf16[40,2400]{1,0:T(8,128)(2,1)S(1)}, u32[]{:S(2)}, u32[]{:S(2)}) collective-permute-start(bf16[40,2400]{1,0:T(8,128)(2,1)S(1)} %reshape.211.refs_0_), channel_id=1, source_target_pairs={{16,0},{32,16},{48,32},{64,48},{80,64},{96,80},{112,96},{0,112},{1... | collective-permute-start | bytes 576008 | tf_op jit(solution)/shard_map/ppermute | solution.py:103
  7.6 40.4 %collective-permute-start.5 = (bf16[40,2400]{1,0:T(8,128)(2,1)S(1)}, bf16[40,2400]{1,0:T(8,128)(2,1)S(1)}, u32[]{:S(2)}, u32[]{:S(2)}) collective-permute-start(bf16[40,2400]{1,0:T(8,128)(2,1)S(1)} %reshape.211.refs_0_), channel_id=1, source_target_pairs={{0,16},{16,32},{32,48},{48,64},{64,80},{80,96},{96,112},{112,0},{1... | collective-permute-start | bytes 576008 | tf_op jit(solution)/shard_map/ppermute | solution.py:99
  9.1 46.7 %copy-start.3 = (f32[2,2,40,320]{3,2,1,0:T(8,128)S(1)}, f32[2,2,40,320]{3,2,1,0:T(8,128)}, u32[]{:S(2)}) copy-start(f32[2,2,40,320]{3,2,1,0:T(8,128)} %constant.136.clone) | copy-start | bytes 614404
  9.1 19.5 %collective-permute-start.2 = (bf16[160,2400]{1,0:T(8,128)(2,1)S(1)}, bf16[160,2400]{1,0:T(8,128)(2,1)S(1)}, u32[]{:S(2)}, u32[]{:S(2)}) collective-permute-start(bf16[160,2400]{1,0:T(8,128)(2,1)S(1)} %get-tuple-element.13), channel_id=1, source_target_pairs={{0,128},{128,0},{1,129},{129,1},{2,130},{130,2},{3,131},{131,3},{4... | collective-permute-start | bytes 2304008 | tf_op jit(solution)/shard_map/ppermute | solution.py:93
  12.1 33.3 %collective-permute-start.1 = (bf16[160,2400]{1,0:T(8,128)(2,1)S(1)}, bf16[160,2400]{1,0:T(8,128)(2,1)}, u32[]{:S(2)}, u32[]{:S(2)}) collective-permute-start(bf16[160,2400]{1,0:T(8,128)(2,1)S(1)} %get-tuple-element.14), channel_id=1, source_target_pairs={{0,128},{128,0},{1,129},{129,1},{2,130},{130,2},{3,131},{131,3},{4... | collective-permute-start | bytes 2304008 | tf_op jit(solution)/shard_map/ppermute | solution.py:92
  12.2 56.1 %collective-permute-start = (bf16[2,160,2400]{2,1,0:T(8,128)(2,1)}, bf16[2,160,2400]{2,1,0:T(8,128)(2,1)}, u32[]{:S(2)}, u32[]{:S(2)}) collective-permute-start(bf16[2,160,2400]{2,1,0:T(8,128)(2,1)} %bitcast.1.own), channel_id=1, source_target_pairs={{0,8},{8,0},{1,9},{9,1},{2,10},{10,2},{3,11},{11,3},{4,12},{12,4},... | collective-permute-start | bytes 4608008 | tf_op jit(solution)/shard_map/ppermute | solution.py:91
  28.6 39.7 %collective-permute-start.4 = (bf16[160,2400]{1,0:T(8,128)(2,1)S(1)}, bf16[160,2400]{1,0:T(8,128)(2,1)}, u32[]{:S(2)}, u32[]{:S(2)}) collective-permute-start(bf16[160,2400]{1,0:T(8,128)(2,1)S(1)} %collective-permute-done.2.far_i), channel_id=1, source_target_pairs={{0,8},{8,0},{1,9},{9,1},{2,10},{10,2},{3,11},{11,3},{4,12},{12,4},... | collective-permute-start | bytes 2304008 | tf_op jit(solution)/shard_map/ppermute | solution.py:95
  45.4 22.9 %collective-permute-start.3 = (bf16[160,2400]{1,0:T(8,128)(2,1)}, bf16[160,2400]{1,0:T(8,128)(2,1)}, u32[]{:S(2)}, u32[]{:S(2)}) collective-permute-start(bf16[160,2400]{1,0:T(8,128)(2,1)} %collective-permute-done.1.far_r), channel_id=1, source_target_pairs={{0,8},{8,0},{1,9},{9,1},{2,10},{10,2},{3,11},{11,3},{4,12},{12,4},... | collective-permute-start | bytes 2304008 | tf_op jit(solution)/shard_map/ppermute | solution.py:94
  48.1 7.7 %collective-permute-start.7 = (bf16[40,2400]{1,0:T(8,128)(2,1)S(1)}, bf16[40,2400]{1,0:T(8,128)(2,1)S(1)}, u32[]{:S(2)}, u32[]{:S(2)}) collective-permute-start(bf16[40,2400]{1,0:T(8,128)(2,1)S(1)} %collective-permute-done.5.refs_1_), channel_id=1, source_target_pairs={{0,16},{16,32},{32,48},{48,64},{64,80},{80,96},{96,112},{112,0},{1... | collective-permute-start | bytes 576008 | tf_op jit(solution)/shard_map/ppermute | solution.py:99
  48.5 8.3 %collective-permute-start.8 = (bf16[40,2400]{1,0:T(8,128)(2,1)S(1)}, bf16[40,2400]{1,0:T(8,128)(2,1)S(1)}, u32[]{:S(2)}, u32[]{:S(2)}) collective-permute-start(bf16[40,2400]{1,0:T(8,128)(2,1)S(1)} %collective-permute-done.6.refs_2_), channel_id=1, source_target_pairs={{16,0},{32,16},{48,32},{64,48},{80,64},{96,80},{112,96},{0,112},{1... | collective-permute-start | bytes 576008 | tf_op jit(solution)/shard_map/ppermute | solution.py:103
  55.8 6.8 %collective-permute-start.9 = (bf16[40,2400]{1,0:T(8,128)(2,1)S(1)}, bf16[40,2400]{1,0:T(8,128)(2,1)S(1)}, u32[]{:S(2)}, u32[]{:S(2)}) collective-permute-start(bf16[40,2400]{1,0:T(8,128)(2,1)S(1)} %collective-permute-done.7.refs_3_), channel_id=1, source_target_pairs={{0,16},{16,32},{32,48},{48,64},{64,80},{80,96},{96,112},{112,0},{1... | collective-permute-start | bytes 576008 | tf_op jit(solution)/shard_map/ppermute | solution.py:99
  56.8 5.8 %collective-permute-start.10 = (bf16[40,2400]{1,0:T(8,128)(2,1)S(1)}, bf16[40,2400]{1,0:T(8,128)(2,1)S(1)}, u32[]{:S(2)}, u32[]{:S(2)}) collective-permute-start(bf16[40,2400]{1,0:T(8,128)(2,1)S(1)} %collective-permute-done.8.refs_4_), channel_id=1, source_target_pairs={{16,0},{32,16},{48,32},{64,48},{80,64},{96,80},{112,96},{0,112},{1... | collective-permute-start | bytes 576008 | tf_op jit(solution)/shard_map/ppermute | solution.py:103
  62.6 5.7 %collective-permute-start.11 = (bf16[40,2400]{1,0:T(8,128)(2,1)S(1)}, bf16[40,2400]{1,0:T(8,128)(2,1)S(1)}, u32[]{:S(2)}, u32[]{:S(2)}) collective-permute-start(bf16[40,2400]{1,0:T(8,128)(2,1)S(1)} %collective-permute-done.9.refs_5_), channel_id=1, source_target_pairs={{0,16},{16,32},{32,48},{48,64},{64,80},{80,96},{96,112},{112,0},{1... | collective-permute-start | bytes 576008 | tf_op jit(solution)/shard_map/ppermute | solution.py:99
  68.3 0.7 copy-start.1
  83.6 12.6 %copy-start.6 = (s32[2,30]{1,0:T(2,128)S(1)}, s32[2,30]{1,0:T(2,128)}, u32[]{:S(2)}) copy-start(s32[2,30]{1,0:T(2,128)} %param.13) | copy-start | bytes 724
  83.6 4.6 %collective-permute-start.12 = (f32[16,80,75]{1,0,2:T(8,128)S(1)}, f32[16,80,75]{1,0,2:T(8,128)S(1)}, u32[]{:S(2)}, u32[]{:S(2)}) collective-permute-start(f32[16,80,75]{1,0,2:T(8,128)S(1)} %copy.16), channel_id=1, source_target_pairs={{0,8},{8,0},{1,9},{9,1},{2,10},{10,2},{3,11},{11,3},{4,12},{12,4},... | collective-permute-start | bytes 1152008 | tf_op jit(solution)/shard_map/ppermute | solution.py:145
  89.3 18.2 %all-to-all-start = ((bf16[16,80,75]{2,1,0:T(8,128)(2,1)}), bf16[16,80,75]{2,1,0:T(8,128)(2,1)S(1)}, u32[]{:S(2)}, u32[]{:S(2)}) async-start(bf16[16,80,75]{2,1,0:T(8,128)(2,1)} %add_convert_fusion), calls=%async_computation | async-start | bytes 655360 | tf_op jit(solution)/shard_map/all_to_all | solution.py:146

commit v2 on v1

v2 whole, which is shorter than its diff:
```python
import jax
import jax.numpy as jnp
import numpy as np
from jax import lax
from jax.experimental import pallas as pl
from jax.experimental.pallas import tpu as pltpu
from jax.sharding import Mesh
from jax.sharding import PartitionSpec as P

AXES = ("yh", "z", "core", "yl", "x")
KA = ("yh", "z", "core")
BAND = ("yl", "x")
PARTS = (2, 8, 2, 2, 4)
F32 = jnp.float32
BF16 = jnp.bfloat16


def phase_signs(width, blocks):
    rows = np.arange(8 * width)
    cols = np.arange(2 * blocks * width)
    partner, part = (rows // (4 * width))[:, None], (rows // width % 2)[:, None]
    part_m = (cols // width % 2)[None, :]
    same = (rows % width)[:, None] == (cols % width)[None, :]
    real = np.where(partner == 0, part == 0, part == 1)
    sign = np.where((partner == 1) & (part == 0), -1, 1)
    cos_sign = same * sign * np.where(real, part_m == 0, part_m == 1)
    sin_sign = same * sign * np.where(real, -1 * (part_m == 1), part_m == 0)
    return cos_sign.astype(np.float32), sin_sign.astype(np.float32)


def cluster_kernel(core_ref, own, far, b0, b1, b2, b3, w_own, w_far, g, mine, other, b_ref, u_ref):
    at = 0
    for part in (b0, b1, b2, b3):
        b_ref[pl.ds(at, part.shape[0]), :] = part[...]
        at += part.shape[0]
    k_rows = b_ref.shape[0]
    width = u_ref.shape[0] // 4
    outs = 8 * width
    occupied = own.shape[1]
    contract = (((1,), (1,)), ((), ()))
    is_real = lax.broadcasted_iota(jnp.int32, (k_rows, occupied), 0) % (2 * width) < width
    ms = []
    for q_ref, w in ((own, w_own), (far, w_far)):
        m = lax.dot_general(b_ref[...], q_ref[0], contract, preferred_element_type=F32)
        turn = lax.dot_general(b_ref[...], q_ref[1], contract, preferred_element_type=F32)
        turn = jnp.where(is_real, pltpu.roll(turn, k_rows - width, 0), -pltpu.roll(turn, width, 0))
        ms.append((w[...] * (m + turn)).astype(BF16))
    us = []
    for q_ref, m in zip((own, far), ms):
        t = jnp.dot(g[...], m, preferred_element_type=F32)
        t = t[:outs] + t[outs:]
        t_high = t.astype(BF16)
        t_low = (t - t_high.astype(F32)).astype(BF16)
        half = outs // 2
        for part in range(2):
            rows = slice(part * half, (part + 1) * half)
            pair = jnp.concatenate([t_high[rows], t_low[rows]], 0)
            us.append(jnp.dot(pair, q_ref[part], preferred_element_type=F32))
    u = (us[0] + us[1]) + (us[2] + us[3])
    u_ref[...] = u[: outs // 2] + u[outs // 2 :]
    chips, _, columns = mine.shape
    for core in range(2):

        @pl.when(core_ref[0] == core)
        def _():
            for chip in range(chips):
                at = (2 * chip + core) * columns
                mine[chip] = u_ref[:, at : at + columns]
                at = (2 * chip + 1 - core) * columns
                other[chip] = u_ref[:, at : at + columns]


def shards(coefficients, class_weight, diff_class, frag_cells, block_pattern):
    own = coefficients[0]
    _, occupied, functions = own.shape
    yh, z, core = (lax.axis_index(name) for name in KA)
    band = lax.axis_index("yl") * PARTS[4] + lax.axis_index("x")
    width = occupied // (PARTS[3] * PARTS[4])
    kpoint_count = PARTS[0] * PARTS[1] * PARTS[2]
    up = [(i, (i + 1) % PARTS[1]) for i in range(PARTS[1])]
    down = [(j, i) for i, j in up]
    swap = [(0, 1), (1, 0)]

    block = lax.dynamic_slice_in_dim(own, band * width, width, 1).reshape(2 * width, functions)
    far = lax.ppermute(own, "yh", swap)
    blocks = [block]
    offsets = [0, -1, 1, -2, 2, -3, 3, -4]
    from_below = from_above = block
    for step in range(1, PARTS[1] // 2 + 1):
        from_below = lax.ppermute(from_below, "z", up)
        blocks.append(from_below)
        if step < PARTS[1] // 2:
            from_above = lax.ppermute(from_above, "z", down)
            blocks.append(from_above)
    split = 5
    first = jnp.concatenate(blocks[:split], 0)
    first_near = lax.ppermute(first, "core", swap)
    last = jnp.concatenate(blocks[split:], 0)
    last_near = lax.ppermute(last, "core", swap)

    order = offsets[:split] * 2 + offsets[split:] * 2
    cores = [0] * split + [1] * split + [0] * (len(offsets) - split) + [1] * (len(offsets) - split)
    cores = jnp.bitwise_xor(jnp.array(cores, jnp.int32), core)
    kpoints = (yh * PARTS[1] + jnp.bitwise_and(z + jnp.array(order, jnp.int32), PARTS[1] - 1)) * 2 + cores
    all_points = jnp.arange(kpoint_count, dtype=jnp.int32)
    high = lax.Precision.HIGHEST
    classes = (diff_class[:, :, None] == all_points).astype(F32)
    pair_weight = jnp.sum(classes * class_weight, axis=2)
    k_onehot = (kpoints[:, None] == all_points).astype(F32)
    q_points = (jnp.stack([yh, 1 - yh]) * PARTS[1] + z) * 2 + core
    q_onehot = (q_points[:, None] == all_points).astype(F32)
    weights = jnp.einsum("ka,ab,qb->qk", k_onehot, pair_weight, q_onehot, precision=high) / functions
    weights = jnp.repeat(weights, 2 * width, axis=1)[:, :, None]

    phase_index = frag_cells[:, None] * kpoints[None, :] % kpoint_count
    angles = 2.0 * jnp.pi * phase_index.astype(F32) / kpoint_count
    cells = frag_cells.shape[0]
    full = (2, cells, 2 * width, 2 * width * kpoints.shape[0])
    cosines = jnp.repeat(jnp.cos(angles) / kpoint_count, 2 * width, axis=1)[None, :, None, :]
    sines = jnp.repeat(jnp.sin(angles) / kpoint_count, 2 * width, axis=1)[None, :, None, :]
    cos_sign, sin_sign = (jnp.asarray(a.reshape(full)) for a in phase_signs(width, kpoints.shape[0]))
    g = (cos_sign * cosines + sin_sign * sines).reshape(8 * width, -1)
    g_high = g.astype(BF16)
    g_low = (g - g_high.astype(F32)).astype(BF16)
    g = jnp.concatenate([g_high, g_low], 0)

    chips = PARTS[0] * PARTS[1]
    columns = functions // kpoint_count
    piece = jax.ShapeDtypeStruct((chips, 4 * width, columns), F32)
    mine, other = pl.pallas_call(
        cluster_kernel,
        out_shape=(piece, piece),
        in_specs=[pl.BlockSpec(memory_space=pltpu.SMEM)] + [pl.BlockSpec(memory_space=pltpu.VMEM)] * 9,
        out_specs=(pl.BlockSpec(memory_space=pltpu.VMEM),) * 2,
        scratch_shapes=[
            pltpu.VMEM((2 * width * kpoints.shape[0], functions), BF16),
            pltpu.VMEM((4 * width, functions), F32),
        ],
        compiler_params=pltpu.CompilerParams(vmem_limit_bytes=32 * 2**20),
        cost_estimate=pl.CostEstimate(flops=3 * 10**9, bytes_accessed=10**7, transcendentals=0),
        name="cluster_terms",
    )(core[None], own, far, first, first_near, last, last_near, weights[0], weights[1], g)

    sums = mine + lax.ppermute(other, "core", swap)
    arrived = lax.all_to_all(sums, ("yh", "z"), 0, 0, tiled=True)
    cluster = jnp.sum(arrived, axis=0).reshape(cells, 2, width, columns)
    index = (yh * PARTS[1] + z) * 2 + core
    block_size = functions // block_pattern.shape[1]
    local_ids = (index * columns + jnp.arange(columns, dtype=jnp.int32)) // block_size
    block_ids = jnp.arange(block_pattern.shape[1], dtype=jnp.int32)
    onehot = (block_ids[:, None] == local_ids[None, :]).astype(F32)
    mask = jnp.dot(block_pattern.astype(F32), onehot, precision=high)
    return cluster * mask[:, None, None, :]


def solution(mesh):
    placed = (P(KA, None, None, None), P(), P(), P(), P())
    return jax.shard_map(
        shards,
        mesh=Mesh(mesh.devices.reshape(PARTS), AXES),
        in_specs=placed,
        out_specs=P(None, None, BAND, KA),
        check_vma=False,
    )
```

time: 109 us -> 82.8 us (0.76)
  waiting for transfers between devices: 52.5 us -> 35.3 us
  Pallas kernels: 14.3 us -> 6.43 us
  local copies, waits for them, and re-layouts: 7.28 us -> 4.34 us
  other arithmetic: 2.45 us -> 3.76 us
    ppermute x6 -> x4, waiting for transfers between devices: 28 us -> 5.56 us  [the longest x1 2.42 us: shards(): far = lax.ppermute(own, 'yh', swap)]
    pallas_call x1, Pallas kernels: 14.3 us -> 6.43 us  [shards(): pl.pallas_call(cluster_kernel, out_shape=(piece, piece), in_specs=[pl.Blo...]
    all_to_all x1, waiting for transfers between devices: 11.2 us -> 18.3 us  [shards(): arrived = lax.all_to_all(sums, ('yh', 'z'), 0, 0, tiled=True)]
    ppermute x4, waiting for transfers between devices: 13.3 us -> 7.45 us  [shards(): from_below = lax.ppermute(from_below, 'z', up)]
    ppermute x3, waiting for transfers between devices: 0.01 us -> 3.95 us  [shards(): from_above = lax.ppermute(from_above, 'z', down)]
    gather x4 -> x0, local copies, waits for them, and re-layouts: 1.9 us -> none  [the longest x2 1.12 us: shards(): picked = jnp.take(jnp.take(diff_class, kpoints, axis=0), q_points, axis=1)]
    add x0 -> x3, other arithmetic: none -> 1.67 us  [the longest x1 0.91 us: shards(): sums = mine + lax.ppermute(other, 'core', swap)]
    squeeze x1 -> x0, local copies, waits for them, and re-layouts: 1.47 us -> none  [shards(): far_i = lax.ppermute(own[1], 'yh', swap)]
  transfers between devices with their start and end apart: 14 -> 12, of which waited for: 7 -> 8; matrix products, arithmetic and copies ran while one was open for 5% -> 6% of each run, Pallas kernels for 0% -> 0%
where the time goes in v2:
time: 82.8 us; the launch traced here: 81.5 us
  waiting for transfers between devices  35.3 us (43%)
  starting transfers between devices  31 us (37%)
  Pallas kernels  6.43 us (8%)
  local copies, waits for them, and re-layouts  4.34 us (5%)
  other arithmetic  3.76 us (5%)
    all_to_all x1, waiting for transfers between devices, shards(): arrived = lax.all_to_all(sums, ('yh', 'z'), 0, 0, tiled=True)  18.3 us
    ppermute x3, starting transfers between devices, shards(): from_above = lax.ppermute(from_above, 'z', down)  12.2 us
    ppermute x4, waiting for transfers between devices, shards(): from_below = lax.ppermute(from_below, 'z', up)  7.45 us
    all_to_all x1, starting transfers between devices, shards(): arrived = lax.all_to_all(sums, ('yh', 'z'), 0, 0, tiled=True)  6.81 us
    pallas_call x1, Pallas kernels, shards(): pl.pallas_call(cluster_kernel, out_shape=(piece, piece), in_specs=[pl.Blo...  6.43 us
    ppermute x1, starting transfers between devices, shards(): last_near = lax.ppermute(last, 'core', swap)  4.45 us
    ppermute x3, waiting for transfers between devices, shards(): from_above = lax.ppermute(from_above, 'z', down)  3.95 us
    ppermute x1, starting transfers between devices, shards(): far = lax.ppermute(own, 'yh', swap)  2.91 us
  transfers between devices with their start and end apart: 12, of which 8 were waited for; matrix products, arithmetic and copies ran while one was open for 6% of the time, Pallas kernels for 0%

profile of v2, /device:TPU:1, one launch (start us, length us, event | category | flops | bytes accessed | tf_op | source)
XLA Modules:
  0.0 81.5 jit_solution(4330947420717118706)
XLA Ops:
  0.0 1.0 %constant_dynamic-slice_fusion = bf16[1,2,20,2400]{3,2,1,0:T(8,128)(2,1)S(1)} fusion(bf16[1,2,160,2400]{3,2,1,0:T(8,128)(2,1)} %param.9, s32[]{:T(128)S(6)} %select_n.19), kind=kLoop, calls=%fused_computation.43 | loop fusion | bytes 384004 | tf_op jit(solution)/shard_map/dynamic_slice | solution.py:84
  1.1 6.5 %collective-permute-start.2 = (bf16[40,2400]{1,0:T(8,128)(2,1)S(1)}, bf16[40,2400]{1,0:T(8,128)(2,1)S(1)}, u32[]{:S(2)}, u32[]{:S(2)}) collective-permute-start(bf16[40,2400]{1,0:T(8,128)(2,1)S(1)} %reshape.63), channel_id=1, source_target_pairs={{16,0},{32,16},{48,32},{64,48},{80,64},{96,80},{112,96},{0,112},{1... | collective-permute-start | bytes 576008 | tf_op jit(solution)/shard_map/ppermute | solution.py:93
  7.6 2.9 %collective-permute-start = (bf16[2,160,2400]{2,1,0:T(8,128)(2,1)}, bf16[2,160,2400]{2,1,0:T(8,128)(2,1)S(1)}, u32[]{:S(2)}, u32[]{:S(2)}) collective-permute-start(bf16[2,160,2400]{2,1,0:T(8,128)(2,1)} %bitcast.18), channel_id=1, source_target_pairs={{0,128},{128,0},{1,129},{129,1},{2,130},{130,2},{3,131},{131,3},{4... | collective-permute-start | bytes 4608008 | tf_op jit(solution)/shard_map/ppermute | solution.py:85
  10.5 0.7 xor_add_fusion
  11.2 0.8 cosine_multiply_fusion
  12.0 0.1 mul.95
  12.4 1.1 %select_reduce_fusion = f32[32,32]{1,0:T(8,128)S(1)} fusion(f32[32]{0:T(128)} %param.10, s32[32,32]{1,0:T(8,128)} %param.11), kind=kLoop, calls=%fused_computation.2 | loop fusion | flops 97280 | bytes 8320 | tf_op jit(solution)/shard_map/reduce_sum | solution.py:108
  13.5 0.2 fusion.3
  13.7 0.2 convolution_multiply_fusion
  13.9 0.2 broadcast_in_dim.37.w_own
  14.2 0.2 broadcast_in_dim.38.w_far
  14.4 2.8 %collective-permute-start.4 = (bf16[40,2400]{1,0:T(8,128)(2,1)S(1)}, bf16[40,2400]{1,0:T(8,128)(2,1)S(1)}, u32[]{:S(2)}, u32[]{:S(2)}) collective-permute-start(bf16[40,2400]{1,0:T(8,128)(2,1)S(1)} %collective-permute-done.2), channel_id=1, source_target_pairs={{16,0},{32,16},{48,32},{64,48},{80,64},{96,80},{112,96},{0,112},{1... | collective-permute-start | bytes 576008 | tf_op jit(solution)/shard_map/ppermute | solution.py:93
  17.2 1.0 %constant_dynamic-update-slice_fusion.3 = bf16[200,2400]{1,0:T(8,128)(2,1)S(1)} fusion(bf16[200,2400]{1,0:T(8,128)(2,1)S(1)} %constant_dynamic-update-slice_fusion.4, bf16[40,2400]{1,0:T(8,128)(2,1)} %collective-permute-done.1), kind=kLoop, calls=%fused_computation.13 | loop fusion | bytes 386560
  18.2 5.2 %collective-permute-done.3 = bf16[40,2400]{1,0:T(8,128)(2,1)S(1)} collective-permute-done((bf16[40,2400]{1,0:T(8,128)(2,1)}, bf16[40,2400]{1,0:T(8,128)(2,1)S(1)}, u32[]{:S(2)}, u32[]{:S(2)}) %collective-permute-start.3) | collective-permute-done | bytes 192032 | tf_op jit(solution)/shard_map/ppermute | solution.py:90
  23.4 2.7 %collective-permute-start.5 = (bf16[200,2400]{1,0:T(8,128)(2,1)S(1)}, bf16[200,2400]{1,0:T(8,128)(2,1)S(1)}, u32[]{:S(2)}, u32[]{:S(2)}) collective-permute-start(bf16[200,2400]{1,0:T(8,128)(2,1)S(1)} %constant_dynamic-update-slice_fusion.b0), channel_id=1, source_target_pairs={{0,8},{8,0},{1,9},{9,1},{2,10},{10,2},{3,11},{11,3},{4,12},{12,4},... | collective-permute-start | bytes 2880008 | tf_op jit(solution)/shard_map/ppermute | solution.py:97
  26.2 3.0 %collective-permute-start.7 = (bf16[40,2400]{1,0:T(8,128)(2,1)S(1)}, bf16[40,2400]{1,0:T(8,128)(2,1)S(1)}, u32[]{:S(2)}, u32[]{:S(2)}) collective-permute-start(bf16[40,2400]{1,0:T(8,128)(2,1)S(1)} %collective-permute-done.4), channel_id=1, source_target_pairs={{16,0},{32,16},{48,32},{64,48},{80,64},{96,80},{112,96},{0,112},{1... | collective-permute-start | bytes 576008 | tf_op jit(solution)/shard_map/ppermute | solution.py:93
  29.1 0.2 collective-permute-done.6
  29.4 3.9 %collective-permute-done.7 = bf16[40,2400]{1,0:T(8,128)(2,1)S(1)} collective-permute-done((bf16[40,2400]{1,0:T(8,128)(2,1)S(1)}, bf16[40,2400]{1,0:T(8,128)(2,1)S(1)}, u32[]{:S(2)}, u32[]{:S(2)}) %collective-permute-start.7) | collective-permute-done | bytes 192032 | tf_op jit(solution)/shard_map/ppermute | solution.py:93
  33.4 2.0 %collective-permute-done.8 = bf16[40,2400]{1,0:T(8,128)(2,1)S(1)} collective-permute-done((bf16[40,2400]{1,0:T(8,128)(2,1)S(1)}, bf16[40,2400]{1,0:T(8,128)(2,1)S(1)}, u32[]{:S(2)}, u32[]{:S(2)}) %collective-permute-start.8) | collective-permute-done | bytes 192032 | tf_op jit(solution)/shard_map/ppermute | solution.py:90
  35.4 4.4 %collective-permute-start.9 = (bf16[120,2400]{1,0:T(8,128)(2,1)S(1)}, bf16[120,2400]{1,0:T(8,128)(2,1)S(1)}, u32[]{:S(2)}, u32[]{:S(2)}) collective-permute-start(bf16[120,2400]{1,0:T(8,128)(2,1)S(1)} %constant_dynamic-update-slice_fusion.5.b2), channel_id=1, source_target_pairs={{0,8},{8,0},{1,9},{9,1},{2,10},{10,2},{3,11},{11,3},{4,12},{12,4},... | collective-permute-start | bytes 1728008 | tf_op jit(solution)/shard_map/ppermute | solution.py:99
  40.0 1.5 %collective-permute-done.9.b3 = bf16[120,2400]{1,0:T(8,128)(2,1)S(1)} collective-permute-done((bf16[120,2400]{1,0:T(8,128)(2,1)S(1)}, bf16[120,2400]{1,0:T(8,128)(2,1)S(1)}, u32[]{:S(2)}, u32[]{:S(2)}) %collective-permute-start.9) | collective-permute-done | bytes 576032 | tf_op jit(solution)/shard_map/ppermute | solution.py:99
  41.5 2.4 %collective-permute-done.far = bf16[2,160,2400]{2,1,0:T(8,128)(2,1)S(1)} collective-permute-done((bf16[2,160,2400]{2,1,0:T(8,128)(2,1)}, bf16[2,160,2400]{2,1,0:T(8,128)(2,1)S(1)}, u32[]{:S(2)}, u32[]{:S(2)}) %collective-permute-start) | collective-permute-done | bytes 1536032 | tf_op jit(solution)/shard_map/ppermute | solution.py:85
  43.9 6.4 %cluster_terms.1 = (f32[16,80,75]{2,1,0:T(8,128)S(1)}, f32[16,80,75]{2,1,0:T(8,128)S(1)}) custom-call(s32[1]{0:T(128)} %bitcast.core_ref, bf16[2,160,2400]{2,1,0:T(8,128)(2,1)S(1)} %bitcast.19, bf16[2,160,2400]{2,1,0:T(8,128)(2,1)S(1)} %collective-permute-done.far, bf16[200,2400]{1,0:T(8,128)(2,1)S(1)} %constant_dynamic-update-slice_fusion.b0, ...), custom_call_target="tpu_custom_call" | custom-call | flops 3000000000 | bytes 10000000 | tf_op jit(solution)/shard_map/cluster_terms/pallas_call | solution.py:130
  50.3 0.3 copy.20
  50.7 1.9 %collective-permute-start.10 = (f32[16,80,75]{1,0,2:T(8,128)S(1)}, f32[16,80,75]{1,0,2:T(8,128)S(1)}, u32[]{:S(2)}, u32[]{:S(2)}) collective-permute-start(f32[16,80,75]{1,0,2:T(8,128)S(1)} %copy.20), channel_id=1, source_target_pairs={{0,8},{8,0},{1,9},{9,1},{2,10},{10,2},{3,11},{11,3},{4,12},{12,4},... | collective-permute-start | bytes 1152008 | tf_op jit(solution)/shard_map/ppermute | solution.py:144
  52.6 1.7 %collective-permute-done.10 = f32[16,80,75]{1,0,2:T(8,128)S(1)} collective-permute-done((f32[16,80,75]{1,0,2:T(8,128)S(1)}, f32[16,80,75]{1,0,2:T(8,128)S(1)}, u32[]{:S(2)}, u32[]{:S(2)}) %collective-permute-start.10) | collective-permute-done | bytes 384032 | tf_op jit(solution)/shard_map/ppermute | solution.py:144
  54.2 0.3 copy.21
  54.6 0.9 %add.87 = f32[16,80,75]{2,1,0:T(8,128)} add(f32[16,80,75]{2,1,0:T(8,128)S(1)} %get-tuple-element.7, f32[16,80,75]{2,1,0:T(8,128)S(1)} %copy.21) | non-fusion elementwise | flops 96000 | bytes 1152000 | tf_op jit(solution)/shard_map/add | solution.py:144
  55.5 6.8 %all-to-all-start = ((f32[16,80,75]{2,1,0:T(8,128)}), f32[16,80,75]{2,1,0:T(8,128)S(1)}, u32[]{:S(2)}, u32[]{:S(2)}) async-start(f32[16,80,75]{2,1,0:T(8,128)} %add.87), calls=%async_computation | async-start | bytes 1310720 | tf_op jit(solution)/shard_map/all_to_all | solution.py:145
  62.3 0.1 convolution_bitcast_fusion
  62.4 18.3 %all-to-all-done = f32[16,80,75]{2,1,0:T(8,128)S(1)} async-done(((f32[16,80,75]{2,1,0:T(8,128)}), f32[16,80,75]{2,1,0:T(8,128)S(1)}, u32[]{:S(2)}, u32[]{:S(2)}) %all-to-all-start) | async-done | bytes 384032 | tf_op jit(solution)/shard_map/all_to_all | solution.py:145
  80.9 0.6 copy.22
  (38 shorter events, 0.9 us)
Async XLA Ops:
  1.1 13.3 %collective-permute-start.2 = (bf16[40,2400]{1,0:T(8,128)(2,1)S(1)}, bf16[40,2400]{1,0:T(8,128)(2,1)S(1)}, u32[]{:S(2)}, u32[]{:S(2)}) collective-permute-start(bf16[40,2400]{1,0:T(8,128)(2,1)S(1)} %reshape.63), channel_id=1, source_target_pairs={{16,0},{32,16},{48,32},{64,48},{80,64},{96,80},{112,96},{0,112},{1... | collective-permute-start | bytes 576008 | tf_op jit(solution)/shard_map/ppermute | solution.py:93
  7.6 9.6 %collective-permute-start.1 = (bf16[40,2400]{1,0:T(8,128)(2,1)S(1)}, bf16[40,2400]{1,0:T(8,128)(2,1)}, u32[]{:S(2)}, u32[]{:S(2)}) collective-permute-start(bf16[40,2400]{1,0:T(8,128)(2,1)S(1)} %reshape.63), channel_id=1, source_target_pairs={{0,16},{16,32},{32,48},{48,64},{64,80},{80,96},{96,112},{112,0},{1... | collective-permute-start | bytes 576008 | tf_op jit(solution)/shard_map/ppermute | solution.py:90
  7.6 36.3 %collective-permute-start = (bf16[2,160,2400]{2,1,0:T(8,128)(2,1)}, bf16[2,160,2400]{2,1,0:T(8,128)(2,1)S(1)}, u32[]{:S(2)}, u32[]{:S(2)}) collective-permute-start(bf16[2,160,2400]{2,1,0:T(8,128)(2,1)} %bitcast.18), channel_id=1, source_target_pairs={{0,128},{128,0},{1,129},{129,1},{2,130},{130,2},{3,131},{131,3},{4... | collective-permute-start | bytes 4608008 | tf_op jit(solution)/shard_map/ppermute | solution.py:85
  14.3 25.5 %copy-start.1 = (f32[2,2,40,640]{3,2,1,0:T(8,128)S(1)}, f32[2,2,40,640]{3,2,1,0:T(8,128)}, u32[]{:S(2)}) copy-start(f32[2,2,40,640]{3,2,1,0:T(8,128)} %constant.90.clone) | copy-start | bytes 1228804
  14.3 25.5 %copy-start.2 = (f32[2,2,40,640]{3,2,1,0:T(8,128)S(1)}, f32[2,2,40,640]{3,2,1,0:T(8,128)}, u32[]{:S(2)}) copy-start(f32[2,2,40,640]{3,2,1,0:T(8,128)} %constant.89.clone) | copy-start | bytes 1228804
  14.4 9.0 %collective-permute-start.4 = (bf16[40,2400]{1,0:T(8,128)(2,1)S(1)}, bf16[40,2400]{1,0:T(8,128)(2,1)S(1)}, u32[]{:S(2)}, u32[]{:S(2)}) collective-permute-start(bf16[40,2400]{1,0:T(8,128)(2,1)S(1)} %collective-permute-done.2), channel_id=1, source_target_pairs={{16,0},{32,16},{48,32},{64,48},{80,64},{96,80},{112,96},{0,112},{1... | collective-permute-start | bytes 576008 | tf_op jit(solution)/shard_map/ppermute | solution.py:93
  17.1 6.2 %collective-permute-start.3 = (bf16[40,2400]{1,0:T(8,128)(2,1)}, bf16[40,2400]{1,0:T(8,128)(2,1)S(1)}, u32[]{:S(2)}, u32[]{:S(2)}) collective-permute-start(bf16[40,2400]{1,0:T(8,128)(2,1)} %collective-permute-done.1), channel_id=1, source_target_pairs={{0,16},{16,32},{32,48},{48,64},{64,80},{80,96},{96,112},{112,0},{1... | collective-permute-start | bytes 576008 | tf_op jit(solution)/shard_map/ppermute | solution.py:90
  23.4 6.0 %collective-permute-start.6 = (bf16[40,2400]{1,0:T(8,128)(2,1)S(1)}, bf16[40,2400]{1,0:T(8,128)(2,1)S(1)}, u32[]{:S(2)}, u32[]{:S(2)}) collective-permute-start(bf16[40,2400]{1,0:T(8,128)(2,1)S(1)} %collective-permute-done.3), channel_id=1, source_target_pairs={{0,16},{16,32},{32,48},{48,64},{64,80},{80,96},{96,112},{112,0},{1... | collective-permute-start | bytes 576008 | tf_op jit(solution)/shard_map/ppermute | solution.py:90
  23.4 18.0 %collective-permute-start.5 = (bf16[200,2400]{1,0:T(8,128)(2,1)S(1)}, bf16[200,2400]{1,0:T(8,128)(2,1)S(1)}, u32[]{:S(2)}, u32[]{:S(2)}) collective-permute-start(bf16[200,2400]{1,0:T(8,128)(2,1)S(1)} %constant_dynamic-update-slice_fusion.b0), channel_id=1, source_target_pairs={{0,8},{8,0},{1,9},{9,1},{2,10},{10,2},{3,11},{11,3},{4,12},{12,4},... | collective-permute-start | bytes 2880008 | tf_op jit(solution)/shard_map/ppermute | solution.py:97
  26.2 7.2 %collective-permute-start.7 = (bf16[40,2400]{1,0:T(8,128)(2,1)S(1)}, bf16[40,2400]{1,0:T(8,128)(2,1)S(1)}, u32[]{:S(2)}, u32[]{:S(2)}) collective-permute-start(bf16[40,2400]{1,0:T(8,128)(2,1)S(1)} %collective-permute-done.4), channel_id=1, source_target_pairs={{16,0},{32,16},{48,32},{64,48},{80,64},{96,80},{112,96},{0,112},{1... | collective-permute-start | bytes 576008 | tf_op jit(solution)/shard_map/ppermute | solution.py:93
  29.4 6.0 %collective-permute-start.8 = (bf16[40,2400]{1,0:T(8,128)(2,1)S(1)}, bf16[40,2400]{1,0:T(8,128)(2,1)S(1)}, u32[]{:S(2)}, u32[]{:S(2)}) collective-permute-start(bf16[40,2400]{1,0:T(8,128)(2,1)S(1)} %collective-permute-done.6), channel_id=1, source_target_pairs={{0,16},{16,32},{32,48},{48,64},{64,80},{80,96},{96,112},{112,0},{1... | collective-permute-start | bytes 576008 | tf_op jit(solution)/shard_map/ppermute | solution.py:90
  33.4 10.5 %copy-start = (bf16[1,2,160,2400]{3,2,1,0:T(8,128)(2,1)S(1)}, bf16[1,2,160,2400]{3,2,1,0:T(8,128)(2,1)}, u32[]{:S(2)}) copy-start(bf16[1,2,160,2400]{3,2,1,0:T(8,128)(2,1)} %param.9) | copy-start | bytes 4608004
  35.4 6.1 %collective-permute-start.9 = (bf16[120,2400]{1,0:T(8,128)(2,1)S(1)}, bf16[120,2400]{1,0:T(8,128)(2,1)S(1)}, u32[]{:S(2)}, u32[]{:S(2)}) collective-permute-start(bf16[120,2400]{1,0:T(8,128)(2,1)S(1)} %constant_dynamic-update-slice_fusion.5.b2), channel_id=1, source_target_pairs={{0,8},{8,0},{1,9},{9,1},{2,10},{10,2},{3,11},{11,3},{4,12},{12,4},... | collective-permute-start | bytes 1728008 | tf_op jit(solution)/shard_map/ppermute | solution.py:99
  50.7 3.6 %collective-permute-start.10 = (f32[16,80,75]{1,0,2:T(8,128)S(1)}, f32[16,80,75]{1,0,2:T(8,128)S(1)}, u32[]{:S(2)}, u32[]{:S(2)}) collective-permute-start(f32[16,80,75]{1,0,2:T(8,128)S(1)} %copy.20), channel_id=1, source_target_pairs={{0,8},{8,0},{1,9},{9,1},{2,10},{10,2},{3,11},{11,3},{4,12},{12,4},... | collective-permute-start | bytes 1152008 | tf_op jit(solution)/shard_map/ppermute | solution.py:144
  54.5 7.8 %copy-start.3 = (s32[2,30]{1,0:T(2,128)S(1)}, s32[2,30]{1,0:T(2,128)}, u32[]{:S(2)}) copy-start(s32[2,30]{1,0:T(2,128)} %param.13) | copy-start | bytes 724
  55.5 25.3 %all-to-all-start = ((f32[16,80,75]{2,1,0:T(8,128)}), f32[16,80,75]{2,1,0:T(8,128)S(1)}, u32[]{:S(2)}, u32[]{:S(2)}) async-start(f32[16,80,75]{2,1,0:T(8,128)} %add.87), calls=%async_computation | async-start | bytes 1310720 | tf_op jit(solution)/shard_map/all_to_all | solution.py:145

commit v3 on v2

--- a/solution.py
+++ b/solution.py
@@ -1,3 +1,5 @@
+import functools
+
 import jax
 import jax.numpy as jnp
 import numpy as np
@@ -28,46 +30,91 @@
     return cos_sign.astype(np.float32), sin_sign.astype(np.float32)
 
 
-def cluster_kernel(core_ref, own, far, b0, b1, b2, b3, w_own, w_far, g, mine, other, b_ref, u_ref):
+def scaled_m(b, q_ref, w_ref, q, k_start, width):
+    contract = (((1,), (1,)), ((), ()))
+    m = lax.dot_general(b, q_ref[0], contract, preferred_element_type=F32)
+    turn = lax.dot_general(b, q_ref[1], contract, preferred_element_type=F32)
+    rows = m.shape[0]
+    is_real = lax.broadcasted_iota(jnp.int32, m.shape, 0) % (2 * width) < width
+    turn = jnp.where(is_real, pltpu.roll(turn, rows - width, 0), -pltpu.roll(turn, width, 0))
+    m = m + turn
+    blocks = range(rows // (2 * width))
+    scaled = [m[k * 2 * width : (k + 1) * 2 * width] * w_ref[q, k_start + k] for k in blocks]
+    return jnp.concatenate(scaled, 0).astype(BF16)
+
+
+def phased(g_ref, m):
+    t = jnp.dot(g_ref[...], m, preferred_element_type=F32)
+    half = t.shape[0] // 2
+    return t[:half] + t[half:]
+
+
+def early_kernel(width, w, own, b0, b1, g, t_ref, b_ref):
+    half = b0.shape[0]
+    b_ref[:half, :] = b0[...]
+    b_ref[half:, :] = b1[...]
+    t_ref[...] = phased(g, scaled_m(b_ref[...], own, w, 0, 0, width))
+
+
+def packed(u, at, columns):
+    third = columns // 3
+    tall = jnp.concatenate([u[:, at + p * third : at + (p + 1) * third] for p in range(3)], 0)
+    rows = tall.shape[0] // 5
+    return jnp.concatenate([tall[g * rows : (g + 1) * rows] for g in range(5)], 1)
+
+
+def unpacked(value, columns):
+    third = columns // 3
+    tall = jnp.concatenate([value[:, g * third : (g + 1) * third] for g in range(5)], 0)
+    rows = tall.shape[0] // 3
+    return jnp.concatenate([tall[p * rows : (p + 1) * rows] for p in range(3)], 1)
+
+
+def cluster_kernel(columns, core_ref, w, own, far, b0, b1, b2, b3, g0, g1, t_early, mine, other, b_ref, u_ref):
     at = 0
     for part in (b0, b1, b2, b3):
         b_ref[pl.ds(at, part.shape[0]), :] = part[...]
         at += part.shape[0]
-    k_rows = b_ref.shape[0]
+    early = b0.shape[0] + b1.shape[0]
     width = u_ref.shape[0] // 4
-    outs = 8 * width
-    occupied = own.shape[1]
-    contract = (((1,), (1,)), ((), ()))
-    is_real = lax.broadcasted_iota(jnp.int32, (k_rows, occupied), 0) % (2 * width) < width
-    ms = []
-    for q_ref, w in ((own, w_own), (far, w_far)):
-        m = lax.dot_general(b_ref[...], q_ref[0], contract, preferred_element_type=F32)
-        turn = lax.dot_general(b_ref[...], q_ref[1], contract, preferred_element_type=F32)
-        turn = jnp.where(is_real, pltpu.roll(turn, k_rows - width, 0), -pltpu.roll(turn, width, 0))
-        ms.append((w[...] * (m + turn)).astype(BF16))
+    half = 4 * width
+    m_far = scaled_m(b_ref[...], far, w, 1, 0, width)
+    m_own = scaled_m(b_ref[early:, :], own, w, 0, early // (2 * width), width)
+    t_far = phased(g0, m_far[:early]) + phased(g1, m_far[early:])
+    t_own = t_early[...] + phased(g1, m_own)
     us = []
-    for q_ref, m in zip((own, far), ms):
-        t = jnp.dot(g[...], m, preferred_element_type=F32)
-        t = t[:outs] + t[outs:]
+    for q_ref, t in ((own, t_own), (far, t_far)):
         t_high = t.astype(BF16)
         t_low = (t - t_high.astype(F32)).astype(BF16)
-        half = outs // 2
         for part in range(2):
             rows = slice(part * half, (part + 1) * half)
             pair = jnp.concatenate([t_high[rows], t_low[rows]], 0)
             us.append(jnp.dot(pair, q_ref[part], preferred_element_type=F32))
     u = (us[0] + us[1]) + (us[2] + us[3])
-    u_ref[...] = u[: outs // 2] + u[outs // 2 :]
-    chips, _, columns = mine.shape
+    u_ref[...] = u[:half] + u[half:]
+    chips, _, lanes = mine.shape
     for core in range(2):
 
         @pl.when(core_ref[0] == core)
         def _():
             for chip in range(chips):
-                at = (2 * chip + core) * columns
-                mine[chip] = u_ref[:, at : at + columns]
-                at = (2 * chip + 1 - core) * columns
-                other[chip] = u_ref[:, at : at + columns]
+                for out, parity in ((mine, core), (other, 1 - core)):
+                    piece = packed(u_ref[...], (2 * chip + parity) * columns, columns)
+                    spare = jnp.zeros((piece.shape[0], lanes - piece.shape[1]), F32)
+                    out[chip] = jnp.concatenate([piece, spare], 1)
+
+
+def final_kernel(arrived, mask, out):
+    total = arrived[0]
+    for chip in range(1, arrived.shape[0]):
+        total = total + arrived[chip]
+    cells, width, parts, columns = out.shape
+    value = unpacked(total, columns)
+    for f in range(cells):
+        for part in range(parts):
+            for j in range(width):
+                row = (f * parts + part) * width + j
+                out[f, j, pl.ds(part, 1), :] = value[row : row + 1] * mask[pl.ds(f, 1), :]
 
 
 def shards(coefficients, class_weight, diff_class, frag_cells, block_pattern):
@@ -86,12 +133,13 @@
     blocks = [block]
     offsets = [0, -1, 1, -2, 2, -3, 3, -4]
     from_below = from_above = block
-    for step in range(1, PARTS[1] // 2 + 1):
+    for step in range(1, PARTS[1] // 2):
         from_below = lax.ppermute(from_below, "z", up)
-        blocks.append(from_below)
-        if step < PARTS[1] // 2:
-            from_above = lax.ppermute(from_above, "z", down)
-            blocks.append(from_above)
+        from_above = lax.ppermute(from_above, "z", down)
+        blocks += [from_below, from_above]
+    cut = 24
+    blocks.append(lax.ppermute(from_below[:cut], "z", up))
+    blocks.append(lax.ppermute(from_above[cut:], "z", down))
     split = 5
     first = jnp.concatenate(blocks[:split], 0)
     first_near = lax.ppermute(first, "core", swap)
@@ -110,7 +158,6 @@
     q_points = (jnp.stack([yh, 1 - yh]) * PARTS[1] + z) * 2 + core
     q_onehot = (q_points[:, None] == all_points).astype(F32)
     weights = jnp.einsum("ka,ab,qb->qk", k_onehot, pair_weight, q_onehot, precision=high) / functions
-    weights = jnp.repeat(weights, 2 * width, axis=1)[:, :, None]
 
     phase_index = frag_cells[:, None] * kpoints[None, :] % kpoint_count
     angles = 2.0 * jnp.pi * phase_index.astype(F32) / kpoint_count
@@ -120,37 +167,57 @@
     sines = jnp.repeat(jnp.sin(angles) / kpoint_count, 2 * width, axis=1)[None, :, None, :]
     cos_sign, sin_sign = (jnp.asarray(a.reshape(full)) for a in phase_signs(width, kpoints.shape[0]))
     g = (cos_sign * cosines + sin_sign * sines).reshape(8 * width, -1)
-    g_high = g.astype(BF16)
-    g_low = (g - g_high.astype(F32)).astype(BF16)
-    g = jnp.concatenate([g_high, g_low], 0)
+    g_high = lax.reduce_precision(g, 8, 7)
+    g = jnp.concatenate([g_high, g - g_high], 0).astype(BF16)
+    early = 2 * split * 2 * width
+    g0, g1 = g[:, :early], g[:, early:]
+
+    vmem, smem = (pl.BlockSpec(memory_space=space) for space in (pltpu.VMEM, pltpu.SMEM))
+    t_early = pl.pallas_call(
+        functools.partial(early_kernel, width),
+        out_shape=jax.ShapeDtypeStruct((8 * width, occupied), F32),
+        in_specs=[smem] + [vmem] * 4,
+        out_specs=vmem,
+        scratch_shapes=[pltpu.VMEM((early, functions), BF16)],
+        compiler_params=pltpu.CompilerParams(vmem_limit_bytes=16 * 2**20),
+        cost_estimate=pl.CostEstimate(flops=10**9, bytes_accessed=4 * 10**6, transcendentals=0),
+        name="early_terms",
+    )(weights, own, first, first_near, g0)
 
     chips = PARTS[0] * PARTS[1]
     columns = functions // kpoint_count
-    piece = jax.ShapeDtypeStruct((chips, 4 * width, columns), F32)
+    piece = jax.ShapeDtypeStruct((chips, 4 * width * 3 // 5, 128), F32)
     mine, other = pl.pallas_call(
-        cluster_kernel,
+        functools.partial(cluster_kernel, columns),
         out_shape=(piece, piece),
-        in_specs=[pl.BlockSpec(memory_space=pltpu.SMEM)] + [pl.BlockSpec(memory_space=pltpu.VMEM)] * 9,
-        out_specs=(pl.BlockSpec(memory_space=pltpu.VMEM),) * 2,
+        in_specs=[smem] * 2 + [vmem] * 9,
+        out_specs=(vmem, vmem),
         scratch_shapes=[
             pltpu.VMEM((2 * width * kpoints.shape[0], functions), BF16),
             pltpu.VMEM((4 * width, functions), F32),
         ],
-        compiler_params=pltpu.CompilerParams(vmem_limit_bytes=32 * 2**20),
+        compiler_params=pltpu.CompilerParams(vmem_limit_bytes=24 * 2**20),
         cost_estimate=pl.CostEstimate(flops=3 * 10**9, bytes_accessed=10**7, transcendentals=0),
         name="cluster_terms",
-    )(core[None], own, far, first, first_near, last, last_near, weights[0], weights[1], g)
+    )(core[None], weights, own, far, first, first_near, last, last_near, g0, g1, t_early)
 
     sums = mine + lax.ppermute(other, "core", swap)
     arrived = lax.all_to_all(sums, ("yh", "z"), 0, 0, tiled=True)
-    cluster = jnp.sum(arrived, axis=0).reshape(cells, 2, width, columns)
     index = (yh * PARTS[1] + z) * 2 + core
     block_size = functions // block_pattern.shape[1]
     local_ids = (index * columns + jnp.arange(columns, dtype=jnp.int32)) // block_size
     block_ids = jnp.arange(block_pattern.shape[1], dtype=jnp.int32)
     onehot = (block_ids[:, None] == local_ids[None, :]).astype(F32)
     mask = jnp.dot(block_pattern.astype(F32), onehot, precision=high)
-    return cluster * mask[:, None, None, :]
+    cluster = pl.pallas_call(
+        final_kernel,
+        out_shape=jax.ShapeDtypeStruct((cells, width, 2, columns), F32),
+        in_specs=[vmem] * 2,
+        out_specs=vmem,
+        compiler_params=pltpu.CompilerParams(vmem_limit_bytes=4 * 2**20),
+        name="sum_and_mask",
+    )(arrived, mask)
+    return jnp.transpose(cluster, (0, 2, 1, 3))
 
 
 def solution(mesh):

time: 82.8 us -> 77.7 us (0.938)
  waiting for transfers between devices: 35.3 us -> 20.3 us
  Pallas kernels: 6.43 us -> 10.8 us
  local copies, waits for them, and re-layouts: 4.34 us -> 7.49 us
  starting transfers between devices: 31 us -> 32.6 us
    ppermute x4 -> x3, waiting for transfers between devices: 7.45 us -> 0.01 us  [shards(): from_below = lax.ppermute(from_below, 'z', up)]
    all_to_all x1, waiting for transfers between devices: 18.3 us -> 12.5 us  [shards(): arrived = lax.all_to_all(sums, ('yh', 'z'), 0, 0, tiled=True)]
    ppermute x0 -> x2, waiting for transfers between devices: none -> 5.11 us  [the longest x1 5.11 us: shards(): blocks.append(lax.ppermute(from_below[:cut], 'z', up))]
    pallas_call x1 -> x3, Pallas kernels: 6.43 us -> 10.8 us  [the longest x1 7.9 us: shards(): pl.pallas_call(functools.partial(cluster_kernel, columns), out_shape=(pie...]
    ppermute x0 -> x2, starting transfers between devices: none -> 3.24 us  [the longest x1 3.16 us: shards(): blocks.append(lax.ppermute(from_above[cut:], 'z', down))]
    ppermute x3, waiting for transfers between devices: 3.95 us -> 0.98 us  [shards(): from_above = lax.ppermute(from_above, 'z', down)]
    ppermute x1, waiting for transfers between devices: 2.42 us -> 0.01 us  [shards(): far = lax.ppermute(own, 'yh', swap)]
    mul x2, local copies, waits for them, and re-layouts: 0.19 us -> 2.2 us  [shards(): g = (cos_sign * cosines + sin_sign * sines).reshape(8 * width, -1)]
  transfers between devices with their start and end apart: 12 -> 13, of which waited for: 8 -> 4; matrix products, arithmetic and copies ran while one was open for 6% -> 13% of each run, Pallas kernels for 0% -> 3%
where the time goes in v3:
time: 77.7 us; the launch traced here: 76.1 us
  starting transfers between devices  32.6 us (42%)
  waiting for transfers between devices  20.3 us (26%)
  Pallas kernels  10.8 us (14%)
  local copies, waits for them, and re-layouts  7.49 us (10%)
  other arithmetic  4.27 us (5%)
    ppermute x3, starting transfers between devices, shards(): from_above = lax.ppermute(from_above, 'z', down)  12.6 us
    all_to_all x1, waiting for transfers between devices, shards(): arrived = lax.all_to_all(sums, ('yh', 'z'), 0, 0, tiled=True)  12.5 us
    pallas_call x1, Pallas kernels, shards(): pl.pallas_call(functools.partial(cluster_kernel, columns), out_shape=(pie...  7.9 us
    all_to_all x1, starting transfers between devices, shards(): arrived = lax.all_to_all(sums, ('yh', 'z'), 0, 0, tiled=True)  6.25 us
    ppermute x1, waiting for transfers between devices, shards(): blocks.append(lax.ppermute(from_below[:cut], 'z', up))  5.11 us
    ppermute x1, starting transfers between devices, shards(): last_near = lax.ppermute(last, 'core', swap)  4.67 us
    ppermute x1, starting transfers between devices, shards(): blocks.append(lax.ppermute(from_above[cut:], 'z', down))  3.16 us
    ppermute x1, starting transfers between devices, shards(): far = lax.ppermute(own, 'yh', swap)  2.91 us
  transfers between devices with their start and end apart: 13, of which 4 were waited for; matrix products, arithmetic and copies ran while one was open for 13% of the time, Pallas kernels for 3%

profile of v3, /device:TPU:1, one launch (start us, length us, event | category | flops | bytes accessed | tf_op | source)
XLA Modules:
  0.0 76.1 jit_solution(4516874819313155954)
XLA Ops:
  0.0 1.1 %constant_dynamic-slice_fusion = bf16[1,2,20,2400]{3,2,1,0:T(8,128)(2,1)S(1)} fusion(bf16[1,2,160,2400]{3,2,1,0:T(8,128)(2,1)} %param.9, s32[]{:T(128)S(6)} %select_n.19), kind=kLoop, calls=%fused_computation.44 | loop fusion | bytes 384004 | tf_op jit(solution)/shard_map/dynamic_slice | solution.py:131
  1.2 6.5 %collective-permute-start.2 = (bf16[40,2400]{1,0:T(8,128)(2,1)S(1)}, bf16[40,2400]{1,0:T(8,128)(2,1)}, u32[]{:S(2)}, u32[]{:S(2)}) collective-permute-start(bf16[40,2400]{1,0:T(8,128)(2,1)S(1)} %reshape.47), channel_id=1, source_target_pairs={{16,0},{32,16},{48,32},{64,48},{80,64},{96,80},{112,96},{0,112},{1... | collective-permute-start | bytes 576008 | tf_op jit(solution)/shard_map/ppermute | solution.py:138
  7.7 2.9 %collective-permute-start = (bf16[2,160,2400]{2,1,0:T(8,128)(2,1)}, bf16[2,160,2400]{2,1,0:T(8,128)(2,1)S(1)}, u32[]{:S(2)}, u32[]{:S(2)}) collective-permute-start(bf16[2,160,2400]{2,1,0:T(8,128)(2,1)} %bitcast.12), channel_id=1, source_target_pairs={{0,128},{128,0},{1,129},{129,1},{2,130},{130,2},{3,131},{131,3},{4... | collective-permute-start | bytes 4608008 | tf_op jit(solution)/shard_map/ppermute | solution.py:132
  10.6 0.7 xor_add_fusion
  11.3 1.4 %cosine_multiply_fusion = (f32[2,16]{1,0:T(2,128)S(1)}, f32[2,16]{1,0:T(2,128)}) fusion(s32[16]{0:T(128)S(1)} %xor_add_fusion, s32[2]{0:T(128)} %param.12), kind=kLoop, calls=%fused_computation.37 | loop fusion | flops 512 | bytes 328 | tf_op jit(solution)/shard_map/div | solution.py:166
  12.6 0.7 broadcast_in_dim.7
  13.3 0.8 %mul.87 = f32[2,640]{1,0:T(2,128)S(1)} reshape(f32[2,16,40]{2,1,0:T(8,128)} %broadcast_in_dim.7) | data formatting | bytes 10240 | tf_op jit(solution)/shard_map/mul | solution.py:169
  14.1 1.4 %broadcast_in_dim.8 = f32[2,16,40]{2,1,0:T(8,128)} broadcast(f32[2,16]{1,0:T(2,128)} %get-tuple-element.12), dimensions={0,1} | broadcast | bytes 5248 | tf_op jit(solution)/shard_map/broadcast_in_dim | solution.py:167
  15.5 1.4 %mul.90 = f32[2,640]{1,0:T(2,128)} reshape(f32[2,16,40]{2,1,0:T(8,128)} %broadcast_in_dim.8) | data formatting | bytes 10240 | tf_op jit(solution)/shard_map/mul | solution.py:169
  16.9 0.8 %multiply_add_fusion = f32[2,2,40,640]{3,2,1,0:T(8,128)S(1)} fusion(f32[2,2,40,640]{3,2,1,0:T(8,128)S(1)} %copy-done.1, f32[2,2,40,640]{3,2,1,0:T(8,128)S(1)} %copy-done.2, f32[2,640]{1,0:T(2,128)} %mul.90, f32[2,640]{1,0:T(2,128)S(1)} %mul.87), kind=kLoop, calls=%fused_computation.9 | loop fusion | flops 307200 | bytes 1239040 | tf_op jit(solution)/shard_map/add | solution.py:169
  17.7 0.1 pad_maximum_fusion.g1
  17.9 0.4 select_reduce_fusion
  18.3 2.8 %collective-permute-start.4 = (bf16[40,2400]{1,0:T(8,128)(2,1)}, bf16[40,2400]{1,0:T(8,128)(2,1)S(1)}, u32[]{:S(2)}, u32[]{:S(2)}) collective-permute-start(bf16[40,2400]{1,0:T(8,128)(2,1)} %collective-permute-done.2), channel_id=1, source_target_pairs={{16,0},{32,16},{48,32},{64,48},{80,64},{96,80},{112,96},{0,112},{1... | collective-permute-start | bytes 576008 | tf_op jit(solution)/shard_map/ppermute | solution.py:138
  21.1 1.0 %constant_dynamic-update-slice_fusion.3 = bf16[200,2400]{1,0:T(8,128)(2,1)S(1)} fusion(bf16[200,2400]{1,0:T(8,128)(2,1)S(1)} %constant_dynamic-update-slice_fusion.4, bf16[40,2400]{1,0:T(8,128)(2,1)} %collective-permute-done.1), kind=kLoop, calls=%fused_computation.15 | loop fusion | bytes 386560
  22.0 0.9 %constant_dynamic-update-slice_fusion.2 = bf16[200,2400]{1,0:T(8,128)(2,1)S(1)} fusion(bf16[200,2400]{1,0:T(8,128)(2,1)S(1)} %constant_dynamic-update-slice_fusion.3, bf16[40,2400]{1,0:T(8,128)(2,1)} %collective-permute-done.2), kind=kLoop, calls=%fused_computation.14 | loop fusion | bytes 386560
  23.0 1.0 %collective-permute-done.4 = bf16[40,2400]{1,0:T(8,128)(2,1)S(1)} collective-permute-done((bf16[40,2400]{1,0:T(8,128)(2,1)}, bf16[40,2400]{1,0:T(8,128)(2,1)S(1)}, u32[]{:S(2)}, u32[]{:S(2)}) %collective-permute-start.4) | collective-permute-done | bytes 192032 | tf_op jit(solution)/shard_map/ppermute | solution.py:138
  24.0 3.3 %collective-permute-start.7 = (bf16[40,2400]{1,0:T(8,128)(2,1)S(1)}, bf16[40,2400]{1,0:T(8,128)(2,1)S(1)}, u32[]{:S(2)}, u32[]{:S(2)}) collective-permute-start(bf16[40,2400]{1,0:T(8,128)(2,1)S(1)} %collective-permute-done.4), channel_id=1, source_target_pairs={{16,0},{32,16},{48,32},{64,48},{80,64},{96,80},{112,96},{0,112},{1... | collective-permute-start | bytes 576008 | tf_op jit(solution)/shard_map/ppermute | solution.py:138
  27.4 2.8 %collective-permute-start.5 = (bf16[200,2400]{1,0:T(8,128)(2,1)S(1)}, bf16[200,2400]{1,0:T(8,128)(2,1)S(1)}, u32[]{:S(2)}, u32[]{:S(2)}) collective-permute-start(bf16[200,2400]{1,0:T(8,128)(2,1)S(1)} %constant_dynamic-update-slice_fusion.b0), channel_id=1, source_target_pairs={{0,8},{8,0},{1,9},{9,1},{2,10},{10,2},{3,11},{11,3},{4,12},{12,4},... | collective-permute-start | bytes 2880008 | tf_op jit(solution)/shard_map/ppermute | solution.py:145
  30.2 3.2 %collective-permute-start.9 = (bf16[16,2400]{1,0:T(8,128)(2,1)S(1)}, bf16[16,2400]{1,0:T(8,128)(2,1)S(1)}, u32[]{:S(2)}, u32[]{:S(2)}) collective-permute-start(bf16[16,2400]{1,0:T(8,128)(2,1)S(1)} %slice.17), channel_id=1, source_target_pairs={{16,0},{32,16},{48,32},{64,48},{80,64},{96,80},{112,96},{0,112},{1... | collective-permute-start | bytes 230408 | tf_op jit(solution)/shard_map/ppermute | solution.py:142
  33.5 5.1 %collective-permute-done.8 = bf16[24,2400]{1,0:T(8,128)(2,1)S(1)} collective-permute-done((bf16[24,2400]{1,0:T(8,128)(2,1)S(1)}, bf16[24,2400]{1,0:T(8,128)(2,1)S(1)}, u32[]{:S(2)}, u32[]{:S(2)}) %collective-permute-start.8) | collective-permute-done | bytes 115232 | tf_op jit(solution)/shard_map/ppermute | solution.py:141
  38.6 4.7 %collective-permute-start.10 = (bf16[120,2400]{1,0:T(8,128)(2,1)S(1)}, bf16[120,2400]{1,0:T(8,128)(2,1)S(1)}, u32[]{:S(2)}, u32[]{:S(2)}) collective-permute-start(bf16[120,2400]{1,0:T(8,128)(2,1)S(1)} %constant_dynamic-update-slice_fusion.5.b2), channel_id=1, source_target_pairs={{0,8},{8,0},{1,9},{9,1},{2,10},{10,2},{3,11},{11,3},{4,12},{12,4},... | collective-permute-start | bytes 1728008 | tf_op jit(solution)/shard_map/ppermute | solution.py:147
  43.4 0.2 fusion.4
  43.6 0.2 convolution_multiply_fusion.w
  43.8 2.0 %early_terms.1.t_early = f32[160,160]{1,0:T(8,128)S(1)} custom-call(f32[2,16]{1,0:T(2,128)S(1)} %convolution_multiply_fusion.w, bf16[2,160,2400]{2,1,0:T(8,128)(2,1)S(1)} %bitcast.13, bf16[200,2400]{1,0:T(8,128)(2,1)S(1)} %constant_dynamic-update-slice_fusion.b0, bf16[200,2400]{1,0:T(8,128)(2,1)S(1)} %collective-permute-done.5.b1, ...), custom_call_target="tpu_custom_call" | custom-call | flops 1000000000 | bytes 4000000 | tf_op jit(solution)/shard_map/early_terms/pallas_call | solution.py:176
  45.9 7.9 %cluster_terms.1 = (f32[16,48,128]{2,1,0:T(8,128)S(1)}, f32[16,48,128]{2,1,0:T(8,128)S(1)}) custom-call(s32[1]{0:T(128)} %bitcast.core_ref, f32[2,16]{1,0:T(2,128)S(1)} %convolution_multiply_fusion.w, bf16[2,160,2400]{2,1,0:T(8,128)(2,1)S(1)} %bitcast.14, bf16[2,160,2400]{2,1,0:T(8,128)(2,1)S(1)} %collective-permute-done.far, ...), custom_call_target="tpu_custom_call" | custom-call | flops 3000000000 | bytes 10000000 | tf_op jit(solution)/shard_map/cluster_terms/pallas_call | solution.py:190
  53.8 0.1 collective-permute-start.11
  53.9 1.7 %collective-permute-done.11 = f32[16,48,128]{2,1,0:T(8,128)S(1)} collective-permute-done((f32[16,48,128]{2,1,0:T(8,128)S(1)}, f32[16,48,128]{2,1,0:T(8,128)S(1)}, u32[]{:S(2)}, u32[]{:S(2)}) %collective-permute-start.11) | collective-permute-done | bytes 393248 | tf_op jit(solution)/shard_map/ppermute | solution.py:204
  55.6 0.8 %add.87 = f32[16,48,128]{2,1,0:T(8,128)} add(f32[16,48,128]{2,1,0:T(8,128)S(1)} %get-tuple-element.7, f32[16,48,128]{2,1,0:T(8,128)S(1)} %collective-permute-done.11) | non-fusion elementwise | flops 98304 | bytes 1179648 | tf_op jit(solution)/shard_map/add | solution.py:204
  56.4 6.3 %all-to-all-start = ((f32[16,48,128]{2,1,0:T(8,128)}), f32[16,48,128]{2,1,0:T(8,128)S(1)}, u32[]{:S(2)}, u32[]{:S(2)}) async-start(f32[16,48,128]{2,1,0:T(8,128)} %add.87), calls=%async_computation | async-start | bytes 786432 | tf_op jit(solution)/shard_map/all_to_all | solution.py:205
  62.7 0.1 convolution_bitcast_fusion.mask
  62.8 12.5 %all-to-all-done.arrived = f32[16,48,128]{2,1,0:T(8,128)S(1)} async-done(((f32[16,48,128]{2,1,0:T(8,128)}), f32[16,48,128]{2,1,0:T(8,128)S(1)}, u32[]{:S(2)}, u32[]{:S(2)}) %all-to-all-start) | async-done | bytes 393248 | tf_op jit(solution)/shard_map/all_to_all | solution.py:205
  75.3 0.8 %sum_and_mask.1 = f32[2,20,2,75]{3,2,1,0:T(2,128)} custom-call(f32[16,48,128]{2,1,0:T(8,128)S(1)} %all-to-all-done.arrived, f32[2,75]{1,0:T(2,128)S(1)} %convolution_bitcast_fusion.mask), custom_call_target="tpu_custom_call" | custom-call | tf_op jit(solution)/shard_map/sum_and_mask/pallas_call | solution.py:212
  (43 shorter events, 0.5 us)
Async XLA Ops:
  0.0 16.9 %copy-start.1 = (f32[2,2,40,640]{3,2,1,0:T(8,128)S(1)}, f32[2,2,40,640]{3,2,1,0:T(8,128)}, u32[]{:S(2)}) copy-start(f32[2,2,40,640]{3,2,1,0:T(8,128)} %constant.90.clone) | copy-start | bytes 1228804
  0.0 16.9 %copy-start.2 = (f32[2,2,40,640]{3,2,1,0:T(8,128)S(1)}, f32[2,2,40,640]{3,2,1,0:T(8,128)}, u32[]{:S(2)}) copy-start(f32[2,2,40,640]{3,2,1,0:T(8,128)} %constant.89.clone) | copy-start | bytes 1228804
  1.2 17.1 %collective-permute-start.2 = (bf16[40,2400]{1,0:T(8,128)(2,1)S(1)}, bf16[40,2400]{1,0:T(8,128)(2,1)}, u32[]{:S(2)}, u32[]{:S(2)}) collective-permute-start(bf16[40,2400]{1,0:T(8,128)(2,1)S(1)} %reshape.47), channel_id=1, source_target_pairs={{16,0},{32,16},{48,32},{64,48},{80,64},{96,80},{112,96},{0,112},{1... | collective-permute-start | bytes 576008 | tf_op jit(solution)/shard_map/ppermute | solution.py:138
  7.7 13.4 %collective-permute-start.1 = (bf16[40,2400]{1,0:T(8,128)(2,1)S(1)}, bf16[40,2400]{1,0:T(8,128)(2,1)}, u32[]{:S(2)}, u32[]{:S(2)}) collective-permute-start(bf16[40,2400]{1,0:T(8,128)(2,1)S(1)} %reshape.47), channel_id=1, source_target_pairs={{0,16},{16,32},{32,48},{48,64},{64,80},{80,96},{96,112},{112,0},{1... | collective-permute-start | bytes 576008 | tf_op jit(solution)/shard_map/ppermute | solution.py:137
  7.7 38.2 %collective-permute-start = (bf16[2,160,2400]{2,1,0:T(8,128)(2,1)}, bf16[2,160,2400]{2,1,0:T(8,128)(2,1)S(1)}, u32[]{:S(2)}, u32[]{:S(2)}) collective-permute-start(bf16[2,160,2400]{2,1,0:T(8,128)(2,1)} %bitcast.12), channel_id=1, source_target_pairs={{0,128},{128,0},{1,129},{129,1},{2,130},{130,2},{3,131},{131,3},{4... | collective-permute-start | bytes 4608008 | tf_op jit(solution)/shard_map/ppermute | solution.py:132
  11.3 1.4 %copy-start.4 = (s32[16]{0:T(128)}, s32[16]{0:T(128)S(1)}, u32[]{:S(2)}) copy-start(s32[16]{0:T(128)S(1)} %xor_add_fusion) | copy-start | bytes 196
  16.9 1.0 %copy-start.3 = (s32[32,32]{1,0:T(8,128)S(1)}, s32[32,32]{1,0:T(8,128)}, u32[]{:S(2)}) copy-start(s32[32,32]{1,0:T(8,128)} %param.11) | copy-start | bytes 12292
  16.9 1.0 %copy-start.6 = (f32[32]{0:T(128)S(1)}, f32[32]{0:T(128)}, u32[]{:S(2)}) copy-start(f32[32]{0:T(128)} %param.10) | copy-start | bytes 388
  18.3 25.3 %copy-start.5 = (s32[16]{0:T(128)S(1)}, s32[16]{0:T(128)}, u32[]{:S(2)}) copy-start(s32[16]{0:T(128)} %copy-done.4) | copy-start | bytes 196
  18.3 25.5 %copy-start = (bf16[1,2,160,2400]{3,2,1,0:T(8,128)(2,1)S(1)}, bf16[1,2,160,2400]{3,2,1,0:T(8,128)(2,1)}, u32[]{:S(2)}) copy-start(bf16[1,2,160,2400]{3,2,1,0:T(8,128)(2,1)} %param.9) | copy-start | bytes 4608004
  18.3 5.7 %collective-permute-start.4 = (bf16[40,2400]{1,0:T(8,128)(2,1)}, bf16[40,2400]{1,0:T(8,128)(2,1)S(1)}, u32[]{:S(2)}, u32[]{:S(2)}) collective-permute-start(bf16[40,2400]{1,0:T(8,128)(2,1)} %collective-permute-done.2), channel_id=1, source_target_pairs={{16,0},{32,16},{48,32},{64,48},{80,64},{96,80},{112,96},{0,112},{1... | collective-permute-start | bytes 576008 | tf_op jit(solution)/shard_map/ppermute | solution.py:138
  21.1 6.3 %collective-permute-start.3 = (bf16[40,2400]{1,0:T(8,128)(2,1)}, bf16[40,2400]{1,0:T(8,128)(2,1)S(1)}, u32[]{:S(2)}, u32[]{:S(2)}) collective-permute-start(bf16[40,2400]{1,0:T(8,128)(2,1)} %collective-permute-done.1), channel_id=1, source_target_pairs={{0,16},{16,32},{32,48},{48,64},{64,80},{80,96},{96,112},{112,0},{1... | collective-permute-start | bytes 576008 | tf_op jit(solution)/shard_map/ppermute | solution.py:137
  24.0 6.2 %collective-permute-start.7 = (bf16[40,2400]{1,0:T(8,128)(2,1)S(1)}, bf16[40,2400]{1,0:T(8,128)(2,1)S(1)}, u32[]{:S(2)}, u32[]{:S(2)}) collective-permute-start(bf16[40,2400]{1,0:T(8,128)(2,1)S(1)} %collective-permute-done.4), channel_id=1, source_target_pairs={{16,0},{32,16},{48,32},{64,48},{80,64},{96,80},{112,96},{0,112},{1... | collective-permute-start | bytes 576008 | tf_op jit(solution)/shard_map/ppermute | solution.py:138
  27.3 6.0 %collective-permute-start.6 = (bf16[40,2400]{1,0:T(8,128)(2,1)S(1)}, bf16[40,2400]{1,0:T(8,128)(2,1)S(1)}, u32[]{:S(2)}, u32[]{:S(2)}) collective-permute-start(bf16[40,2400]{1,0:T(8,128)(2,1)S(1)} %collective-permute-done.3), channel_id=1, source_target_pairs={{0,16},{16,32},{32,48},{48,64},{64,80},{80,96},{96,112},{112,0},{1... | collective-permute-start | bytes 576008 | tf_op jit(solution)/shard_map/ppermute | solution.py:137
  27.4 16.4 %collective-permute-start.5 = (bf16[200,2400]{1,0:T(8,128)(2,1)S(1)}, bf16[200,2400]{1,0:T(8,128)(2,1)S(1)}, u32[]{:S(2)}, u32[]{:S(2)}) collective-permute-start(bf16[200,2400]{1,0:T(8,128)(2,1)S(1)} %constant_dynamic-update-slice_fusion.b0), channel_id=1, source_target_pairs={{0,8},{8,0},{1,9},{9,1},{2,10},{10,2},{3,11},{11,3},{4,12},{12,4},... | collective-permute-start | bytes 2880008 | tf_op jit(solution)/shard_map/ppermute | solution.py:145
  30.2 8.4 %collective-permute-start.9 = (bf16[16,2400]{1,0:T(8,128)(2,1)S(1)}, bf16[16,2400]{1,0:T(8,128)(2,1)S(1)}, u32[]{:S(2)}, u32[]{:S(2)}) collective-permute-start(bf16[16,2400]{1,0:T(8,128)(2,1)S(1)} %slice.17), channel_id=1, source_target_pairs={{16,0},{32,16},{48,32},{64,48},{80,64},{96,80},{112,96},{0,112},{1... | collective-permute-start | bytes 230408 | tf_op jit(solution)/shard_map/ppermute | solution.py:142
  33.4 5.2 %collective-permute-start.8 = (bf16[24,2400]{1,0:T(8,128)(2,1)S(1)}, bf16[24,2400]{1,0:T(8,128)(2,1)S(1)}, u32[]{:S(2)}, u32[]{:S(2)}) collective-permute-start(bf16[24,2400]{1,0:T(8,128)(2,1)S(1)} %slice.16), channel_id=1, source_target_pairs={{0,16},{16,32},{32,48},{48,64},{64,80},{80,96},{96,112},{112,0},{1... | collective-permute-start | bytes 345608 | tf_op jit(solution)/shard_map/ppermute | solution.py:141
  38.6 7.2 %collective-permute-start.10 = (bf16[120,2400]{1,0:T(8,128)(2,1)S(1)}, bf16[120,2400]{1,0:T(8,128)(2,1)S(1)}, u32[]{:S(2)}, u32[]{:S(2)}) collective-permute-start(bf16[120,2400]{1,0:T(8,128)(2,1)S(1)} %constant_dynamic-update-slice_fusion.5.b2), channel_id=1, source_target_pairs={{0,8},{8,0},{1,9},{9,1},{2,10},{10,2},{3,11},{11,3},{4,12},{12,4},... | collective-permute-start | bytes 1728008 | tf_op jit(solution)/shard_map/ppermute | solution.py:147
  53.8 8.9 %copy-start.7 = (s32[2,30]{1,0:T(2,128)S(1)}, s32[2,30]{1,0:T(2,128)}, u32[]{:S(2)}) copy-start(s32[2,30]{1,0:T(2,128)} %param.13) | copy-start | bytes 724
  53.8 1.8 %collective-permute-start.11 = (f32[16,48,128]{2,1,0:T(8,128)S(1)}, f32[16,48,128]{2,1,0:T(8,128)S(1)}, u32[]{:S(2)}, u32[]{:S(2)}) collective-permute-start(f32[16,48,128]{2,1,0:T(8,128)S(1)} %get-tuple-element.8), channel_id=1, source_target_pairs={{0,8},{8,0},{1,9},{9,1},{2,10},{10,2},{3,11},{11,3},{4,12},{12,4},... | collective-permute-start | bytes 1179656 | tf_op jit(solution)/shard_map/ppermute | solution.py:204
  56.4 18.9 %all-to-all-start = ((f32[16,48,128]{2,1,0:T(8,128)}), f32[16,48,128]{2,1,0:T(8,128)S(1)}, u32[]{:S(2)}, u32[]{:S(2)}) async-start(f32[16,48,128]{2,1,0:T(8,128)} %add.87), calls=%async_computation | async-start | bytes 786432 | tf_op jit(solution)/shard_map/all_to_all | solution.py:205

commit v4 on v3

v4 whole, which is shorter than its diff:
```python
import functools

import jax
import jax.numpy as jnp
import numpy as np
from jax import lax
from jax.experimental import pallas as pl
from jax.experimental.pallas import tpu as pltpu
from jax.sharding import Mesh
from jax.sharding import PartitionSpec as P

AXES = ("yh", "z", "core", "yl", "x")
KA = ("yh", "z", "core")
BAND = ("yl", "x")
PARTS = (2, 8, 2, 2, 4)
F32 = jnp.float32
BF16 = jnp.bfloat16


def prep_kernel(width, functions, k_points, ids, cells, diff_class, class_weight, cos_table, sin_table, w_ref, g0, g1):
    yh, z, core = ids[0], ids[1], ids[2]
    group = 2 * width
    count = len(k_points)
    rows, lanes = 4 * width, group * count
    points = []
    for offset, flip in k_points:
        points.append((yh * PARTS[1] + lax.rem(z + offset + PARTS[1], PARTS[1])) * 2 + (1 - core if flip else core))
    for q, row in enumerate((yh, 1 - yh)):
        q_point = (row * PARTS[1] + z) * 2 + core
        for at, point in enumerate(points):
            weight = jnp.full((group, 1), class_weight[diff_class[point, q_point]], F32)
            w_ref[q, pl.ds(at * group, group), :] = weight / functions
    lane = lax.broadcasted_iota(jnp.int32, (1, lanes), 1)
    tables = []
    for f in range(2):
        cosines = jnp.zeros((1, lanes), F32)
        sines = jnp.zeros((1, lanes), F32)
        for at, point in enumerate(points):
            here = (lane >= at * group) & (lane < (at + 1) * group)
            index = lax.rem(point * cells[f], cos_table.shape[0])
            cosines = jnp.where(here, cos_table[index], cosines)
            sines = jnp.where(here, sin_table[index], sines)
        tables.append((cosines, sines))
    row = lax.broadcasted_iota(jnp.int32, (rows, lanes), 0)
    col = lax.broadcasted_iota(jnp.int32, (rows, lanes), 1)
    first = row < group
    cosines = jnp.where(first, tables[0][0], tables[1][0])
    sines = jnp.where(first, tables[0][1], tables[1][1])
    real, real_m = row % group < width, col % group < width
    value = jnp.where(real == real_m, cosines, jnp.where(real, -sines, sines))
    value = jnp.where(row % width == col % width, value, 0.0)
    high = value.astype(BF16)
    low = (value - high.astype(F32)).astype(BF16)
    both = jnp.concatenate([high, low], 0)
    g0[...] = both[:, : g0.shape[1]]
    g1[...] = both[:, g0.shape[1] :]


def turned(value, width, sign):
    rows = value.shape[0]
    real = lax.broadcasted_iota(jnp.int32, value.shape, 0) % (2 * width) < width
    up, down = pltpu.roll(value, rows - width, 0), pltpu.roll(value, width, 0)
    return jnp.where(real, up, -down) if sign > 0 else jnp.where(real, -up, down)


def part_of_t(b, q_ref, w, g, width):
    contract = (((1,), (1,)), ((), ()))
    m = lax.dot_general(b, q_ref[0], contract, preferred_element_type=F32)
    m = m + turned(lax.dot_general(b, q_ref[1], contract, preferred_element_type=F32), width, 1)
    t = jnp.dot(g, (w * m).astype(BF16), preferred_element_type=F32)
    half = t.shape[0] // 2
    return t[:half] + t[half:]


def first_kernel(width, q, q_ref, b0, b1, w, g, t_ref, b_ref):
    half = b0.shape[0]
    b_ref[:half, :] = b0[...]
    b_ref[half:, :] = b1[...]
    t_ref[...] = part_of_t(b_ref[...], q_ref, w[q, : 2 * half, :], g[...], width)


def last_kernel(width, own, far, b0, b1, w, g, t_own, t_far, t_ref, b_ref):
    half = b0.shape[0]
    b_ref[:half, :] = b0[...]
    b_ref[half:, :] = b1[...]
    start = w.shape[1] - 2 * half
    for q, (q_ref, t) in enumerate(((own, t_own), (far, t_far))):
        t_ref[q] = t[...] + part_of_t(b_ref[...], q_ref, w[q, start:, :], g[...], width)


def packed(u, at, columns):
    third = columns // 3
    tall = jnp.concatenate([u[:, at + p * third : at + (p + 1) * third] for p in range(3)], 0)
    rows = tall.shape[0] // 5
    return jnp.concatenate([tall[g * rows : (g + 1) * rows] for g in range(5)], 1)


def unpacked(value, columns):
    third = columns // 3
    tall = jnp.concatenate([value[:, g * third : (g + 1) * third] for g in range(5)], 0)
    rows = tall.shape[0] // 3
    return jnp.concatenate([tall[p * rows : (p + 1) * rows] for p in range(3)], 1)


def cluster_kernel(width, columns, ids, own, far, near, diag, t, t_yh, t_core, t_diag, out, u_ref):
    yh, core = ids[0], ids[2]
    chips, _, lanes = out.shape
    span = 2 * chips * columns
    shift = span % 128
    window = pl.ds(pl.multiple_of(yh * (span - shift), 128), span + shift)
    half = 4 * width
    total = None
    sums = (
        (own, t[0] + t_yh[1]),
        (far, t[1] + t_yh[0]),
        (near, t_core[0] + t_diag[1]),
        (diag, t_core[1] + t_diag[0]),
    )
    for q_ref, value in sums:
        for part in range(2):
            piece = value if part == 0 else turned(value, width, -1)
            high = piece.astype(BF16)
            low = (piece - high.astype(F32)).astype(BF16)
            u = jnp.dot(jnp.concatenate([high, low], 0), q_ref[part, :, window], preferred_element_type=F32)
            total = u if total is None else total + u
    u_ref[...] = total[:half] + total[half:]
    for row in range(2):
        for parity in range(2):

            @pl.when((yh == row) & (core == parity))
            def _():
                for chip in range(chips):
                    piece = packed(u_ref[...], (2 * chip + parity) * columns + row * shift, columns)
                    spare = jnp.zeros((piece.shape[0], lanes - piece.shape[1]), F32)
                    out[chip] = jnp.concatenate([piece, spare], 1)


def final_kernel(arrived, mask, out):
    total = arrived[0]
    for chip in range(1, arrived.shape[0]):
        total = total + arrived[chip]
    cells, width, parts, columns = out.shape
    value = unpacked(total, columns)
    for f in range(cells):
        for part in range(parts):
            for j in range(width):
                row = (f * parts + part) * width + j
                out[f, j, pl.ds(part, 1), :] = value[row : row + 1] * mask[pl.ds(f, 1), :]


def call(kernel, name, shapes, specs, scratch=(), mib=16, flops=0):
    return pl.pallas_call(
        kernel,
        out_shape=shapes,
        in_specs=[pl.BlockSpec(memory_space=space) for space in specs],
        out_specs=jax.tree.map(lambda _: pl.BlockSpec(memory_space=pltpu.VMEM), shapes),
        scratch_shapes=scratch,
        compiler_params=pltpu.CompilerParams(vmem_limit_bytes=mib * 2**20),
        cost_estimate=pl.CostEstimate(flops=flops, bytes_accessed=2**20, transcendentals=0),
        name=name,
    )


def shards(coefficients, class_weight, diff_class, frag_cells, block_pattern):
    own = coefficients[0]
    _, occupied, functions = own.shape
    yh, z, core = (lax.axis_index(name) for name in KA)
    band = lax.axis_index("yl") * PARTS[4] + lax.axis_index("x")
    width = occupied // (PARTS[3] * PARTS[4])
    group = 2 * width
    kpoint_count = PARTS[0] * PARTS[1] * PARTS[2]
    cells = frag_cells.shape[0]
    up = [(i, (i + 1) % PARTS[1]) for i in range(PARTS[1])]
    down = [(j, i) for i, j in up]
    swap = [(0, 1), (1, 0)]
    cross = [(0, 3), (1, 2), (2, 1), (3, 0)]
    vmem, smem = pltpu.VMEM, pltpu.SMEM

    far = lax.ppermute(own, "yh", swap)
    near = lax.ppermute(own, "core", swap)
    diag = lax.ppermute(far, "core", swap)
    block = lax.dynamic_slice_in_dim(own, band * width, width, 1).reshape(group, functions)
    blocks = [block]
    offsets = [0, -1, 1, -2, 2, -3, 3, -4]
    from_below = from_above = block
    for step in range(1, PARTS[1] // 2):
        from_below = lax.ppermute(from_below, "z", up)
        from_above = lax.ppermute(from_above, "z", down)
        blocks += [from_below, from_above]
    cut = 24
    blocks.append(lax.ppermute(from_below[:cut], "z", up))
    blocks.append(lax.ppermute(from_above[cut:], "z", down))
    split = 5
    first = jnp.concatenate(blocks[:split], 0)
    first_near = lax.ppermute(first, "core", swap)
    last = jnp.concatenate(blocks[split:], 0)
    last_near = lax.ppermute(last, "core", swap)

    k_points = []
    for these in (offsets[:split], offsets[split:]):
        k_points += [(offset, False) for offset in these] + [(offset, True) for offset in these]
    early, late = 2 * split * group, 2 * (len(offsets) - split) * group
    angles = 2.0 * np.pi * np.arange(kpoint_count) / kpoint_count
    tables = [jnp.asarray((f(angles) / kpoint_count).astype(np.float32)) for f in (np.cos, np.sin)]
    ids = jnp.stack([yh, z, core]).astype(jnp.int32)
    weights, g_first, g_last = call(
        functools.partial(prep_kernel, width, functions, k_points),
        "phases",
        (
            jax.ShapeDtypeStruct((2, early + late, 1), F32),
            jax.ShapeDtypeStruct((8 * width, early), BF16),
            jax.ShapeDtypeStruct((8 * width, late), BF16),
        ),
        [smem] * 6,
    )(ids, frag_cells, diff_class, class_weight, *tables)

    one = jax.ShapeDtypeStruct((4 * width, occupied), F32)
    t_first = []
    for q, (name, q_block) in enumerate((("own_first", own), ("far_first", far))):
        t_first.append(
            call(
                functools.partial(first_kernel, width, q),
                name,
                one,
                [vmem] * 5,
                [pltpu.VMEM((early, functions), BF16)],
                flops=(1 + 20 * q) * 10**9,
            )(q_block, first, first_near, weights, g_first)
        )
    t = call(
        functools.partial(last_kernel, width),
        "last_terms",
        jax.ShapeDtypeStruct((2,) + one.shape, F32),
        [vmem] * 8,
        [pltpu.VMEM((late, functions), BF16)],
        flops=10**9,
    )(own, far, last, last_near, weights, g_last, *t_first)

    t_core = lax.ppermute(t, "core", swap)
    t_yh = lax.ppermute(t, "yh", swap)
    t_diag = lax.ppermute(t, ("yh", "core"), cross)
    chips = PARTS[1]
    columns = functions // kpoint_count
    span = 2 * chips * columns
    pieces = call(
        functools.partial(cluster_kernel, width, columns),
        "cluster_terms",
        jax.ShapeDtypeStruct((chips, 4 * width * 3 // 5, 128), F32),
        [smem] + [vmem] * 8,
        [pltpu.VMEM((4 * width, span + span % 128), F32)],
        flops=10**9,
    )(ids, own, far, near, diag, t, t_yh, t_core, t_diag)

    arrived = lax.all_to_all(pieces, "z", 0, 0, tiled=True)
    index = (yh * PARTS[1] + z) * 2 + core
    block_size = functions // block_pattern.shape[1]
    local_ids = (index * columns + jnp.arange(columns, dtype=jnp.int32)) // block_size
    block_ids = jnp.arange(block_pattern.shape[1], dtype=jnp.int32)
    onehot = (block_ids[:, None] == local_ids[None, :]).astype(F32)
    mask = jnp.dot(block_pattern.astype(F32), onehot, precision=lax.Precision.HIGHEST)
    cluster = call(
        final_kernel,
        "sum_and_mask",
        jax.ShapeDtypeStruct((cells, width, 2, columns), F32),
        [vmem] * 2,
        mib=4,
    )(arrived, mask)
    return jnp.transpose(cluster, (0, 2, 1, 3))


def solution(mesh):
    placed = (P(KA, None, None, None), P(), P(), P(), P())
    return jax.shard_map(
        shards,
        mesh=Mesh(mesh.devices.reshape(PARTS), AXES),
        in_specs=placed,
        out_specs=P(None, None, BAND, KA),
        check_vma=False,
    )
```

time: 77.7 us -> 79.5 us (1.023); the launches traced: 76.1 us -> 78.8 us
  waiting for transfers between devices: 20.3 us -> 28.9 us
  other arithmetic: 4.27 us -> 0.09 us
  local copies, waits for them, and re-layouts: 7.49 us -> 5.64 us
  starting transfers between devices: 32.6 us -> 34.2 us
  Pallas kernels: 10.8 us -> 9.65 us
    ppermute x1 -> x5, starting transfers between devices: 0.09 us -> 6.6 us  [the longest x1 3 us: shards(): t_yh = lax.ppermute(t, 'yh', swap)]
    ppermute x3, waiting for transfers between devices: 0.01 us -> 6.25 us  [shards(): from_below = lax.ppermute(from_below, 'z', up)]
    ppermute x1 -> x5, waiting for transfers between devices: 1.71 us -> 7.55 us  [the longest x1 3.91 us: shards(): t_yh = lax.ppermute(t, 'yh', swap)]
    ppermute x1, waiting for transfers between devices: 0.01 us -> 3.4 us  [shards(): far = lax.ppermute(own, 'yh', swap)]
    all_to_all x1, waiting for transfers between devices: 12.5 us -> 9.38 us  [shards(): arrived = lax.all_to_all(pieces, 'z', 0, 0, tiled=True)]
    ppermute x1, waiting for transfers between devices: 5.11 us -> 2.3 us  [shards(): blocks.append(lax.ppermute(from_below[:cut], 'z', up))]
    ppermute x3, starting transfers between devices: 12.6 us -> 9.88 us  [shards(): from_above = lax.ppermute(from_above, 'z', down)]
    ppermute x3, starting transfers between devices: 0.01 us -> 2.63 us  [shards(): from_below = lax.ppermute(from_below, 'z', up)]
  transfers between devices with their start and end apart: 13 -> 17, of which waited for: 4 -> 7; matrix products, arithmetic and copies ran while one was open for 13% -> 2% of each run, Pallas kernels for 3% -> 7%
where the time goes in v4:
time: 79.5 us; the launch traced here: 78.8 us
  starting transfers between devices  34.2 us (43%)
  waiting for transfers between devices  28.9 us (36%)
  Pallas kernels  9.65 us (12%)
  local copies, waits for them, and re-layouts  5.64 us (7%)
    ppermute x3, starting transfers between devices, shards(): from_above = lax.ppermute(from_above, 'z', down)  9.88 us
    all_to_all x1, waiting for transfers between devices, shards(): arrived = lax.all_to_all(pieces, 'z', 0, 0, tiled=True)  9.38 us
    ppermute x3, waiting for transfers between devices, shards(): from_below = lax.ppermute(from_below, 'z', up)  6.25 us
    all_to_all x1, starting transfers between devices, shards(): arrived = lax.all_to_all(pieces, 'z', 0, 0, tiled=True)  5.21 us
    unnamed x21, local copies, waits for them, and re-layouts  4.5 us
    ppermute x1, waiting for transfers between devices, shards(): t_yh = lax.ppermute(t, 'yh', swap)  3.91 us
    ppermute x1, waiting for transfers between devices, shards(): t_diag = lax.ppermute(t, ('yh', 'core'), cross)  3.63 us
    ppermute x1, waiting for transfers between devices, shards(): far = lax.ppermute(own, 'yh', swap)  3.4 us
  transfers between devices with their start and end apart: 17, of which 7 were waited for; matrix products, arithmetic and copies ran while one was open for 2% of the time, Pallas kernels for 7%

profile of v4, /device:TPU:1, one launch (start us, length us, event | category | flops | bytes accessed | tf_op | source)
XLA Modules:
  0.0 78.8 jit_solution(606011958200606648)
XLA Ops:
  0.0 1.0 %constant_dynamic-slice_fusion = bf16[1,2,20,2400]{3,2,1,0:T(8,128)(2,1)S(1)} fusion(bf16[1,2,160,2400]{3,2,1,0:T(8,128)(2,1)} %param.7, s32[]{:T(128)S(6)} %select_n.12), kind=kLoop, calls=%fused_computation.15 | loop fusion | bytes 384004 | tf_op jit(solution)/shard_map/dynamic_slice | solution.py:182
  1.1 2.5 %collective-permute-start.3 = (bf16[40,2400]{1,0:T(8,128)(2,1)S(1)}, bf16[40,2400]{1,0:T(8,128)(2,1)}, u32[]{:S(2)}, u32[]{:S(2)}) collective-permute-start(bf16[40,2400]{1,0:T(8,128)(2,1)S(1)} %reshape.17), channel_id=1, source_target_pairs={{0,16},{16,32},{32,48},{48,64},{64,80},{80,96},{96,112},{112,0},{1... | collective-permute-start | bytes 576008 | tf_op jit(solution)/shard_map/ppermute | solution.py:187
  3.6 4.0 %collective-permute-start.6 = (bf16[40,2400]{1,0:T(8,128)(2,1)S(1)}, bf16[40,2400]{1,0:T(8,128)(2,1)S(1)}, u32[]{:S(2)}, u32[]{:S(2)}) collective-permute-start(bf16[40,2400]{1,0:T(8,128)(2,1)S(1)} %reshape.17), channel_id=1, source_target_pairs={{16,0},{32,16},{48,32},{64,48},{80,64},{96,80},{112,96},{0,112},{1... | collective-permute-start | bytes 576008 | tf_op jit(solution)/shard_map/ppermute | solution.py:188
  7.7 2.9 %collective-permute-start = (bf16[2,160,2400]{2,1,0:T(8,128)(2,1)}, bf16[2,160,2400]{2,1,0:T(8,128)(2,1)S(1)}, u32[]{:S(2)}, u32[]{:S(2)}) collective-permute-start(bf16[2,160,2400]{2,1,0:T(8,128)(2,1)} %bitcast.7), channel_id=1, source_target_pairs={{0,128},{128,0},{1,129},{129,1},{2,130},{130,2},{3,131},{131,3},{4... | collective-permute-start | bytes 4608008 | tf_op jit(solution)/shard_map/ppermute | solution.py:179
  10.6 1.2 %collective-permute-start.1 = (bf16[2,160,2400]{2,1,0:T(8,128)(2,1)}, bf16[2,160,2400]{2,1,0:T(8,128)(2,1)S(1)}, u32[]{:S(2)}, u32[]{:S(2)}) collective-permute-start(bf16[2,160,2400]{2,1,0:T(8,128)(2,1)} %bitcast.8), channel_id=1, source_target_pairs={{0,8},{8,0},{1,9},{9,1},{2,10},{10,2},{3,11},{11,3},{4,12},{12,4},... | collective-permute-start | bytes 4608008 | tf_op jit(solution)/shard_map/ppermute | solution.py:180
  11.9 0.7 copy-done.1
  12.6 0.7 copy-done.2
  13.3 0.7 copy-done.3
  13.9 0.7 copy-done.4
  14.6 0.7 copy-done.5
  15.2 1.1 %phases.1 = (f32[2,640,1]{2,1,0:T(8,128)S(1)}, bf16[160,400]{1,0:T(8,128)(2,1)S(1)}, bf16[160,240]{1,0:T(8,128)(2,1)S(1)}) custom-call(s32[3]{0:T(128)S(1)} %pad_add_fusion.ids, s32[2]{0:T(128)S(1)} %copy-done.2, s32[32,32]{1,0:T(8,128)S(1)} %copy-done.1, f32[32]{0:T(128)S(1)} %copy-done.3, f32[32]{0:T(128)S(1)} %copy-done.4, f32[32]{0:T(128)S(1)} %copy-done.5), custom_call_target="tpu_custom_call" | custom-call | bytes 1048576 | tf_op jit(solution)/shard_map/phases/pallas_call | solution.py:206
  16.5 1.0 %constant_dynamic-update-slice_fusion.7 = bf16[200,2400]{1,0:T(8,128)(2,1)S(1)} fusion(bf16[200,2400]{1,0:T(8,128)(2,1)S(1)} %constant_dynamic-update-slice_fusion.8, bf16[40,2400]{1,0:T(8,128)(2,1)} %collective-permute-done.3), kind=kLoop, calls=%fused_computation.8 | loop fusion | bytes 386560
  17.5 2.7 %collective-permute-start.7 = (bf16[40,2400]{1,0:T(8,128)(2,1)S(1)}, bf16[40,2400]{1,0:T(8,128)(2,1)S(1)}, u32[]{:S(2)}, u32[]{:S(2)}) collective-permute-start(bf16[40,2400]{1,0:T(8,128)(2,1)S(1)} %collective-permute-done.6), channel_id=1, source_target_pairs={{16,0},{32,16},{48,32},{64,48},{80,64},{96,80},{112,96},{0,112},{1... | collective-permute-start | bytes 576008 | tf_op jit(solution)/shard_map/ppermute | solution.py:188
  20.2 4.1 %collective-permute-done.4 = bf16[40,2400]{1,0:T(8,128)(2,1)S(1)} collective-permute-done((bf16[40,2400]{1,0:T(8,128)(2,1)}, bf16[40,2400]{1,0:T(8,128)(2,1)S(1)}, u32[]{:S(2)}, u32[]{:S(2)}) %collective-permute-start.4) | collective-permute-done | bytes 192032 | tf_op jit(solution)/shard_map/ppermute | solution.py:187
  24.4 3.2 %collective-permute-start.8 = (bf16[40,2400]{1,0:T(8,128)(2,1)S(1)}, bf16[40,2400]{1,0:T(8,128)(2,1)S(1)}, u32[]{:S(2)}, u32[]{:S(2)}) collective-permute-start(bf16[40,2400]{1,0:T(8,128)(2,1)S(1)} %collective-permute-done.7), channel_id=1, source_target_pairs={{16,0},{32,16},{48,32},{64,48},{80,64},{96,80},{112,96},{0,112},{1... | collective-permute-start | bytes 576008 | tf_op jit(solution)/shard_map/ppermute | solution.py:188
  27.6 1.5 %collective-permute-start.12 = (bf16[200,2400]{1,0:T(8,128)(2,1)S(1)}, bf16[200,2400]{1,0:T(8,128)(2,1)S(1)}, u32[]{:S(2)}, u32[]{:S(2)}) collective-permute-start(bf16[200,2400]{1,0:T(8,128)(2,1)S(1)} %constant_dynamic-update-slice_fusion.4.b0), channel_id=1, source_target_pairs={{0,8},{8,0},{1,9},{9,1},{2,10},{10,2},{3,11},{11,3},{4,12},{12,4},... | collective-permute-start | bytes 2880008 | tf_op jit(solution)/shard_map/ppermute | solution.py:195
  29.1 2.1 %collective-permute-done.5 = bf16[40,2400]{1,0:T(8,128)(2,1)S(1)} collective-permute-done((bf16[40,2400]{1,0:T(8,128)(2,1)S(1)}, bf16[40,2400]{1,0:T(8,128)(2,1)S(1)}, u32[]{:S(2)}, u32[]{:S(2)}) %collective-permute-start.5) | collective-permute-done | bytes 192032 | tf_op jit(solution)/shard_map/ppermute | solution.py:187
  31.3 2.8 %collective-permute-start.10 = (bf16[16,2400]{1,0:T(8,128)(2,1)S(1)}, bf16[16,2400]{1,0:T(8,128)(2,1)S(1)}, u32[]{:S(2)}, u32[]{:S(2)}) collective-permute-start(bf16[16,2400]{1,0:T(8,128)(2,1)S(1)} %slice.9), channel_id=1, source_target_pairs={{16,0},{32,16},{48,32},{64,48},{80,64},{96,80},{112,96},{0,112},{1... | collective-permute-start | bytes 230408 | tf_op jit(solution)/shard_map/ppermute | solution.py:192
  34.2 2.3 %collective-permute-done.9 = bf16[24,2400]{1,0:T(8,128)(2,1)S(1)} collective-permute-done((bf16[24,2400]{1,0:T(8,128)(2,1)S(1)}, bf16[24,2400]{1,0:T(8,128)(2,1)S(1)}, u32[]{:S(2)}, u32[]{:S(2)}) %collective-permute-start.9) | collective-permute-done | bytes 115232 | tf_op jit(solution)/shard_map/ppermute | solution.py:191
  36.5 2.6 %collective-permute-start.11 = (bf16[120,2400]{1,0:T(8,128)(2,1)S(1)}, bf16[120,2400]{1,0:T(8,128)(2,1)S(1)}, u32[]{:S(2)}, u32[]{:S(2)}) collective-permute-start(bf16[120,2400]{1,0:T(8,128)(2,1)S(1)} %constant_dynamic-update-slice_fusion.b0), channel_id=1, source_target_pairs={{0,8},{8,0},{1,9},{9,1},{2,10},{10,2},{3,11},{11,3},{4,12},{12,4},... | collective-permute-start | bytes 1728008 | tf_op jit(solution)/shard_map/ppermute | solution.py:197
  39.1 1.4 %own_first.1.t_own = f32[80,160]{1,0:T(8,128)S(1)} custom-call(bf16[2,160,2400]{2,1,0:T(8,128)(2,1)S(1)} %bitcast.9, bf16[200,2400]{1,0:T(8,128)(2,1)S(1)} %constant_dynamic-update-slice_fusion.4.b0, bf16[200,2400]{1,0:T(8,128)(2,1)S(1)} %collective-permute-done.12.b1, f32[2,640,1]{2,1,0:T(8,128)S(1)} %get-tuple-element.8.w, ...), custom_call_target="tpu_custom_call" | custom-call | flops 1000000000 | bytes 1048576 | tf_op jit(solution)/shard_map/own_first/pallas_call | solution.py:221
  40.6 3.4 %collective-permute-done.q_ref.far = bf16[2,160,2400]{2,1,0:T(8,128)(2,1)S(1)} collective-permute-done((bf16[2,160,2400]{2,1,0:T(8,128)(2,1)}, bf16[2,160,2400]{2,1,0:T(8,128)(2,1)S(1)}, u32[]{:S(2)}, u32[]{:S(2)}) %collective-permute-start) | collective-permute-done | bytes 1536032 | tf_op jit(solution)/shard_map/ppermute | solution.py:179
  44.0 1.9 %collective-permute-start.2 = (bf16[2,160,2400]{2,1,0:T(8,128)(2,1)S(1)}, bf16[2,160,2400]{2,1,0:T(8,128)(2,1)S(1)}, u32[]{:S(2)}, u32[]{:S(2)}) collective-permute-start(bf16[2,160,2400]{2,1,0:T(8,128)(2,1)S(1)} %collective-permute-done.q_ref.far), channel_id=1, source_target_pairs={{0,8},{8,0},{1,9},{9,1},{2,10},{10,2},{3,11},{11,3},{4,12},{12,4},... | collective-permute-start | bytes 4608008 | tf_op jit(solution)/shard_map/ppermute | solution.py:181
  45.8 1.4 %far_first.1.t_far = f32[80,160]{1,0:T(8,128)S(1)} custom-call(bf16[2,160,2400]{2,1,0:T(8,128)(2,1)S(1)} %collective-permute-done.q_ref.far, bf16[200,2400]{1,0:T(8,128)(2,1)S(1)} %constant_dynamic-update-slice_fusion.4.b0, bf16[200,2400]{1,0:T(8,128)(2,1)S(1)} %collective-permute-done.12.b1, f32[2,640,1]{2,1,0:T(8,128)S(1)} %get-tuple-element.8.w, ...), custom_call_target="tpu_custom_call" | custom-call | flops 20999999488 | bytes 1048576 | tf_op jit(solution)/shard_map/far_first/pallas_call | solution.py:221
  47.3 1.8 %last_terms.1.t = f32[2,80,160]{2,1,0:T(8,128)S(1)} custom-call(bf16[2,160,2400]{2,1,0:T(8,128)(2,1)S(1)} %bitcast.10, bf16[2,160,2400]{2,1,0:T(8,128)(2,1)S(1)} %collective-permute-done.q_ref.far, bf16[120,2400]{1,0:T(8,128)(2,1)S(1)} %constant_dynamic-update-slice_fusion.b0, bf16[120,2400]{1,0:T(8,128)(2,1)S(1)} %collective-permute-done.11.b1, ...), custom_call_target="tpu_custom_call" | custom-call | flops 1000000000 | bytes 1048576 | tf_op jit(solution)/shard_map/last_terms/pallas_call | solution.py:230
  49.1 3.0 %collective-permute-start.13 = (f32[2,80,160]{2,1,0:T(8,128)S(1)}, f32[2,80,160]{2,1,0:T(8,128)S(1)}, u32[]{:S(2)}, u32[]{:S(2)}) collective-permute-start(f32[2,80,160]{2,1,0:T(8,128)S(1)} %last_terms.1.t), channel_id=1, source_target_pairs={{0,128},{128,0},{1,129},{129,1},{2,130},{130,2},{3,131},{131,3},{4... | collective-permute-start | bytes 307208 | tf_op jit(solution)/shard_map/ppermute | solution.py:240
  52.6 3.9 %collective-permute-done.13.t_yh = f32[2,80,160]{2,1,0:T(8,128)S(1)} collective-permute-done((f32[2,80,160]{2,1,0:T(8,128)S(1)}, f32[2,80,160]{2,1,0:T(8,128)S(1)}, u32[]{:S(2)}, u32[]{:S(2)}) %collective-permute-start.13) | collective-permute-done | bytes 102432 | tf_op jit(solution)/shard_map/ppermute | solution.py:240
  56.5 3.6 %collective-permute-done.15.t_diag = f32[2,80,160]{2,1,0:T(8,128)S(1)} collective-permute-done((f32[2,80,160]{2,1,0:T(8,128)S(1)}, f32[2,80,160]{2,1,0:T(8,128)S(1)}, u32[]{:S(2)}, u32[]{:S(2)}) %collective-permute-start.15) | collective-permute-done | bytes 102432 | tf_op jit(solution)/shard_map/ppermute | solution.py:241
  60.2 3.1 %cluster_terms.1 = f32[8,48,128]{2,1,0:T(8,128)} custom-call(s32[3]{0:T(128)S(1)} %pad_add_fusion.ids, bf16[2,160,2400]{2,1,0:T(8,128)(2,1)S(1)} %bitcast.11, bf16[2,160,2400]{2,1,0:T(8,128)(2,1)S(1)} %collective-permute-done.q_ref.far, bf16[2,160,2400]{2,1,0:T(8,128)(2,1)S(1)} %collective-permute-done.1.near, ...), custom_call_target="tpu_custom_call" | custom-call | flops 1000000000 | bytes 1048576 | tf_op jit(solution)/shard_map/cluster_terms/pallas_call | solution.py:245
  63.2 5.2 %all-to-all-start = ((f32[8,48,128]{2,1,0:T(8,128)}), f32[8,48,128]{2,1,0:T(8,128)S(1)}, u32[]{:S(2)}, u32[]{:S(2)}) async-start(f32[8,48,128]{2,1,0:T(8,128)} %cluster_terms.1), calls=%async_computation | async-start | bytes 393216 | tf_op jit(solution)/shard_map/all_to_all | solution.py:254
  68.6 9.4 %all-to-all-done.arrived = f32[8,48,128]{2,1,0:T(8,128)S(1)} async-done(((f32[8,48,128]{2,1,0:T(8,128)}), f32[8,48,128]{2,1,0:T(8,128)S(1)}, u32[]{:S(2)}, u32[]{:S(2)}) %all-to-all-start) | async-done | bytes 196640 | tf_op jit(solution)/shard_map/all_to_all | solution.py:254
  78.0 0.8 %sum_and_mask.1 = f32[2,20,2,75]{3,2,1,0:T(2,128)} custom-call(f32[8,48,128]{2,1,0:T(8,128)S(1)} %all-to-all-done.arrived, f32[2,75]{1,0:T(2,128)S(1)} %convolution_bitcast_fusion.mask), custom_call_target="tpu_custom_call" | custom-call | bytes 1048576 | tf_op jit(solution)/shard_map/sum_and_mask/pallas_call | solution.py:261
  (38 shorter events, 1.1 us)
Async XLA Ops:
  1.1 15.3 %collective-permute-start.3 = (bf16[40,2400]{1,0:T(8,128)(2,1)S(1)}, bf16[40,2400]{1,0:T(8,128)(2,1)}, u32[]{:S(2)}, u32[]{:S(2)}) collective-permute-start(bf16[40,2400]{1,0:T(8,128)(2,1)S(1)} %reshape.17), channel_id=1, source_target_pairs={{0,16},{16,32},{32,48},{48,64},{64,80},{80,96},{96,112},{112,0},{1... | collective-permute-start | bytes 576008 | tf_op jit(solution)/shard_map/ppermute | solution.py:187
  3.6 13.9 %collective-permute-start.6 = (bf16[40,2400]{1,0:T(8,128)(2,1)S(1)}, bf16[40,2400]{1,0:T(8,128)(2,1)S(1)}, u32[]{:S(2)}, u32[]{:S(2)}) collective-permute-start(bf16[40,2400]{1,0:T(8,128)(2,1)S(1)} %reshape.17), channel_id=1, source_target_pairs={{16,0},{32,16},{48,32},{64,48},{80,64},{96,80},{112,96},{0,112},{1... | collective-permute-start | bytes 576008 | tf_op jit(solution)/shard_map/ppermute | solution.py:188
  7.7 36.3 %collective-permute-start = (bf16[2,160,2400]{2,1,0:T(8,128)(2,1)}, bf16[2,160,2400]{2,1,0:T(8,128)(2,1)S(1)}, u32[]{:S(2)}, u32[]{:S(2)}) collective-permute-start(bf16[2,160,2400]{2,1,0:T(8,128)(2,1)} %bitcast.7), channel_id=1, source_target_pairs={{0,128},{128,0},{1,129},{129,1},{2,130},{130,2},{3,131},{131,3},{4... | collective-permute-start | bytes 4608008 | tf_op jit(solution)/shard_map/ppermute | solution.py:179
  10.6 42.0 %collective-permute-start.1 = (bf16[2,160,2400]{2,1,0:T(8,128)(2,1)}, bf16[2,160,2400]{2,1,0:T(8,128)(2,1)S(1)}, u32[]{:S(2)}, u32[]{:S(2)}) collective-permute-start(bf16[2,160,2400]{2,1,0:T(8,128)(2,1)} %bitcast.8), channel_id=1, source_target_pairs={{0,8},{8,0},{1,9},{9,1},{2,10},{10,2},{3,11},{11,3},{4,12},{12,4},... | collective-permute-start | bytes 4608008 | tf_op jit(solution)/shard_map/ppermute | solution.py:180
  11.9 0.7 copy-start.1
  12.6 0.7 copy-start.2
  13.3 0.7 copy-start.3
  13.9 0.7 copy-start.4
  14.6 0.7 copy-start.5
  16.4 22.7 %copy-start = (bf16[1,2,160,2400]{3,2,1,0:T(8,128)(2,1)S(1)}, bf16[1,2,160,2400]{3,2,1,0:T(8,128)(2,1)}, u32[]{:S(2)}) copy-start(bf16[1,2,160,2400]{3,2,1,0:T(8,128)(2,1)} %param.7) | copy-start | bytes 4608004
  16.4 8.0 %collective-permute-start.4 = (bf16[40,2400]{1,0:T(8,128)(2,1)}, bf16[40,2400]{1,0:T(8,128)(2,1)S(1)}, u32[]{:S(2)}, u32[]{:S(2)}) collective-permute-start(bf16[40,2400]{1,0:T(8,128)(2,1)} %collective-permute-done.3), channel_id=1, source_target_pairs={{0,16},{16,32},{32,48},{48,64},{64,80},{80,96},{96,112},{112,0},{1... | collective-permute-start | bytes 576008 | tf_op jit(solution)/shard_map/ppermute | solution.py:187
  17.5 6.9 %collective-permute-start.7 = (bf16[40,2400]{1,0:T(8,128)(2,1)S(1)}, bf16[40,2400]{1,0:T(8,128)(2,1)S(1)}, u32[]{:S(2)}, u32[]{:S(2)}) collective-permute-start(bf16[40,2400]{1,0:T(8,128)(2,1)S(1)} %collective-permute-done.6), channel_id=1, source_target_pairs={{16,0},{32,16},{48,32},{64,48},{80,64},{96,80},{112,96},{0,112},{1... | collective-permute-start | bytes 576008 | tf_op jit(solution)/shard_map/ppermute | solution.py:188
  24.4 6.8 %collective-permute-start.5 = (bf16[40,2400]{1,0:T(8,128)(2,1)S(1)}, bf16[40,2400]{1,0:T(8,128)(2,1)S(1)}, u32[]{:S(2)}, u32[]{:S(2)}) collective-permute-start(bf16[40,2400]{1,0:T(8,128)(2,1)S(1)} %collective-permute-done.4), channel_id=1, source_target_pairs={{0,16},{16,32},{32,48},{48,64},{64,80},{80,96},{96,112},{112,0},{1... | collective-permute-start | bytes 576008 | tf_op jit(solution)/shard_map/ppermute | solution.py:187
  24.4 6.9 %collective-permute-start.8 = (bf16[40,2400]{1,0:T(8,128)(2,1)S(1)}, bf16[40,2400]{1,0:T(8,128)(2,1)S(1)}, u32[]{:S(2)}, u32[]{:S(2)}) collective-permute-start(bf16[40,2400]{1,0:T(8,128)(2,1)S(1)} %collective-permute-done.7), channel_id=1, source_target_pairs={{16,0},{32,16},{48,32},{64,48},{80,64},{96,80},{112,96},{0,112},{1... | collective-permute-start | bytes 576008 | tf_op jit(solution)/shard_map/ppermute | solution.py:188
  27.6 11.5 %collective-permute-start.12 = (bf16[200,2400]{1,0:T(8,128)(2,1)S(1)}, bf16[200,2400]{1,0:T(8,128)(2,1)S(1)}, u32[]{:S(2)}, u32[]{:S(2)}) collective-permute-start(bf16[200,2400]{1,0:T(8,128)(2,1)S(1)} %constant_dynamic-update-slice_fusion.4.b0), channel_id=1, source_target_pairs={{0,8},{8,0},{1,9},{9,1},{2,10},{10,2},{3,11},{11,3},{4,12},{12,4},... | collective-permute-start | bytes 2880008 | tf_op jit(solution)/shard_map/ppermute | solution.py:195
  31.2 5.2 %collective-permute-start.9 = (bf16[24,2400]{1,0:T(8,128)(2,1)S(1)}, bf16[24,2400]{1,0:T(8,128)(2,1)S(1)}, u32[]{:S(2)}, u32[]{:S(2)}) collective-permute-start(bf16[24,2400]{1,0:T(8,128)(2,1)S(1)} %slice.8), channel_id=1, source_target_pairs={{0,16},{16,32},{32,48},{48,64},{64,80},{80,96},{96,112},{112,0},{1... | collective-permute-start | bytes 345608 | tf_op jit(solution)/shard_map/ppermute | solution.py:191
  31.3 5.1 %collective-permute-start.10 = (bf16[16,2400]{1,0:T(8,128)(2,1)S(1)}, bf16[16,2400]{1,0:T(8,128)(2,1)S(1)}, u32[]{:S(2)}, u32[]{:S(2)}) collective-permute-start(bf16[16,2400]{1,0:T(8,128)(2,1)S(1)} %slice.9), channel_id=1, source_target_pairs={{16,0},{32,16},{48,32},{64,48},{80,64},{96,80},{112,96},{0,112},{1... | collective-permute-start | bytes 230408 | tf_op jit(solution)/shard_map/ppermute | solution.py:192
  36.5 10.8 %collective-permute-start.11 = (bf16[120,2400]{1,0:T(8,128)(2,1)S(1)}, bf16[120,2400]{1,0:T(8,128)(2,1)S(1)}, u32[]{:S(2)}, u32[]{:S(2)}) collective-permute-start(bf16[120,2400]{1,0:T(8,128)(2,1)S(1)} %constant_dynamic-update-slice_fusion.b0), channel_id=1, source_target_pairs={{0,8},{8,0},{1,9},{9,1},{2,10},{10,2},{3,11},{11,3},{4,12},{12,4},... | collective-permute-start | bytes 1728008 | tf_op jit(solution)/shard_map/ppermute | solution.py:197
  44.0 16.2 %collective-permute-start.2 = (bf16[2,160,2400]{2,1,0:T(8,128)(2,1)S(1)}, bf16[2,160,2400]{2,1,0:T(8,128)(2,1)S(1)}, u32[]{:S(2)}, u32[]{:S(2)}) collective-permute-start(bf16[2,160,2400]{2,1,0:T(8,128)(2,1)S(1)} %collective-permute-done.q_ref.far), channel_id=1, source_target_pairs={{0,8},{8,0},{1,9},{9,1},{2,10},{10,2},{3,11},{11,3},{4,12},{12,4},... | collective-permute-start | bytes 4608008 | tf_op jit(solution)/shard_map/ppermute | solution.py:181
  49.1 19.3 %copy-start.6 = (s32[2,30]{1,0:T(2,128)S(1)}, s32[2,30]{1,0:T(2,128)}, u32[]{:S(2)}) copy-start(s32[2,30]{1,0:T(2,128)} %param.11) | copy-start | bytes 724
  49.1 7.4 %collective-permute-start.13 = (f32[2,80,160]{2,1,0:T(8,128)S(1)}, f32[2,80,160]{2,1,0:T(8,128)S(1)}, u32[]{:S(2)}, u32[]{:S(2)}) collective-permute-start(f32[2,80,160]{2,1,0:T(8,128)S(1)} %last_terms.1.t), channel_id=1, source_target_pairs={{0,128},{128,0},{1,129},{129,1},{2,130},{130,2},{3,131},{131,3},{4... | collective-permute-start | bytes 307208 | tf_op jit(solution)/shard_map/ppermute | solution.py:240
  52.1 4.4 %collective-permute-start.14 = (f32[2,80,160]{2,1,0:T(8,128)S(1)}, f32[2,80,160]{2,1,0:T(8,128)S(1)}, u32[]{:S(2)}, u32[]{:S(2)}) collective-permute-start(f32[2,80,160]{2,1,0:T(8,128)S(1)} %last_terms.1.t), channel_id=1, source_target_pairs={{0,8},{8,0},{1,9},{9,1},{2,10},{10,2},{3,11},{11,3},{4,12},{12,4},... | collective-permute-start | bytes 307208 | tf_op jit(solution)/shard_map/ppermute | solution.py:239
  52.4 7.8 %collective-permute-start.15 = (f32[2,80,160]{2,1,0:T(8,128)S(1)}, f32[2,80,160]{2,1,0:T(8,128)S(1)}, u32[]{:S(2)}, u32[]{:S(2)}) collective-permute-start(f32[2,80,160]{2,1,0:T(8,128)S(1)} %last_terms.1.t), channel_id=1, source_target_pairs={{0,136},{8,128},{128,8},{136,0},{1,137},{9,129},{129,9},{137,1},{2... | collective-permute-start | bytes 307208 | tf_op jit(solution)/shard_map/ppermute | solution.py:241
  63.2 14.7 %all-to-all-start = ((f32[8,48,128]{2,1,0:T(8,128)}), f32[8,48,128]{2,1,0:T(8,128)S(1)}, u32[]{:S(2)}, u32[]{:S(2)}) async-start(f32[8,48,128]{2,1,0:T(8,128)} %cluster_terms.1), calls=%async_computation | async-start | bytes 393216 | tf_op jit(solution)/shard_map/all_to_all | solution.py:254

commit v5 on v4

--- a/solution.py
+++ b/solution.py
@@ -173,12 +173,14 @@
     up = [(i, (i + 1) % PARTS[1]) for i in range(PARTS[1])]
     down = [(j, i) for i, j in up]
     swap = [(0, 1), (1, 0)]
-    cross = [(0, 3), (1, 2), (2, 1), (3, 0)]
+    right = [(i, (i + 1) % PARTS[4]) for i in range(PARTS[4])]
+    left = [(j, i) for i, j in right]
     vmem, smem = pltpu.VMEM, pltpu.SMEM
 
-    far = lax.ppermute(own, "yh", swap)
+    x = lax.axis_index("x")
+    quarters = own.reshape(PARTS[4], -1, functions)
+    quarter = lax.ppermute(lax.dynamic_index_in_dim(quarters, x, 0, keepdims=False), "yh", swap)
     near = lax.ppermute(own, "core", swap)
-    diag = lax.ppermute(far, "core", swap)
     block = lax.dynamic_slice_in_dim(own, band * width, width, 1).reshape(group, functions)
     blocks = [block]
     offsets = [0, -1, 1, -2, 2, -3, 3, -4]
@@ -187,6 +189,28 @@
         from_below = lax.ppermute(from_below, "z", up)
         from_above = lax.ppermute(from_above, "z", down)
         blocks += [from_below, from_above]
+        if step == 2:
+            held = (from_below, from_above, quarter, near)
+            from_below, from_above, quarter, near = lax.optimization_barrier(held)
+            from_left = lax.ppermute(quarter, "x", right)
+            from_right = lax.ppermute(quarter, "x", left)
+    held = (from_below, from_above, from_left, from_right)
+    from_below, from_above, from_left, from_right = lax.optimization_barrier(held)
+    mid = quarter.shape[0] // 2
+    from_left_2 = lax.ppermute(from_left[:mid], "x", right)
+    from_right_2 = lax.ppermute(from_right[mid:], "x", left)
+    far = jnp.zeros(quarters.shape, BF16)
+    for value, distance, row in (
+        (quarter, 0, 0),
+        (from_left, 3, 0),
+        (from_right, 1, 0),
+        (from_left_2, 2, 0),
+        (from_right_2, 2, mid),
+    ):
+        slot = jnp.bitwise_and(x + distance, PARTS[4] - 1)
+        far = lax.dynamic_update_slice(far, value[None], (slot, row, 0))
+    far = far.reshape(own.shape)
+    diag = lax.ppermute(far, "core", swap)
     cut = 24
     blocks.append(lax.ppermute(from_below[:cut], "z", up))
     blocks.append(lax.ppermute(from_above[cut:], "z", down))
@@ -203,6 +227,7 @@
     angles = 2.0 * np.pi * np.arange(kpoint_count) / kpoint_count
     tables = [jnp.asarray((f(angles) / kpoint_count).astype(np.float32)) for f in (np.cos, np.sin)]
     ids = jnp.stack([yh, z, core]).astype(jnp.int32)
+    later_ids, _ = lax.optimization_barrier((ids, last))
     weights, g_first, g_last = call(
         functools.partial(prep_kernel, width, functions, k_points),
         "phases",
@@ -212,7 +237,7 @@
             jax.ShapeDtypeStruct((8 * width, late), BF16),
         ),
         [smem] * 6,
-    )(ids, frag_cells, diff_class, class_weight, *tables)
+    )(later_ids, frag_cells, diff_class, class_weight, *tables)
 
     one = jax.ShapeDtypeStruct((4 * width, occupied), F32)
     t_first = []
@@ -238,7 +263,7 @@
 
     t_core = lax.ppermute(t, "core", swap)
     t_yh = lax.ppermute(t, "yh", swap)
-    t_diag = lax.ppermute(t, ("yh", "core"), cross)
+    t_diag = lax.ppermute(t_yh, "core", swap)
     chips = PARTS[1]
     columns = functions // kpoint_count
     span = 2 * chips * columns

time: 79.5 us -> 82.3 us (1.035)
  local copies, waits for them, and re-layouts: 5.64 us -> 8.83 us
  starting transfers between devices: 34.2 us -> 31.4 us
  waiting for transfers between devices: 28.9 us -> 31.6 us
    ppermute x2 -> x6, starting transfers between devices: 3.12 us -> 7.9 us  [the longest x1 2.91 us: shards(): lax.ppermute(lax.dynamic_index_in_dim(quarters, x, 0, keepdims=False), 'y...]
    ppermute x1, starting transfers between devices: 2.79 us -> 0.01 us  [shards(): blocks.append(lax.ppermute(from_above[cut:], 'z', down))]
    ppermute x3, starting transfers between devices: 2.63 us -> 0.01 us  [shards(): from_below = lax.ppermute(from_below, 'z', up)]
    ppermute x1, starting transfers between devices: 3 us -> 0.46 us  [shards(): t_yh = lax.ppermute(t, 'yh', swap)]
    ppermute x3, waiting for transfers between devices: 6.25 us -> 8.73 us  [shards(): from_below = lax.ppermute(from_below, 'z', up)]
    ppermute x1, waiting for transfers between devices: 3.91 us -> 6.37 us  [shards(): t_yh = lax.ppermute(t, 'yh', swap)]
    ppermute x3, starting transfers between devices: 9.88 us -> 12.1 us  [shards(): from_above = lax.ppermute(from_above, 'z', down)]
    squeeze x0 -> x1, local copies, waits for them, and re-layouts: none -> 1.77 us  [shards(): lax.dynamic_index_in_dim(quarters, x, 0, keepdims=False)]
  transfers between devices with their start and end apart: 17 -> 21, of which waited for: 7 -> 8; matrix products, arithmetic and copies ran while one was open for 2% -> 10% of each run, Pallas kernels for 7% -> 7%
where the time goes in v5:
time: 82.3 us; the launch traced here: 82 us
  waiting for transfers between devices  31.6 us (38%)
  starting transfers between devices  31.4 us (38%)
  Pallas kernels  9.67 us (12%)
  local copies, waits for them, and re-layouts  8.83 us (11%)
    ppermute x3, starting transfers between devices, shards(): from_above = lax.ppermute(from_above, 'z', down)  12.1 us
    all_to_all x1, waiting for transfers between devices, shards(): arrived = lax.all_to_all(pieces, 'z', 0, 0, tiled=True)  9.43 us
    ppermute x3, waiting for transfers between devices, shards(): from_below = lax.ppermute(from_below, 'z', up)  8.73 us
    ppermute x1, waiting for transfers between devices, shards(): t_yh = lax.ppermute(t, 'yh', swap)  6.37 us
    unnamed x23, local copies, waits for them, and re-layouts  3.84 us
    all_to_all x1, starting transfers between devices, shards(): arrived = lax.all_to_all(pieces, 'z', 0, 0, tiled=True)  3.58 us
    pallas_call x1, Pallas kernels, shards(): call(functools.partial(cluster_kernel, width, columns), 'cluster_terms',...  3.05 us
    ppermute x1, waiting for transfers between devices, shards(): from_left = lax.ppermute(quarter, 'x', right)  2.99 us
  transfers between devices with their start and end apart: 21, of which 8 were waited for; matrix products, arithmetic and copies ran while one was open for 10% of the time, Pallas kernels for 7%

profile of v5, /device:TPU:1, one launch (start us, length us, event | category | flops | bytes accessed | tf_op | source)
XLA Modules:
  0.0 82.0 jit_solution(5275502747057866323)
XLA Ops:
  0.0 1.1 %constant_dynamic-slice_fusion = bf16[1,2,20,2400]{3,2,1,0:T(8,128)(2,1)S(1)} fusion(bf16[1,2,160,2400]{3,2,1,0:T(8,128)(2,1)} %param.7, s32[]{:T(128)S(6)} %select_n.29), kind=kLoop, calls=%fused_computation.19 | loop fusion | bytes 384004 | tf_op jit(solution)/shard_map/dynamic_slice | solution.py:184
  1.2 6.5 %collective-permute-start.2 = (bf16[40,2400]{1,0:T(8,128)(2,1)S(1)}, bf16[40,2400]{1,0:T(8,128)(2,1)S(1)}, u32[]{:S(2)}, u32[]{:S(2)}) collective-permute-start(bf16[40,2400]{1,0:T(8,128)(2,1)S(1)} %reshape.20), channel_id=1, source_target_pairs={{16,0},{32,16},{48,32},{64,48},{80,64},{96,80},{112,96},{0,112},{1... | collective-permute-start | bytes 576008 | tf_op jit(solution)/shard_map/ppermute | solution.py:190
  7.7 1.8 %dynamic-slice_bitcast_fusion = bf16[80,2400]{1,0:T(8,128)(2,1)} fusion(bf16[4,80,2400]{2,1,0:T(8,128)(2,1)} %bitcast.21, s32[]{:T(128)S(6)} %select_n.30), kind=kLoop, calls=%fused_computation.4 | loop fusion | bytes 768004 | tf_op jit(solution)/shard_map/jit(dynamic_index_in_dim)/squeeze | solution.py:182
  9.5 2.9 %collective-permute-start.4 = (bf16[80,2400]{1,0:T(8,128)(2,1)}, bf16[80,2400]{1,0:T(8,128)(2,1)}, u32[]{:S(2)}, u32[]{:S(2)}) collective-permute-start(bf16[80,2400]{1,0:T(8,128)(2,1)} %dynamic-slice_bitcast_fusion), channel_id=1, source_target_pairs={{0,128},{128,0},{1,129},{129,1},{2,130},{130,2},{3,131},{131,3},{4... | collective-permute-start | bytes 1152008 | tf_op jit(solution)/shard_map/ppermute | solution.py:182
  12.4 1.2 %collective-permute-start.5 = (bf16[2,160,2400]{2,1,0:T(8,128)(2,1)S(1)}, bf16[2,160,2400]{2,1,0:T(8,128)(2,1)S(1)}, u32[]{:S(2)}, u32[]{:S(2)}) collective-permute-start(bf16[2,160,2400]{2,1,0:T(8,128)(2,1)S(1)} %bitcast.22), channel_id=1, source_target_pairs={{0,8},{8,0},{1,9},{9,1},{2,10},{10,2},{3,11},{11,3},{4,12},{12,4},... | collective-permute-start | bytes 4608008 | tf_op jit(solution)/shard_map/ppermute | solution.py:183
  13.6 0.7 constant_dynamic-update-slice_fusion.8
  14.4 3.0 %collective-permute-start.3 = (bf16[40,2400]{1,0:T(8,128)(2,1)S(1)}, bf16[40,2400]{1,0:T(8,128)(2,1)S(1)}, u32[]{:S(2)}, u32[]{:S(2)}) collective-permute-start(bf16[40,2400]{1,0:T(8,128)(2,1)S(1)} %collective-permute-done.2), channel_id=1, source_target_pairs={{16,0},{32,16},{48,32},{64,48},{80,64},{96,80},{112,96},{0,112},{1... | collective-permute-start | bytes 576008 | tf_op jit(solution)/shard_map/ppermute | solution.py:190
  17.4 1.6 %constant_dynamic-update-slice_fusion.7 = bf16[200,2400]{1,0:T(8,128)(2,1)} fusion(bf16[200,2400]{1,0:T(8,128)(2,1)} %constant_dynamic-update-slice_fusion.8, bf16[40,2400]{1,0:T(8,128)(2,1)} %collective-permute-done), kind=kLoop, calls=%fused_computation.14 | loop fusion | bytes 389120
  19.7 5.2 %collective-permute-done.1 = bf16[40,2400]{1,0:T(8,128)(2,1)S(1)} collective-permute-done((bf16[40,2400]{1,0:T(8,128)(2,1)}, bf16[40,2400]{1,0:T(8,128)(2,1)S(1)}, u32[]{:S(2)}, u32[]{:S(2)}) %collective-permute-start.1) | collective-permute-done | bytes 192032 | tf_op jit(solution)/shard_map/ppermute | solution.py:189
  25.0 0.7 constant_dynamic-update-slice_fusion.5
  26.4 1.1 %collective-permute-start.16 = (bf16[200,2400]{1,0:T(8,128)(2,1)}, bf16[200,2400]{1,0:T(8,128)(2,1)S(1)}, u32[]{:S(2)}, u32[]{:S(2)}) collective-permute-start(bf16[200,2400]{1,0:T(8,128)(2,1)} %constant_dynamic-update-slice_fusion.4.b0), channel_id=1, source_target_pairs={{0,8},{8,0},{1,9},{9,1},{2,10},{10,2},{3,11},{11,3},{4,12},{12,4},... | collective-permute-start | bytes 2880008 | tf_op jit(solution)/shard_map/ppermute | solution.py:219
  27.5 2.5 %collective-permute-start.9 = (bf16[80,2400]{1,0:T(8,128)(2,1)}, bf16[80,2400]{1,0:T(8,128)(2,1)S(1)}, u32[]{:S(2)}, u32[]{:S(2)}) collective-permute-start(bf16[80,2400]{1,0:T(8,128)(2,1)} %collective-permute-done.4), channel_id=1, source_target_pairs={{1,0},{2,1},{3,2},{0,3},{5,4},{6,5},{7,6},{4,7},{9,8},{10,9},{11,1... | collective-permute-start | bytes 1152008 | tf_op jit(solution)/shard_map/ppermute | solution.py:196
  30.0 2.7 %collective-permute-start.7 = (bf16[40,2400]{1,0:T(8,128)(2,1)S(1)}, bf16[40,2400]{1,0:T(8,128)(2,1)S(1)}, u32[]{:S(2)}, u32[]{:S(2)}) collective-permute-start(bf16[40,2400]{1,0:T(8,128)(2,1)S(1)} %collective-permute-done.3), channel_id=1, source_target_pairs={{16,0},{32,16},{48,32},{64,48},{80,64},{96,80},{112,96},{0,112},{1... | collective-permute-start | bytes 576008 | tf_op jit(solution)/shard_map/ppermute | solution.py:190
  32.8 1.0 %bitcast_dynamic-update-slice_fusion.2 = bf16[4,80,2400]{2,1,0:T(8,128)(2,1)S(1)} fusion(bf16[4,80,2400]{2,1,0:T(8,128)(2,1)S(1)} %broadcast_in_dim.20, s32[]{:T(128)S(6)} %select_n.31, bf16[80,2400]{1,0:T(8,128)(2,1)} %collective-permute-done.4), kind=kLoop, calls=%fused_computation.3 | loop fusion | bytes 773124 | tf_op jit(solution)/shard_map/dynamic_update_slice | solution.py:211
  33.8 3.5 %collective-permute-done.6 = bf16[40,2400]{1,0:T(8,128)(2,1)S(1)} collective-permute-done((bf16[40,2400]{1,0:T(8,128)(2,1)S(1)}, bf16[40,2400]{1,0:T(8,128)(2,1)S(1)}, u32[]{:S(2)}, u32[]{:S(2)}) %collective-permute-start.6) | collective-permute-done | bytes 192032 | tf_op jit(solution)/shard_map/ppermute | solution.py:189
  37.4 1.3 %collective-permute-done.9 = bf16[80,2400]{1,0:T(8,128)(2,1)S(1)} collective-permute-done((bf16[80,2400]{1,0:T(8,128)(2,1)}, bf16[80,2400]{1,0:T(8,128)(2,1)S(1)}, u32[]{:S(2)}, u32[]{:S(2)}) %collective-permute-start.9) | collective-permute-done | bytes 384032 | tf_op jit(solution)/shard_map/ppermute | solution.py:196
  38.7 3.0 %collective-permute-done.8 = bf16[80,2400]{1,0:T(8,128)(2,1)S(1)} collective-permute-done((bf16[80,2400]{1,0:T(8,128)(2,1)}, bf16[80,2400]{1,0:T(8,128)(2,1)S(1)}, u32[]{:S(2)}, u32[]{:S(2)}) %collective-permute-start.8) | collective-permute-done | bytes 384032 | tf_op jit(solution)/shard_map/ppermute | solution.py:195
  41.7 1.5 %collective-permute-start.13 = (bf16[24,2400]{1,0:T(8,128)(2,1)S(1)}, bf16[24,2400]{1,0:T(8,128)(2,1)S(1)}, u32[]{:S(2)}, u32[]{:S(2)}) collective-permute-start(bf16[24,2400]{1,0:T(8,128)(2,1)S(1)} %slice.14), channel_id=1, source_target_pairs={{0,16},{16,32},{32,48},{48,64},{64,80},{80,96},{96,112},{112,0},{1... | collective-permute-start | bytes 345608 | tf_op jit(solution)/shard_map/ppermute | solution.py:215
  43.7 1.1 %collective-permute-start.10 = (bf16[40,2400]{1,0:T(8,128)(2,1)S(1)}, bf16[40,2400]{1,0:T(8,128)(2,1)S(1)}, u32[]{:S(2)}, u32[]{:S(2)}) collective-permute-start(bf16[40,2400]{1,0:T(8,128)(2,1)S(1)} %slice.12), channel_id=1, source_target_pairs={{0,1},{1,2},{2,3},{3,0},{4,5},{5,6},{6,7},{7,4},{8,9},{9,10},{10,1... | collective-permute-start | bytes 576008 | tf_op jit(solution)/shard_map/ppermute | solution.py:200
  44.9 1.8 %collective-permute-done.13 = bf16[24,2400]{1,0:T(8,128)(2,1)S(1)} collective-permute-done((bf16[24,2400]{1,0:T(8,128)(2,1)S(1)}, bf16[24,2400]{1,0:T(8,128)(2,1)S(1)}, u32[]{:S(2)}, u32[]{:S(2)}) %collective-permute-start.13) | collective-permute-done | bytes 115232 | tf_op jit(solution)/shard_map/ppermute | solution.py:215
  46.7 2.6 %collective-permute-start.15 = (bf16[120,2400]{1,0:T(8,128)(2,1)S(1)}, bf16[120,2400]{1,0:T(8,128)(2,1)S(1)}, u32[]{:S(2)}, u32[]{:S(2)}) collective-permute-start(bf16[120,2400]{1,0:T(8,128)(2,1)S(1)} %constant_dynamic-update-slice_fusion.b0), channel_id=1, source_target_pairs={{0,8},{8,0},{1,9},{9,1},{2,10},{10,2},{3,11},{11,3},{4,12},{12,4},... | collective-permute-start | bytes 1728008 | tf_op jit(solution)/shard_map/ppermute | solution.py:221
  49.3 1.1 %phases.1 = (f32[2,640,1]{2,1,0:T(8,128)S(1)}, bf16[160,400]{1,0:T(8,128)(2,1)S(1)}, bf16[160,240]{1,0:T(8,128)(2,1)S(1)}) custom-call(s32[3]{0:T(128)S(1)} %pad_add_fusion.ids, s32[2]{0:T(128)S(1)} %copy-done.3, s32[32,32]{1,0:T(8,128)S(1)} %copy-done.2, f32[32]{0:T(128)S(1)} %copy-done.4, f32[32]{0:T(128)S(1)} %copy-done.6, f32[32]{0:T(128)S(1)} %copy-done.5), custom_call_target="tpu_custom_call" | custom-call | bytes 1048576 | tf_op jit(solution)/shard_map/phases/pallas_call | solution.py:231
  50.4 1.4 %own_first.1.t_own = f32[80,160]{1,0:T(8,128)S(1)} custom-call(bf16[2,160,2400]{2,1,0:T(8,128)(2,1)S(1)} %bitcast.23, bf16[200,2400]{1,0:T(8,128)(2,1)S(1)} %copy-done.1, bf16[200,2400]{1,0:T(8,128)(2,1)S(1)} %collective-permute-done.16.b1, f32[2,640,1]{2,1,0:T(8,128)S(1)} %get-tuple-element.26.w, bf16[160,400]{1,0:T(8,128)(2,1)S(1)} %get-tuple-element.28.g), custom_call_target="tpu_custom_call" | custom-call | flops 1000000000 | bytes 1048576 | tf_op jit(solution)/shard_map/own_first/pallas_call | solution.py:246
  52.4 1.4 %far_first.1.t_far = f32[80,160]{1,0:T(8,128)S(1)} custom-call(bf16[2,160,2400]{2,1,0:T(8,128)(2,1)S(1)} %bitcast.27, bf16[200,2400]{1,0:T(8,128)(2,1)S(1)} %copy-done.1, bf16[200,2400]{1,0:T(8,128)(2,1)S(1)} %collective-permute-done.16.b1, f32[2,640,1]{2,1,0:T(8,128)S(1)} %get-tuple-element.26.w, bf16[160,400]{1,0:T(8,128)(2,1)S(1)} %get-tuple-element.28.g), custom_call_target="tpu_custom_call" | custom-call | flops 20999999488 | bytes 1048576 | tf_op jit(solution)/shard_map/far_first/pallas_call | solution.py:246
  53.9 1.8 %last_terms.1.t = f32[2,80,160]{2,1,0:T(8,128)S(1)} custom-call(bf16[2,160,2400]{2,1,0:T(8,128)(2,1)S(1)} %bitcast.24, bf16[2,160,2400]{2,1,0:T(8,128)(2,1)S(1)} %bitcast.28, bf16[120,2400]{1,0:T(8,128)(2,1)S(1)} %constant_dynamic-update-slice_fusion.b0, bf16[120,2400]{1,0:T(8,128)(2,1)S(1)} %collective-permute-done.15.b1, ...), custom_call_target="tpu_custom_call" | custom-call | flops 1000000000 | bytes 1048576 | tf_op jit(solution)/shard_map/last_terms/pallas_call | solution.py:255
  56.6 6.4 %collective-permute-done.17.t_yh = f32[2,80,160]{2,1,0:T(8,128)S(1)} collective-permute-done((f32[2,80,160]{2,1,0:T(8,128)S(1)}, f32[2,80,160]{2,1,0:T(8,128)S(1)}, u32[]{:S(2)}, u32[]{:S(2)}) %collective-permute-start.17) | collective-permute-done | bytes 102432 | tf_op jit(solution)/shard_map/ppermute | solution.py:265
  63.0 0.9 %collective-permute-start.19 = (f32[2,80,160]{2,1,0:T(8,128)S(1)}, f32[2,80,160]{2,1,0:T(8,128)S(1)}, u32[]{:S(2)}, u32[]{:S(2)}) collective-permute-start(f32[2,80,160]{2,1,0:T(8,128)S(1)} %collective-permute-done.17.t_yh), channel_id=1, source_target_pairs={{0,8},{8,0},{1,9},{9,1},{2,10},{10,2},{3,11},{11,3},{4,12},{12,4},... | collective-permute-start | bytes 307208 | tf_op jit(solution)/shard_map/ppermute | solution.py:266
  63.9 1.0 %collective-permute-done.19.t_diag = f32[2,80,160]{2,1,0:T(8,128)S(1)} collective-permute-done((f32[2,80,160]{2,1,0:T(8,128)S(1)}, f32[2,80,160]{2,1,0:T(8,128)S(1)}, u32[]{:S(2)}, u32[]{:S(2)}) %collective-permute-start.19) | collective-permute-done | bytes 102432 | tf_op jit(solution)/shard_map/ppermute | solution.py:266
  65.0 3.1 %cluster_terms.1 = f32[8,48,128]{2,1,0:T(8,128)} custom-call(s32[3]{0:T(128)S(1)} %pad_add_fusion.ids, bf16[2,160,2400]{2,1,0:T(8,128)(2,1)S(1)} %bitcast.25, bf16[2,160,2400]{2,1,0:T(8,128)(2,1)S(1)} %bitcast.29, bf16[2,160,2400]{2,1,0:T(8,128)(2,1)S(1)} %collective-permute-done.5.near, bf16[2,160,2400]{2,1,0:T(8,128)(2,1)S(1)} %collective-permute-done.12.diag, ...), custom_call_target="tpu_custom_call" | custom-call | flops 1000000000 | bytes 1048576 | tf_op jit(solution)/shard_map/cluster_terms/pallas_call | solution.py:270
  68.0 3.6 %all-to-all-start = ((f32[8,48,128]{2,1,0:T(8,128)}), f32[8,48,128]{2,1,0:T(8,128)S(1)}, u32[]{:S(2)}, u32[]{:S(2)}) async-start(f32[8,48,128]{2,1,0:T(8,128)} %cluster_terms.1), calls=%async_computation | async-start | bytes 393216 | tf_op jit(solution)/shard_map/all_to_all | solution.py:279
  71.8 9.4 %all-to-all-done.arrived = f32[8,48,128]{2,1,0:T(8,128)S(1)} async-done(((f32[8,48,128]{2,1,0:T(8,128)}), f32[8,48,128]{2,1,0:T(8,128)S(1)}, u32[]{:S(2)}, u32[]{:S(2)}) %all-to-all-start) | async-done | bytes 196640 | tf_op jit(solution)/shard_map/all_to_all | solution.py:279
  81.2 0.8 sum_and_mask.1
  (57 shorter events, 3.9 us)
Async XLA Ops:
  0.0 12.4 %copy-start = (bf16[1,2,160,2400]{3,2,1,0:T(8,128)(2,1)S(1)}, bf16[1,2,160,2400]{3,2,1,0:T(8,128)(2,1)}, u32[]{:S(2)}) copy-start(bf16[1,2,160,2400]{3,2,1,0:T(8,128)(2,1)} %param.7) | copy-start | bytes 4608004
  1.2 13.2 %collective-permute-start.2 = (bf16[40,2400]{1,0:T(8,128)(2,1)S(1)}, bf16[40,2400]{1,0:T(8,128)(2,1)S(1)}, u32[]{:S(2)}, u32[]{:S(2)}) collective-permute-start(bf16[40,2400]{1,0:T(8,128)(2,1)S(1)} %reshape.20), channel_id=1, source_target_pairs={{16,0},{32,16},{48,32},{64,48},{80,64},{96,80},{112,96},{0,112},{1... | collective-permute-start | bytes 576008 | tf_op jit(solution)/shard_map/ppermute | solution.py:190
  7.7 9.7 %collective-permute-start = (bf16[40,2400]{1,0:T(8,128)(2,1)S(1)}, bf16[40,2400]{1,0:T(8,128)(2,1)}, u32[]{:S(2)}, u32[]{:S(2)}) collective-permute-start(bf16[40,2400]{1,0:T(8,128)(2,1)S(1)} %reshape.20), channel_id=1, source_target_pairs={{0,16},{16,32},{32,48},{48,64},{64,80},{80,96},{96,112},{112,0},{1... | collective-permute-start | bytes 576008 | tf_op jit(solution)/shard_map/ppermute | solution.py:189
  9.5 18.0 %collective-permute-start.4 = (bf16[80,2400]{1,0:T(8,128)(2,1)}, bf16[80,2400]{1,0:T(8,128)(2,1)}, u32[]{:S(2)}, u32[]{:S(2)}) collective-permute-start(bf16[80,2400]{1,0:T(8,128)(2,1)} %dynamic-slice_bitcast_fusion), channel_id=1, source_target_pairs={{0,128},{128,0},{1,129},{129,1},{2,130},{130,2},{3,131},{131,3},{4... | collective-permute-start | bytes 1152008 | tf_op jit(solution)/shard_map/ppermute | solution.py:182
  12.4 15.1 %collective-permute-start.5 = (bf16[2,160,2400]{2,1,0:T(8,128)(2,1)S(1)}, bf16[2,160,2400]{2,1,0:T(8,128)(2,1)S(1)}, u32[]{:S(2)}, u32[]{:S(2)}) collective-permute-start(bf16[2,160,2400]{2,1,0:T(8,128)(2,1)S(1)} %bitcast.22), channel_id=1, source_target_pairs={{0,8},{8,0},{1,9},{9,1},{2,10},{10,2},{3,11},{11,3},{4,12},{12,4},... | collective-permute-start | bytes 4608008 | tf_op jit(solution)/shard_map/ppermute | solution.py:183
  14.4 11.3 %collective-permute-start.3 = (bf16[40,2400]{1,0:T(8,128)(2,1)S(1)}, bf16[40,2400]{1,0:T(8,128)(2,1)S(1)}, u32[]{:S(2)}, u32[]{:S(2)}) collective-permute-start(bf16[40,2400]{1,0:T(8,128)(2,1)S(1)} %collective-permute-done.2), channel_id=1, source_target_pairs={{16,0},{32,16},{48,32},{64,48},{80,64},{96,80},{112,96},{0,112},{1... | collective-permute-start | bytes 576008 | tf_op jit(solution)/shard_map/ppermute | solution.py:190
  17.4 7.6 %collective-permute-start.1 = (bf16[40,2400]{1,0:T(8,128)(2,1)}, bf16[40,2400]{1,0:T(8,128)(2,1)S(1)}, u32[]{:S(2)}, u32[]{:S(2)}) collective-permute-start(bf16[40,2400]{1,0:T(8,128)(2,1)} %collective-permute-done), channel_id=1, source_target_pairs={{0,16},{16,32},{32,48},{48,64},{64,80},{80,96},{96,112},{112,0},{1... | collective-permute-start | bytes 576008 | tf_op jit(solution)/shard_map/ppermute | solution.py:189
  26.4 24.1 %collective-permute-start.16 = (bf16[200,2400]{1,0:T(8,128)(2,1)}, bf16[200,2400]{1,0:T(8,128)(2,1)S(1)}, u32[]{:S(2)}, u32[]{:S(2)}) collective-permute-start(bf16[200,2400]{1,0:T(8,128)(2,1)} %constant_dynamic-update-slice_fusion.4.b0), channel_id=1, source_target_pairs={{0,8},{8,0},{1,9},{9,1},{2,10},{10,2},{3,11},{11,3},{4,12},{12,4},... | collective-permute-start | bytes 2880008 | tf_op jit(solution)/shard_map/ppermute | solution.py:219
  27.5 11.2 %collective-permute-start.9 = (bf16[80,2400]{1,0:T(8,128)(2,1)}, bf16[80,2400]{1,0:T(8,128)(2,1)S(1)}, u32[]{:S(2)}, u32[]{:S(2)}) collective-permute-start(bf16[80,2400]{1,0:T(8,128)(2,1)} %collective-permute-done.4), channel_id=1, source_target_pairs={{1,0},{2,1},{3,2},{0,3},{5,4},{6,5},{7,6},{4,7},{9,8},{10,9},{11,1... | collective-permute-start | bytes 1152008 | tf_op jit(solution)/shard_map/ppermute | solution.py:196
  30.0 11.7 %collective-permute-start.8 = (bf16[80,2400]{1,0:T(8,128)(2,1)}, bf16[80,2400]{1,0:T(8,128)(2,1)S(1)}, u32[]{:S(2)}, u32[]{:S(2)}) collective-permute-start(bf16[80,2400]{1,0:T(8,128)(2,1)} %collective-permute-done.4), channel_id=1, source_target_pairs={{0,1},{1,2},{2,3},{3,0},{4,5},{5,6},{6,7},{7,4},{8,9},{9,10},{10,1... | collective-permute-start | bytes 1152008 | tf_op jit(solution)/shard_map/ppermute | solution.py:195
  30.0 7.3 %collective-permute-start.6 = (bf16[40,2400]{1,0:T(8,128)(2,1)S(1)}, bf16[40,2400]{1,0:T(8,128)(2,1)S(1)}, u32[]{:S(2)}, u32[]{:S(2)}) collective-permute-start(bf16[40,2400]{1,0:T(8,128)(2,1)S(1)} %collective-permute-done.1), channel_id=1, source_target_pairs={{0,16},{16,32},{32,48},{48,64},{64,80},{80,96},{96,112},{112,0},{1... | collective-permute-start | bytes 576008 | tf_op jit(solution)/shard_map/ppermute | solution.py:189
  30.0 7.3 %collective-permute-start.7 = (bf16[40,2400]{1,0:T(8,128)(2,1)S(1)}, bf16[40,2400]{1,0:T(8,128)(2,1)S(1)}, u32[]{:S(2)}, u32[]{:S(2)}) collective-permute-start(bf16[40,2400]{1,0:T(8,128)(2,1)S(1)} %collective-permute-done.3), channel_id=1, source_target_pairs={{16,0},{32,16},{48,32},{64,48},{80,64},{96,80},{112,96},{0,112},{1... | collective-permute-start | bytes 576008 | tf_op jit(solution)/shard_map/ppermute | solution.py:190
  37.3 11.9 %copy-start.2 = (s32[32,32]{1,0:T(8,128)S(1)}, s32[32,32]{1,0:T(8,128)}, u32[]{:S(2)}) copy-start(s32[32,32]{1,0:T(8,128)} %diff_class.1) | copy-start | bytes 12292
  37.3 11.9 %copy-start.3 = (s32[2]{0:T(128)S(1)}, s32[2]{0:T(128)}, u32[]{:S(2)}) copy-start(s32[2]{0:T(128)} %cells.1) | copy-start | bytes 28
  37.4 11.9 %copy-start.4 = (f32[32]{0:T(128)S(1)}, f32[32]{0:T(128)}, u32[]{:S(2)}) copy-start(f32[32]{0:T(128)} %class_weight.1) | copy-start | bytes 388
  37.4 11.9 %copy-start.5 = (f32[32]{0:T(128)S(1)}, f32[32]{0:T(128)}, u32[]{:S(2)}) copy-start(f32[32]{0:T(128)} %constant.61.clone.sin_table) | copy-start | bytes 388
  37.4 11.9 %copy-start.6 = (f32[32]{0:T(128)S(1)}, f32[32]{0:T(128)}, u32[]{:S(2)}) copy-start(f32[32]{0:T(128)} %constant.60.clone.cos_table) | copy-start | bytes 388
  37.4 13.0 %copy-start.1 = (bf16[200,2400]{1,0:T(8,128)(2,1)S(1)}, bf16[200,2400]{1,0:T(8,128)(2,1)}, u32[]{:S(2)}) copy-start(bf16[200,2400]{1,0:T(8,128)(2,1)} %constant_dynamic-update-slice_fusion.4.b0) | copy-start | bytes 2880004
  41.7 5.0 %collective-permute-start.14 = (bf16[16,2400]{1,0:T(8,128)(2,1)S(1)}, bf16[16,2400]{1,0:T(8,128)(2,1)S(1)}, u32[]{:S(2)}, u32[]{:S(2)}) collective-permute-start(bf16[16,2400]{1,0:T(8,128)(2,1)S(1)} %slice.15), channel_id=1, source_target_pairs={{16,0},{32,16},{48,32},{64,48},{80,64},{96,80},{112,96},{0,112},{1... | collective-permute-start | bytes 230408 | tf_op jit(solution)/shard_map/ppermute | solution.py:216
  41.7 5.0 %collective-permute-start.13 = (bf16[24,2400]{1,0:T(8,128)(2,1)S(1)}, bf16[24,2400]{1,0:T(8,128)(2,1)S(1)}, u32[]{:S(2)}, u32[]{:S(2)}) collective-permute-start(bf16[24,2400]{1,0:T(8,128)(2,1)S(1)} %slice.14), channel_id=1, source_target_pairs={{0,16},{16,32},{32,48},{48,64},{64,80},{80,96},{96,112},{112,0},{1... | collective-permute-start | bytes 345608 | tf_op jit(solution)/shard_map/ppermute | solution.py:215
  43.3 8.7 %collective-permute-start.11 = (bf16[40,2400]{1,0:T(8,128)(2,1)S(1)}, bf16[40,2400]{1,0:T(8,128)(2,1)S(1)}, u32[]{:S(2)}, u32[]{:S(2)}) collective-permute-start(bf16[40,2400]{1,0:T(8,128)(2,1)S(1)} %slice.13), channel_id=1, source_target_pairs={{1,0},{2,1},{3,2},{0,3},{5,4},{6,5},{7,6},{4,7},{9,8},{10,9},{11,1... | collective-permute-start | bytes 576008 | tf_op jit(solution)/shard_map/ppermute | solution.py:201
  43.7 8.2 %collective-permute-start.10 = (bf16[40,2400]{1,0:T(8,128)(2,1)S(1)}, bf16[40,2400]{1,0:T(8,128)(2,1)S(1)}, u32[]{:S(2)}, u32[]{:S(2)}) collective-permute-start(bf16[40,2400]{1,0:T(8,128)(2,1)S(1)} %slice.12), channel_id=1, source_target_pairs={{0,1},{1,2},{2,3},{3,0},{4,5},{5,6},{6,7},{7,4},{8,9},{9,10},{10,1... | collective-permute-start | bytes 576008 | tf_op jit(solution)/shard_map/ppermute | solution.py:200
  46.7 7.2 %collective-permute-start.15 = (bf16[120,2400]{1,0:T(8,128)(2,1)S(1)}, bf16[120,2400]{1,0:T(8,128)(2,1)S(1)}, u32[]{:S(2)}, u32[]{:S(2)}) collective-permute-start(bf16[120,2400]{1,0:T(8,128)(2,1)S(1)} %constant_dynamic-update-slice_fusion.b0), channel_id=1, source_target_pairs={{0,8},{8,0},{1,9},{9,1},{2,10},{10,2},{3,11},{11,3},{4,12},{12,4},... | collective-permute-start | bytes 1728008 | tf_op jit(solution)/shard_map/ppermute | solution.py:221
  52.0 13.0 %collective-permute-start.12 = (bf16[2,160,2400]{2,1,0:T(8,128)(2,1)S(1)}, bf16[2,160,2400]{2,1,0:T(8,128)(2,1)S(1)}, u32[]{:S(2)}, u32[]{:S(2)}) collective-permute-start(bf16[2,160,2400]{2,1,0:T(8,128)(2,1)S(1)} %bitcast.26), channel_id=1, source_target_pairs={{0,8},{8,0},{1,9},{9,1},{2,10},{10,2},{3,11},{11,3},{4,12},{12,4},... | collective-permute-start | bytes 4608008 | tf_op jit(solution)/shard_map/ppermute | solution.py:213
  55.7 15.9 %copy-start.7 = (s32[2,30]{1,0:T(2,128)S(1)}, s32[2,30]{1,0:T(2,128)}, u32[]{:S(2)}) copy-start(s32[2,30]{1,0:T(2,128)} %param.11) | copy-start | bytes 724
  55.7 7.3 %collective-permute-start.17 = (f32[2,80,160]{2,1,0:T(8,128)S(1)}, f32[2,80,160]{2,1,0:T(8,128)S(1)}, u32[]{:S(2)}, u32[]{:S(2)}) collective-permute-start(f32[2,80,160]{2,1,0:T(8,128)S(1)} %last_terms.1.t), channel_id=1, source_target_pairs={{0,128},{128,0},{1,129},{129,1},{2,130},{130,2},{3,131},{131,3},{4... | collective-permute-start | bytes 307208 | tf_op jit(solution)/shard_map/ppermute | solution.py:265
  56.2 7.7 %collective-permute-start.18 = (f32[2,80,160]{2,1,0:T(8,128)S(1)}, f32[2,80,160]{2,1,0:T(8,128)S(1)}, u32[]{:S(2)}, u32[]{:S(2)}) collective-permute-start(f32[2,80,160]{2,1,0:T(8,128)S(1)} %last_terms.1.t), channel_id=1, source_target_pairs={{0,8},{8,0},{1,9},{9,1},{2,10},{10,2},{3,11},{11,3},{4,12},{12,4},... | collective-permute-start | bytes 307208 | tf_op jit(solution)/shard_map/ppermute | solution.py:264
  63.0 2.0 %collective-permute-start.19 = (f32[2,80,160]{2,1,0:T(8,128)S(1)}, f32[2,80,160]{2,1,0:T(8,128)S(1)}, u32[]{:S(2)}, u32[]{:S(2)}) collective-permute-start(f32[2,80,160]{2,1,0:T(8,128)S(1)} %collective-permute-done.17.t_yh), channel_id=1, source_target_pairs={{0,8},{8,0},{1,9},{9,1},{2,10},{10,2},{3,11},{11,3},{4,12},{12,4},... | collective-permute-start | bytes 307208 | tf_op jit(solution)/shard_map/ppermute | solution.py:266
  68.0 13.2 %all-to-all-start = ((f32[8,48,128]{2,1,0:T(8,128)}), f32[8,48,128]{2,1,0:T(8,128)S(1)}, u32[]{:S(2)}, u32[]{:S(2)}) async-start(f32[8,48,128]{2,1,0:T(8,128)} %cluster_terms.1), calls=%async_computation | async-start | bytes 393216 | tf_op jit(solution)/shard_map/all_to_all | solution.py:279

commit v6 on v4

--- a/solution.py
+++ b/solution.py
@@ -63,29 +63,40 @@
     return jnp.where(real, up, -down) if sign > 0 else jnp.where(real, -up, down)
 
 
-def part_of_t(b, q_ref, w, g, width):
+def part_of_t(b, parts, swapped, w, g, width):
     contract = (((1,), (1,)), ((), ()))
-    m = lax.dot_general(b, q_ref[0], contract, preferred_element_type=F32)
-    m = m + turned(lax.dot_general(b, q_ref[1], contract, preferred_element_type=F32), width, 1)
+    real, imag = (lax.dot_general(b, part, contract, preferred_element_type=F32) for part in parts)
+    if swapped is not None:
+        swap = jnp.full(real.shape, swapped) > 0
+        real, imag = jnp.where(swap, imag, real), jnp.where(swap, real, imag)
+    m = real + turned(imag, width, 1)
     t = jnp.dot(g, (w * m).astype(BF16), preferred_element_type=F32)
     half = t.shape[0] // 2
     return t[:half] + t[half:]
 
 
-def first_kernel(width, q, q_ref, b0, b1, w, g, t_ref, b_ref):
+def own_kernel(width, own, b0, b1, w, g, t_ref, b_ref):
     half = b0.shape[0]
     b_ref[:half, :] = b0[...]
     b_ref[half:, :] = b1[...]
-    t_ref[...] = part_of_t(b_ref[...], q_ref, w[q, : 2 * half, :], g[...], width)
-
-
-def last_kernel(width, own, far, b0, b1, w, g, t_own, t_far, t_ref, b_ref):
+    t_ref[...] = part_of_t(b_ref[...], (own[0], own[1]), None, w[0, : 2 * half, :], g[...], width)
+
+
+def far_kernel(width, ids, far_a, far_b, b0, b1, w, g, t_ref, b_ref):
     half = b0.shape[0]
     b_ref[:half, :] = b0[...]
     b_ref[half:, :] = b1[...]
+    t_ref[...] = part_of_t(b_ref[...], (far_a[...], far_b[...]), ids[3], w[1, : 2 * half, :], g[...], width)
+
+
+def last_kernel(width, ids, own, far_a, far_b, b0, b1, w, g, t_own, t_far, t_ref, b_ref):
+    half = b0.shape[0]
+    b_ref[:half, :] = b0[...]
+    b_ref[half:, :] = b1[...]
+    b = b_ref[...]
     start = w.shape[1] - 2 * half
-    for q, (q_ref, t) in enumerate(((own, t_own), (far, t_far))):
-        t_ref[q] = t[...] + part_of_t(b_ref[...], q_ref, w[q, start:, :], g[...], width)
+    t_ref[0] = t_own[...] + part_of_t(b, (own[0], own[1]), None, w[0, start:, :], g[...], width)
+    t_ref[1] = t_far[...] + part_of_t(b, (far_a[...], far_b[...]), ids[3], w[1, start:, :], g[...], width)
 
 
 def packed(u, at, columns):
@@ -102,27 +113,27 @@
     return jnp.concatenate([tall[p * rows : (p + 1) * rows] for p in range(3)], 1)
 
 
-def cluster_kernel(width, columns, ids, own, far, near, diag, t, t_yh, t_core, t_diag, out, u_ref):
-    yh, core = ids[0], ids[2]
-    chips, _, lanes = out.shape
+def cluster_kernel(width, columns, ids, own, far_a, far_b, t, t_yh, mine, other, u_ref):
+    yh, core, swapped = ids[0], ids[2], ids[3]
+    chips, _, lanes = mine.shape
     span = 2 * chips * columns
     shift = span % 128
     window = pl.ds(pl.multiple_of(yh * (span - shift), 128), span + shift)
     half = 4 * width
+    t_own, t_far = t[0] + t_yh[1], t[1] + t_yh[0]
+    own_2, far_2 = turned(t_own, width, -1), turned(t_far, width, -1)
+    swap = jnp.full(t_far.shape, swapped) > 0
     total = None
-    sums = (
-        (own, t[0] + t_yh[1]),
-        (far, t[1] + t_yh[0]),
-        (near, t_core[0] + t_diag[1]),
-        (diag, t_core[1] + t_diag[0]),
-    )
-    for q_ref, value in sums:
-        for part in range(2):
-            piece = value if part == 0 else turned(value, width, -1)
-            high = piece.astype(BF16)
-            low = (piece - high.astype(F32)).astype(BF16)
-            u = jnp.dot(jnp.concatenate([high, low], 0), q_ref[part, :, window], preferred_element_type=F32)
-            total = u if total is None else total + u
+    for value, data in (
+        (t_own, own[0, :, window]),
+        (own_2, own[1, :, window]),
+        (jnp.where(swap, far_2, t_far), far_a[:, window]),
+        (jnp.where(swap, t_far, far_2), far_b[:, window]),
+    ):
+        high = value.astype(BF16)
+        low = (value - high.astype(F32)).astype(BF16)
+        u = jnp.dot(jnp.concatenate([high, low], 0), data, preferred_element_type=F32)
+        total = u if total is None else total + u
     u_ref[...] = total[:half] + total[half:]
     for row in range(2):
         for parity in range(2):
@@ -130,9 +141,10 @@
             @pl.when((yh == row) & (core == parity))
             def _():
                 for chip in range(chips):
-                    piece = packed(u_ref[...], (2 * chip + parity) * columns + row * shift, columns)
-                    spare = jnp.zeros((piece.shape[0], lanes - piece.shape[1]), F32)
-                    out[chip] = jnp.concatenate([piece, spare], 1)
+                    for out, odd in ((mine, parity), (other, 1 - parity)):
+                        piece = packed(u_ref[...], (2 * chip + odd) * columns + row * shift, columns)
+                        spare = jnp.zeros((piece.shape[0], lanes - piece.shape[1]), F32)
+                        out[chip] = jnp.concatenate([piece, spare], 1)
 
 
 def final_kernel(arrived, mask, out):
@@ -173,12 +185,12 @@
     up = [(i, (i + 1) % PARTS[1]) for i in range(PARTS[1])]
     down = [(j, i) for i, j in up]
     swap = [(0, 1), (1, 0)]
-    cross = [(0, 3), (1, 2), (2, 1), (3, 0)]
+    right = [(i, (i + 1) % PARTS[4]) for i in range(PARTS[4])]
+    left = [(j, i) for i, j in right]
     vmem, smem = pltpu.VMEM, pltpu.SMEM
 
-    far = lax.ppermute(own, "yh", swap)
-    near = lax.ppermute(own, "core", swap)
-    diag = lax.ppermute(far, "core", swap)
+    odd = jnp.bitwise_and(lax.axis_index("x"), 1)
+    far_a = lax.ppermute(lax.dynamic_index_in_dim(own, odd, 0, keepdims=False), "yh", swap)
     block = lax.dynamic_slice_in_dim(own, band * width, width, 1).reshape(group, functions)
     blocks = [block]
     offsets = [0, -1, 1, -2, 2, -3, 3, -4]
@@ -187,6 +199,13 @@
         from_below = lax.ppermute(from_below, "z", up)
         from_above = lax.ppermute(from_above, "z", down)
         blocks += [from_below, from_above]
+        if step == 3:
+            held = (from_below, from_above, far_a)
+            from_below, from_above, far_a = lax.optimization_barrier(held)
+    mid = occupied // 2
+    from_left = lax.ppermute(far_a[:mid], "x", right)
+    from_right = lax.ppermute(far_a[mid:], "x", left)
+    far_b = jnp.concatenate([from_left, from_right], 0)
     cut = 24
     blocks.append(lax.ppermute(from_below[:cut], "z", up))
     blocks.append(lax.ppermute(from_above[cut:], "z", down))
@@ -202,7 +221,8 @@
     early, late = 2 * split * group, 2 * (len(offsets) - split) * group
     angles = 2.0 * np.pi * np.arange(kpoint_count) / kpoint_count
     tables = [jnp.asarray((f(angles) / kpoint_count).astype(np.float32)) for f in (np.cos, np.sin)]
-    ids = jnp.stack([yh, z, core]).astype(jnp.int32)
+    ids = jnp.stack([yh, z, core, odd]).astype(jnp.int32)
+    later_ids, _ = lax.optimization_barrier((ids, last))
     weights, g_first, g_last = call(
         functools.partial(prep_kernel, width, functions, k_points),
         "phases",
@@ -212,44 +232,38 @@
             jax.ShapeDtypeStruct((8 * width, late), BF16),
         ),
         [smem] * 6,
-    )(ids, frag_cells, diff_class, class_weight, *tables)
+    )(later_ids, frag_cells, diff_class, class_weight, *tables)
 
     one = jax.ShapeDtypeStruct((4 * width, occupied), F32)
-    t_first = []
-    for q, (name, q_block) in enumerate((("own_first", own), ("far_first", far))):
-        t_first.append(
-            call(
-                functools.partial(first_kernel, width, q),
-                name,
-                one,
-                [vmem] * 5,
-                [pltpu.VMEM((early, functions), BF16)],
-                flops=(1 + 20 * q) * 10**9,
-            )(q_block, first, first_near, weights, g_first)
-        )
+    scratch = [pltpu.VMEM((early, functions), BF16)]
+    b_first = (first, first_near, weights, g_first)
+    kernel = functools.partial(own_kernel, width)
+    t_own = call(kernel, "own_first", one, [vmem] * 5, scratch, flops=10**9)(own, *b_first)
+    kernel = functools.partial(far_kernel, width)
+    t_far = call(kernel, "far_first", one, [smem] + [vmem] * 6, scratch, flops=10**9)(ids, far_a, far_b, *b_first)
     t = call(
         functools.partial(last_kernel, width),
         "last_terms",
         jax.ShapeDtypeStruct((2,) + one.shape, F32),
-        [vmem] * 8,
+        [smem] + [vmem] * 9,
         [pltpu.VMEM((late, functions), BF16)],
         flops=10**9,
-    )(own, far, last, last_near, weights, g_last, *t_first)
-
-    t_core = lax.ppermute(t, "core", swap)
+    )(ids, own, far_a, far_b, last, last_near, weights, g_last, t_own, t_far)
+
     t_yh = lax.ppermute(t, "yh", swap)
-    t_diag = lax.ppermute(t, ("yh", "core"), cross)
     chips = PARTS[1]
     columns = functions // kpoint_count
     span = 2 * chips * columns
-    pieces = call(
+    piece = jax.ShapeDtypeStruct((chips, 4 * width * 3 // 5, 128), F32)
+    mine, other = call(
         functools.partial(cluster_kernel, width, columns),
         "cluster_terms",
-        jax.ShapeDtypeStruct((chips, 4 * width * 3 // 5, 128), F32),
-        [smem] + [vmem] * 8,
+        (piece, piece),
+        [smem] + [vmem] * 5,
         [pltpu.VMEM((4 * width, span + span % 128), F32)],
         flops=10**9,
-    )(ids, own, far, near, diag, t, t_yh, t_core, t_diag)
+    )(ids, own, far_a, far_b, t, t_yh)
+    pieces = mine + lax.ppermute(other, "core", swap)
 
     arrived = lax.all_to_all(pieces, "z", 0, 0, tiled=True)
     index = (yh * PARTS[1] + z) * 2 + core

time: 79.5 us -> 78.1 us (0.982)
  waiting for transfers between devices: 28.9 us -> 24.7 us
  starting transfers between devices: 34.2 us -> 38.2 us
  local copies, waits for them, and re-layouts: 5.64 us -> 2.61 us
  Pallas kernels: 9.65 us -> 10.5 us
    unnamed x21 -> x22, local copies, waits for them, and re-layouts: 4.5 us -> 0.2 us
    ppermute x3, waiting for transfers between devices: 0.01 us -> 3.52 us  [shards(): from_above = lax.ppermute(from_above, 'z', down)]
    ppermute x5 -> x4, starting transfers between devices: 6.51 us -> 9.77 us  [the longest x1 4.02 us: shards(): pieces = mine + lax.ppermute(other, 'core', swap)]
    ppermute x5 -> x4, waiting for transfers between devices: 7.04 us -> 4.64 us  [the longest x1 3.25 us: shards(): from_left = lax.ppermute(far_a[:mid], 'x', right)]
    ppermute x1, waiting for transfers between devices: 2.3 us -> 0.01 us  [shards(): blocks.append(lax.ppermute(from_below[:cut], 'z', up))]
    ppermute x3, waiting for transfers between devices: 6.25 us -> 4.48 us  [shards(): from_below = lax.ppermute(from_below, 'z', up)]
    squeeze x0 -> x1, local copies, waits for them, and re-layouts: none -> 1.18 us  [shards(): lax.dynamic_index_in_dim(own, odd, 0, keepdims=False)]
    ppermute x1, waiting for transfers between devices: 3.91 us -> 2.76 us  [shards(): t_yh = lax.ppermute(t, 'yh', swap)]
  transfers between devices with their start and end apart: 17 -> 16, of which waited for: 7 -> 9; matrix products, arithmetic and copies ran while one was open for 2% -> 2% of each run, Pallas kernels for 7% -> 6%
where the time goes in v6:
time: 78.1 us; the launch traced here: 77.2 us
  starting transfers between devices  38.2 us (49%)
  waiting for transfers between devices  24.7 us (32%)
  Pallas kernels  10.5 us (13%)
  local copies, waits for them, and re-layouts  2.61 us (3%)
  other arithmetic  0.79 us (1%)
    ppermute x3, starting transfers between devices, shards(): from_above = lax.ppermute(from_above, 'z', down)  9.67 us
    all_to_all x1, waiting for transfers between devices, shards(): arrived = lax.all_to_all(pieces, 'z', 0, 0, tiled=True)  9.28 us
    all_to_all x1, starting transfers between devices, shards(): arrived = lax.all_to_all(pieces, 'z', 0, 0, tiled=True)  5.02 us
    ppermute x3, waiting for transfers between devices, shards(): from_below = lax.ppermute(from_below, 'z', up)  4.48 us
    ppermute x1, starting transfers between devices, shards(): pieces = mine + lax.ppermute(other, 'core', swap)  4.02 us
    ppermute x3, waiting for transfers between devices, shards(): from_above = lax.ppermute(from_above, 'z', down)  3.52 us
    ppermute x1, waiting for transfers between devices, shards(): from_left = lax.ppermute(far_a[:mid], 'x', right)  3.25 us
    ppermute x1, starting transfers between devices, shards(): blocks.append(lax.ppermute(from_above[cut:], 'z', down))  3.19 us
  transfers between devices with their start and end apart: 16, of which 9 were waited for; matrix products, arithmetic and copies ran while one was open for 2% of the time, Pallas kernels for 6%

profile of v6, /device:TPU:1, one launch (start us, length us, event | category | flops | bytes accessed | tf_op | source)
XLA Modules:
  0.0 77.2 jit_solution(9095412430379031983)
XLA Ops:
  0.0 1.0 %constant_dynamic-slice_fusion = bf16[1,2,20,2400]{3,2,1,0:T(8,128)(2,1)S(1)} fusion(bf16[1,2,160,2400]{3,2,1,0:T(8,128)(2,1)} %param.7, s32[]{:T(128)S(6)} %select_n.16), kind=kLoop, calls=%fused_computation.18 | loop fusion | bytes 384004 | tf_op jit(solution)/shard_map/dynamic_slice | solution.py:194
  1.1 2.5 %collective-permute-start = (bf16[40,2400]{1,0:T(8,128)(2,1)S(1)}, bf16[40,2400]{1,0:T(8,128)(2,1)S(1)}, u32[]{:S(2)}, u32[]{:S(2)}) collective-permute-start(bf16[40,2400]{1,0:T(8,128)(2,1)S(1)} %reshape.19), channel_id=1, source_target_pairs={{0,16},{16,32},{32,48},{48,64},{64,80},{80,96},{96,112},{112,0},{1... | collective-permute-start | bytes 576008 | tf_op jit(solution)/shard_map/ppermute | solution.py:199
  3.6 4.0 %collective-permute-start.3 = (bf16[40,2400]{1,0:T(8,128)(2,1)S(1)}, bf16[40,2400]{1,0:T(8,128)(2,1)S(1)}, u32[]{:S(2)}, u32[]{:S(2)}) collective-permute-start(bf16[40,2400]{1,0:T(8,128)(2,1)S(1)} %reshape.19), channel_id=1, source_target_pairs={{16,0},{32,16},{48,32},{64,48},{80,64},{96,80},{112,96},{0,112},{1... | collective-permute-start | bytes 576008 | tf_op jit(solution)/shard_map/ppermute | solution.py:200
  7.7 1.2 %dynamic-slice_bitcast_fusion = bf16[160,2400]{1,0:T(8,128)(2,1)S(1)} fusion(bf16[1,2,160,2400]{3,2,1,0:T(8,128)(2,1)} %param.7, s32[]{:T(128)S(6)} %select_n.17), kind=kLoop, calls=%fused_computation.1 | loop fusion | bytes 1536004 | tf_op jit(solution)/shard_map/jit(dynamic_index_in_dim)/squeeze | solution.py:193
  8.8 3.0 %collective-permute-start.6 = (bf16[160,2400]{1,0:T(8,128)(2,1)S(1)}, bf16[160,2400]{1,0:T(8,128)(2,1)S(1)}, u32[]{:S(2)}, u32[]{:S(2)}) collective-permute-start(bf16[160,2400]{1,0:T(8,128)(2,1)S(1)} %dynamic-slice_bitcast_fusion), channel_id=1, source_target_pairs={{0,128},{128,0},{1,129},{129,1},{2,130},{130,2},{3,131},{131,3},{4... | collective-permute-start | bytes 2304008 | tf_op jit(solution)/shard_map/ppermute | solution.py:193
  12.0 0.2 collective-permute-done
  12.2 2.7 %collective-permute-start.4 = (bf16[40,2400]{1,0:T(8,128)(2,1)S(1)}, bf16[40,2400]{1,0:T(8,128)(2,1)S(1)}, u32[]{:S(2)}, u32[]{:S(2)}) collective-permute-start(bf16[40,2400]{1,0:T(8,128)(2,1)S(1)} %collective-permute-done.3), channel_id=1, source_target_pairs={{16,0},{32,16},{48,32},{64,48},{80,64},{96,80},{112,96},{0,112},{1... | collective-permute-start | bytes 576008 | tf_op jit(solution)/shard_map/ppermute | solution.py:200
  14.9 3.6 %collective-permute-done.1 = bf16[40,2400]{1,0:T(8,128)(2,1)S(1)} collective-permute-done((bf16[40,2400]{1,0:T(8,128)(2,1)S(1)}, bf16[40,2400]{1,0:T(8,128)(2,1)S(1)}, u32[]{:S(2)}, u32[]{:S(2)}) %collective-permute-start.1) | collective-permute-done | bytes 192032 | tf_op jit(solution)/shard_map/ppermute | solution.py:199
  18.6 2.2 %collective-permute-start.12 = (bf16[200,2400]{1,0:T(8,128)(2,1)S(1)}, bf16[200,2400]{1,0:T(8,128)(2,1)S(1)}, u32[]{:S(2)}, u32[]{:S(2)}) collective-permute-start(bf16[200,2400]{1,0:T(8,128)(2,1)S(1)} %constant_dynamic-update-slice_fusion.6.b0), channel_id=1, source_target_pairs={{0,8},{8,0},{1,9},{9,1},{2,10},{10,2},{3,11},{11,3},{4,12},{12,4},... | collective-permute-start | bytes 2880008 | tf_op jit(solution)/shard_map/ppermute | solution.py:214
  20.9 3.0 %collective-permute-start.5 = (bf16[40,2400]{1,0:T(8,128)(2,1)S(1)}, bf16[40,2400]{1,0:T(8,128)(2,1)S(1)}, u32[]{:S(2)}, u32[]{:S(2)}) collective-permute-start(bf16[40,2400]{1,0:T(8,128)(2,1)S(1)} %collective-permute-done.4), channel_id=1, source_target_pairs={{16,0},{32,16},{48,32},{64,48},{80,64},{96,80},{112,96},{0,112},{1... | collective-permute-start | bytes 576008 | tf_op jit(solution)/shard_map/ppermute | solution.py:200
  23.8 0.7 collective-permute-done.2
  24.5 3.5 %collective-permute-done.5 = bf16[40,2400]{1,0:T(8,128)(2,1)S(1)} collective-permute-done((bf16[40,2400]{1,0:T(8,128)(2,1)S(1)}, bf16[40,2400]{1,0:T(8,128)(2,1)S(1)}, u32[]{:S(2)}, u32[]{:S(2)}) %collective-permute-start.5) | collective-permute-done | bytes 192032 | tf_op jit(solution)/shard_map/ppermute | solution.py:200
  28.0 0.3 collective-permute-done.6.far_a
  28.5 3.2 %collective-permute-start.10 = (bf16[16,2400]{1,0:T(8,128)(2,1)S(1)}, bf16[16,2400]{1,0:T(8,128)(2,1)S(1)}, u32[]{:S(2)}, u32[]{:S(2)}) collective-permute-start(bf16[16,2400]{1,0:T(8,128)(2,1)S(1)} %slice.15), channel_id=1, source_target_pairs={{16,0},{32,16},{48,32},{64,48},{80,64},{96,80},{112,96},{0,112},{1... | collective-permute-start | bytes 230408 | tf_op jit(solution)/shard_map/ppermute | solution.py:211
  31.7 1.3 %collective-permute-start.7 = (bf16[80,2400]{1,0:T(8,128)(2,1)S(1)}, bf16[80,2400]{1,0:T(8,128)(2,1)S(1)}, u32[]{:S(2)}, u32[]{:S(2)}) collective-permute-start(bf16[80,2400]{1,0:T(8,128)(2,1)S(1)} %get-tuple-element.24), channel_id=1, source_target_pairs={{0,1},{1,2},{2,3},{3,0},{4,5},{5,6},{6,7},{7,4},{8,9},{9,10},{10,1... | collective-permute-start | bytes 1152008 | tf_op jit(solution)/shard_map/ppermute | solution.py:206
  33.0 1.5 %collective-permute-start.8 = (bf16[80,2400]{1,0:T(8,128)(2,1)S(1)}, bf16[80,2400]{1,0:T(8,128)(2,1)S(1)}, u32[]{:S(2)}, u32[]{:S(2)}) collective-permute-start(bf16[80,2400]{1,0:T(8,128)(2,1)S(1)} %get-tuple-element.23), channel_id=1, source_target_pairs={{1,0},{2,1},{3,2},{0,3},{5,4},{6,5},{7,6},{4,7},{9,8},{10,9},{11,1... | collective-permute-start | bytes 1152008 | tf_op jit(solution)/shard_map/ppermute | solution.py:207
  34.5 2.7 %collective-permute-start.11 = (bf16[120,2400]{1,0:T(8,128)(2,1)S(1)}, bf16[120,2400]{1,0:T(8,128)(2,1)S(1)}, u32[]{:S(2)}, u32[]{:S(2)}) collective-permute-start(bf16[120,2400]{1,0:T(8,128)(2,1)S(1)} %constant_dynamic-update-slice_fusion.2.b0), channel_id=1, source_target_pairs={{0,8},{8,0},{1,9},{9,1},{2,10},{10,2},{3,11},{11,3},{4,12},{12,4},... | collective-permute-start | bytes 1728008 | tf_op jit(solution)/shard_map/ppermute | solution.py:216
  37.3 1.1 %phases.1 = (f32[2,640,1]{2,1,0:T(8,128)S(1)}, bf16[160,400]{1,0:T(8,128)(2,1)S(1)}, bf16[160,240]{1,0:T(8,128)(2,1)S(1)}) custom-call(s32[4]{0:T(128)S(1)} %pad_add_fusion.ids, s32[2]{0:T(128)S(1)} %copy-done.2, s32[32,32]{1,0:T(8,128)S(1)} %copy-done.1, f32[32]{0:T(128)S(1)} %copy-done.3, f32[32]{0:T(128)S(1)} %copy-done.4, f32[32]{0:T(128)S(1)} %copy-done.5), custom_call_target="tpu_custom_call" | custom-call | bytes 1048576 | tf_op jit(solution)/shard_map/phases/pallas_call | solution.py:226
  38.4 3.3 %collective-permute-done.7 = bf16[80,2400]{1,0:T(8,128)(2,1)S(1)} collective-permute-done((bf16[80,2400]{1,0:T(8,128)(2,1)S(1)}, bf16[80,2400]{1,0:T(8,128)(2,1)S(1)}, u32[]{:S(2)}, u32[]{:S(2)}) %collective-permute-start.7) | collective-permute-done | bytes 384032 | tf_op jit(solution)/shard_map/ppermute | solution.py:206
  41.7 2.1 %far_first.1.t_far = f32[80,160]{1,0:T(8,128)S(1)} custom-call(s32[4]{0:T(128)S(1)} %pad_add_fusion.ids, bf16[160,2400]{1,0:T(8,128)(2,1)S(1)} %collective-permute-done.6.far_a, bf16[160,2400]{1,0:T(8,128)(2,1)S(1)} %constant_dynamic-update-slice_fusion.far_b, bf16[200,2400]{1,0:T(8,128)(2,1)S(1)} %constant_dynamic-update-slice_fusion.6.b0, ...), custom_call_target="tpu_custom_call" | custom-call | flops 1000000000 | bytes 1048576 | tf_op jit(solution)/shard_map/far_first/pallas_call | solution.py:243
  43.9 1.5 %own_first.1.t_own = f32[80,160]{1,0:T(8,128)S(1)} custom-call(bf16[2,160,2400]{2,1,0:T(8,128)(2,1)S(1)} %bitcast.10, bf16[200,2400]{1,0:T(8,128)(2,1)S(1)} %constant_dynamic-update-slice_fusion.6.b0, bf16[200,2400]{1,0:T(8,128)(2,1)S(1)} %collective-permute-done.12.b1, f32[2,640,1]{2,1,0:T(8,128)S(1)} %get-tuple-element.18.w, ...), custom_call_target="tpu_custom_call" | custom-call | flops 1000000000 | bytes 1048576 | tf_op jit(solution)/shard_map/own_first/pallas_call | solution.py:241
  45.4 2.4 %last_terms.1.t = f32[2,80,160]{2,1,0:T(8,128)S(1)} custom-call(s32[4]{0:T(128)S(1)} %pad_add_fusion.ids, bf16[2,160,2400]{2,1,0:T(8,128)(2,1)S(1)} %bitcast.11, bf16[160,2400]{1,0:T(8,128)(2,1)S(1)} %collective-permute-done.6.far_a, bf16[160,2400]{1,0:T(8,128)(2,1)S(1)} %constant_dynamic-update-slice_fusion.far_b, ...), custom_call_target="tpu_custom_call" | custom-call | flops 1000000000 | bytes 1048576 | tf_op jit(solution)/shard_map/last_terms/pallas_call | solution.py:244
  47.8 3.0 %collective-permute-start.13 = (f32[2,80,160]{2,1,0:T(8,128)S(1)}, f32[2,80,160]{2,1,0:T(8,128)S(1)}, u32[]{:S(2)}, u32[]{:S(2)}) collective-permute-start(f32[2,80,160]{2,1,0:T(8,128)S(1)} %last_terms.1.t), channel_id=1, source_target_pairs={{0,128},{128,0},{1,129},{129,1},{2,130},{130,2},{3,131},{131,3},{4... | collective-permute-start | bytes 307208 | tf_op jit(solution)/shard_map/ppermute | solution.py:253
  50.8 2.8 %collective-permute-done.13.t_yh = f32[2,80,160]{2,1,0:T(8,128)S(1)} collective-permute-done((f32[2,80,160]{2,1,0:T(8,128)S(1)}, f32[2,80,160]{2,1,0:T(8,128)S(1)}, u32[]{:S(2)}, u32[]{:S(2)}) %collective-permute-start.13) | collective-permute-done | bytes 102432 | tf_op jit(solution)/shard_map/ppermute | solution.py:253
  53.5 2.7 %cluster_terms.1 = (f32[8,48,128]{2,1,0:T(8,128)S(1)}, f32[8,48,128]{2,1,0:T(8,128)S(1)}) custom-call(s32[4]{0:T(128)S(1)} %pad_add_fusion.ids, bf16[2,160,2400]{2,1,0:T(8,128)(2,1)S(1)} %bitcast.12, bf16[160,2400]{1,0:T(8,128)(2,1)S(1)} %collective-permute-done.6.far_a, bf16[160,2400]{1,0:T(8,128)(2,1)S(1)} %constant_dynamic-update-slice_fusion.far_b, ...), custom_call_target="tpu_custom_call" | custom-call | flops 1000000000 | bytes 1048576 | tf_op jit(solution)/shard_map/cluster_terms/pallas_call | solution.py:258
  56.2 4.0 %collective-permute-start.14 = (f32[8,48,128]{2,1,0:T(8,128)S(1)}, f32[8,48,128]{2,1,0:T(8,128)S(1)}, u32[]{:S(2)}, u32[]{:S(2)}) collective-permute-start(f32[8,48,128]{2,1,0:T(8,128)S(1)} %get-tuple-element.22), channel_id=1, source_target_pairs={{0,8},{8,0},{1,9},{9,1},{2,10},{10,2},{3,11},{11,3},{4,12},{12,4},... | collective-permute-start | bytes 589832 | tf_op jit(solution)/shard_map/ppermute | solution.py:266
  60.2 1.1 %collective-permute-done.14 = f32[8,48,128]{2,1,0:T(8,128)S(1)} collective-permute-done((f32[8,48,128]{2,1,0:T(8,128)S(1)}, f32[8,48,128]{2,1,0:T(8,128)S(1)}, u32[]{:S(2)}, u32[]{:S(2)}) %collective-permute-start.14) | collective-permute-done | bytes 196640 | tf_op jit(solution)/shard_map/ppermute | solution.py:266
  61.3 0.7 add.37
  62.0 5.0 %all-to-all-start = ((f32[8,48,128]{2,1,0:T(8,128)}), f32[8,48,128]{2,1,0:T(8,128)S(1)}, u32[]{:S(2)}, u32[]{:S(2)}) async-start(f32[8,48,128]{2,1,0:T(8,128)} %add.37), calls=%async_computation | async-start | bytes 393216 | tf_op jit(solution)/shard_map/all_to_all | solution.py:268
  67.0 0.1 convolution_bitcast_fusion.mask
  67.2 9.3 %all-to-all-done.arrived = f32[8,48,128]{2,1,0:T(8,128)S(1)} async-done(((f32[8,48,128]{2,1,0:T(8,128)}), f32[8,48,128]{2,1,0:T(8,128)S(1)}, u32[]{:S(2)}, u32[]{:S(2)}) %all-to-all-start) | async-done | bytes 196640 | tf_op jit(solution)/shard_map/all_to_all | solution.py:268
  76.4 0.8 %sum_and_mask.1 = f32[2,20,2,75]{3,2,1,0:T(2,128)} custom-call(f32[8,48,128]{2,1,0:T(8,128)S(1)} %all-to-all-done.arrived, f32[2,75]{1,0:T(2,128)S(1)} %convolution_bitcast_fusion.mask), custom_call_target="tpu_custom_call" | custom-call | bytes 1048576 | tf_op jit(solution)/shard_map/sum_and_mask/pallas_call | solution.py:275
  (41 shorter events, 0.6 us)
Async XLA Ops:
  1.1 11.1 %collective-permute-start = (bf16[40,2400]{1,0:T(8,128)(2,1)S(1)}, bf16[40,2400]{1,0:T(8,128)(2,1)S(1)}, u32[]{:S(2)}, u32[]{:S(2)}) collective-permute-start(bf16[40,2400]{1,0:T(8,128)(2,1)S(1)} %reshape.19), channel_id=1, source_target_pairs={{0,16},{16,32},{32,48},{48,64},{64,80},{80,96},{96,112},{112,0},{1... | collective-permute-start | bytes 576008 | tf_op jit(solution)/shard_map/ppermute | solution.py:199
  3.6 8.5 %collective-permute-start.3 = (bf16[40,2400]{1,0:T(8,128)(2,1)S(1)}, bf16[40,2400]{1,0:T(8,128)(2,1)S(1)}, u32[]{:S(2)}, u32[]{:S(2)}) collective-permute-start(bf16[40,2400]{1,0:T(8,128)(2,1)S(1)} %reshape.19), channel_id=1, source_target_pairs={{16,0},{32,16},{48,32},{64,48},{80,64},{96,80},{112,96},{0,112},{1... | collective-permute-start | bytes 576008 | tf_op jit(solution)/shard_map/ppermute | solution.py:200
  8.8 19.5 %collective-permute-start.6 = (bf16[160,2400]{1,0:T(8,128)(2,1)S(1)}, bf16[160,2400]{1,0:T(8,128)(2,1)S(1)}, u32[]{:S(2)}, u32[]{:S(2)}) collective-permute-start(bf16[160,2400]{1,0:T(8,128)(2,1)S(1)} %dynamic-slice_bitcast_fusion), channel_id=1, source_target_pairs={{0,128},{128,0},{1,129},{129,1},{2,130},{130,2},{3,131},{131,3},{4... | collective-permute-start | bytes 2304008 | tf_op jit(solution)/shard_map/ppermute | solution.py:193
  12.2 6.3 %collective-permute-start.1 = (bf16[40,2400]{1,0:T(8,128)(2,1)S(1)}, bf16[40,2400]{1,0:T(8,128)(2,1)S(1)}, u32[]{:S(2)}, u32[]{:S(2)}) collective-permute-start(bf16[40,2400]{1,0:T(8,128)(2,1)S(1)} %collective-permute-done), channel_id=1, source_target_pairs={{0,16},{16,32},{32,48},{48,64},{64,80},{80,96},{96,112},{112,0},{1... | collective-permute-start | bytes 576008 | tf_op jit(solution)/shard_map/ppermute | solution.py:199
  12.2 6.4 %collective-permute-start.4 = (bf16[40,2400]{1,0:T(8,128)(2,1)S(1)}, bf16[40,2400]{1,0:T(8,128)(2,1)S(1)}, u32[]{:S(2)}, u32[]{:S(2)}) collective-permute-start(bf16[40,2400]{1,0:T(8,128)(2,1)S(1)} %collective-permute-done.3), channel_id=1, source_target_pairs={{16,0},{32,16},{48,32},{64,48},{80,64},{96,80},{112,96},{0,112},{1... | collective-permute-start | bytes 576008 | tf_op jit(solution)/shard_map/ppermute | solution.py:200
  18.5 6.0 %collective-permute-start.2 = (bf16[40,2400]{1,0:T(8,128)(2,1)S(1)}, bf16[40,2400]{1,0:T(8,128)(2,1)S(1)}, u32[]{:S(2)}, u32[]{:S(2)}) collective-permute-start(bf16[40,2400]{1,0:T(8,128)(2,1)S(1)} %collective-permute-done.1), channel_id=1, source_target_pairs={{0,16},{16,32},{32,48},{48,64},{64,80},{80,96},{96,112},{112,0},{1... | collective-permute-start | bytes 576008 | tf_op jit(solution)/shard_map/ppermute | solution.py:199
  18.6 18.7 %copy-start.1 = (s32[32,32]{1,0:T(8,128)S(1)}, s32[32,32]{1,0:T(8,128)}, u32[]{:S(2)}) copy-start(s32[32,32]{1,0:T(8,128)} %diff_class.1) | copy-start | bytes 12292
  18.6 18.7 %copy-start.2 = (s32[2]{0:T(128)S(1)}, s32[2]{0:T(128)}, u32[]{:S(2)}) copy-start(s32[2]{0:T(128)} %cells.1) | copy-start | bytes 28
  18.6 18.7 %copy-start.3 = (f32[32]{0:T(128)S(1)}, f32[32]{0:T(128)}, u32[]{:S(2)}) copy-start(f32[32]{0:T(128)} %class_weight.1) | copy-start | bytes 388
  18.6 18.7 %copy-start.4 = (f32[32]{0:T(128)S(1)}, f32[32]{0:T(128)}, u32[]{:S(2)}) copy-start(f32[32]{0:T(128)} %constant.55.clone.cos_table) | copy-start | bytes 388
  18.6 18.7 %copy-start.5 = (f32[32]{0:T(128)S(1)}, f32[32]{0:T(128)}, u32[]{:S(2)}) copy-start(f32[32]{0:T(128)} %constant.56.clone.sin_table) | copy-start | bytes 388
  18.6 23.1 %collective-permute-start.12 = (bf16[200,2400]{1,0:T(8,128)(2,1)S(1)}, bf16[200,2400]{1,0:T(8,128)(2,1)S(1)}, u32[]{:S(2)}, u32[]{:S(2)}) collective-permute-start(bf16[200,2400]{1,0:T(8,128)(2,1)S(1)} %constant_dynamic-update-slice_fusion.6.b0), channel_id=1, source_target_pairs={{0,8},{8,0},{1,9},{9,1},{2,10},{10,2},{3,11},{11,3},{4,12},{12,4},... | collective-permute-start | bytes 2880008 | tf_op jit(solution)/shard_map/ppermute | solution.py:214
  20.9 7.2 %collective-permute-start.5 = (bf16[40,2400]{1,0:T(8,128)(2,1)S(1)}, bf16[40,2400]{1,0:T(8,128)(2,1)S(1)}, u32[]{:S(2)}, u32[]{:S(2)}) collective-permute-start(bf16[40,2400]{1,0:T(8,128)(2,1)S(1)} %collective-permute-done.4), channel_id=1, source_target_pairs={{16,0},{32,16},{48,32},{64,48},{80,64},{96,80},{112,96},{0,112},{1... | collective-permute-start | bytes 576008 | tf_op jit(solution)/shard_map/ppermute | solution.py:200
  28.4 6.1 %collective-permute-start.9 = (bf16[24,2400]{1,0:T(8,128)(2,1)S(1)}, bf16[24,2400]{1,0:T(8,128)(2,1)S(1)}, u32[]{:S(2)}, u32[]{:S(2)}) collective-permute-start(bf16[24,2400]{1,0:T(8,128)(2,1)S(1)} %slice.14), channel_id=1, source_target_pairs={{0,16},{16,32},{32,48},{48,64},{64,80},{80,96},{96,112},{112,0},{1... | collective-permute-start | bytes 345608 | tf_op jit(solution)/shard_map/ppermute | solution.py:210
  28.5 6.0 %collective-permute-start.10 = (bf16[16,2400]{1,0:T(8,128)(2,1)S(1)}, bf16[16,2400]{1,0:T(8,128)(2,1)S(1)}, u32[]{:S(2)}, u32[]{:S(2)}) collective-permute-start(bf16[16,2400]{1,0:T(8,128)(2,1)S(1)} %slice.15), channel_id=1, source_target_pairs={{16,0},{32,16},{48,32},{64,48},{80,64},{96,80},{112,96},{0,112},{1... | collective-permute-start | bytes 230408 | tf_op jit(solution)/shard_map/ppermute | solution.py:211
  31.7 9.9 %collective-permute-start.7 = (bf16[80,2400]{1,0:T(8,128)(2,1)S(1)}, bf16[80,2400]{1,0:T(8,128)(2,1)S(1)}, u32[]{:S(2)}, u32[]{:S(2)}) collective-permute-start(bf16[80,2400]{1,0:T(8,128)(2,1)S(1)} %get-tuple-element.24), channel_id=1, source_target_pairs={{0,1},{1,2},{2,3},{3,0},{4,5},{5,6},{6,7},{7,4},{8,9},{9,10},{10,1... | collective-permute-start | bytes 1152008 | tf_op jit(solution)/shard_map/ppermute | solution.py:206
  33.0 8.7 %collective-permute-start.8 = (bf16[80,2400]{1,0:T(8,128)(2,1)S(1)}, bf16[80,2400]{1,0:T(8,128)(2,1)S(1)}, u32[]{:S(2)}, u32[]{:S(2)}) collective-permute-start(bf16[80,2400]{1,0:T(8,128)(2,1)S(1)} %get-tuple-element.23), channel_id=1, source_target_pairs={{1,0},{2,1},{3,2},{0,3},{5,4},{6,5},{7,6},{4,7},{9,8},{10,9},{11,1... | collective-permute-start | bytes 1152008 | tf_op jit(solution)/shard_map/ppermute | solution.py:207
  34.5 10.8 %collective-permute-start.11 = (bf16[120,2400]{1,0:T(8,128)(2,1)S(1)}, bf16[120,2400]{1,0:T(8,128)(2,1)S(1)}, u32[]{:S(2)}, u32[]{:S(2)}) collective-permute-start(bf16[120,2400]{1,0:T(8,128)(2,1)S(1)} %constant_dynamic-update-slice_fusion.2.b0), channel_id=1, source_target_pairs={{0,8},{8,0},{1,9},{9,1},{2,10},{10,2},{3,11},{11,3},{4,12},{12,4},... | collective-permute-start | bytes 1728008 | tf_op jit(solution)/shard_map/ppermute | solution.py:216
  41.7 2.1 %copy-start = (bf16[1,2,160,2400]{3,2,1,0:T(8,128)(2,1)S(1)}, bf16[1,2,160,2400]{3,2,1,0:T(8,128)(2,1)}, u32[]{:S(2)}) copy-start(bf16[1,2,160,2400]{3,2,1,0:T(8,128)(2,1)} %param.7) | copy-start | bytes 4608004
  47.8 19.3 %copy-start.6 = (s32[2,30]{1,0:T(2,128)S(1)}, s32[2,30]{1,0:T(2,128)}, u32[]{:S(2)}) copy-start(s32[2,30]{1,0:T(2,128)} %param.11) | copy-start | bytes 724
  47.8 5.8 %collective-permute-start.13 = (f32[2,80,160]{2,1,0:T(8,128)S(1)}, f32[2,80,160]{2,1,0:T(8,128)S(1)}, u32[]{:S(2)}, u32[]{:S(2)}) collective-permute-start(f32[2,80,160]{2,1,0:T(8,128)S(1)} %last_terms.1.t), channel_id=1, source_target_pairs={{0,128},{128,0},{1,129},{129,1},{2,130},{130,2},{3,131},{131,3},{4... | collective-permute-start | bytes 307208 | tf_op jit(solution)/shard_map/ppermute | solution.py:253
  56.2 5.1 %collective-permute-start.14 = (f32[8,48,128]{2,1,0:T(8,128)S(1)}, f32[8,48,128]{2,1,0:T(8,128)S(1)}, u32[]{:S(2)}, u32[]{:S(2)}) collective-permute-start(f32[8,48,128]{2,1,0:T(8,128)S(1)} %get-tuple-element.22), channel_id=1, source_target_pairs={{0,8},{8,0},{1,9},{9,1},{2,10},{10,2},{3,11},{11,3},{4,12},{12,4},... | collective-permute-start | bytes 589832 | tf_op jit(solution)/shard_map/ppermute | solution.py:266
  62.0 14.4 %all-to-all-start = ((f32[8,48,128]{2,1,0:T(8,128)}), f32[8,48,128]{2,1,0:T(8,128)S(1)}, u32[]{:S(2)}, u32[]{:S(2)}) async-start(f32[8,48,128]{2,1,0:T(8,128)} %add.37), calls=%async_computation | async-start | bytes 393216 | tf_op jit(solution)/shard_map/all_to_all | solution.py:268

commit v7 on v6

--- a/solution.py
+++ b/solution.py
@@ -63,40 +63,55 @@
     return jnp.where(real, up, -down) if sign > 0 else jnp.where(real, -up, down)
 
 
-def part_of_t(b, parts, swapped, w, g, width):
+def part_of_t(b, real, imag, w, g, width):
     contract = (((1,), (1,)), ((), ()))
-    real, imag = (lax.dot_general(b, part, contract, preferred_element_type=F32) for part in parts)
-    if swapped is not None:
-        swap = jnp.full(real.shape, swapped) > 0
-        real, imag = jnp.where(swap, imag, real), jnp.where(swap, real, imag)
-    m = real + turned(imag, width, 1)
+    m = lax.dot_general(b, real[...], contract, preferred_element_type=F32)
+    m = m + turned(lax.dot_general(b, imag[...], contract, preferred_element_type=F32), width, 1)
     t = jnp.dot(g, (w * m).astype(BF16), preferred_element_type=F32)
     half = t.shape[0] // 2
     return t[:half] + t[half:]
 
 
-def own_kernel(width, own, b0, b1, w, g, t_ref, b_ref):
+def either_way(odd, far_a, far_b, run):
+    @pl.when(odd == 0)
+    def _():
+        run(far_a, far_b)
+
+    @pl.when(odd != 0)
+    def _():
+        run(far_b, far_a)
+
+
+def gathered(b_ref, b0, b1):
     half = b0.shape[0]
     b_ref[:half, :] = b0[...]
     b_ref[half:, :] = b1[...]
-    t_ref[...] = part_of_t(b_ref[...], (own[0], own[1]), None, w[0, : 2 * half, :], g[...], width)
+    return b_ref[...]
+
+
+def own_kernel(width, own, b0, b1, w, g, t_ref, b_ref):
+    b = gathered(b_ref, b0, b1)
+    t_ref[...] = part_of_t(b, own.at[0], own.at[1], w[0, : b.shape[0], :], g[...], width)
 
 
 def far_kernel(width, ids, far_a, far_b, b0, b1, w, g, t_ref, b_ref):
-    half = b0.shape[0]
-    b_ref[:half, :] = b0[...]
-    b_ref[half:, :] = b1[...]
-    t_ref[...] = part_of_t(b_ref[...], (far_a[...], far_b[...]), ids[3], w[1, : 2 * half, :], g[...], width)
+    b = gathered(b_ref, b0, b1)
+
+    def run(real, imag):
+        t_ref[...] = part_of_t(b, real, imag, w[1, : b.shape[0], :], g[...], width)
+
+    either_way(ids[3], far_a, far_b, run)
 
 
 def last_kernel(width, ids, own, far_a, far_b, b0, b1, w, g, t_own, t_far, t_ref, b_ref):
-    half = b0.shape[0]
-    b_ref[:half, :] = b0[...]
-    b_ref[half:, :] = b1[...]
-    b = b_ref[...]
-    start = w.shape[1] - 2 * half
-    t_ref[0] = t_own[...] + part_of_t(b, (own[0], own[1]), None, w[0, start:, :], g[...], width)
-    t_ref[1] = t_far[...] + part_of_t(b, (far_a[...], far_b[...]), ids[3], w[1, start:, :], g[...], width)
+    b = gathered(b_ref, b0, b1)
+    start = w.shape[1] - b.shape[0]
+
+    def run(real, imag):
+        t_ref[0] = t_own[...] + part_of_t(b, own.at[0], own.at[1], w[0, start:, :], g[...], width)
+        t_ref[1] = t_far[...] + part_of_t(b, real, imag, w[1, start:, :], g[...], width)
+
+    either_way(ids[3], far_a, far_b, run)
 
 
 def packed(u, at, columns):
@@ -113,27 +128,31 @@
     return jnp.concatenate([tall[p * rows : (p + 1) * rows] for p in range(3)], 1)
 
 
-def cluster_kernel(width, columns, ids, own, far_a, far_b, t, t_yh, mine, other, u_ref):
-    yh, core, swapped = ids[0], ids[2], ids[3]
-    chips, _, lanes = mine.shape
+def cluster_kernel(
+    width, columns, ids, own, near, far_a, far_b, diag_a, diag_b, t, t_yh, t_core, t_diag, out, u_ref
+):
+    yh, core, odd = ids[0], ids[2], ids[3]
+    chips, _, lanes = out.shape
     span = 2 * chips * columns
     shift = span % 128
     window = pl.ds(pl.multiple_of(yh * (span - shift), 128), span + shift)
     half = 4 * width
-    t_own, t_far = t[0] + t_yh[1], t[1] + t_yh[0]
-    own_2, far_2 = turned(t_own, width, -1), turned(t_far, width, -1)
-    swap = jnp.full(t_far.shape, swapped) > 0
+    swap = jnp.full(t.shape[1:], odd) > 0
     total = None
-    for value, data in (
-        (t_own, own[0, :, window]),
-        (own_2, own[1, :, window]),
-        (jnp.where(swap, far_2, t_far), far_a[:, window]),
-        (jnp.where(swap, t_far, far_2), far_b[:, window]),
+    for value, first, second, swapped in (
+        (t[0] + t_yh[1], own.at[0], own.at[1], False),
+        (t_core[0] + t_diag[1], near.at[0], near.at[1], False),
+        (t[1] + t_yh[0], far_a, far_b, True),
+        (t_core[1] + t_diag[0], diag_a, diag_b, True),
     ):
-        high = value.astype(BF16)
-        low = (value - high.astype(F32)).astype(BF16)
-        u = jnp.dot(jnp.concatenate([high, low], 0), data, preferred_element_type=F32)
-        total = u if total is None else total + u
+        partner = turned(value, width, -1)
+        if swapped:
+            value, partner = jnp.where(swap, partner, value), jnp.where(swap, value, partner)
+        for factor, data in ((value, first), (partner, second)):
+            high = factor.astype(BF16)
+            low = (factor - high.astype(F32)).astype(BF16)
+            u = jnp.dot(jnp.concatenate([high, low], 0), data[:, window], preferred_element_type=F32)
+            total = u if total is None else total + u
     u_ref[...] = total[:half] + total[half:]
     for row in range(2):
         for parity in range(2):
@@ -141,10 +160,9 @@
             @pl.when((yh == row) & (core == parity))
             def _():
                 for chip in range(chips):
-                    for out, odd in ((mine, parity), (other, 1 - parity)):
-                        piece = packed(u_ref[...], (2 * chip + odd) * columns + row * shift, columns)
-                        spare = jnp.zeros((piece.shape[0], lanes - piece.shape[1]), F32)
-                        out[chip] = jnp.concatenate([piece, spare], 1)
+                    piece = packed(u_ref[...], (2 * chip + parity) * columns + row * shift, columns)
+                    spare = jnp.zeros((piece.shape[0], lanes - piece.shape[1]), F32)
+                    out[chip] = jnp.concatenate([piece, spare], 1)
 
 
 def final_kernel(arrived, mask, out):
@@ -191,6 +209,7 @@
 
     odd = jnp.bitwise_and(lax.axis_index("x"), 1)
     far_a = lax.ppermute(lax.dynamic_index_in_dim(own, odd, 0, keepdims=False), "yh", swap)
+    near = lax.ppermute(own, "core", swap)
     block = lax.dynamic_slice_in_dim(own, band * width, width, 1).reshape(group, functions)
     blocks = [block]
     offsets = [0, -1, 1, -2, 2, -3, 3, -4]
@@ -198,22 +217,17 @@
     for step in range(1, PARTS[1] // 2):
         from_below = lax.ppermute(from_below, "z", up)
         from_above = lax.ppermute(from_above, "z", down)
+        if step == 2:
+            from_below, from_above, near = lax.optimization_barrier((from_below, from_above, near))
+        if step == 3:
+            from_below, from_above, far_a = lax.optimization_barrier((from_below, from_above, far_a))
         blocks += [from_below, from_above]
-        if step == 3:
-            held = (from_below, from_above, far_a)
-            from_below, from_above, far_a = lax.optimization_barrier(held)
     mid = occupied // 2
     from_left = lax.ppermute(far_a[:mid], "x", right)
     from_right = lax.ppermute(far_a[mid:], "x", left)
-    far_b = jnp.concatenate([from_left, from_right], 0)
-    cut = 24
-    blocks.append(lax.ppermute(from_below[:cut], "z", up))
-    blocks.append(lax.ppermute(from_above[cut:], "z", down))
     split = 5
     first = jnp.concatenate(blocks[:split], 0)
     first_near = lax.ppermute(first, "core", swap)
-    last = jnp.concatenate(blocks[split:], 0)
-    last_near = lax.ppermute(last, "core", swap)
 
     k_points = []
     for these in (offsets[:split], offsets[split:]):
@@ -222,7 +236,7 @@
     angles = 2.0 * np.pi * np.arange(kpoint_count) / kpoint_count
     tables = [jnp.asarray((f(angles) / kpoint_count).astype(np.float32)) for f in (np.cos, np.sin)]
     ids = jnp.stack([yh, z, core, odd]).astype(jnp.int32)
-    later_ids, _ = lax.optimization_barrier((ids, last))
+    later_ids, _ = lax.optimization_barrier((ids, first))
     weights, g_first, g_last = call(
         functools.partial(prep_kernel, width, functions, k_points),
         "phases",
@@ -239,6 +253,16 @@
     b_first = (first, first_near, weights, g_first)
     kernel = functools.partial(own_kernel, width)
     t_own = call(kernel, "own_first", one, [vmem] * 5, scratch, flops=10**9)(own, *b_first)
+    from_below, from_above, t_own = lax.optimization_barrier((from_below, from_above, t_own))
+    cut = 24
+    blocks.append(lax.ppermute(from_below[:cut], "z", up))
+    blocks.append(lax.ppermute(from_above[cut:], "z", down))
+    last = jnp.concatenate(blocks[split:], 0)
+    last_near = lax.ppermute(last, "core", swap)
+    from_left, from_right, _ = lax.optimization_barrier((from_left, from_right, last))
+    far_b = jnp.concatenate([from_left, from_right], 0)
+    later_a, _ = lax.optimization_barrier((far_a, far_b))
+    diag_a, diag_b = (lax.ppermute(half, "core", swap) for half in (later_a, far_b))
     kernel = functools.partial(far_kernel, width)
     t_far = call(kernel, "far_first", one, [smem] + [vmem] * 6, scratch, flops=10**9)(ids, far_a, far_b, *b_first)
     t = call(
@@ -251,19 +275,19 @@
     )(ids, own, far_a, far_b, last, last_near, weights, g_last, t_own, t_far)
 
     t_yh = lax.ppermute(t, "yh", swap)
+    t_core = lax.ppermute(t, "core", swap)
+    t_diag = lax.ppermute(t_yh, "core", swap)
     chips = PARTS[1]
     columns = functions // kpoint_count
     span = 2 * chips * columns
-    piece = jax.ShapeDtypeStruct((chips, 4 * width * 3 // 5, 128), F32)
-    mine, other = call(
+    pieces = call(
         functools.partial(cluster_kernel, width, columns),
         "cluster_terms",
-        (piece, piece),
-        [smem] + [vmem] * 5,
+        jax.ShapeDtypeStruct((chips, 4 * width * 3 // 5, 128), F32),
+        [smem] + [vmem] * 10,
         [pltpu.VMEM((4 * width, span + span % 128), F32)],
         flops=10**9,
-    )(ids, own, far_a, far_b, t, t_yh)
-    pieces = mine + lax.ppermute(other, "core", swap)
+    )(ids, own, near, far_a, far_b, diag_a, diag_b, t, t_yh, t_core, t_diag)
 
     arrived = lax.all_to_all(pieces, "z", 0, 0, tiled=True)
     index = (yh * PARTS[1] + z) * 2 + core

time: 78.1 us -> 80.9 us (1.036)
  local copies, waits for them, and re-layouts: 2.61 us -> 5.54 us
    ppermute x1 -> x5, starting transfers between devices: 4.02 us -> 7.85 us  [the longest x1 3.24 us: shards(): near = lax.ppermute(own, 'core', swap)]
    ppermute x3, starting transfers between devices: 2.55 us -> 0.01 us  [shards(): from_below = lax.ppermute(from_below, 'z', up)]
    unnamed x22, local copies, waits for them, and re-layouts: 0.2 us -> 2.2 us
    ppermute x3, waiting for transfers between devices: 3.52 us -> 1.59 us  [shards(): from_above = lax.ppermute(from_above, 'z', down)]
    ppermute x3, waiting for transfers between devices: 4.48 us -> 3.01 us  [shards(): from_below = lax.ppermute(from_below, 'z', up)]
    ppermute x1, waiting for transfers between devices: 0.01 us -> 1.43 us  [shards(): blocks.append(lax.ppermute(from_above[cut:], 'z', down))]
    ppermute x1, starting transfers between devices: 1.29 us -> 0.01 us  [shards(): from_left = lax.ppermute(far_a[:mid], 'x', right)]
    ppermute x1, waiting for transfers between devices: 0.31 us -> 1.45 us  [shards(): lax.ppermute(lax.dynamic_index_in_dim(own, odd, 0, keepdims=False), 'yh',...]
  transfers between devices with their start and end apart: 16 -> 20, of which waited for: 9 -> 9; matrix products, arithmetic and copies ran while one was open for 2% -> 7% of each run, Pallas kernels for 6% -> 7%
where the time goes in v7:
time: 80.9 us; the launch traced here: 80.3 us
  starting transfers between devices  38.4 us (47%)
  waiting for transfers between devices  24.8 us (31%)
  Pallas kernels  11.1 us (14%)
  local copies, waits for them, and re-layouts  5.54 us (7%)
    all_to_all x1, waiting for transfers between devices, shards(): arrived = lax.all_to_all(pieces, 'z', 0, 0, tiled=True)  9.42 us
    ppermute x3, starting transfers between devices, shards(): from_above = lax.ppermute(from_above, 'z', down)  9.29 us
    all_to_all x1, starting transfers between devices, shards(): arrived = lax.all_to_all(pieces, 'z', 0, 0, tiled=True)  4.79 us
    ppermute x1, waiting for transfers between devices, shards(): t_yh = lax.ppermute(t, 'yh', swap)  3.27 us
    ppermute x1, starting transfers between devices, shards(): near = lax.ppermute(own, 'core', swap)  3.24 us
    ppermute x1, waiting for transfers between devices, shards(): from_left = lax.ppermute(far_a[:mid], 'x', right)  3.13 us
    pallas_call x1, Pallas kernels, shards(): call(functools.partial(cluster_kernel, width, columns), 'cluster_terms',...  3.06 us
    ppermute x3, waiting for transfers between devices, shards(): from_below = lax.ppermute(from_below, 'z', up)  3.01 us
  transfers between devices with their start and end apart: 20, of which 9 were waited for; matrix products, arithmetic and copies ran while one was open for 7% of the time, Pallas kernels for 7%

profile of v7, /device:TPU:1, one launch (start us, length us, event | category | flops | bytes accessed | tf_op | source)
XLA Modules:
  0.0 80.3 jit_solution(5977868202204794026)
XLA Ops:
  0.0 3.2 %collective-permute-start.4 = (bf16[2,160,2400]{2,1,0:T(8,128)(2,1)}, bf16[2,160,2400]{2,1,0:T(8,128)(2,1)S(1)}, u32[]{:S(2)}, u32[]{:S(2)}) collective-permute-start(bf16[2,160,2400]{2,1,0:T(8,128)(2,1)} %bitcast.10), channel_id=1, source_target_pairs={{0,8},{8,0},{1,9},{9,1},{2,10},{10,2},{3,11},{11,3},{4,12},{12,4},... | collective-permute-start | bytes 4608008 | tf_op jit(solution)/shard_map/ppermute | solution.py:212
  3.2 1.0 %constant_dynamic-slice_fusion = bf16[1,2,20,2400]{3,2,1,0:T(8,128)(2,1)S(1)} fusion(bf16[1,2,160,2400]{3,2,1,0:T(8,128)(2,1)} %param.7, s32[]{:T(128)S(6)} %select_n.16), kind=kLoop, calls=%fused_computation.18 | loop fusion | bytes 384004 | tf_op jit(solution)/shard_map/dynamic_slice | solution.py:213
  4.3 3.9 %collective-permute-start.2 = (bf16[40,2400]{1,0:T(8,128)(2,1)S(1)}, bf16[40,2400]{1,0:T(8,128)(2,1)}, u32[]{:S(2)}, u32[]{:S(2)}) collective-permute-start(bf16[40,2400]{1,0:T(8,128)(2,1)S(1)} %reshape.19), channel_id=1, source_target_pairs={{16,0},{32,16},{48,32},{64,48},{80,64},{96,80},{112,96},{0,112},{1... | collective-permute-start | bytes 576008 | tf_op jit(solution)/shard_map/ppermute | solution.py:219
  8.3 2.1 %dynamic-slice_bitcast_fusion = bf16[160,2400]{1,0:T(8,128)(2,1)} fusion(bf16[1,2,160,2400]{3,2,1,0:T(8,128)(2,1)} %param.7, s32[]{:T(128)S(6)} %select_n.17), kind=kLoop, calls=%fused_computation.1 | loop fusion | bytes 1536004 | tf_op jit(solution)/shard_map/jit(dynamic_index_in_dim)/squeeze | solution.py:211
  10.4 2.9 %collective-permute-start.7 = (bf16[160,2400]{1,0:T(8,128)(2,1)}, bf16[160,2400]{1,0:T(8,128)(2,1)S(1)}, u32[]{:S(2)}, u32[]{:S(2)}) collective-permute-start(bf16[160,2400]{1,0:T(8,128)(2,1)} %dynamic-slice_bitcast_fusion), channel_id=1, source_target_pairs={{0,128},{128,0},{1,129},{129,1},{2,130},{130,2},{3,131},{131,3},{4... | collective-permute-start | bytes 2304008 | tf_op jit(solution)/shard_map/ppermute | solution.py:211
  13.4 2.7 %collective-permute-start.3 = (bf16[40,2400]{1,0:T(8,128)(2,1)}, bf16[40,2400]{1,0:T(8,128)(2,1)S(1)}, u32[]{:S(2)}, u32[]{:S(2)}) collective-permute-start(bf16[40,2400]{1,0:T(8,128)(2,1)} %collective-permute-done.2), channel_id=1, source_target_pairs={{16,0},{32,16},{48,32},{64,48},{80,64},{96,80},{112,96},{0,112},{1... | collective-permute-start | bytes 576008 | tf_op jit(solution)/shard_map/ppermute | solution.py:219
  16.1 1.0 %constant_dynamic-update-slice_fusion.3 = bf16[200,2400]{1,0:T(8,128)(2,1)S(1)} fusion(bf16[200,2400]{1,0:T(8,128)(2,1)S(1)} %constant_dynamic-update-slice_fusion.4, bf16[40,2400]{1,0:T(8,128)(2,1)} %collective-permute-done), kind=kLoop, calls=%fused_computation.5 | loop fusion | bytes 386560
  17.1 1.1 %constant_dynamic-update-slice_fusion.2 = bf16[200,2400]{1,0:T(8,128)(2,1)S(1)} fusion(bf16[200,2400]{1,0:T(8,128)(2,1)S(1)} %constant_dynamic-update-slice_fusion.3, bf16[40,2400]{1,0:T(8,128)(2,1)} %collective-permute-done.2), kind=kLoop, calls=%fused_computation.4 | loop fusion | bytes 386560
  18.2 1.6 %collective-permute-done.3 = bf16[40,2400]{1,0:T(8,128)(2,1)S(1)} collective-permute-done((bf16[40,2400]{1,0:T(8,128)(2,1)}, bf16[40,2400]{1,0:T(8,128)(2,1)S(1)}, u32[]{:S(2)}, u32[]{:S(2)}) %collective-permute-start.3) | collective-permute-done | bytes 192032 | tf_op jit(solution)/shard_map/ppermute | solution.py:219
  19.8 3.0 %collective-permute-done.1 = bf16[40,2400]{1,0:T(8,128)(2,1)S(1)} collective-permute-done((bf16[40,2400]{1,0:T(8,128)(2,1)}, bf16[40,2400]{1,0:T(8,128)(2,1)S(1)}, u32[]{:S(2)}, u32[]{:S(2)}) %collective-permute-start.1) | collective-permute-done | bytes 192032 | tf_op jit(solution)/shard_map/ppermute | solution.py:218
  22.8 2.7 %collective-permute-start.6 = (bf16[40,2400]{1,0:T(8,128)(2,1)S(1)}, bf16[40,2400]{1,0:T(8,128)(2,1)S(1)}, u32[]{:S(2)}, u32[]{:S(2)}) collective-permute-start(bf16[40,2400]{1,0:T(8,128)(2,1)S(1)} %collective-permute-done.3), channel_id=1, source_target_pairs={{16,0},{32,16},{48,32},{64,48},{80,64},{96,80},{112,96},{0,112},{1... | collective-permute-start | bytes 576008 | tf_op jit(solution)/shard_map/ppermute | solution.py:219
  25.5 2.7 %collective-permute-start.10 = (bf16[200,2400]{1,0:T(8,128)(2,1)S(1)}, bf16[200,2400]{1,0:T(8,128)(2,1)S(1)}, u32[]{:S(2)}, u32[]{:S(2)}) collective-permute-start(bf16[200,2400]{1,0:T(8,128)(2,1)S(1)} %constant_dynamic-update-slice_fusion.b0), channel_id=1, source_target_pairs={{0,8},{8,0},{1,9},{9,1},{2,10},{10,2},{3,11},{11,3},{4,12},{12,4},... | collective-permute-start | bytes 2880008 | tf_op jit(solution)/shard_map/ppermute | solution.py:230
  28.2 1.1 %phases.1 = (f32[2,640,1]{2,1,0:T(8,128)S(1)}, bf16[160,400]{1,0:T(8,128)(2,1)S(1)}, bf16[160,240]{1,0:T(8,128)(2,1)S(1)}) custom-call(s32[4]{0:T(128)S(1)} %pad_add_fusion.ids, s32[2]{0:T(128)S(1)} %copy-done.2, s32[32,32]{1,0:T(8,128)S(1)} %copy-done.1, f32[32]{0:T(128)S(1)} %copy-done.3, f32[32]{0:T(128)S(1)} %copy-done.5, f32[32]{0:T(128)S(1)} %copy-done.4), custom_call_target="tpu_custom_call" | custom-call | bytes 1048576 | tf_op jit(solution)/shard_map/phases/pallas_call | solution.py:240
  29.3 1.5 %collective-permute-done.7.far_a = bf16[160,2400]{1,0:T(8,128)(2,1)S(1)} collective-permute-done((bf16[160,2400]{1,0:T(8,128)(2,1)}, bf16[160,2400]{1,0:T(8,128)(2,1)S(1)}, u32[]{:S(2)}, u32[]{:S(2)}) %collective-permute-start.7) | collective-permute-done | bytes 768032 | tf_op jit(solution)/shard_map/ppermute | solution.py:211
  30.9 1.5 %own_first.1.t_own = f32[80,160]{1,0:T(8,128)S(1)} custom-call(bf16[2,160,2400]{2,1,0:T(8,128)(2,1)S(1)} %bitcast.11, bf16[200,2400]{1,0:T(8,128)(2,1)S(1)} %constant_dynamic-update-slice_fusion.b0, bf16[200,2400]{1,0:T(8,128)(2,1)S(1)} %collective-permute-done.10.b1, f32[2,640,1]{2,1,0:T(8,128)S(1)} %get-tuple-element.28.w, ...), custom_call_target="tpu_custom_call" | custom-call | flops 1000000000 | bytes 1048576 | tf_op jit(solution)/shard_map/own_first/pallas_call | solution.py:255
  32.5 2.5 %collective-permute-start.9 = (bf16[80,2400]{1,0:T(8,128)(2,1)S(1)}, bf16[80,2400]{1,0:T(8,128)(2,1)S(1)}, u32[]{:S(2)}, u32[]{:S(2)}) collective-permute-start(bf16[80,2400]{1,0:T(8,128)(2,1)S(1)} %get-tuple-element.37), channel_id=1, source_target_pairs={{1,0},{2,1},{3,2},{0,3},{5,4},{6,5},{7,6},{4,7},{9,8},{10,9},{11,1... | collective-permute-start | bytes 1152008 | tf_op jit(solution)/shard_map/ppermute | solution.py:227
  35.1 2.7 %collective-permute-start.12 = (bf16[16,2400]{1,0:T(8,128)(2,1)S(1)}, bf16[16,2400]{1,0:T(8,128)(2,1)S(1)}, u32[]{:S(2)}, u32[]{:S(2)}) collective-permute-start(bf16[16,2400]{1,0:T(8,128)(2,1)S(1)} %slice.15), channel_id=1, source_target_pairs={{16,0},{32,16},{48,32},{64,48},{80,64},{96,80},{112,96},{0,112},{1... | collective-permute-start | bytes 230408 | tf_op jit(solution)/shard_map/ppermute | solution.py:259
  37.8 1.4 %collective-permute-done.12 = bf16[16,2400]{1,0:T(8,128)(2,1)S(1)} collective-permute-done((bf16[16,2400]{1,0:T(8,128)(2,1)S(1)}, bf16[16,2400]{1,0:T(8,128)(2,1)S(1)}, u32[]{:S(2)}, u32[]{:S(2)}) %collective-permute-start.12) | collective-permute-done | bytes 76832 | tf_op jit(solution)/shard_map/ppermute | solution.py:259
  39.3 2.5 %collective-permute-start.15 = (bf16[120,2400]{1,0:T(8,128)(2,1)S(1)}, bf16[120,2400]{1,0:T(8,128)(2,1)S(1)}, u32[]{:S(2)}, u32[]{:S(2)}) collective-permute-start(bf16[120,2400]{1,0:T(8,128)(2,1)S(1)} %constant_dynamic-update-slice_fusion.5.b0), channel_id=1, source_target_pairs={{0,8},{8,0},{1,9},{9,1},{2,10},{10,2},{3,11},{11,3},{4,12},{12,4},... | collective-permute-start | bytes 1728008 | tf_op jit(solution)/shard_map/ppermute | solution.py:261
  42.3 3.1 %collective-permute-done.8 = bf16[80,2400]{1,0:T(8,128)(2,1)S(1)} collective-permute-done((bf16[80,2400]{1,0:T(8,128)(2,1)S(1)}, bf16[80,2400]{1,0:T(8,128)(2,1)S(1)}, u32[]{:S(2)}, u32[]{:S(2)}) %collective-permute-start.8) | collective-permute-done | bytes 384032 | tf_op jit(solution)/shard_map/ppermute | solution.py:226
  45.5 2.6 %collective-permute-start.13 = (bf16[160,2400]{1,0:T(8,128)(2,1)S(1)}, bf16[160,2400]{1,0:T(8,128)(2,1)S(1)}, u32[]{:S(2)}, u32[]{:S(2)}) collective-permute-start(bf16[160,2400]{1,0:T(8,128)(2,1)S(1)} %collective-permute-done.7.far_a), channel_id=1, source_target_pairs={{0,8},{8,0},{1,9},{9,1},{2,10},{10,2},{3,11},{11,3},{4,12},{12,4},... | collective-permute-start | bytes 2304008 | tf_op jit(solution)/shard_map/ppermute | solution.py:265
  48.2 2.2 %far_first.1.t_far = f32[80,160]{1,0:T(8,128)S(1)} custom-call(s32[4]{0:T(128)S(1)} %pad_add_fusion.ids, bf16[160,2400]{1,0:T(8,128)(2,1)S(1)} %collective-permute-done.7.far_a, bf16[160,2400]{1,0:T(8,128)(2,1)S(1)} %constant_dynamic-update-slice_fusion.9.far_b, bf16[200,2400]{1,0:T(8,128)(2,1)S(1)} %constant_dynamic-update-slice_fusion.b0, ...), custom_call_target="tpu_custom_call" | custom-call | flops 1000000000 | bytes 1048576 | tf_op jit(solution)/shard_map/far_first/pallas_call | solution.py:267
  50.4 2.4 %last_terms.1.t = f32[2,80,160]{2,1,0:T(8,128)S(1)} custom-call(s32[4]{0:T(128)S(1)} %pad_add_fusion.ids, bf16[2,160,2400]{2,1,0:T(8,128)(2,1)S(1)} %bitcast.12, bf16[160,2400]{1,0:T(8,128)(2,1)S(1)} %collective-permute-done.7.far_a, bf16[160,2400]{1,0:T(8,128)(2,1)S(1)} %constant_dynamic-update-slice_fusion.9.far_b, ...), custom_call_target="tpu_custom_call" | custom-call | flops 1000000000 | bytes 1048576 | tf_op jit(solution)/shard_map/last_terms/pallas_call | solution.py:268
  52.8 3.0 %collective-permute-start.16 = (f32[2,80,160]{2,1,0:T(8,128)S(1)}, f32[2,80,160]{2,1,0:T(8,128)S(1)}, u32[]{:S(2)}, u32[]{:S(2)}) collective-permute-start(f32[2,80,160]{2,1,0:T(8,128)S(1)} %last_terms.1.t), channel_id=1, source_target_pairs={{0,128},{128,0},{1,129},{129,1},{2,130},{130,2},{3,131},{131,3},{4... | collective-permute-start | bytes 307208 | tf_op jit(solution)/shard_map/ppermute | solution.py:277
  55.8 0.7 collective-permute-start.17
  56.5 3.3 %collective-permute-done.16.t_yh = f32[2,80,160]{2,1,0:T(8,128)S(1)} collective-permute-done((f32[2,80,160]{2,1,0:T(8,128)S(1)}, f32[2,80,160]{2,1,0:T(8,128)S(1)}, u32[]{:S(2)}, u32[]{:S(2)}) %collective-permute-start.16) | collective-permute-done | bytes 102432 | tf_op jit(solution)/shard_map/ppermute | solution.py:277
  59.8 1.2 %collective-permute-start.18 = (f32[2,80,160]{2,1,0:T(8,128)S(1)}, f32[2,80,160]{2,1,0:T(8,128)S(1)}, u32[]{:S(2)}, u32[]{:S(2)}) collective-permute-start(f32[2,80,160]{2,1,0:T(8,128)S(1)} %collective-permute-done.16.t_yh), channel_id=1, source_target_pairs={{0,8},{8,0},{1,9},{9,1},{2,10},{10,2},{3,11},{11,3},{4,12},{12,4},... | collective-permute-start | bytes 307208 | tf_op jit(solution)/shard_map/ppermute | solution.py:279
  61.0 1.0 %collective-permute-done.18.t_diag = f32[2,80,160]{2,1,0:T(8,128)S(1)} collective-permute-done((f32[2,80,160]{2,1,0:T(8,128)S(1)}, f32[2,80,160]{2,1,0:T(8,128)S(1)}, u32[]{:S(2)}, u32[]{:S(2)}) %collective-permute-start.18) | collective-permute-done | bytes 102432 | tf_op jit(solution)/shard_map/ppermute | solution.py:279
  62.1 3.1 %cluster_terms.1 = f32[8,48,128]{2,1,0:T(8,128)} custom-call(s32[4]{0:T(128)S(1)} %pad_add_fusion.ids, bf16[2,160,2400]{2,1,0:T(8,128)(2,1)S(1)} %bitcast.13, bf16[2,160,2400]{2,1,0:T(8,128)(2,1)S(1)} %collective-permute-done.4.near, bf16[160,2400]{1,0:T(8,128)(2,1)S(1)} %collective-permute-done.7.far_a, ...), custom_call_target="tpu_custom_call" | custom-call | flops 1000000000 | bytes 1048576 | tf_op jit(solution)/shard_map/cluster_terms/pallas_call | solution.py:283
  65.1 4.8 %all-to-all-start = ((f32[8,48,128]{2,1,0:T(8,128)}), f32[8,48,128]{2,1,0:T(8,128)S(1)}, u32[]{:S(2)}, u32[]{:S(2)}) async-start(f32[8,48,128]{2,1,0:T(8,128)} %cluster_terms.1), calls=%async_computation | async-start | bytes 393216 | tf_op jit(solution)/shard_map/all_to_all | solution.py:292
  70.1 9.4 %all-to-all-done.arrived = f32[8,48,128]{2,1,0:T(8,128)S(1)} async-done(((f32[8,48,128]{2,1,0:T(8,128)}), f32[8,48,128]{2,1,0:T(8,128)S(1)}, u32[]{:S(2)}, u32[]{:S(2)}) %all-to-all-start) | async-done | bytes 196640 | tf_op jit(solution)/shard_map/all_to_all | solution.py:292
  79.5 0.8 sum_and_mask.1
  (48 shorter events, 1.3 us)
Async XLA Ops:
  0.0 22.8 %collective-permute-start.4 = (bf16[2,160,2400]{2,1,0:T(8,128)(2,1)}, bf16[2,160,2400]{2,1,0:T(8,128)(2,1)S(1)}, u32[]{:S(2)}, u32[]{:S(2)}) collective-permute-start(bf16[2,160,2400]{2,1,0:T(8,128)(2,1)} %bitcast.10), channel_id=1, source_target_pairs={{0,8},{8,0},{1,9},{9,1},{2,10},{10,2},{3,11},{11,3},{4,12},{12,4},... | collective-permute-start | bytes 4608008 | tf_op jit(solution)/shard_map/ppermute | solution.py:212
  4.3 9.1 %collective-permute-start.2 = (bf16[40,2400]{1,0:T(8,128)(2,1)S(1)}, bf16[40,2400]{1,0:T(8,128)(2,1)}, u32[]{:S(2)}, u32[]{:S(2)}) collective-permute-start(bf16[40,2400]{1,0:T(8,128)(2,1)S(1)} %reshape.19), channel_id=1, source_target_pairs={{16,0},{32,16},{48,32},{64,48},{80,64},{96,80},{112,96},{0,112},{1... | collective-permute-start | bytes 576008 | tf_op jit(solution)/shard_map/ppermute | solution.py:219
  8.2 7.9 %collective-permute-start = (bf16[40,2400]{1,0:T(8,128)(2,1)S(1)}, bf16[40,2400]{1,0:T(8,128)(2,1)}, u32[]{:S(2)}, u32[]{:S(2)}) collective-permute-start(bf16[40,2400]{1,0:T(8,128)(2,1)S(1)} %reshape.19), channel_id=1, source_target_pairs={{0,16},{16,32},{32,48},{48,64},{64,80},{80,96},{96,112},{112,0},{1... | collective-permute-start | bytes 576008 | tf_op jit(solution)/shard_map/ppermute | solution.py:218
  8.3 20.0 %copy-start.1 = (s32[32,32]{1,0:T(8,128)S(1)}, s32[32,32]{1,0:T(8,128)}, u32[]{:S(2)}) copy-start(s32[32,32]{1,0:T(8,128)} %diff_class.1) | copy-start | bytes 12292
  8.3 20.0 %copy-start.2 = (s32[2]{0:T(128)S(1)}, s32[2]{0:T(128)}, u32[]{:S(2)}) copy-start(s32[2]{0:T(128)} %cells.1) | copy-start | bytes 28
  8.3 20.0 %copy-start.3 = (f32[32]{0:T(128)S(1)}, f32[32]{0:T(128)}, u32[]{:S(2)}) copy-start(f32[32]{0:T(128)} %class_weight.1) | copy-start | bytes 388
  8.3 19.9 %copy-start.4 = (f32[32]{0:T(128)S(1)}, f32[32]{0:T(128)}, u32[]{:S(2)}) copy-start(f32[32]{0:T(128)} %constant.56.clone.sin_table) | copy-start | bytes 388
  8.3 19.9 %copy-start.5 = (f32[32]{0:T(128)S(1)}, f32[32]{0:T(128)}, u32[]{:S(2)}) copy-start(f32[32]{0:T(128)} %constant.55.clone.cos_table) | copy-start | bytes 388
  10.4 20.4 %collective-permute-start.7 = (bf16[160,2400]{1,0:T(8,128)(2,1)}, bf16[160,2400]{1,0:T(8,128)(2,1)S(1)}, u32[]{:S(2)}, u32[]{:S(2)}) collective-permute-start(bf16[160,2400]{1,0:T(8,128)(2,1)} %dynamic-slice_bitcast_fusion), channel_id=1, source_target_pairs={{0,128},{128,0},{1,129},{129,1},{2,130},{130,2},{3,131},{131,3},{4... | collective-permute-start | bytes 2304008 | tf_op jit(solution)/shard_map/ppermute | solution.py:211
  13.4 6.3 %collective-permute-start.3 = (bf16[40,2400]{1,0:T(8,128)(2,1)}, bf16[40,2400]{1,0:T(8,128)(2,1)S(1)}, u32[]{:S(2)}, u32[]{:S(2)}) collective-permute-start(bf16[40,2400]{1,0:T(8,128)(2,1)} %collective-permute-done.2), channel_id=1, source_target_pairs={{16,0},{32,16},{48,32},{64,48},{80,64},{96,80},{112,96},{0,112},{1... | collective-permute-start | bytes 576008 | tf_op jit(solution)/shard_map/ppermute | solution.py:219
  16.1 6.6 %collective-permute-start.1 = (bf16[40,2400]{1,0:T(8,128)(2,1)}, bf16[40,2400]{1,0:T(8,128)(2,1)S(1)}, u32[]{:S(2)}, u32[]{:S(2)}) collective-permute-start(bf16[40,2400]{1,0:T(8,128)(2,1)} %collective-permute-done), channel_id=1, source_target_pairs={{0,16},{16,32},{32,48},{48,64},{64,80},{80,96},{96,112},{112,0},{1... | collective-permute-start | bytes 576008 | tf_op jit(solution)/shard_map/ppermute | solution.py:218
  17.1 13.8 %copy-start = (bf16[1,2,160,2400]{3,2,1,0:T(8,128)(2,1)S(1)}, bf16[1,2,160,2400]{3,2,1,0:T(8,128)(2,1)}, u32[]{:S(2)}) copy-start(bf16[1,2,160,2400]{3,2,1,0:T(8,128)(2,1)} %param.7) | copy-start | bytes 4608004
  22.8 8.0 %collective-permute-start.5 = (bf16[40,2400]{1,0:T(8,128)(2,1)S(1)}, bf16[40,2400]{1,0:T(8,128)(2,1)S(1)}, u32[]{:S(2)}, u32[]{:S(2)}) collective-permute-start(bf16[40,2400]{1,0:T(8,128)(2,1)S(1)} %collective-permute-done.1), channel_id=1, source_target_pairs={{0,16},{16,32},{32,48},{48,64},{64,80},{80,96},{96,112},{112,0},{1... | collective-permute-start | bytes 576008 | tf_op jit(solution)/shard_map/ppermute | solution.py:218
  22.8 8.0 %collective-permute-start.6 = (bf16[40,2400]{1,0:T(8,128)(2,1)S(1)}, bf16[40,2400]{1,0:T(8,128)(2,1)S(1)}, u32[]{:S(2)}, u32[]{:S(2)}) collective-permute-start(bf16[40,2400]{1,0:T(8,128)(2,1)S(1)} %collective-permute-done.3), channel_id=1, source_target_pairs={{16,0},{32,16},{48,32},{64,48},{80,64},{96,80},{112,96},{0,112},{1... | collective-permute-start | bytes 576008 | tf_op jit(solution)/shard_map/ppermute | solution.py:219
  25.5 5.4 %collective-permute-start.10 = (bf16[200,2400]{1,0:T(8,128)(2,1)S(1)}, bf16[200,2400]{1,0:T(8,128)(2,1)S(1)}, u32[]{:S(2)}, u32[]{:S(2)}) collective-permute-start(bf16[200,2400]{1,0:T(8,128)(2,1)S(1)} %constant_dynamic-update-slice_fusion.b0), channel_id=1, source_target_pairs={{0,8},{8,0},{1,9},{9,1},{2,10},{10,2},{3,11},{11,3},{4,12},{12,4},... | collective-permute-start | bytes 2880008 | tf_op jit(solution)/shard_map/ppermute | solution.py:230
  32.4 5.4 %collective-permute-start.11 = (bf16[24,2400]{1,0:T(8,128)(2,1)S(1)}, bf16[24,2400]{1,0:T(8,128)(2,1)S(1)}, u32[]{:S(2)}, u32[]{:S(2)}) collective-permute-start(bf16[24,2400]{1,0:T(8,128)(2,1)S(1)} %slice.14), channel_id=1, source_target_pairs={{0,16},{16,32},{32,48},{48,64},{64,80},{80,96},{96,112},{112,0},{1... | collective-permute-start | bytes 345608 | tf_op jit(solution)/shard_map/ppermute | solution.py:258
  32.5 9.8 %collective-permute-start.9 = (bf16[80,2400]{1,0:T(8,128)(2,1)S(1)}, bf16[80,2400]{1,0:T(8,128)(2,1)S(1)}, u32[]{:S(2)}, u32[]{:S(2)}) collective-permute-start(bf16[80,2400]{1,0:T(8,128)(2,1)S(1)} %get-tuple-element.37), channel_id=1, source_target_pairs={{1,0},{2,1},{3,2},{0,3},{5,4},{6,5},{7,6},{4,7},{9,8},{10,9},{11,1... | collective-permute-start | bytes 1152008 | tf_op jit(solution)/shard_map/ppermute | solution.py:227
  35.1 10.3 %collective-permute-start.8 = (bf16[80,2400]{1,0:T(8,128)(2,1)S(1)}, bf16[80,2400]{1,0:T(8,128)(2,1)S(1)}, u32[]{:S(2)}, u32[]{:S(2)}) collective-permute-start(bf16[80,2400]{1,0:T(8,128)(2,1)S(1)} %get-tuple-element.38), channel_id=1, source_target_pairs={{0,1},{1,2},{2,3},{3,0},{4,5},{5,6},{6,7},{7,4},{8,9},{9,10},{10,1... | collective-permute-start | bytes 1152008 | tf_op jit(solution)/shard_map/ppermute | solution.py:226
  35.1 4.2 %collective-permute-start.12 = (bf16[16,2400]{1,0:T(8,128)(2,1)S(1)}, bf16[16,2400]{1,0:T(8,128)(2,1)S(1)}, u32[]{:S(2)}, u32[]{:S(2)}) collective-permute-start(bf16[16,2400]{1,0:T(8,128)(2,1)S(1)} %slice.15), channel_id=1, source_target_pairs={{16,0},{32,16},{48,32},{64,48},{80,64},{96,80},{112,96},{0,112},{1... | collective-permute-start | bytes 230408 | tf_op jit(solution)/shard_map/ppermute | solution.py:259
  39.3 11.1 %collective-permute-start.15 = (bf16[120,2400]{1,0:T(8,128)(2,1)S(1)}, bf16[120,2400]{1,0:T(8,128)(2,1)S(1)}, u32[]{:S(2)}, u32[]{:S(2)}) collective-permute-start(bf16[120,2400]{1,0:T(8,128)(2,1)S(1)} %constant_dynamic-update-slice_fusion.5.b0), channel_id=1, source_target_pairs={{0,8},{8,0},{1,9},{9,1},{2,10},{10,2},{3,11},{11,3},{4,12},{12,4},... | collective-permute-start | bytes 1728008 | tf_op jit(solution)/shard_map/ppermute | solution.py:261
  45.5 15.6 %collective-permute-start.13 = (bf16[160,2400]{1,0:T(8,128)(2,1)S(1)}, bf16[160,2400]{1,0:T(8,128)(2,1)S(1)}, u32[]{:S(2)}, u32[]{:S(2)}) collective-permute-start(bf16[160,2400]{1,0:T(8,128)(2,1)S(1)} %collective-permute-done.7.far_a), channel_id=1, source_target_pairs={{0,8},{8,0},{1,9},{9,1},{2,10},{10,2},{3,11},{11,3},{4,12},{12,4},... | collective-permute-start | bytes 2304008 | tf_op jit(solution)/shard_map/ppermute | solution.py:265
  48.1 13.0 %collective-permute-start.14 = (bf16[160,2400]{1,0:T(8,128)(2,1)S(1)}, bf16[160,2400]{1,0:T(8,128)(2,1)S(1)}, u32[]{:S(2)}, u32[]{:S(2)}) collective-permute-start(bf16[160,2400]{1,0:T(8,128)(2,1)S(1)} %constant_dynamic-update-slice_fusion.9.far_b), channel_id=1, source_target_pairs={{0,8},{8,0},{1,9},{9,1},{2,10},{10,2},{3,11},{11,3},{4,12},{12,4},... | collective-permute-start | bytes 2304008 | tf_op jit(solution)/shard_map/ppermute | solution.py:265
  52.8 17.1 %copy-start.6 = (s32[2,30]{1,0:T(2,128)S(1)}, s32[2,30]{1,0:T(2,128)}, u32[]{:S(2)}) copy-start(s32[2,30]{1,0:T(2,128)} %param.11) | copy-start | bytes 724
  52.8 7.0 %collective-permute-start.16 = (f32[2,80,160]{2,1,0:T(8,128)S(1)}, f32[2,80,160]{2,1,0:T(8,128)S(1)}, u32[]{:S(2)}, u32[]{:S(2)}) collective-permute-start(f32[2,80,160]{2,1,0:T(8,128)S(1)} %last_terms.1.t), channel_id=1, source_target_pairs={{0,128},{128,0},{1,129},{129,1},{2,130},{130,2},{3,131},{131,3},{4... | collective-permute-start | bytes 307208 | tf_op jit(solution)/shard_map/ppermute | solution.py:277
  55.8 5.2 %collective-permute-start.17 = (f32[2,80,160]{2,1,0:T(8,128)S(1)}, f32[2,80,160]{2,1,0:T(8,128)S(1)}, u32[]{:S(2)}, u32[]{:S(2)}) collective-permute-start(f32[2,80,160]{2,1,0:T(8,128)S(1)} %last_terms.1.t), channel_id=1, source_target_pairs={{0,8},{8,0},{1,9},{9,1},{2,10},{10,2},{3,11},{11,3},{4,12},{12,4},... | collective-permute-start | bytes 307208 | tf_op jit(solution)/shard_map/ppermute | solution.py:278
  59.8 2.3 %collective-permute-start.18 = (f32[2,80,160]{2,1,0:T(8,128)S(1)}, f32[2,80,160]{2,1,0:T(8,128)S(1)}, u32[]{:S(2)}, u32[]{:S(2)}) collective-permute-start(f32[2,80,160]{2,1,0:T(8,128)S(1)} %collective-permute-done.16.t_yh), channel_id=1, source_target_pairs={{0,8},{8,0},{1,9},{9,1},{2,10},{10,2},{3,11},{11,3},{4,12},{12,4},... | collective-permute-start | bytes 307208 | tf_op jit(solution)/shard_map/ppermute | solution.py:279
  65.1 14.4 %all-to-all-start = ((f32[8,48,128]{2,1,0:T(8,128)}), f32[8,48,128]{2,1,0:T(8,128)S(1)}, u32[]{:S(2)}, u32[]{:S(2)}) async-start(f32[8,48,128]{2,1,0:T(8,128)} %cluster_terms.1), calls=%async_computation | async-start | bytes 393216 | tf_op jit(solution)/shard_map/all_to_all | solution.py:292

commit v8 on v7

--- a/solution.py
+++ b/solution.py
@@ -17,8 +17,8 @@
 BF16 = jnp.bfloat16
 
 
-def prep_kernel(width, functions, k_points, ids, cells, diff_class, class_weight, cos_table, sin_table, w_ref, g0, g1):
-    yh, z, core = ids[0], ids[1], ids[2]
+def prep_kernel(width, functions, k_points, cells, diff_class, class_weight, cos_table, sin_table, w_ref, g0, g1):
+    yh, z, core = (lax.axis_index(name) for name in KA)
     group = 2 * width
     count = len(k_points)
     rows, lanes = 4 * width, group * count
@@ -72,7 +72,13 @@
     return t[:half] + t[half:]
 
 
-def either_way(odd, far_a, far_b, run):
+def odd_x():
+    return jnp.bitwise_and(lax.axis_index("x"), 1)
+
+
+def either_way(far_a, far_b, run):
+    odd = odd_x()
+
     @pl.when(odd == 0)
     def _():
         run(far_a, far_b)
@@ -94,16 +100,16 @@
     t_ref[...] = part_of_t(b, own.at[0], own.at[1], w[0, : b.shape[0], :], g[...], width)
 
 
-def far_kernel(width, ids, far_a, far_b, b0, b1, w, g, t_ref, b_ref):
+def far_kernel(width, far_a, far_b, b0, b1, w, g, t_ref, b_ref):
     b = gathered(b_ref, b0, b1)
 
     def run(real, imag):
         t_ref[...] = part_of_t(b, real, imag, w[1, : b.shape[0], :], g[...], width)
 
-    either_way(ids[3], far_a, far_b, run)
-
-
-def last_kernel(width, ids, own, far_a, far_b, b0, b1, w, g, t_own, t_far, t_ref, b_ref):
+    either_way(far_a, far_b, run)
+
+
+def last_kernel(width, own, far_a, far_b, b0, b1, w, g, t_own, t_far, t_ref, b_ref):
     b = gathered(b_ref, b0, b1)
     start = w.shape[1] - b.shape[0]
 
@@ -111,7 +117,7 @@
         t_ref[0] = t_own[...] + part_of_t(b, own.at[0], own.at[1], w[0, start:, :], g[...], width)
         t_ref[1] = t_far[...] + part_of_t(b, real, imag, w[1, start:, :], g[...], width)
 
-    either_way(ids[3], far_a, far_b, run)
+    either_way(far_a, far_b, run)
 
 
 def packed(u, at, columns):
@@ -129,9 +135,9 @@
 
 
 def cluster_kernel(
-    width, columns, ids, own, near, far_a, far_b, diag_a, diag_b, t, t_yh, t_core, t_diag, out, u_ref
+    width, columns, own, near, far_a, far_b, diag_a, diag_b, t, t_yh, t_core, t_diag, out, u_ref
 ):
-    yh, core, odd = ids[0], ids[2], ids[3]
+    yh, core, odd = lax.axis_index("yh"), lax.axis_index("core"), odd_x()
     chips, _, lanes = out.shape
     span = 2 * chips * columns
     shift = span % 128
@@ -207,8 +213,7 @@
     left = [(j, i) for i, j in right]
     vmem, smem = pltpu.VMEM, pltpu.SMEM
 
-    odd = jnp.bitwise_and(lax.axis_index("x"), 1)
-    far_a = lax.ppermute(lax.dynamic_index_in_dim(own, odd, 0, keepdims=False), "yh", swap)
+    far_a = lax.ppermute(lax.dynamic_index_in_dim(own, odd_x(), 0, keepdims=False), "yh", swap)
     near = lax.ppermute(own, "core", swap)
     block = lax.dynamic_slice_in_dim(own, band * width, width, 1).reshape(group, functions)
     blocks = [block]
@@ -235,8 +240,7 @@
     early, late = 2 * split * group, 2 * (len(offsets) - split) * group
     angles = 2.0 * np.pi * np.arange(kpoint_count) / kpoint_count
     tables = [jnp.asarray((f(angles) / kpoint_count).astype(np.float32)) for f in (np.cos, np.sin)]
-    ids = jnp.stack([yh, z, core, odd]).astype(jnp.int32)
-    later_ids, _ = lax.optimization_barrier((ids, first))
+    later_cells, _ = lax.optimization_barrier((frag_cells, first))
     weights, g_first, g_last = call(
         functools.partial(prep_kernel, width, functions, k_points),
         "phases",
@@ -245,34 +249,35 @@
             jax.ShapeDtypeStruct((8 * width, early), BF16),
             jax.ShapeDtypeStruct((8 * width, late), BF16),
         ),
-        [smem] * 6,
-    )(later_ids, frag_cells, diff_class, class_weight, *tables)
+        [smem] * 5,
+    )(later_cells, diff_class, class_weight, *tables)
 
     one = jax.ShapeDtypeStruct((4 * width, occupied), F32)
     scratch = [pltpu.VMEM((early, functions), BF16)]
     b_first = (first, first_near, weights, g_first)
     kernel = functools.partial(own_kernel, width)
     t_own = call(kernel, "own_first", one, [vmem] * 5, scratch, flops=10**9)(own, *b_first)
-    from_below, from_above, t_own = lax.optimization_barrier((from_below, from_above, t_own))
     cut = 24
     blocks.append(lax.ppermute(from_below[:cut], "z", up))
     blocks.append(lax.ppermute(from_above[cut:], "z", down))
+    held = (blocks[-2], blocks[-1], from_left, from_right, t_own)
+    blocks[-2], blocks[-1], from_left, from_right, t_own = lax.optimization_barrier(held)
     last = jnp.concatenate(blocks[split:], 0)
+    far_b = jnp.concatenate([from_left, from_right], 0)
+    last, far_b = lax.optimization_barrier((last, far_b))
     last_near = lax.ppermute(last, "core", swap)
-    from_left, from_right, _ = lax.optimization_barrier((from_left, from_right, last))
-    far_b = jnp.concatenate([from_left, from_right], 0)
     later_a, _ = lax.optimization_barrier((far_a, far_b))
     diag_a, diag_b = (lax.ppermute(half, "core", swap) for half in (later_a, far_b))
     kernel = functools.partial(far_kernel, width)
-    t_far = call(kernel, "far_first", one, [smem] + [vmem] * 6, scratch, flops=10**9)(ids, far_a, far_b, *b_first)
+    t_far = call(kernel, "far_first", one, [vmem] * 6, scratch, flops=10**9)(far_a, far_b, *b_first)
     t = call(
         functools.partial(last_kernel, width),
         "last_terms",
         jax.ShapeDtypeStruct((2,) + one.shape, F32),
-        [smem] + [vmem] * 9,
+        [vmem] * 9,
         [pltpu.VMEM((late, functions), BF16)],
         flops=10**9,
-    )(ids, own, far_a, far_b, last, last_near, weights, g_last, t_own, t_far)
+    )(own, far_a, far_b, last, last_near, weights, g_last, t_own, t_far)
 
     t_yh = lax.ppermute(t, "yh", swap)
     t_core = lax.ppermute(t, "core", swap)
@@ -284,10 +289,10 @@
         functools.partial(cluster_kernel, width, columns),
         "cluster_terms",
         jax.ShapeDtypeStruct((chips, 4 * width * 3 // 5, 128), F32),
-        [smem] + [vmem] * 10,
+        [vmem] * 10,
         [pltpu.VMEM((4 * width, span + span % 128), F32)],
         flops=10**9,
-    )(ids, own, near, far_a, far_b, diag_a, diag_b, t, t_yh, t_core, t_diag)
+    )(own, near, far_a, far_b, diag_a, diag_b, t, t_yh, t_core, t_diag)
 
     arrived = lax.all_to_all(pieces, "z", 0, 0, tiled=True)
     index = (yh * PARTS[1] + z) * 2 + core

time: 80.9 us -> 74.7 us (0.923)
  starting transfers between devices: 38.4 us -> 35 us
  local copies, waits for them, and re-layouts: 5.54 us -> 2.48 us
  waiting for transfers between devices: 24.8 us -> 26.5 us
  Pallas kernels: 11.1 us -> 9.42 us
    ppermute x1, waiting for transfers between devices: 1.45 us -> 4.45 us  [shards(): lax.ppermute(lax.dynamic_index_in_dim(own, odd_x(), 0, keepdims=False), '...]
    ppermute x3, waiting for transfers between devices: 3.01 us -> 5.18 us  [shards(): from_below = lax.ppermute(from_below, 'z', up)]
    ppermute x2, starting transfers between devices: 2.67 us -> 0.51 us  [shards(): lax.ppermute(half, 'core', swap)]
    unnamed x22 -> x18, local copies, waits for them, and re-layouts: 2.2 us -> 0.12 us
    ppermute x3, waiting for transfers between devices: 1.59 us -> 0.01 us  [shards(): from_above = lax.ppermute(from_above, 'z', down)]
    ppermute x1, waiting for transfers between devices: 1.43 us -> 0.01 us  [shards(): blocks.append(lax.ppermute(from_above[cut:], 'z', down))]
    ppermute x1, starting transfers between devices: 0.01 us -> 1.29 us  [shards(): from_left = lax.ppermute(far_a[:mid], 'x', right)]
    ppermute x1, starting transfers between devices: 2.55 us -> 1.47 us  [shards(): from_right = lax.ppermute(far_a[mid:], 'x', left)]
  transfers between devices with their start and end apart: 20 -> 20, of which waited for: 9 -> 7; matrix products, arithmetic and copies ran while one was open for 7% -> 3% of each run, Pallas kernels for 7% -> 8%
where the time goes in v8:
time: 74.7 us; the launch traced here: 73.9 us
  starting transfers between devices  35 us (47%)
  waiting for transfers between devices  26.5 us (35%)
  Pallas kernels  9.42 us (13%)
  local copies, waits for them, and re-layouts  2.48 us (3%)
    all_to_all x1, waiting for transfers between devices, shards(): arrived = lax.all_to_all(pieces, 'z', 0, 0, tiled=True)  9.41 us
    ppermute x3, starting transfers between devices, shards(): from_above = lax.ppermute(from_above, 'z', down)  9.26 us
    ppermute x3, waiting for transfers between devices, shards(): from_below = lax.ppermute(from_below, 'z', up)  5.18 us
    all_to_all x1, starting transfers between devices, shards(): arrived = lax.all_to_all(pieces, 'z', 0, 0, tiled=True)  4.88 us
    ppermute x1, waiting for transfers between devices, shards(): lax.ppermute(lax.dynamic_index_in_dim(own, odd_x(), 0, keepdims=False), '...  4.45 us
    ppermute x1, waiting for transfers between devices, shards(): t_yh = lax.ppermute(t, 'yh', swap)  3.97 us
    ppermute x1, starting transfers between devices, shards(): near = lax.ppermute(own, 'core', swap)  3.24 us
    ppermute x1, starting transfers between devices, shards(): t_yh = lax.ppermute(t, 'yh', swap)  3.02 us
  transfers between devices with their start and end apart: 20, of which 7 were waited for; matrix products, arithmetic and copies ran while one was open for 3% of the time, Pallas kernels for 8%

profile of v8, /device:TPU:1, one launch (start us, length us, event | category | flops | bytes accessed | tf_op | source)
XLA Modules:
  0.0 73.9 jit_solution(2224731743021289757)
XLA Ops:
  0.0 3.2 %collective-permute-start.4 = (bf16[2,160,2400]{2,1,0:T(8,128)(2,1)}, bf16[2,160,2400]{2,1,0:T(8,128)(2,1)S(1)}, u32[]{:S(2)}, u32[]{:S(2)}) collective-permute-start(bf16[2,160,2400]{2,1,0:T(8,128)(2,1)} %bitcast.6), channel_id=1, source_target_pairs={{0,8},{8,0},{1,9},{9,1},{2,10},{10,2},{3,11},{11,3},{4,12},{12,4},... | collective-permute-start | bytes 4608008 | tf_op jit(solution)/shard_map/ppermute | solution.py:217
  3.2 1.0 %constant_dynamic-slice_fusion = bf16[1,2,20,2400]{3,2,1,0:T(8,128)(2,1)S(1)} fusion(bf16[1,2,160,2400]{3,2,1,0:T(8,128)(2,1)} %param.7, s32[]{:T(128)S(6)} %select_n.16), kind=kLoop, calls=%fused_computation.13 | loop fusion | bytes 384004 | tf_op jit(solution)/shard_map/dynamic_slice | solution.py:218
  4.4 3.9 %collective-permute-start.2 = (bf16[40,2400]{1,0:T(8,128)(2,1)S(1)}, bf16[40,2400]{1,0:T(8,128)(2,1)S(1)}, u32[]{:S(2)}, u32[]{:S(2)}) collective-permute-start(bf16[40,2400]{1,0:T(8,128)(2,1)S(1)} %reshape.19), channel_id=1, source_target_pairs={{16,0},{32,16},{48,32},{64,48},{80,64},{96,80},{112,96},{0,112},{1... | collective-permute-start | bytes 576008 | tf_op jit(solution)/shard_map/ppermute | solution.py:224
  8.3 1.2 %dynamic-slice_bitcast_fusion = bf16[160,2400]{1,0:T(8,128)(2,1)S(1)} fusion(bf16[1,2,160,2400]{3,2,1,0:T(8,128)(2,1)} %param.7, s32[]{:T(128)S(6)} %select_n.17), kind=kLoop, calls=%fused_computation.2 | loop fusion | bytes 1536004 | tf_op jit(solution)/shard_map/jit(dynamic_index_in_dim)/squeeze | solution.py:216
  9.5 3.0 %collective-permute-start.7 = (bf16[160,2400]{1,0:T(8,128)(2,1)S(1)}, bf16[160,2400]{1,0:T(8,128)(2,1)S(1)}, u32[]{:S(2)}, u32[]{:S(2)}) collective-permute-start(bf16[160,2400]{1,0:T(8,128)(2,1)S(1)} %dynamic-slice_bitcast_fusion), channel_id=1, source_target_pairs={{0,128},{128,0},{1,129},{129,1},{2,130},{130,2},{3,131},{131,3},{4... | collective-permute-start | bytes 2304008 | tf_op jit(solution)/shard_map/ppermute | solution.py:216
  12.5 0.9 %collective-permute-done = bf16[40,2400]{1,0:T(8,128)(2,1)S(1)} collective-permute-done((bf16[40,2400]{1,0:T(8,128)(2,1)S(1)}, bf16[40,2400]{1,0:T(8,128)(2,1)S(1)}, u32[]{:S(2)}, u32[]{:S(2)}) %collective-permute-start) | collective-permute-done | bytes 192032 | tf_op jit(solution)/shard_map/ppermute | solution.py:223
  13.5 2.7 %collective-permute-start.3 = (bf16[40,2400]{1,0:T(8,128)(2,1)S(1)}, bf16[40,2400]{1,0:T(8,128)(2,1)S(1)}, u32[]{:S(2)}, u32[]{:S(2)}) collective-permute-start(bf16[40,2400]{1,0:T(8,128)(2,1)S(1)} %collective-permute-done.2), channel_id=1, source_target_pairs={{16,0},{32,16},{48,32},{64,48},{80,64},{96,80},{112,96},{0,112},{1... | collective-permute-start | bytes 576008 | tf_op jit(solution)/shard_map/ppermute | solution.py:224
  16.3 4.2 %collective-permute-done.1 = bf16[40,2400]{1,0:T(8,128)(2,1)S(1)} collective-permute-done((bf16[40,2400]{1,0:T(8,128)(2,1)S(1)}, bf16[40,2400]{1,0:T(8,128)(2,1)S(1)}, u32[]{:S(2)}, u32[]{:S(2)}) %collective-permute-start.1) | collective-permute-done | bytes 192032 | tf_op jit(solution)/shard_map/ppermute | solution.py:223
  20.5 2.7 %collective-permute-start.6 = (bf16[40,2400]{1,0:T(8,128)(2,1)S(1)}, bf16[40,2400]{1,0:T(8,128)(2,1)S(1)}, u32[]{:S(2)}, u32[]{:S(2)}) collective-permute-start(bf16[40,2400]{1,0:T(8,128)(2,1)S(1)} %collective-permute-done.3), channel_id=1, source_target_pairs={{16,0},{32,16},{48,32},{64,48},{80,64},{96,80},{112,96},{0,112},{1... | collective-permute-start | bytes 576008 | tf_op jit(solution)/shard_map/ppermute | solution.py:224
  23.3 2.1 %collective-permute-start.12 = (bf16[200,2400]{1,0:T(8,128)(2,1)S(1)}, bf16[200,2400]{1,0:T(8,128)(2,1)S(1)}, u32[]{:S(2)}, u32[]{:S(2)}) collective-permute-start(bf16[200,2400]{1,0:T(8,128)(2,1)S(1)} %constant_dynamic-update-slice_fusion.b0), channel_id=1, source_target_pairs={{0,8},{8,0},{1,9},{9,1},{2,10},{10,2},{3,11},{11,3},{4,12},{12,4},... | collective-permute-start | bytes 2880008 | tf_op jit(solution)/shard_map/ppermute | solution.py:235
  25.3 4.5 %collective-permute-done.7.far_a = bf16[160,2400]{1,0:T(8,128)(2,1)S(1)} collective-permute-done((bf16[160,2400]{1,0:T(8,128)(2,1)S(1)}, bf16[160,2400]{1,0:T(8,128)(2,1)S(1)}, u32[]{:S(2)}, u32[]{:S(2)}) %collective-permute-start.7) | collective-permute-done | bytes 768032 | tf_op jit(solution)/shard_map/ppermute | solution.py:216
  29.9 1.3 %collective-permute-start.10 = (bf16[80,2400]{1,0:T(8,128)(2,1)S(1)}, bf16[80,2400]{1,0:T(8,128)(2,1)S(1)}, u32[]{:S(2)}, u32[]{:S(2)}) collective-permute-start(bf16[80,2400]{1,0:T(8,128)(2,1)S(1)} %get-tuple-element.42), channel_id=1, source_target_pairs={{0,1},{1,2},{2,3},{3,0},{4,5},{5,6},{6,7},{7,4},{8,9},{9,10},{10,1... | collective-permute-start | bytes 1152008 | tf_op jit(solution)/shard_map/ppermute | solution.py:231
  31.2 1.5 %collective-permute-start.11 = (bf16[80,2400]{1,0:T(8,128)(2,1)S(1)}, bf16[80,2400]{1,0:T(8,128)(2,1)S(1)}, u32[]{:S(2)}, u32[]{:S(2)}) collective-permute-start(bf16[80,2400]{1,0:T(8,128)(2,1)S(1)} %get-tuple-element.41), channel_id=1, source_target_pairs={{1,0},{2,1},{3,2},{0,3},{5,4},{6,5},{7,6},{4,7},{9,8},{10,9},{11,1... | collective-permute-start | bytes 1152008 | tf_op jit(solution)/shard_map/ppermute | solution.py:232
  32.8 1.1 %phases.1 = (f32[2,640,1]{2,1,0:T(8,128)S(1)}, bf16[160,400]{1,0:T(8,128)(2,1)S(1)}, bf16[160,240]{1,0:T(8,128)(2,1)S(1)}) custom-call(s32[2]{0:T(128)S(1)} %copy-done.2, s32[32,32]{1,0:T(8,128)S(1)} %copy-done.1, f32[32]{0:T(128)S(1)} %copy-done.3, f32[32]{0:T(128)S(1)} %copy-done.4, f32[32]{0:T(128)S(1)} %copy-done.5), custom_call_target="tpu_custom_call" | custom-call | bytes 1048576 | tf_op jit(solution)/shard_map/phases/pallas_call | solution.py:244
  33.9 2.7 %collective-permute-start.9 = (bf16[16,2400]{1,0:T(8,128)(2,1)S(1)}, bf16[16,2400]{1,0:T(8,128)(2,1)S(1)}, u32[]{:S(2)}, u32[]{:S(2)}) collective-permute-start(bf16[16,2400]{1,0:T(8,128)(2,1)S(1)} %slice.13), channel_id=1, source_target_pairs={{16,0},{32,16},{48,32},{64,48},{80,64},{96,80},{112,96},{0,112},{1... | collective-permute-start | bytes 230408 | tf_op jit(solution)/shard_map/ppermute | solution.py:262
  36.6 1.4 %own_first.1.t_own = f32[80,160]{1,0:T(8,128)S(1)} custom-call(bf16[2,160,2400]{2,1,0:T(8,128)(2,1)S(1)} %bitcast.7, bf16[200,2400]{1,0:T(8,128)(2,1)S(1)} %constant_dynamic-update-slice_fusion.b0, bf16[200,2400]{1,0:T(8,128)(2,1)S(1)} %collective-permute-done.12.b1, f32[2,640,1]{2,1,0:T(8,128)S(1)} %get-tuple-element.30.w, ...), custom_call_target="tpu_custom_call" | custom-call | flops 1000000000 | bytes 1048576 | tf_op jit(solution)/shard_map/own_first/pallas_call | solution.py:259
  38.1 2.5 %collective-permute-done.10 = bf16[80,2400]{1,0:T(8,128)(2,1)S(1)} collective-permute-done((bf16[80,2400]{1,0:T(8,128)(2,1)S(1)}, bf16[80,2400]{1,0:T(8,128)(2,1)S(1)}, u32[]{:S(2)}, u32[]{:S(2)}) %collective-permute-start.10) | collective-permute-done | bytes 384032 | tf_op jit(solution)/shard_map/ppermute | solution.py:231
  40.7 2.1 %collective-permute-start.15 = (bf16[120,2400]{1,0:T(8,128)(2,1)S(1)}, bf16[120,2400]{1,0:T(8,128)(2,1)S(1)}, u32[]{:S(2)}, u32[]{:S(2)}) collective-permute-start(bf16[120,2400]{1,0:T(8,128)(2,1)S(1)} %pad_maximum_fusion.1.b0), channel_id=1, source_target_pairs={{0,8},{8,0},{1,9},{9,1},{2,10},{10,2},{3,11},{11,3},{4,12},{12,4},... | collective-permute-start | bytes 1728008 | tf_op jit(solution)/shard_map/ppermute | solution.py:268
  42.8 0.1 collective-permute-start.13
  42.9 0.4 collective-permute-start.14
  43.3 1.6 %far_first.1.t_far = f32[80,160]{1,0:T(8,128)S(1)} custom-call(bf16[160,2400]{1,0:T(8,128)(2,1)S(1)} %collective-permute-done.7.far_a, bf16[160,2400]{1,0:T(8,128)(2,1)S(1)} %pad_maximum_fusion.far_b, bf16[200,2400]{1,0:T(8,128)(2,1)S(1)} %constant_dynamic-update-slice_fusion.b0, bf16[200,2400]{1,0:T(8,128)(2,1)S(1)} %collective-permute-done.12.b1, ...), custom_call_target="tpu_custom_call" | custom-call | flops 1000000000 | bytes 1048576 | tf_op jit(solution)/shard_map/far_first/pallas_call | solution.py:272
  45.0 1.9 %last_terms.1.t = f32[2,80,160]{2,1,0:T(8,128)S(1)} custom-call(bf16[2,160,2400]{2,1,0:T(8,128)(2,1)S(1)} %bitcast.8, bf16[160,2400]{1,0:T(8,128)(2,1)S(1)} %collective-permute-done.7.far_a, bf16[160,2400]{1,0:T(8,128)(2,1)S(1)} %pad_maximum_fusion.far_b, bf16[120,2400]{1,0:T(8,128)(2,1)S(1)} %pad_maximum_fusion.1.b0, ...), custom_call_target="tpu_custom_call" | custom-call | flops 1000000000 | bytes 1048576 | tf_op jit(solution)/shard_map/last_terms/pallas_call | solution.py:273
  46.9 3.0 %collective-permute-start.16 = (f32[2,80,160]{2,1,0:T(8,128)S(1)}, f32[2,80,160]{2,1,0:T(8,128)S(1)}, u32[]{:S(2)}, u32[]{:S(2)}) collective-permute-start(f32[2,80,160]{2,1,0:T(8,128)S(1)} %last_terms.1.t), channel_id=1, source_target_pairs={{0,128},{128,0},{1,129},{129,1},{2,130},{130,2},{3,131},{131,3},{4... | collective-permute-start | bytes 307208 | tf_op jit(solution)/shard_map/ppermute | solution.py:282
  49.9 0.4 collective-permute-start.17
  50.3 4.0 %collective-permute-done.16.t_yh = f32[2,80,160]{2,1,0:T(8,128)S(1)} collective-permute-done((f32[2,80,160]{2,1,0:T(8,128)S(1)}, f32[2,80,160]{2,1,0:T(8,128)S(1)}, u32[]{:S(2)}, u32[]{:S(2)}) %collective-permute-start.16) | collective-permute-done | bytes 102432 | tf_op jit(solution)/shard_map/ppermute | solution.py:282
  54.3 0.9 %collective-permute-start.18 = (f32[2,80,160]{2,1,0:T(8,128)S(1)}, f32[2,80,160]{2,1,0:T(8,128)S(1)}, u32[]{:S(2)}, u32[]{:S(2)}) collective-permute-start(f32[2,80,160]{2,1,0:T(8,128)S(1)} %collective-permute-done.16.t_yh), channel_id=1, source_target_pairs={{0,8},{8,0},{1,9},{9,1},{2,10},{10,2},{3,11},{11,3},{4,12},{12,4},... | collective-permute-start | bytes 307208 | tf_op jit(solution)/shard_map/ppermute | solution.py:284
  55.1 1.0 %collective-permute-done.18.t_diag = f32[2,80,160]{2,1,0:T(8,128)S(1)} collective-permute-done((f32[2,80,160]{2,1,0:T(8,128)S(1)}, f32[2,80,160]{2,1,0:T(8,128)S(1)}, u32[]{:S(2)}, u32[]{:S(2)}) %collective-permute-start.18) | collective-permute-done | bytes 102432 | tf_op jit(solution)/shard_map/ppermute | solution.py:284
  56.2 2.5 %cluster_terms.1 = f32[8,48,128]{2,1,0:T(8,128)} custom-call(bf16[2,160,2400]{2,1,0:T(8,128)(2,1)S(1)} %bitcast.9, bf16[2,160,2400]{2,1,0:T(8,128)(2,1)S(1)} %collective-permute-done.4.near, bf16[160,2400]{1,0:T(8,128)(2,1)S(1)} %collective-permute-done.7.far_a, bf16[160,2400]{1,0:T(8,128)(2,1)S(1)} %pad_maximum_fusion.far_b, ...), custom_call_target="tpu_custom_call" | custom-call | flops 1000000000 | bytes 1048576 | tf_op jit(solution)/shard_map/cluster_terms/pallas_call | solution.py:288
  58.7 4.9 %all-to-all-start = ((f32[8,48,128]{2,1,0:T(8,128)}), f32[8,48,128]{2,1,0:T(8,128)S(1)}, u32[]{:S(2)}, u32[]{:S(2)}) async-start(f32[8,48,128]{2,1,0:T(8,128)} %cluster_terms.1), calls=%async_computation | async-start | bytes 393216 | tf_op jit(solution)/shard_map/all_to_all | solution.py:297
  63.6 0.1 convolution_bitcast_fusion.mask
  63.7 9.4 %all-to-all-done.arrived = f32[8,48,128]{2,1,0:T(8,128)S(1)} async-done(((f32[8,48,128]{2,1,0:T(8,128)}), f32[8,48,128]{2,1,0:T(8,128)S(1)}, u32[]{:S(2)}, u32[]{:S(2)}) %all-to-all-start) | async-done | bytes 196640 | tf_op jit(solution)/shard_map/all_to_all | solution.py:297
  73.1 0.8 %sum_and_mask.1 = f32[2,20,2,75]{3,2,1,0:T(2,128)} custom-call(f32[8,48,128]{2,1,0:T(8,128)S(1)} %all-to-all-done.arrived, f32[2,75]{1,0:T(2,128)S(1)} %convolution_bitcast_fusion.mask), custom_call_target="tpu_custom_call" | custom-call | bytes 1048576 | tf_op jit(solution)/shard_map/sum_and_mask/pallas_call | solution.py:304
  (43 shorter events, 0.6 us)
Async XLA Ops:
  0.0 20.5 %collective-permute-start.4 = (bf16[2,160,2400]{2,1,0:T(8,128)(2,1)}, bf16[2,160,2400]{2,1,0:T(8,128)(2,1)S(1)}, u32[]{:S(2)}, u32[]{:S(2)}) collective-permute-start(bf16[2,160,2400]{2,1,0:T(8,128)(2,1)} %bitcast.6), channel_id=1, source_target_pairs={{0,8},{8,0},{1,9},{9,1},{2,10},{10,2},{3,11},{11,3},{4,12},{12,4},... | collective-permute-start | bytes 4608008 | tf_op jit(solution)/shard_map/ppermute | solution.py:217
  4.3 9.1 %collective-permute-start = (bf16[40,2400]{1,0:T(8,128)(2,1)S(1)}, bf16[40,2400]{1,0:T(8,128)(2,1)S(1)}, u32[]{:S(2)}, u32[]{:S(2)}) collective-permute-start(bf16[40,2400]{1,0:T(8,128)(2,1)S(1)} %reshape.19), channel_id=1, source_target_pairs={{0,16},{16,32},{32,48},{48,64},{64,80},{80,96},{96,112},{112,0},{1... | collective-permute-start | bytes 576008 | tf_op jit(solution)/shard_map/ppermute | solution.py:223
  4.4 9.1 %collective-permute-start.2 = (bf16[40,2400]{1,0:T(8,128)(2,1)S(1)}, bf16[40,2400]{1,0:T(8,128)(2,1)S(1)}, u32[]{:S(2)}, u32[]{:S(2)}) collective-permute-start(bf16[40,2400]{1,0:T(8,128)(2,1)S(1)} %reshape.19), channel_id=1, source_target_pairs={{16,0},{32,16},{48,32},{64,48},{80,64},{96,80},{112,96},{0,112},{1... | collective-permute-start | bytes 576008 | tf_op jit(solution)/shard_map/ppermute | solution.py:224
  9.5 20.3 %collective-permute-start.7 = (bf16[160,2400]{1,0:T(8,128)(2,1)S(1)}, bf16[160,2400]{1,0:T(8,128)(2,1)S(1)}, u32[]{:S(2)}, u32[]{:S(2)}) collective-permute-start(bf16[160,2400]{1,0:T(8,128)(2,1)S(1)} %dynamic-slice_bitcast_fusion), channel_id=1, source_target_pairs={{0,128},{128,0},{1,129},{129,1},{2,130},{130,2},{3,131},{131,3},{4... | collective-permute-start | bytes 2304008 | tf_op jit(solution)/shard_map/ppermute | solution.py:216
  13.5 7.0 %collective-permute-start.1 = (bf16[40,2400]{1,0:T(8,128)(2,1)S(1)}, bf16[40,2400]{1,0:T(8,128)(2,1)S(1)}, u32[]{:S(2)}, u32[]{:S(2)}) collective-permute-start(bf16[40,2400]{1,0:T(8,128)(2,1)S(1)} %collective-permute-done), channel_id=1, source_target_pairs={{0,16},{16,32},{32,48},{48,64},{64,80},{80,96},{96,112},{112,0},{1... | collective-permute-start | bytes 576008 | tf_op jit(solution)/shard_map/ppermute | solution.py:223
  13.5 7.0 %collective-permute-start.3 = (bf16[40,2400]{1,0:T(8,128)(2,1)S(1)}, bf16[40,2400]{1,0:T(8,128)(2,1)S(1)}, u32[]{:S(2)}, u32[]{:S(2)}) collective-permute-start(bf16[40,2400]{1,0:T(8,128)(2,1)S(1)} %collective-permute-done.2), channel_id=1, source_target_pairs={{16,0},{32,16},{48,32},{64,48},{80,64},{96,80},{112,96},{0,112},{1... | collective-permute-start | bytes 576008 | tf_op jit(solution)/shard_map/ppermute | solution.py:224
  16.2 16.5 %copy-start.1 = (s32[32,32]{1,0:T(8,128)S(1)}, s32[32,32]{1,0:T(8,128)}, u32[]{:S(2)}) copy-start(s32[32,32]{1,0:T(8,128)} %diff_class.1) | copy-start | bytes 12292
  16.2 16.5 %copy-start.2 = (s32[2]{0:T(128)S(1)}, s32[2]{0:T(128)}, u32[]{:S(2)}) copy-start(s32[2]{0:T(128)} %cells) | copy-start | bytes 28
  16.2 16.5 %copy-start.3 = (f32[32]{0:T(128)S(1)}, f32[32]{0:T(128)}, u32[]{:S(2)}) copy-start(f32[32]{0:T(128)} %class_weight.1) | copy-start | bytes 388
  16.2 16.5 %copy-start.4 = (f32[32]{0:T(128)S(1)}, f32[32]{0:T(128)}, u32[]{:S(2)}) copy-start(f32[32]{0:T(128)} %constant.55.clone.cos_table) | copy-start | bytes 388
  16.2 16.5 %copy-start.5 = (f32[32]{0:T(128)S(1)}, f32[32]{0:T(128)}, u32[]{:S(2)}) copy-start(f32[32]{0:T(128)} %constant.56.clone.sin_table) | copy-start | bytes 388
  16.2 20.4 %copy-start = (bf16[1,2,160,2400]{3,2,1,0:T(8,128)(2,1)S(1)}, bf16[1,2,160,2400]{3,2,1,0:T(8,128)(2,1)}, u32[]{:S(2)}) copy-start(bf16[1,2,160,2400]{3,2,1,0:T(8,128)(2,1)} %param.7) | copy-start | bytes 4608004
  20.5 9.3 %collective-permute-start.5 = (bf16[40,2400]{1,0:T(8,128)(2,1)S(1)}, bf16[40,2400]{1,0:T(8,128)(2,1)S(1)}, u32[]{:S(2)}, u32[]{:S(2)}) collective-permute-start(bf16[40,2400]{1,0:T(8,128)(2,1)S(1)} %collective-permute-done.1), channel_id=1, source_target_pairs={{0,16},{16,32},{32,48},{48,64},{64,80},{80,96},{96,112},{112,0},{1... | collective-permute-start | bytes 576008 | tf_op jit(solution)/shard_map/ppermute | solution.py:223
  20.5 9.3 %collective-permute-start.6 = (bf16[40,2400]{1,0:T(8,128)(2,1)S(1)}, bf16[40,2400]{1,0:T(8,128)(2,1)S(1)}, u32[]{:S(2)}, u32[]{:S(2)}) collective-permute-start(bf16[40,2400]{1,0:T(8,128)(2,1)S(1)} %collective-permute-done.3), channel_id=1, source_target_pairs={{16,0},{32,16},{48,32},{64,48},{80,64},{96,80},{112,96},{0,112},{1... | collective-permute-start | bytes 576008 | tf_op jit(solution)/shard_map/ppermute | solution.py:224
  23.3 13.4 %collective-permute-start.12 = (bf16[200,2400]{1,0:T(8,128)(2,1)S(1)}, bf16[200,2400]{1,0:T(8,128)(2,1)S(1)}, u32[]{:S(2)}, u32[]{:S(2)}) collective-permute-start(bf16[200,2400]{1,0:T(8,128)(2,1)S(1)} %constant_dynamic-update-slice_fusion.b0), channel_id=1, source_target_pairs={{0,8},{8,0},{1,9},{9,1},{2,10},{10,2},{3,11},{11,3},{4,12},{12,4},... | collective-permute-start | bytes 2880008 | tf_op jit(solution)/shard_map/ppermute | solution.py:235
  29.9 10.7 %collective-permute-start.10 = (bf16[80,2400]{1,0:T(8,128)(2,1)S(1)}, bf16[80,2400]{1,0:T(8,128)(2,1)S(1)}, u32[]{:S(2)}, u32[]{:S(2)}) collective-permute-start(bf16[80,2400]{1,0:T(8,128)(2,1)S(1)} %get-tuple-element.42), channel_id=1, source_target_pairs={{0,1},{1,2},{2,3},{3,0},{4,5},{5,6},{6,7},{7,4},{8,9},{9,10},{10,1... | collective-permute-start | bytes 1152008 | tf_op jit(solution)/shard_map/ppermute | solution.py:231
  31.2 9.4 %collective-permute-start.11 = (bf16[80,2400]{1,0:T(8,128)(2,1)S(1)}, bf16[80,2400]{1,0:T(8,128)(2,1)S(1)}, u32[]{:S(2)}, u32[]{:S(2)}) collective-permute-start(bf16[80,2400]{1,0:T(8,128)(2,1)S(1)} %get-tuple-element.41), channel_id=1, source_target_pairs={{1,0},{2,1},{3,2},{0,3},{5,4},{6,5},{7,6},{4,7},{9,8},{10,9},{11,1... | collective-permute-start | bytes 1152008 | tf_op jit(solution)/shard_map/ppermute | solution.py:232
  32.6 5.5 %collective-permute-start.8 = (bf16[24,2400]{1,0:T(8,128)(2,1)S(1)}, bf16[24,2400]{1,0:T(8,128)(2,1)S(1)}, u32[]{:S(2)}, u32[]{:S(2)}) collective-permute-start(bf16[24,2400]{1,0:T(8,128)(2,1)S(1)} %slice.12), channel_id=1, source_target_pairs={{0,16},{16,32},{32,48},{48,64},{64,80},{80,96},{96,112},{112,0},{1... | collective-permute-start | bytes 345608 | tf_op jit(solution)/shard_map/ppermute | solution.py:261
  33.9 4.2 %collective-permute-start.9 = (bf16[16,2400]{1,0:T(8,128)(2,1)S(1)}, bf16[16,2400]{1,0:T(8,128)(2,1)S(1)}, u32[]{:S(2)}, u32[]{:S(2)}) collective-permute-start(bf16[16,2400]{1,0:T(8,128)(2,1)S(1)} %slice.13), channel_id=1, source_target_pairs={{16,0},{32,16},{48,32},{64,48},{80,64},{96,80},{112,96},{0,112},{1... | collective-permute-start | bytes 230408 | tf_op jit(solution)/shard_map/ppermute | solution.py:262
  40.7 4.3 %collective-permute-start.15 = (bf16[120,2400]{1,0:T(8,128)(2,1)S(1)}, bf16[120,2400]{1,0:T(8,128)(2,1)S(1)}, u32[]{:S(2)}, u32[]{:S(2)}) collective-permute-start(bf16[120,2400]{1,0:T(8,128)(2,1)S(1)} %pad_maximum_fusion.1.b0), channel_id=1, source_target_pairs={{0,8},{8,0},{1,9},{9,1},{2,10},{10,2},{3,11},{11,3},{4,12},{12,4},... | collective-permute-start | bytes 1728008 | tf_op jit(solution)/shard_map/ppermute | solution.py:268
  42.8 12.3 %collective-permute-start.13 = (bf16[160,2400]{1,0:T(8,128)(2,1)S(1)}, bf16[160,2400]{1,0:T(8,128)(2,1)S(1)}, u32[]{:S(2)}, u32[]{:S(2)}) collective-permute-start(bf16[160,2400]{1,0:T(8,128)(2,1)S(1)} %collective-permute-done.7.far_a), channel_id=1, source_target_pairs={{0,8},{8,0},{1,9},{9,1},{2,10},{10,2},{3,11},{11,3},{4,12},{12,4},... | collective-permute-start | bytes 2304008 | tf_op jit(solution)/shard_map/ppermute | solution.py:270
  42.9 12.2 %collective-permute-start.14 = (bf16[160,2400]{1,0:T(8,128)(2,1)S(1)}, bf16[160,2400]{1,0:T(8,128)(2,1)S(1)}, u32[]{:S(2)}, u32[]{:S(2)}) collective-permute-start(bf16[160,2400]{1,0:T(8,128)(2,1)S(1)} %pad_maximum_fusion.far_b), channel_id=1, source_target_pairs={{0,8},{8,0},{1,9},{9,1},{2,10},{10,2},{3,11},{11,3},{4,12},{12,4},... | collective-permute-start | bytes 2304008 | tf_op jit(solution)/shard_map/ppermute | solution.py:270
  46.9 16.7 %copy-start.6 = (s32[2,30]{1,0:T(2,128)S(1)}, s32[2,30]{1,0:T(2,128)}, u32[]{:S(2)}) copy-start(s32[2,30]{1,0:T(2,128)} %param.11) | copy-start | bytes 724
  46.9 7.4 %collective-permute-start.16 = (f32[2,80,160]{2,1,0:T(8,128)S(1)}, f32[2,80,160]{2,1,0:T(8,128)S(1)}, u32[]{:S(2)}, u32[]{:S(2)}) collective-permute-start(f32[2,80,160]{2,1,0:T(8,128)S(1)} %last_terms.1.t), channel_id=1, source_target_pairs={{0,128},{128,0},{1,129},{129,1},{2,130},{130,2},{3,131},{131,3},{4... | collective-permute-start | bytes 307208 | tf_op jit(solution)/shard_map/ppermute | solution.py:282
  49.9 5.2 %collective-permute-start.17 = (f32[2,80,160]{2,1,0:T(8,128)S(1)}, f32[2,80,160]{2,1,0:T(8,128)S(1)}, u32[]{:S(2)}, u32[]{:S(2)}) collective-permute-start(f32[2,80,160]{2,1,0:T(8,128)S(1)} %last_terms.1.t), channel_id=1, source_target_pairs={{0,8},{8,0},{1,9},{9,1},{2,10},{10,2},{3,11},{11,3},{4,12},{12,4},... | collective-permute-start | bytes 307208 | tf_op jit(solution)/shard_map/ppermute | solution.py:283
  54.3 1.9 %collective-permute-start.18 = (f32[2,80,160]{2,1,0:T(8,128)S(1)}, f32[2,80,160]{2,1,0:T(8,128)S(1)}, u32[]{:S(2)}, u32[]{:S(2)}) collective-permute-start(f32[2,80,160]{2,1,0:T(8,128)S(1)} %collective-permute-done.16.t_yh), channel_id=1, source_target_pairs={{0,8},{8,0},{1,9},{9,1},{2,10},{10,2},{3,11},{11,3},{4,12},{12,4},... | collective-permute-start | bytes 307208 | tf_op jit(solution)/shard_map/ppermute | solution.py:284
  58.7 14.4 %all-to-all-start = ((f32[8,48,128]{2,1,0:T(8,128)}), f32[8,48,128]{2,1,0:T(8,128)S(1)}, u32[]{:S(2)}, u32[]{:S(2)}) async-start(f32[8,48,128]{2,1,0:T(8,128)} %cluster_terms.1), calls=%async_computation | async-start | bytes 393216 | tf_op jit(solution)/shard_map/all_to_all | solution.py:297

commit v9 on v8

--- a/solution.py
+++ b/solution.py
@@ -114,10 +114,42 @@
     start = w.shape[1] - b.shape[0]
 
     def run(real, imag):
-        t_ref[0] = t_own[...] + part_of_t(b, own.at[0], own.at[1], w[0, start:, :], g[...], width)
-        t_ref[1] = t_far[...] + part_of_t(b, real, imag, w[1, start:, :], g[...], width)
+        of_own = t_own[...] + part_of_t(b, own.at[0], own.at[1], w[0, start:, :], g[...], width)
+        of_far = t_far[...] + part_of_t(b, real, imag, w[1, start:, :], g[...], width)
+        t_ref[...] = dense(of_own, of_far)
 
     either_way(far_a, far_b, run)
+
+
+def dense(own, far):
+    mid, tail = own.shape[0] // 2, own.shape[1] - 128
+    rest = [part[rows, 128:] for rows in (slice(None, mid), slice(mid, None)) for part in (own, far)]
+    assert 4 * tail == 128
+    return jnp.concatenate([own[:, :128], far[:, :128], jnp.concatenate(rest, 1)], 0)
+
+
+def spread(value):
+    rows = value.shape[0] * 2 // 5
+    rest = value[2 * rows :]
+    pairs = []
+    for at in range(2):
+        tail = [rest[:, 32 * part : 32 * (part + 1)] for part in (at, at + 2)]
+        pairs.append(jnp.concatenate([value[at * rows : (at + 1) * rows], jnp.concatenate(tail, 0)], 1))
+    return pairs
+
+
+def coded(piece, lanes):
+    largest = jnp.maximum(jnp.max(jnp.abs(piece), axis=1, keepdims=True), 1e-30)
+    exponent = jnp.floor(jnp.log2(largest)) + 1.0
+    values = jnp.floor(piece * jnp.exp2(14.0 - exponent) + 0.5)
+    rows, columns = piece.shape
+    tail = jnp.broadcast_to(exponent, (rows, lanes - columns))
+    return jnp.concatenate([values, tail], 1).astype(jnp.int32).astype(jnp.int16)
+
+
+def decoded(value):
+    value = value.astype(jnp.int32).astype(F32)
+    return value * jnp.exp2(value[:, 125:126] - 14.0)
 
 
 def packed(u, at, columns):
@@ -143,7 +175,8 @@
     shift = span % 128
     window = pl.ds(pl.multiple_of(yh * (span - shift), 128), span + shift)
     half = 4 * width
-    swap = jnp.full(t.shape[1:], odd) > 0
+    t, t_yh, t_core, t_diag = (spread(ref[...]) for ref in (t, t_yh, t_core, t_diag))
+    swap = jnp.full(t[0].shape, odd) > 0
     total = None
     for value, first, second, swapped in (
         (t[0] + t_yh[1], own.at[0], own.at[1], False),
@@ -167,14 +200,13 @@
             def _():
                 for chip in range(chips):
                     piece = packed(u_ref[...], (2 * chip + parity) * columns + row * shift, columns)
-                    spare = jnp.zeros((piece.shape[0], lanes - piece.shape[1]), F32)
-                    out[chip] = jnp.concatenate([piece, spare], 1)
+                    out[chip] = coded(piece, lanes)
 
 
 def final_kernel(arrived, mask, out):
-    total = arrived[0]
+    total = decoded(arrived[0])
     for chip in range(1, arrived.shape[0]):
-        total = total + arrived[chip]
+        total = total + decoded(arrived[chip])
     cells, width, parts, columns = out.shape
     value = unpacked(total, columns)
     for f in range(cells):
@@ -184,7 +216,7 @@
                 out[f, j, pl.ds(part, 1), :] = value[row : row + 1] * mask[pl.ds(f, 1), :]
 
 
-def call(kernel, name, shapes, specs, scratch=(), mib=16, flops=0):
+def call(kernel, name, shapes, specs, scratch=(), mib=8, flops=0):
     return pl.pallas_call(
         kernel,
         out_shape=shapes,
@@ -273,7 +305,7 @@
     t = call(
         functools.partial(last_kernel, width),
         "last_terms",
-        jax.ShapeDtypeStruct((2,) + one.shape, F32),
+        jax.ShapeDtypeStruct((20 * width // 2, 128), F32),
         [vmem] * 9,
         [pltpu.VMEM((late, functions), BF16)],
         flops=10**9,
@@ -288,7 +320,7 @@
     pieces = call(
         functools.partial(cluster_kernel, width, columns),
         "cluster_terms",
-        jax.ShapeDtypeStruct((chips, 4 * width * 3 // 5, 128), F32),
+        jax.ShapeDtypeStruct((chips, 4 * width * 3 // 5, 128), jnp.int16),
         [vmem] * 10,
         [pltpu.VMEM((4 * width, span + span % 128), F32)],
         flops=10**9,

time: 74.7 us -> 73.9 us (0.989)
  waiting for transfers between devices: 26.5 us -> 23 us
  Pallas kernels: 9.42 us -> 12 us
    pallas_call x1, Pallas kernels: 2.53 us -> 4.88 us  [shards(): call(functools.partial(cluster_kernel, width, columns), 'cluster_terms',...]
    all_to_all x1, waiting for transfers between devices: 9.41 us -> 7.32 us  [shards(): arrived = lax.all_to_all(pieces, 'z', 0, 0, tiled=True)]
    ppermute x1, waiting for transfers between devices: 3.97 us -> 2.65 us  [shards(): t_yh = lax.ppermute(t, 'yh', swap)]
  transfers between devices with their start and end apart: 20 -> 20, of which waited for: 7 -> 7; matrix products, arithmetic and copies ran while one was open for 3% -> 4% of each run, Pallas kernels for 8% -> 8%
where the time goes in v9:
time: 73.9 us; the launch traced here: 72.9 us
  starting transfers between devices  35 us (47%)
  waiting for transfers between devices  23 us (31%)
  Pallas kernels  12 us (16%)
  local copies, waits for them, and re-layouts  2.48 us (3%)
    ppermute x3, starting transfers between devices, shards(): from_above = lax.ppermute(from_above, 'z', down)  9.26 us
    all_to_all x1, waiting for transfers between devices, shards(): arrived = lax.all_to_all(pieces, 'z', 0, 0, tiled=True)  7.32 us
    ppermute x3, waiting for transfers between devices, shards(): from_below = lax.ppermute(from_below, 'z', up)  5.18 us
    pallas_call x1, Pallas kernels, shards(): call(functools.partial(cluster_kernel, width, columns), 'cluster_terms',...  4.88 us
    all_to_all x1, starting transfers between devices, shards(): arrived = lax.all_to_all(pieces, 'z', 0, 0, tiled=True)  4.88 us
    ppermute x1, waiting for transfers between devices, shards(): lax.ppermute(lax.dynamic_index_in_dim(own, odd_x(), 0, keepdims=False), '...  4.45 us
    ppermute x1, starting transfers between devices, shards(): near = lax.ppermute(own, 'core', swap)  3.24 us
    ppermute x1, starting transfers between devices, shards(): t_yh = lax.ppermute(t, 'yh', swap)  3.02 us
  transfers between devices with their start and end apart: 20, of which 7 were waited for; matrix products, arithmetic and copies ran while one was open for 4% of the time, Pallas kernels for 8%

profile of v9, /device:TPU:1, one launch (start us, length us, event | category | flops | bytes accessed | tf_op | source)
XLA Modules:
  0.0 72.9 jit_solution(7995847886743158511)
XLA Ops:
  0.0 3.2 %collective-permute-start.4 = (bf16[2,160,2400]{2,1,0:T(8,128)(2,1)}, bf16[2,160,2400]{2,1,0:T(8,128)(2,1)}, u32[]{:S(2)}, u32[]{:S(2)}) collective-permute-start(bf16[2,160,2400]{2,1,0:T(8,128)(2,1)} %bitcast.6), channel_id=1, source_target_pairs={{0,8},{8,0},{1,9},{9,1},{2,10},{10,2},{3,11},{11,3},{4,12},{12,4},... | collective-permute-start | bytes 4608008 | tf_op jit(solution)/shard_map/ppermute | solution.py:249
  3.2 1.0 %constant_dynamic-slice_fusion = bf16[1,2,20,2400]{3,2,1,0:T(8,128)(2,1)S(1)} fusion(bf16[1,2,160,2400]{3,2,1,0:T(8,128)(2,1)} %param.7, s32[]{:T(128)S(6)} %select_n.16), kind=kLoop, calls=%fused_computation.13 | loop fusion | bytes 384004 | tf_op jit(solution)/shard_map/dynamic_slice | solution.py:250
  4.4 3.9 %collective-permute-start.2 = (bf16[40,2400]{1,0:T(8,128)(2,1)S(1)}, bf16[40,2400]{1,0:T(8,128)(2,1)S(1)}, u32[]{:S(2)}, u32[]{:S(2)}) collective-permute-start(bf16[40,2400]{1,0:T(8,128)(2,1)S(1)} %reshape.19), channel_id=1, source_target_pairs={{16,0},{32,16},{48,32},{64,48},{80,64},{96,80},{112,96},{0,112},{1... | collective-permute-start | bytes 576008 | tf_op jit(solution)/shard_map/ppermute | solution.py:256
  8.3 1.2 %dynamic-slice_bitcast_fusion = bf16[160,2400]{1,0:T(8,128)(2,1)S(1)} fusion(bf16[1,2,160,2400]{3,2,1,0:T(8,128)(2,1)} %param.7, s32[]{:T(128)S(6)} %select_n.17), kind=kLoop, calls=%fused_computation.2 | loop fusion | bytes 1536004 | tf_op jit(solution)/shard_map/jit(dynamic_index_in_dim)/squeeze | solution.py:248
  9.5 3.0 %collective-permute-start.7 = (bf16[160,2400]{1,0:T(8,128)(2,1)S(1)}, bf16[160,2400]{1,0:T(8,128)(2,1)S(1)}, u32[]{:S(2)}, u32[]{:S(2)}) collective-permute-start(bf16[160,2400]{1,0:T(8,128)(2,1)S(1)} %dynamic-slice_bitcast_fusion), channel_id=1, source_target_pairs={{0,128},{128,0},{1,129},{129,1},{2,130},{130,2},{3,131},{131,3},{4... | collective-permute-start | bytes 2304008 | tf_op jit(solution)/shard_map/ppermute | solution.py:248
  12.5 0.9 %collective-permute-done = bf16[40,2400]{1,0:T(8,128)(2,1)S(1)} collective-permute-done((bf16[40,2400]{1,0:T(8,128)(2,1)S(1)}, bf16[40,2400]{1,0:T(8,128)(2,1)S(1)}, u32[]{:S(2)}, u32[]{:S(2)}) %collective-permute-start) | collective-permute-done | bytes 192032 | tf_op jit(solution)/shard_map/ppermute | solution.py:255
  13.5 2.7 %collective-permute-start.3 = (bf16[40,2400]{1,0:T(8,128)(2,1)S(1)}, bf16[40,2400]{1,0:T(8,128)(2,1)S(1)}, u32[]{:S(2)}, u32[]{:S(2)}) collective-permute-start(bf16[40,2400]{1,0:T(8,128)(2,1)S(1)} %collective-permute-done.2), channel_id=1, source_target_pairs={{16,0},{32,16},{48,32},{64,48},{80,64},{96,80},{112,96},{0,112},{1... | collective-permute-start | bytes 576008 | tf_op jit(solution)/shard_map/ppermute | solution.py:256
  16.3 4.2 %collective-permute-done.1 = bf16[40,2400]{1,0:T(8,128)(2,1)S(1)} collective-permute-done((bf16[40,2400]{1,0:T(8,128)(2,1)S(1)}, bf16[40,2400]{1,0:T(8,128)(2,1)S(1)}, u32[]{:S(2)}, u32[]{:S(2)}) %collective-permute-start.1) | collective-permute-done | bytes 192032 | tf_op jit(solution)/shard_map/ppermute | solution.py:255
  20.5 2.7 %collective-permute-start.6 = (bf16[40,2400]{1,0:T(8,128)(2,1)S(1)}, bf16[40,2400]{1,0:T(8,128)(2,1)S(1)}, u32[]{:S(2)}, u32[]{:S(2)}) collective-permute-start(bf16[40,2400]{1,0:T(8,128)(2,1)S(1)} %collective-permute-done.3), channel_id=1, source_target_pairs={{16,0},{32,16},{48,32},{64,48},{80,64},{96,80},{112,96},{0,112},{1... | collective-permute-start | bytes 576008 | tf_op jit(solution)/shard_map/ppermute | solution.py:256
  23.3 2.1 %collective-permute-start.12 = (bf16[200,2400]{1,0:T(8,128)(2,1)S(1)}, bf16[200,2400]{1,0:T(8,128)(2,1)S(1)}, u32[]{:S(2)}, u32[]{:S(2)}) collective-permute-start(bf16[200,2400]{1,0:T(8,128)(2,1)S(1)} %constant_dynamic-update-slice_fusion.b0), channel_id=1, source_target_pairs={{0,8},{8,0},{1,9},{9,1},{2,10},{10,2},{3,11},{11,3},{4,12},{12,4},... | collective-permute-start | bytes 2880008 | tf_op jit(solution)/shard_map/ppermute | solution.py:267
  25.3 4.5 %collective-permute-done.7.far_a = bf16[160,2400]{1,0:T(8,128)(2,1)S(1)} collective-permute-done((bf16[160,2400]{1,0:T(8,128)(2,1)S(1)}, bf16[160,2400]{1,0:T(8,128)(2,1)S(1)}, u32[]{:S(2)}, u32[]{:S(2)}) %collective-permute-start.7) | collective-permute-done | bytes 768032 | tf_op jit(solution)/shard_map/ppermute | solution.py:248
  29.9 1.3 %collective-permute-start.10 = (bf16[80,2400]{1,0:T(8,128)(2,1)S(1)}, bf16[80,2400]{1,0:T(8,128)(2,1)S(1)}, u32[]{:S(2)}, u32[]{:S(2)}) collective-permute-start(bf16[80,2400]{1,0:T(8,128)(2,1)S(1)} %get-tuple-element.42), channel_id=1, source_target_pairs={{0,1},{1,2},{2,3},{3,0},{4,5},{5,6},{6,7},{7,4},{8,9},{9,10},{10,1... | collective-permute-start | bytes 1152008 | tf_op jit(solution)/shard_map/ppermute | solution.py:263
  31.2 1.5 %collective-permute-start.11 = (bf16[80,2400]{1,0:T(8,128)(2,1)S(1)}, bf16[80,2400]{1,0:T(8,128)(2,1)S(1)}, u32[]{:S(2)}, u32[]{:S(2)}) collective-permute-start(bf16[80,2400]{1,0:T(8,128)(2,1)S(1)} %get-tuple-element.41), channel_id=1, source_target_pairs={{1,0},{2,1},{3,2},{0,3},{5,4},{6,5},{7,6},{4,7},{9,8},{10,9},{11,1... | collective-permute-start | bytes 1152008 | tf_op jit(solution)/shard_map/ppermute | solution.py:264
  32.8 1.1 %phases.1 = (f32[2,640,1]{2,1,0:T(8,128)S(1)}, bf16[160,400]{1,0:T(8,128)(2,1)S(1)}, bf16[160,240]{1,0:T(8,128)(2,1)S(1)}) custom-call(s32[2]{0:T(128)S(1)} %copy-done.2, s32[32,32]{1,0:T(8,128)S(1)} %copy-done.1, f32[32]{0:T(128)S(1)} %copy-done.3, f32[32]{0:T(128)S(1)} %copy-done.4, f32[32]{0:T(128)S(1)} %copy-done.5), custom_call_target="tpu_custom_call" | custom-call | bytes 1048576 | tf_op jit(solution)/shard_map/phases/pallas_call | solution.py:276
  33.9 2.7 %collective-permute-start.9 = (bf16[16,2400]{1,0:T(8,128)(2,1)S(1)}, bf16[16,2400]{1,0:T(8,128)(2,1)S(1)}, u32[]{:S(2)}, u32[]{:S(2)}) collective-permute-start(bf16[16,2400]{1,0:T(8,128)(2,1)S(1)} %slice.13), channel_id=1, source_target_pairs={{16,0},{32,16},{48,32},{64,48},{80,64},{96,80},{112,96},{0,112},{1... | collective-permute-start | bytes 230408 | tf_op jit(solution)/shard_map/ppermute | solution.py:294
  36.6 1.4 %own_first.1.t_own = f32[80,160]{1,0:T(8,128)S(1)} custom-call(bf16[2,160,2400]{2,1,0:T(8,128)(2,1)S(1)} %bitcast.7, bf16[200,2400]{1,0:T(8,128)(2,1)S(1)} %constant_dynamic-update-slice_fusion.b0, bf16[200,2400]{1,0:T(8,128)(2,1)S(1)} %collective-permute-done.12.b1, f32[2,640,1]{2,1,0:T(8,128)S(1)} %get-tuple-element.30.w, ...), custom_call_target="tpu_custom_call" | custom-call | flops 1000000000 | bytes 1048576 | tf_op jit(solution)/shard_map/own_first/pallas_call | solution.py:291
  38.1 2.5 %collective-permute-done.10 = bf16[80,2400]{1,0:T(8,128)(2,1)S(1)} collective-permute-done((bf16[80,2400]{1,0:T(8,128)(2,1)S(1)}, bf16[80,2400]{1,0:T(8,128)(2,1)S(1)}, u32[]{:S(2)}, u32[]{:S(2)}) %collective-permute-start.10) | collective-permute-done | bytes 384032 | tf_op jit(solution)/shard_map/ppermute | solution.py:263
  40.7 2.1 %collective-permute-start.15 = (bf16[120,2400]{1,0:T(8,128)(2,1)S(1)}, bf16[120,2400]{1,0:T(8,128)(2,1)S(1)}, u32[]{:S(2)}, u32[]{:S(2)}) collective-permute-start(bf16[120,2400]{1,0:T(8,128)(2,1)S(1)} %pad_maximum_fusion.1.b0), channel_id=1, source_target_pairs={{0,8},{8,0},{1,9},{9,1},{2,10},{10,2},{3,11},{11,3},{4,12},{12,4},... | collective-permute-start | bytes 1728008 | tf_op jit(solution)/shard_map/ppermute | solution.py:300
  42.8 0.1 collective-permute-start.13
  42.9 0.4 collective-permute-start.14
  43.3 1.6 %far_first.1.t_far = f32[80,160]{1,0:T(8,128)S(1)} custom-call(bf16[160,2400]{1,0:T(8,128)(2,1)S(1)} %collective-permute-done.7.far_a, bf16[160,2400]{1,0:T(8,128)(2,1)S(1)} %pad_maximum_fusion.far_b, bf16[200,2400]{1,0:T(8,128)(2,1)S(1)} %constant_dynamic-update-slice_fusion.b0, bf16[200,2400]{1,0:T(8,128)(2,1)S(1)} %collective-permute-done.12.b1, ...), custom_call_target="tpu_custom_call" | custom-call | flops 1000000000 | bytes 1048576 | tf_op jit(solution)/shard_map/far_first/pallas_call | solution.py:304
  45.0 2.0 %last_terms.1.t = f32[200,128]{1,0:T(8,128)S(1)} custom-call(bf16[2,160,2400]{2,1,0:T(8,128)(2,1)S(1)} %bitcast.8, bf16[160,2400]{1,0:T(8,128)(2,1)S(1)} %collective-permute-done.7.far_a, bf16[160,2400]{1,0:T(8,128)(2,1)S(1)} %pad_maximum_fusion.far_b, bf16[120,2400]{1,0:T(8,128)(2,1)S(1)} %pad_maximum_fusion.1.b0, ...), custom_call_target="tpu_custom_call" | custom-call | flops 1000000000 | bytes 1048576 | tf_op jit(solution)/shard_map/last_terms/pallas_call | solution.py:305
  47.0 3.0 %collective-permute-start.16 = (f32[200,128]{1,0:T(8,128)S(1)}, f32[200,128]{1,0:T(8,128)S(1)}, u32[]{:S(2)}, u32[]{:S(2)}) collective-permute-start(f32[200,128]{1,0:T(8,128)S(1)} %last_terms.1.t), channel_id=1, source_target_pairs={{0,128},{128,0},{1,129},{129,1},{2,130},{130,2},{3,131},{131,3},{4... | collective-permute-start | bytes 307208 | tf_op jit(solution)/shard_map/ppermute | solution.py:314
  50.0 0.4 collective-permute-start.17
  50.3 2.7 %collective-permute-done.16.t_yh = f32[200,128]{1,0:T(8,128)S(1)} collective-permute-done((f32[200,128]{1,0:T(8,128)S(1)}, f32[200,128]{1,0:T(8,128)S(1)}, u32[]{:S(2)}, u32[]{:S(2)}) %collective-permute-start.16) | collective-permute-done | bytes 102432 | tf_op jit(solution)/shard_map/ppermute | solution.py:314
  53.0 0.9 %collective-permute-start.18 = (f32[200,128]{1,0:T(8,128)S(1)}, f32[200,128]{1,0:T(8,128)S(1)}, u32[]{:S(2)}, u32[]{:S(2)}) collective-permute-start(f32[200,128]{1,0:T(8,128)S(1)} %collective-permute-done.16.t_yh), channel_id=1, source_target_pairs={{0,8},{8,0},{1,9},{9,1},{2,10},{10,2},{3,11},{11,3},{4,12},{12,4},... | collective-permute-start | bytes 307208 | tf_op jit(solution)/shard_map/ppermute | solution.py:316
  53.9 0.9 %collective-permute-done.18.t_diag = f32[200,128]{1,0:T(8,128)S(1)} collective-permute-done((f32[200,128]{1,0:T(8,128)S(1)}, f32[200,128]{1,0:T(8,128)S(1)}, u32[]{:S(2)}, u32[]{:S(2)}) %collective-permute-start.18) | collective-permute-done | bytes 102432 | tf_op jit(solution)/shard_map/ppermute | solution.py:316
  54.8 4.9 %cluster_terms.1 = s16[8,48,128]{2,1,0:T(8,128)(2,1)} custom-call(bf16[2,160,2400]{2,1,0:T(8,128)(2,1)S(1)} %bitcast.9, bf16[2,160,2400]{2,1,0:T(8,128)(2,1)} %collective-permute-done.4.near, bf16[160,2400]{1,0:T(8,128)(2,1)S(1)} %collective-permute-done.7.far_a, bf16[160,2400]{1,0:T(8,128)(2,1)S(1)} %pad_maximum_fusion.far_b, ...), custom_call_target="tpu_custom_call" | custom-call | flops 1000000000 | bytes 1048576 | tf_op jit(solution)/shard_map/cluster_terms/pallas_call | solution.py:320
  59.7 4.9 %all-to-all-start = ((s16[8,48,128]{2,1,0:T(8,128)(2,1)}), s16[8,48,128]{2,1,0:T(8,128)(2,1)S(1)}, u32[]{:S(2)}, u32[]{:S(2)}) async-start(s16[8,48,128]{2,1,0:T(8,128)(2,1)} %cluster_terms.1), calls=%async_computation | async-start | bytes 196608 | tf_op jit(solution)/shard_map/all_to_all | solution.py:329
  64.6 0.1 convolution_bitcast_fusion.mask
  64.7 7.3 %all-to-all-done.arrived = s16[8,48,128]{2,1,0:T(8,128)(2,1)S(1)} async-done(((s16[8,48,128]{2,1,0:T(8,128)(2,1)}), s16[8,48,128]{2,1,0:T(8,128)(2,1)S(1)}, u32[]{:S(2)}, u32[]{:S(2)}) %all-to-all-start) | async-done | bytes 98336 | tf_op jit(solution)/shard_map/all_to_all | solution.py:329
  72.0 0.9 %sum_and_mask.1 = f32[2,20,2,75]{3,2,1,0:T(2,128)} custom-call(s16[8,48,128]{2,1,0:T(8,128)(2,1)S(1)} %all-to-all-done.arrived, f32[2,75]{1,0:T(2,128)S(1)} %convolution_bitcast_fusion.mask), custom_call_target="tpu_custom_call" | custom-call | bytes 1048576 | tf_op jit(solution)/shard_map/sum_and_mask/pallas_call | solution.py:336
  (43 shorter events, 0.6 us)
Async XLA Ops:
  0.0 20.5 %collective-permute-start.4 = (bf16[2,160,2400]{2,1,0:T(8,128)(2,1)}, bf16[2,160,2400]{2,1,0:T(8,128)(2,1)}, u32[]{:S(2)}, u32[]{:S(2)}) collective-permute-start(bf16[2,160,2400]{2,1,0:T(8,128)(2,1)} %bitcast.6), channel_id=1, source_target_pairs={{0,8},{8,0},{1,9},{9,1},{2,10},{10,2},{3,11},{11,3},{4,12},{12,4},... | collective-permute-start | bytes 4608008 | tf_op jit(solution)/shard_map/ppermute | solution.py:249
  4.3 9.1 %collective-permute-start = (bf16[40,2400]{1,0:T(8,128)(2,1)S(1)}, bf16[40,2400]{1,0:T(8,128)(2,1)S(1)}, u32[]{:S(2)}, u32[]{:S(2)}) collective-permute-start(bf16[40,2400]{1,0:T(8,128)(2,1)S(1)} %reshape.19), channel_id=1, source_target_pairs={{0,16},{16,32},{32,48},{48,64},{64,80},{80,96},{96,112},{112,0},{1... | collective-permute-start | bytes 576008 | tf_op jit(solution)/shard_map/ppermute | solution.py:255
  4.4 9.1 %collective-permute-start.2 = (bf16[40,2400]{1,0:T(8,128)(2,1)S(1)}, bf16[40,2400]{1,0:T(8,128)(2,1)S(1)}, u32[]{:S(2)}, u32[]{:S(2)}) collective-permute-start(bf16[40,2400]{1,0:T(8,128)(2,1)S(1)} %reshape.19), channel_id=1, source_target_pairs={{16,0},{32,16},{48,32},{64,48},{80,64},{96,80},{112,96},{0,112},{1... | collective-permute-start | bytes 576008 | tf_op jit(solution)/shard_map/ppermute | solution.py:256
  9.5 20.3 %collective-permute-start.7 = (bf16[160,2400]{1,0:T(8,128)(2,1)S(1)}, bf16[160,2400]{1,0:T(8,128)(2,1)S(1)}, u32[]{:S(2)}, u32[]{:S(2)}) collective-permute-start(bf16[160,2400]{1,0:T(8,128)(2,1)S(1)} %dynamic-slice_bitcast_fusion), channel_id=1, source_target_pairs={{0,128},{128,0},{1,129},{129,1},{2,130},{130,2},{3,131},{131,3},{4... | collective-permute-start | bytes 2304008 | tf_op jit(solution)/shard_map/ppermute | solution.py:248
  13.5 7.0 %collective-permute-start.1 = (bf16[40,2400]{1,0:T(8,128)(2,1)S(1)}, bf16[40,2400]{1,0:T(8,128)(2,1)S(1)}, u32[]{:S(2)}, u32[]{:S(2)}) collective-permute-start(bf16[40,2400]{1,0:T(8,128)(2,1)S(1)} %collective-permute-done), channel_id=1, source_target_pairs={{0,16},{16,32},{32,48},{48,64},{64,80},{80,96},{96,112},{112,0},{1... | collective-permute-start | bytes 576008 | tf_op jit(solution)/shard_map/ppermute | solution.py:255
  13.5 7.0 %collective-permute-start.3 = (bf16[40,2400]{1,0:T(8,128)(2,1)S(1)}, bf16[40,2400]{1,0:T(8,128)(2,1)S(1)}, u32[]{:S(2)}, u32[]{:S(2)}) collective-permute-start(bf16[40,2400]{1,0:T(8,128)(2,1)S(1)} %collective-permute-done.2), channel_id=1, source_target_pairs={{16,0},{32,16},{48,32},{64,48},{80,64},{96,80},{112,96},{0,112},{1... | collective-permute-start | bytes 576008 | tf_op jit(solution)/shard_map/ppermute | solution.py:256
  16.2 16.5 %copy-start.1 = (s32[32,32]{1,0:T(8,128)S(1)}, s32[32,32]{1,0:T(8,128)}, u32[]{:S(2)}) copy-start(s32[32,32]{1,0:T(8,128)} %diff_class.1) | copy-start | bytes 12292
  16.2 16.5 %copy-start.2 = (s32[2]{0:T(128)S(1)}, s32[2]{0:T(128)}, u32[]{:S(2)}) copy-start(s32[2]{0:T(128)} %cells) | copy-start | bytes 28
  16.2 16.5 %copy-start.3 = (f32[32]{0:T(128)S(1)}, f32[32]{0:T(128)}, u32[]{:S(2)}) copy-start(f32[32]{0:T(128)} %class_weight.1) | copy-start | bytes 388
  16.2 16.5 %copy-start.4 = (f32[32]{0:T(128)S(1)}, f32[32]{0:T(128)}, u32[]{:S(2)}) copy-start(f32[32]{0:T(128)} %constant.55.clone.cos_table) | copy-start | bytes 388
  16.2 16.5 %copy-start.5 = (f32[32]{0:T(128)S(1)}, f32[32]{0:T(128)}, u32[]{:S(2)}) copy-start(f32[32]{0:T(128)} %constant.56.clone.sin_table) | copy-start | bytes 388
  16.2 20.4 %copy-start = (bf16[1,2,160,2400]{3,2,1,0:T(8,128)(2,1)S(1)}, bf16[1,2,160,2400]{3,2,1,0:T(8,128)(2,1)}, u32[]{:S(2)}) copy-start(bf16[1,2,160,2400]{3,2,1,0:T(8,128)(2,1)} %param.7) | copy-start | bytes 4608004
  20.5 9.3 %collective-permute-start.5 = (bf16[40,2400]{1,0:T(8,128)(2,1)S(1)}, bf16[40,2400]{1,0:T(8,128)(2,1)S(1)}, u32[]{:S(2)}, u32[]{:S(2)}) collective-permute-start(bf16[40,2400]{1,0:T(8,128)(2,1)S(1)} %collective-permute-done.1), channel_id=1, source_target_pairs={{0,16},{16,32},{32,48},{48,64},{64,80},{80,96},{96,112},{112,0},{1... | collective-permute-start | bytes 576008 | tf_op jit(solution)/shard_map/ppermute | solution.py:255
  20.5 9.3 %collective-permute-start.6 = (bf16[40,2400]{1,0:T(8,128)(2,1)S(1)}, bf16[40,2400]{1,0:T(8,128)(2,1)S(1)}, u32[]{:S(2)}, u32[]{:S(2)}) collective-permute-start(bf16[40,2400]{1,0:T(8,128)(2,1)S(1)} %collective-permute-done.3), channel_id=1, source_target_pairs={{16,0},{32,16},{48,32},{64,48},{80,64},{96,80},{112,96},{0,112},{1... | collective-permute-start | bytes 576008 | tf_op jit(solution)/shard_map/ppermute | solution.py:256
  23.3 13.4 %collective-permute-start.12 = (bf16[200,2400]{1,0:T(8,128)(2,1)S(1)}, bf16[200,2400]{1,0:T(8,128)(2,1)S(1)}, u32[]{:S(2)}, u32[]{:S(2)}) collective-permute-start(bf16[200,2400]{1,0:T(8,128)(2,1)S(1)} %constant_dynamic-update-slice_fusion.b0), channel_id=1, source_target_pairs={{0,8},{8,0},{1,9},{9,1},{2,10},{10,2},{3,11},{11,3},{4,12},{12,4},... | collective-permute-start | bytes 2880008 | tf_op jit(solution)/shard_map/ppermute | solution.py:267
  29.9 10.7 %collective-permute-start.10 = (bf16[80,2400]{1,0:T(8,128)(2,1)S(1)}, bf16[80,2400]{1,0:T(8,128)(2,1)S(1)}, u32[]{:S(2)}, u32[]{:S(2)}) collective-permute-start(bf16[80,2400]{1,0:T(8,128)(2,1)S(1)} %get-tuple-element.42), channel_id=1, source_target_pairs={{0,1},{1,2},{2,3},{3,0},{4,5},{5,6},{6,7},{7,4},{8,9},{9,10},{10,1... | collective-permute-start | bytes 1152008 | tf_op jit(solution)/shard_map/ppermute | solution.py:263
  31.2 9.4 %collective-permute-start.11 = (bf16[80,2400]{1,0:T(8,128)(2,1)S(1)}, bf16[80,2400]{1,0:T(8,128)(2,1)S(1)}, u32[]{:S(2)}, u32[]{:S(2)}) collective-permute-start(bf16[80,2400]{1,0:T(8,128)(2,1)S(1)} %get-tuple-element.41), channel_id=1, source_target_pairs={{1,0},{2,1},{3,2},{0,3},{5,4},{6,5},{7,6},{4,7},{9,8},{10,9},{11,1... | collective-permute-start | bytes 1152008 | tf_op jit(solution)/shard_map/ppermute | solution.py:264
  32.6 5.5 %collective-permute-start.8 = (bf16[24,2400]{1,0:T(8,128)(2,1)S(1)}, bf16[24,2400]{1,0:T(8,128)(2,1)S(1)}, u32[]{:S(2)}, u32[]{:S(2)}) collective-permute-start(bf16[24,2400]{1,0:T(8,128)(2,1)S(1)} %slice.12), channel_id=1, source_target_pairs={{0,16},{16,32},{32,48},{48,64},{64,80},{80,96},{96,112},{112,0},{1... | collective-permute-start | bytes 345608 | tf_op jit(solution)/shard_map/ppermute | solution.py:293
  33.9 4.2 %collective-permute-start.9 = (bf16[16,2400]{1,0:T(8,128)(2,1)S(1)}, bf16[16,2400]{1,0:T(8,128)(2,1)S(1)}, u32[]{:S(2)}, u32[]{:S(2)}) collective-permute-start(bf16[16,2400]{1,0:T(8,128)(2,1)S(1)} %slice.13), channel_id=1, source_target_pairs={{16,0},{32,16},{48,32},{64,48},{80,64},{96,80},{112,96},{0,112},{1... | collective-permute-start | bytes 230408 | tf_op jit(solution)/shard_map/ppermute | solution.py:294
  40.7 4.3 %collective-permute-start.15 = (bf16[120,2400]{1,0:T(8,128)(2,1)S(1)}, bf16[120,2400]{1,0:T(8,128)(2,1)S(1)}, u32[]{:S(2)}, u32[]{:S(2)}) collective-permute-start(bf16[120,2400]{1,0:T(8,128)(2,1)S(1)} %pad_maximum_fusion.1.b0), channel_id=1, source_target_pairs={{0,8},{8,0},{1,9},{9,1},{2,10},{10,2},{3,11},{11,3},{4,12},{12,4},... | collective-permute-start | bytes 1728008 | tf_op jit(solution)/shard_map/ppermute | solution.py:300
  42.8 11.1 %collective-permute-start.13 = (bf16[160,2400]{1,0:T(8,128)(2,1)S(1)}, bf16[160,2400]{1,0:T(8,128)(2,1)}, u32[]{:S(2)}, u32[]{:S(2)}) collective-permute-start(bf16[160,2400]{1,0:T(8,128)(2,1)S(1)} %collective-permute-done.7.far_a), channel_id=1, source_target_pairs={{0,8},{8,0},{1,9},{9,1},{2,10},{10,2},{3,11},{11,3},{4,12},{12,4},... | collective-permute-start | bytes 2304008 | tf_op jit(solution)/shard_map/ppermute | solution.py:302
  42.9 11.0 %collective-permute-start.14 = (bf16[160,2400]{1,0:T(8,128)(2,1)S(1)}, bf16[160,2400]{1,0:T(8,128)(2,1)}, u32[]{:S(2)}, u32[]{:S(2)}) collective-permute-start(bf16[160,2400]{1,0:T(8,128)(2,1)S(1)} %pad_maximum_fusion.far_b), channel_id=1, source_target_pairs={{0,8},{8,0},{1,9},{9,1},{2,10},{10,2},{3,11},{11,3},{4,12},{12,4},... | collective-permute-start | bytes 2304008 | tf_op jit(solution)/shard_map/ppermute | solution.py:302
  47.0 6.0 %collective-permute-start.16 = (f32[200,128]{1,0:T(8,128)S(1)}, f32[200,128]{1,0:T(8,128)S(1)}, u32[]{:S(2)}, u32[]{:S(2)}) collective-permute-start(f32[200,128]{1,0:T(8,128)S(1)} %last_terms.1.t), channel_id=1, source_target_pairs={{0,128},{128,0},{1,129},{129,1},{2,130},{130,2},{3,131},{131,3},{4... | collective-permute-start | bytes 307208 | tf_op jit(solution)/shard_map/ppermute | solution.py:314
  50.0 3.9 %collective-permute-start.17 = (f32[200,128]{1,0:T(8,128)S(1)}, f32[200,128]{1,0:T(8,128)S(1)}, u32[]{:S(2)}, u32[]{:S(2)}) collective-permute-start(f32[200,128]{1,0:T(8,128)S(1)} %last_terms.1.t), channel_id=1, source_target_pairs={{0,8},{8,0},{1,9},{9,1},{2,10},{10,2},{3,11},{11,3},{4,12},{12,4},... | collective-permute-start | bytes 307208 | tf_op jit(solution)/shard_map/ppermute | solution.py:315
  53.0 1.8 %collective-permute-start.18 = (f32[200,128]{1,0:T(8,128)S(1)}, f32[200,128]{1,0:T(8,128)S(1)}, u32[]{:S(2)}, u32[]{:S(2)}) collective-permute-start(f32[200,128]{1,0:T(8,128)S(1)} %collective-permute-done.16.t_yh), channel_id=1, source_target_pairs={{0,8},{8,0},{1,9},{9,1},{2,10},{10,2},{3,11},{11,3},{4,12},{12,4},... | collective-permute-start | bytes 307208 | tf_op jit(solution)/shard_map/ppermute | solution.py:316
  53.9 10.7 %copy-start.6 = (s32[2,30]{1,0:T(2,128)S(1)}, s32[2,30]{1,0:T(2,128)}, u32[]{:S(2)}) copy-start(s32[2,30]{1,0:T(2,128)} %param.11) | copy-start | bytes 724
  59.7 12.3 %all-to-all-start = ((s16[8,48,128]{2,1,0:T(8,128)(2,1)}), s16[8,48,128]{2,1,0:T(8,128)(2,1)S(1)}, u32[]{:S(2)}, u32[]{:S(2)}) async-start(s16[8,48,128]{2,1,0:T(8,128)(2,1)} %cluster_terms.1), calls=%async_computation | async-start | bytes 196608 | tf_op jit(solution)/shard_map/all_to_all | solution.py:329

commit v10 on v9

--- a/solution.py
+++ b/solution.py
@@ -167,10 +167,15 @@
 
 
 def cluster_kernel(
-    width, columns, own, near, far_a, far_b, diag_a, diag_b, t, t_yh, t_core, t_diag, out, u_ref
+    width, columns, own, far_a, far_b, near_hbm, diag_a_hbm, diag_b_hbm, t, t_yh, t_core, t_diag, out,
+    u_ref, near, diag_a, diag_b, sems
 ):
+    fetches = []
+    for at, (source, target) in enumerate(((near_hbm, near), (diag_a_hbm, diag_a), (diag_b_hbm, diag_b))):
+        fetches.append(pltpu.make_async_copy(source, target, sems.at[at]))
+        fetches[-1].start()
     yh, core, odd = lax.axis_index("yh"), lax.axis_index("core"), odd_x()
-    chips, _, lanes = out.shape
+    chips, lanes = PARTS[1], out.shape[1]
     span = 2 * chips * columns
     shift = span % 128
     window = pl.ds(pl.multiple_of(yh * (span - shift), 128), span + shift)
@@ -178,12 +183,14 @@
     t, t_yh, t_core, t_diag = (spread(ref[...]) for ref in (t, t_yh, t_core, t_diag))
     swap = jnp.full(t[0].shape, odd) > 0
     total = None
-    for value, first, second, swapped in (
-        (t[0] + t_yh[1], own.at[0], own.at[1], False),
-        (t_core[0] + t_diag[1], near.at[0], near.at[1], False),
-        (t[1] + t_yh[0], far_a, far_b, True),
-        (t_core[1] + t_diag[0], diag_a, diag_b, True),
+    for value, first, second, swapped, waits in (
+        (t[0] + t_yh[1], own.at[0], own.at[1], False, []),
+        (t[1] + t_yh[0], far_a, far_b, True, []),
+        (t_core[0] + t_diag[1], near.at[0], near.at[1], False, fetches[:1]),
+        (t_core[1] + t_diag[0], diag_a, diag_b, True, fetches[1:]),
     ):
+        for fetch in waits:
+            fetch.wait()
         partner = turned(value, width, -1)
         if swapped:
             value, partner = jnp.where(swap, partner, value), jnp.where(swap, value, partner)
@@ -198,9 +205,9 @@
 
             @pl.when((yh == row) & (core == parity))
             def _():
-                for chip in range(chips):
-                    piece = packed(u_ref[...], (2 * chip + parity) * columns + row * shift, columns)
-                    out[chip] = coded(piece, lanes)
+                starts = [(2 * chip + parity) * columns + row * shift for chip in range(chips)]
+                pieces = [packed(u_ref[...], at, columns) for at in starts]
+                out[...] = coded(jnp.concatenate(pieces, 0), lanes)
 
 
 def final_kernel(arrived, mask, out):
@@ -317,15 +324,24 @@
     chips = PARTS[1]
     columns = functions // kpoint_count
     span = 2 * chips * columns
+    rows = 4 * width * 3 // 5
     pieces = call(
         functools.partial(cluster_kernel, width, columns),
         "cluster_terms",
-        jax.ShapeDtypeStruct((chips, 4 * width * 3 // 5, 128), jnp.int16),
-        [vmem] * 10,
-        [pltpu.VMEM((4 * width, span + span % 128), F32)],
+        jax.ShapeDtypeStruct((chips * rows, 128), jnp.int16),
+        [vmem] * 3 + [pl.ANY] * 3 + [vmem] * 4,
+        [
+            pltpu.VMEM((4 * width, span + span % 128), F32),
+            pltpu.VMEM(own.shape, BF16),
+            pltpu.VMEM(far_a.shape, BF16),
+            pltpu.VMEM(far_a.shape, BF16),
+            pltpu.SemaphoreType.DMA((3,)),
+        ],
+        mib=12,
         flops=10**9,
-    )(own, near, far_a, far_b, diag_a, diag_b, t, t_yh, t_core, t_diag)
-
+    )(own, far_a, far_b, near, diag_a, diag_b, t, t_yh, t_core, t_diag)
+
+    pieces = pieces.reshape(chips, rows, 128)
     arrived = lax.all_to_all(pieces, "z", 0, 0, tiled=True)
     index = (yh * PARTS[1] + z) * 2 + core
     block_size = functions // block_pattern.shape[1]

time: 73.9 us -> 73.3 us (level)
  transfers between devices with their start and end apart: 20 -> 20, of which waited for: 7 -> 7; matrix products, arithmetic and copies ran while one was open for 4% -> 4% of each run, Pallas kernels for 8% -> 9%
where the time goes in v10:
time: 73.3 us; the launch traced here: 72.3 us
  starting transfers between devices  35 us (48%)
  waiting for transfers between devices  23 us (31%)
  Pallas kernels  11.3 us (15%)
  local copies, waits for them, and re-layouts  2.48 us (3%)
    ppermute x3, starting transfers between devices, shards(): from_above = lax.ppermute(from_above, 'z', down)  9.26 us
    all_to_all x1, waiting for transfers between devices, shards(): arrived = lax.all_to_all(pieces, 'z', 0, 0, tiled=True)  7.32 us
    ppermute x3, waiting for transfers between devices, shards(): from_below = lax.ppermute(from_below, 'z', up)  5.18 us
    all_to_all x1, starting transfers between devices, shards(): arrived = lax.all_to_all(pieces, 'z', 0, 0, tiled=True)  4.9 us
    ppermute x1, waiting for transfers between devices, shards(): lax.ppermute(lax.dynamic_index_in_dim(own, odd_x(), 0, keepdims=False), '...  4.45 us
    pallas_call x1, Pallas kernels, shards(): call(functools.partial(cluster_kernel, width, columns), 'cluster_terms',...  4.25 us
    ppermute x1, starting transfers between devices, shards(): near = lax.ppermute(own, 'core', swap)  3.24 us
    ppermute x1, starting transfers between devices, shards(): t_yh = lax.ppermute(t, 'yh', swap)  3.02 us
  transfers between devices with their start and end apart: 20, of which 7 were waited for; matrix products, arithmetic and copies ran while one was open for 4% of the time, Pallas kernels for 9%

profile of v10, /device:TPU:1, one launch (start us, length us, event | category | flops | bytes accessed | tf_op | source)
XLA Modules:
  0.0 72.3 jit_solution(2515405994364170512)
XLA Ops:
  0.0 3.2 %collective-permute-start.4 = (bf16[2,160,2400]{2,1,0:T(8,128)(2,1)}, bf16[2,160,2400]{2,1,0:T(8,128)(2,1)}, u32[]{:S(2)}, u32[]{:S(2)}) collective-permute-start(bf16[2,160,2400]{2,1,0:T(8,128)(2,1)} %bitcast.7), channel_id=1, source_target_pairs={{0,8},{8,0},{1,9},{9,1},{2,10},{10,2},{3,11},{11,3},{4,12},{12,4},... | collective-permute-start | bytes 4608008 | tf_op jit(solution)/shard_map/ppermute | solution.py:256
  3.2 1.0 %constant_dynamic-slice_fusion = bf16[1,2,20,2400]{3,2,1,0:T(8,128)(2,1)S(1)} fusion(bf16[1,2,160,2400]{3,2,1,0:T(8,128)(2,1)} %param.7, s32[]{:T(128)S(6)} %select_n.16), kind=kLoop, calls=%fused_computation.13 | loop fusion | bytes 384004 | tf_op jit(solution)/shard_map/dynamic_slice | solution.py:257
  4.4 3.9 %collective-permute-start.2 = (bf16[40,2400]{1,0:T(8,128)(2,1)S(1)}, bf16[40,2400]{1,0:T(8,128)(2,1)S(1)}, u32[]{:S(2)}, u32[]{:S(2)}) collective-permute-start(bf16[40,2400]{1,0:T(8,128)(2,1)S(1)} %reshape.22), channel_id=1, source_target_pairs={{16,0},{32,16},{48,32},{64,48},{80,64},{96,80},{112,96},{0,112},{1... | collective-permute-start | bytes 576008 | tf_op jit(solution)/shard_map/ppermute | solution.py:263
  8.3 1.2 %dynamic-slice_bitcast_fusion = bf16[160,2400]{1,0:T(8,128)(2,1)S(1)} fusion(bf16[1,2,160,2400]{3,2,1,0:T(8,128)(2,1)} %param.7, s32[]{:T(128)S(6)} %select_n.17), kind=kLoop, calls=%fused_computation.2 | loop fusion | bytes 1536004 | tf_op jit(solution)/shard_map/jit(dynamic_index_in_dim)/squeeze | solution.py:255
  9.5 3.0 %collective-permute-start.7 = (bf16[160,2400]{1,0:T(8,128)(2,1)S(1)}, bf16[160,2400]{1,0:T(8,128)(2,1)S(1)}, u32[]{:S(2)}, u32[]{:S(2)}) collective-permute-start(bf16[160,2400]{1,0:T(8,128)(2,1)S(1)} %dynamic-slice_bitcast_fusion), channel_id=1, source_target_pairs={{0,128},{128,0},{1,129},{129,1},{2,130},{130,2},{3,131},{131,3},{4... | collective-permute-start | bytes 2304008 | tf_op jit(solution)/shard_map/ppermute | solution.py:255
  12.5 0.9 %collective-permute-done = bf16[40,2400]{1,0:T(8,128)(2,1)S(1)} collective-permute-done((bf16[40,2400]{1,0:T(8,128)(2,1)S(1)}, bf16[40,2400]{1,0:T(8,128)(2,1)S(1)}, u32[]{:S(2)}, u32[]{:S(2)}) %collective-permute-start) | collective-permute-done | bytes 192032 | tf_op jit(solution)/shard_map/ppermute | solution.py:262
  13.5 2.7 %collective-permute-start.3 = (bf16[40,2400]{1,0:T(8,128)(2,1)S(1)}, bf16[40,2400]{1,0:T(8,128)(2,1)S(1)}, u32[]{:S(2)}, u32[]{:S(2)}) collective-permute-start(bf16[40,2400]{1,0:T(8,128)(2,1)S(1)} %collective-permute-done.2), channel_id=1, source_target_pairs={{16,0},{32,16},{48,32},{64,48},{80,64},{96,80},{112,96},{0,112},{1... | collective-permute-start | bytes 576008 | tf_op jit(solution)/shard_map/ppermute | solution.py:263
  16.3 4.2 %collective-permute-done.1 = bf16[40,2400]{1,0:T(8,128)(2,1)S(1)} collective-permute-done((bf16[40,2400]{1,0:T(8,128)(2,1)S(1)}, bf16[40,2400]{1,0:T(8,128)(2,1)S(1)}, u32[]{:S(2)}, u32[]{:S(2)}) %collective-permute-start.1) | collective-permute-done | bytes 192032 | tf_op jit(solution)/shard_map/ppermute | solution.py:262
  20.5 2.7 %collective-permute-start.6 = (bf16[40,2400]{1,0:T(8,128)(2,1)S(1)}, bf16[40,2400]{1,0:T(8,128)(2,1)S(1)}, u32[]{:S(2)}, u32[]{:S(2)}) collective-permute-start(bf16[40,2400]{1,0:T(8,128)(2,1)S(1)} %collective-permute-done.3), channel_id=1, source_target_pairs={{16,0},{32,16},{48,32},{64,48},{80,64},{96,80},{112,96},{0,112},{1... | collective-permute-start | bytes 576008 | tf_op jit(solution)/shard_map/ppermute | solution.py:263
  23.3 2.1 %collective-permute-start.12 = (bf16[200,2400]{1,0:T(8,128)(2,1)S(1)}, bf16[200,2400]{1,0:T(8,128)(2,1)S(1)}, u32[]{:S(2)}, u32[]{:S(2)}) collective-permute-start(bf16[200,2400]{1,0:T(8,128)(2,1)S(1)} %constant_dynamic-update-slice_fusion.b0), channel_id=1, source_target_pairs={{0,8},{8,0},{1,9},{9,1},{2,10},{10,2},{3,11},{11,3},{4,12},{12,4},... | collective-permute-start | bytes 2880008 | tf_op jit(solution)/shard_map/ppermute | solution.py:274
  25.3 4.5 %collective-permute-done.7.far_a = bf16[160,2400]{1,0:T(8,128)(2,1)S(1)} collective-permute-done((bf16[160,2400]{1,0:T(8,128)(2,1)S(1)}, bf16[160,2400]{1,0:T(8,128)(2,1)S(1)}, u32[]{:S(2)}, u32[]{:S(2)}) %collective-permute-start.7) | collective-permute-done | bytes 768032 | tf_op jit(solution)/shard_map/ppermute | solution.py:255
  29.9 1.3 %collective-permute-start.10 = (bf16[80,2400]{1,0:T(8,128)(2,1)S(1)}, bf16[80,2400]{1,0:T(8,128)(2,1)S(1)}, u32[]{:S(2)}, u32[]{:S(2)}) collective-permute-start(bf16[80,2400]{1,0:T(8,128)(2,1)S(1)} %get-tuple-element.42), channel_id=1, source_target_pairs={{0,1},{1,2},{2,3},{3,0},{4,5},{5,6},{6,7},{7,4},{8,9},{9,10},{10,1... | collective-permute-start | bytes 1152008 | tf_op jit(solution)/shard_map/ppermute | solution.py:270
  31.2 1.5 %collective-permute-start.11 = (bf16[80,2400]{1,0:T(8,128)(2,1)S(1)}, bf16[80,2400]{1,0:T(8,128)(2,1)S(1)}, u32[]{:S(2)}, u32[]{:S(2)}) collective-permute-start(bf16[80,2400]{1,0:T(8,128)(2,1)S(1)} %get-tuple-element.41), channel_id=1, source_target_pairs={{1,0},{2,1},{3,2},{0,3},{5,4},{6,5},{7,6},{4,7},{9,8},{10,9},{11,1... | collective-permute-start | bytes 1152008 | tf_op jit(solution)/shard_map/ppermute | solution.py:271
  32.8 1.1 %phases.1 = (f32[2,640,1]{2,1,0:T(8,128)S(1)}, bf16[160,400]{1,0:T(8,128)(2,1)S(1)}, bf16[160,240]{1,0:T(8,128)(2,1)S(1)}) custom-call(s32[2]{0:T(128)S(1)} %copy-done.2, s32[32,32]{1,0:T(8,128)S(1)} %copy-done.1, f32[32]{0:T(128)S(1)} %copy-done.3, f32[32]{0:T(128)S(1)} %copy-done.4, f32[32]{0:T(128)S(1)} %copy-done.5), custom_call_target="tpu_custom_call" | custom-call | bytes 1048576 | tf_op jit(solution)/shard_map/phases/pallas_call | solution.py:283
  33.9 2.7 %collective-permute-start.9 = (bf16[16,2400]{1,0:T(8,128)(2,1)S(1)}, bf16[16,2400]{1,0:T(8,128)(2,1)S(1)}, u32[]{:S(2)}, u32[]{:S(2)}) collective-permute-start(bf16[16,2400]{1,0:T(8,128)(2,1)S(1)} %slice.13), channel_id=1, source_target_pairs={{16,0},{32,16},{48,32},{64,48},{80,64},{96,80},{112,96},{0,112},{1... | collective-permute-start | bytes 230408 | tf_op jit(solution)/shard_map/ppermute | solution.py:301
  36.6 1.4 %own_first.1.t_own = f32[80,160]{1,0:T(8,128)S(1)} custom-call(bf16[2,160,2400]{2,1,0:T(8,128)(2,1)S(1)} %bitcast.8, bf16[200,2400]{1,0:T(8,128)(2,1)S(1)} %constant_dynamic-update-slice_fusion.b0, bf16[200,2400]{1,0:T(8,128)(2,1)S(1)} %collective-permute-done.12.b1, f32[2,640,1]{2,1,0:T(8,128)S(1)} %get-tuple-element.29.w, ...), custom_call_target="tpu_custom_call" | custom-call | flops 1000000000 | bytes 1048576 | tf_op jit(solution)/shard_map/own_first/pallas_call | solution.py:298
  38.1 2.5 %collective-permute-done.10 = bf16[80,2400]{1,0:T(8,128)(2,1)S(1)} collective-permute-done((bf16[80,2400]{1,0:T(8,128)(2,1)S(1)}, bf16[80,2400]{1,0:T(8,128)(2,1)S(1)}, u32[]{:S(2)}, u32[]{:S(2)}) %collective-permute-start.10) | collective-permute-done | bytes 384032 | tf_op jit(solution)/shard_map/ppermute | solution.py:270
  40.7 2.1 %collective-permute-start.15 = (bf16[120,2400]{1,0:T(8,128)(2,1)S(1)}, bf16[120,2400]{1,0:T(8,128)(2,1)S(1)}, u32[]{:S(2)}, u32[]{:S(2)}) collective-permute-start(bf16[120,2400]{1,0:T(8,128)(2,1)S(1)} %pad_maximum_fusion.1.b0), channel_id=1, source_target_pairs={{0,8},{8,0},{1,9},{9,1},{2,10},{10,2},{3,11},{11,3},{4,12},{12,4},... | collective-permute-start | bytes 1728008 | tf_op jit(solution)/shard_map/ppermute | solution.py:307
  42.8 0.1 collective-permute-start.13
  42.9 0.4 collective-permute-start.14
  43.3 1.6 %far_first.1.t_far = f32[80,160]{1,0:T(8,128)S(1)} custom-call(bf16[160,2400]{1,0:T(8,128)(2,1)S(1)} %collective-permute-done.7.far_a, bf16[160,2400]{1,0:T(8,128)(2,1)S(1)} %pad_maximum_fusion.far_b, bf16[200,2400]{1,0:T(8,128)(2,1)S(1)} %constant_dynamic-update-slice_fusion.b0, bf16[200,2400]{1,0:T(8,128)(2,1)S(1)} %collective-permute-done.12.b1, ...), custom_call_target="tpu_custom_call" | custom-call | flops 1000000000 | bytes 1048576 | tf_op jit(solution)/shard_map/far_first/pallas_call | solution.py:311
  45.0 2.0 %last_terms.1.t = f32[200,128]{1,0:T(8,128)S(1)} custom-call(bf16[2,160,2400]{2,1,0:T(8,128)(2,1)S(1)} %bitcast.9, bf16[160,2400]{1,0:T(8,128)(2,1)S(1)} %collective-permute-done.7.far_a, bf16[160,2400]{1,0:T(8,128)(2,1)S(1)} %pad_maximum_fusion.far_b, bf16[120,2400]{1,0:T(8,128)(2,1)S(1)} %pad_maximum_fusion.1.b0, ...), custom_call_target="tpu_custom_call" | custom-call | flops 1000000000 | bytes 1048576 | tf_op jit(solution)/shard_map/last_terms/pallas_call | solution.py:312
  47.0 3.0 %collective-permute-start.16 = (f32[200,128]{1,0:T(8,128)S(1)}, f32[200,128]{1,0:T(8,128)S(1)}, u32[]{:S(2)}, u32[]{:S(2)}) collective-permute-start(f32[200,128]{1,0:T(8,128)S(1)} %last_terms.1.t), channel_id=1, source_target_pairs={{0,128},{128,0},{1,129},{129,1},{2,130},{130,2},{3,131},{131,3},{4... | collective-permute-start | bytes 307208 | tf_op jit(solution)/shard_map/ppermute | solution.py:321
  50.0 0.4 collective-permute-start.17
  50.3 2.7 %collective-permute-done.16.t_yh = f32[200,128]{1,0:T(8,128)S(1)} collective-permute-done((f32[200,128]{1,0:T(8,128)S(1)}, f32[200,128]{1,0:T(8,128)S(1)}, u32[]{:S(2)}, u32[]{:S(2)}) %collective-permute-start.16) | collective-permute-done | bytes 102432 | tf_op jit(solution)/shard_map/ppermute | solution.py:321
  53.0 0.9 %collective-permute-start.18 = (f32[200,128]{1,0:T(8,128)S(1)}, f32[200,128]{1,0:T(8,128)S(1)}, u32[]{:S(2)}, u32[]{:S(2)}) collective-permute-start(f32[200,128]{1,0:T(8,128)S(1)} %collective-permute-done.16.t_yh), channel_id=1, source_target_pairs={{0,8},{8,0},{1,9},{9,1},{2,10},{10,2},{3,11},{11,3},{4,12},{12,4},... | collective-permute-start | bytes 307208 | tf_op jit(solution)/shard_map/ppermute | solution.py:323
  53.9 0.9 %collective-permute-done.18.t_diag = f32[200,128]{1,0:T(8,128)S(1)} collective-permute-done((f32[200,128]{1,0:T(8,128)S(1)}, f32[200,128]{1,0:T(8,128)S(1)}, u32[]{:S(2)}, u32[]{:S(2)}) %collective-permute-start.18) | collective-permute-done | bytes 102432 | tf_op jit(solution)/shard_map/ppermute | solution.py:323
  54.8 4.3 %cluster_terms.1 = s16[384,128]{1,0:T(8,128)(2,1)} custom-call(bf16[2,160,2400]{2,1,0:T(8,128)(2,1)S(1)} %bitcast.10, bf16[160,2400]{1,0:T(8,128)(2,1)S(1)} %collective-permute-done.7.far_a, bf16[160,2400]{1,0:T(8,128)(2,1)S(1)} %pad_maximum_fusion.far_b, bf16[2,160,2400]{2,1,0:T(8,128)(2,1)} %collective-permute-done.4.near_hbm, ...), custom_call_target="tpu_custom_call" | custom-call | flops 1000000000 | bytes 1048576 | tf_op jit(solution)/shard_map/cluster_terms/pallas_call | solution.py:328
  59.1 4.9 %all-to-all-start = ((s16[8,48,128]{2,1,0:T(8,128)(2,1)}), s16[8,48,128]{2,1,0:T(8,128)(2,1)S(1)}, u32[]{:S(2)}, u32[]{:S(2)}) async-start(s16[8,48,128]{2,1,0:T(8,128)(2,1)} %bitcast.2), calls=%async_computation | async-start | bytes 196608 | tf_op jit(solution)/shard_map/all_to_all | solution.py:345
  64.0 0.1 convolution_bitcast_fusion.mask
  64.1 7.3 %all-to-all-done.arrived = s16[8,48,128]{2,1,0:T(8,128)(2,1)S(1)} async-done(((s16[8,48,128]{2,1,0:T(8,128)(2,1)}), s16[8,48,128]{2,1,0:T(8,128)(2,1)S(1)}, u32[]{:S(2)}, u32[]{:S(2)}) %all-to-all-start) | async-done | bytes 98336 | tf_op jit(solution)/shard_map/all_to_all | solution.py:345
  71.4 0.9 %sum_and_mask.1 = f32[2,20,2,75]{3,2,1,0:T(2,128)} custom-call(s16[8,48,128]{2,1,0:T(8,128)(2,1)S(1)} %all-to-all-done.arrived, f32[2,75]{1,0:T(2,128)S(1)} %convolution_bitcast_fusion.mask), custom_call_target="tpu_custom_call" | custom-call | bytes 1048576 | tf_op jit(solution)/shard_map/sum_and_mask/pallas_call | solution.py:352
  (43 shorter events, 0.6 us)
Async XLA Ops:
  0.0 20.5 %collective-permute-start.4 = (bf16[2,160,2400]{2,1,0:T(8,128)(2,1)}, bf16[2,160,2400]{2,1,0:T(8,128)(2,1)}, u32[]{:S(2)}, u32[]{:S(2)}) collective-permute-start(bf16[2,160,2400]{2,1,0:T(8,128)(2,1)} %bitcast.7), channel_id=1, source_target_pairs={{0,8},{8,0},{1,9},{9,1},{2,10},{10,2},{3,11},{11,3},{4,12},{12,4},... | collective-permute-start | bytes 4608008 | tf_op jit(solution)/shard_map/ppermute | solution.py:256
  4.3 9.1 %collective-permute-start = (bf16[40,2400]{1,0:T(8,128)(2,1)S(1)}, bf16[40,2400]{1,0:T(8,128)(2,1)S(1)}, u32[]{:S(2)}, u32[]{:S(2)}) collective-permute-start(bf16[40,2400]{1,0:T(8,128)(2,1)S(1)} %reshape.22), channel_id=1, source_target_pairs={{0,16},{16,32},{32,48},{48,64},{64,80},{80,96},{96,112},{112,0},{1... | collective-permute-start | bytes 576008 | tf_op jit(solution)/shard_map/ppermute | solution.py:262
  4.4 9.1 %collective-permute-start.2 = (bf16[40,2400]{1,0:T(8,128)(2,1)S(1)}, bf16[40,2400]{1,0:T(8,128)(2,1)S(1)}, u32[]{:S(2)}, u32[]{:S(2)}) collective-permute-start(bf16[40,2400]{1,0:T(8,128)(2,1)S(1)} %reshape.22), channel_id=1, source_target_pairs={{16,0},{32,16},{48,32},{64,48},{80,64},{96,80},{112,96},{0,112},{1... | collective-permute-start | bytes 576008 | tf_op jit(solution)/shard_map/ppermute | solution.py:263
  9.5 20.3 %collective-permute-start.7 = (bf16[160,2400]{1,0:T(8,128)(2,1)S(1)}, bf16[160,2400]{1,0:T(8,128)(2,1)S(1)}, u32[]{:S(2)}, u32[]{:S(2)}) collective-permute-start(bf16[160,2400]{1,0:T(8,128)(2,1)S(1)} %dynamic-slice_bitcast_fusion), channel_id=1, source_target_pairs={{0,128},{128,0},{1,129},{129,1},{2,130},{130,2},{3,131},{131,3},{4... | collective-permute-start | bytes 2304008 | tf_op jit(solution)/shard_map/ppermute | solution.py:255
  13.5 7.0 %collective-permute-start.1 = (bf16[40,2400]{1,0:T(8,128)(2,1)S(1)}, bf16[40,2400]{1,0:T(8,128)(2,1)S(1)}, u32[]{:S(2)}, u32[]{:S(2)}) collective-permute-start(bf16[40,2400]{1,0:T(8,128)(2,1)S(1)} %collective-permute-done), channel_id=1, source_target_pairs={{0,16},{16,32},{32,48},{48,64},{64,80},{80,96},{96,112},{112,0},{1... | collective-permute-start | bytes 576008 | tf_op jit(solution)/shard_map/ppermute | solution.py:262
  13.5 7.0 %collective-permute-start.3 = (bf16[40,2400]{1,0:T(8,128)(2,1)S(1)}, bf16[40,2400]{1,0:T(8,128)(2,1)S(1)}, u32[]{:S(2)}, u32[]{:S(2)}) collective-permute-start(bf16[40,2400]{1,0:T(8,128)(2,1)S(1)} %collective-permute-done.2), channel_id=1, source_target_pairs={{16,0},{32,16},{48,32},{64,48},{80,64},{96,80},{112,96},{0,112},{1... | collective-permute-start | bytes 576008 | tf_op jit(solution)/shard_map/ppermute | solution.py:263
  16.2 16.5 %copy-start.1 = (s32[32,32]{1,0:T(8,128)S(1)}, s32[32,32]{1,0:T(8,128)}, u32[]{:S(2)}) copy-start(s32[32,32]{1,0:T(8,128)} %diff_class.1) | copy-start | bytes 12292
  16.2 16.5 %copy-start.2 = (s32[2]{0:T(128)S(1)}, s32[2]{0:T(128)}, u32[]{:S(2)}) copy-start(s32[2]{0:T(128)} %cells) | copy-start | bytes 28
  16.2 16.5 %copy-start.3 = (f32[32]{0:T(128)S(1)}, f32[32]{0:T(128)}, u32[]{:S(2)}) copy-start(f32[32]{0:T(128)} %class_weight.1) | copy-start | bytes 388
  16.2 16.5 %copy-start.4 = (f32[32]{0:T(128)S(1)}, f32[32]{0:T(128)}, u32[]{:S(2)}) copy-start(f32[32]{0:T(128)} %constant.55.clone.cos_table) | copy-start | bytes 388
  16.2 16.5 %copy-start.5 = (f32[32]{0:T(128)S(1)}, f32[32]{0:T(128)}, u32[]{:S(2)}) copy-start(f32[32]{0:T(128)} %constant.56.clone.sin_table) | copy-start | bytes 388
  16.2 20.4 %copy-start = (bf16[1,2,160,2400]{3,2,1,0:T(8,128)(2,1)S(1)}, bf16[1,2,160,2400]{3,2,1,0:T(8,128)(2,1)}, u32[]{:S(2)}) copy-start(bf16[1,2,160,2400]{3,2,1,0:T(8,128)(2,1)} %param.7) | copy-start | bytes 4608004
  20.5 9.3 %collective-permute-start.5 = (bf16[40,2400]{1,0:T(8,128)(2,1)S(1)}, bf16[40,2400]{1,0:T(8,128)(2,1)S(1)}, u32[]{:S(2)}, u32[]{:S(2)}) collective-permute-start(bf16[40,2400]{1,0:T(8,128)(2,1)S(1)} %collective-permute-done.1), channel_id=1, source_target_pairs={{0,16},{16,32},{32,48},{48,64},{64,80},{80,96},{96,112},{112,0},{1... | collective-permute-start | bytes 576008 | tf_op jit(solution)/shard_map/ppermute | solution.py:262
  20.5 9.3 %collective-permute-start.6 = (bf16[40,2400]{1,0:T(8,128)(2,1)S(1)}, bf16[40,2400]{1,0:T(8,128)(2,1)S(1)}, u32[]{:S(2)}, u32[]{:S(2)}) collective-permute-start(bf16[40,2400]{1,0:T(8,128)(2,1)S(1)} %collective-permute-done.3), channel_id=1, source_target_pairs={{16,0},{32,16},{48,32},{64,48},{80,64},{96,80},{112,96},{0,112},{1... | collective-permute-start | bytes 576008 | tf_op jit(solution)/shard_map/ppermute | solution.py:263
  23.3 13.4 %collective-permute-start.12 = (bf16[200,2400]{1,0:T(8,128)(2,1)S(1)}, bf16[200,2400]{1,0:T(8,128)(2,1)S(1)}, u32[]{:S(2)}, u32[]{:S(2)}) collective-permute-start(bf16[200,2400]{1,0:T(8,128)(2,1)S(1)} %constant_dynamic-update-slice_fusion.b0), channel_id=1, source_target_pairs={{0,8},{8,0},{1,9},{9,1},{2,10},{10,2},{3,11},{11,3},{4,12},{12,4},... | collective-permute-start | bytes 2880008 | tf_op jit(solution)/shard_map/ppermute | solution.py:274
  29.9 10.7 %collective-permute-start.10 = (bf16[80,2400]{1,0:T(8,128)(2,1)S(1)}, bf16[80,2400]{1,0:T(8,128)(2,1)S(1)}, u32[]{:S(2)}, u32[]{:S(2)}) collective-permute-start(bf16[80,2400]{1,0:T(8,128)(2,1)S(1)} %get-tuple-element.42), channel_id=1, source_target_pairs={{0,1},{1,2},{2,3},{3,0},{4,5},{5,6},{6,7},{7,4},{8,9},{9,10},{10,1... | collective-permute-start | bytes 1152008 | tf_op jit(solution)/shard_map/ppermute | solution.py:270
  31.2 9.4 %collective-permute-start.11 = (bf16[80,2400]{1,0:T(8,128)(2,1)S(1)}, bf16[80,2400]{1,0:T(8,128)(2,1)S(1)}, u32[]{:S(2)}, u32[]{:S(2)}) collective-permute-start(bf16[80,2400]{1,0:T(8,128)(2,1)S(1)} %get-tuple-element.41), channel_id=1, source_target_pairs={{1,0},{2,1},{3,2},{0,3},{5,4},{6,5},{7,6},{4,7},{9,8},{10,9},{11,1... | collective-permute-start | bytes 1152008 | tf_op jit(solution)/shard_map/ppermute | solution.py:271
  32.6 5.5 %collective-permute-start.8 = (bf16[24,2400]{1,0:T(8,128)(2,1)S(1)}, bf16[24,2400]{1,0:T(8,128)(2,1)S(1)}, u32[]{:S(2)}, u32[]{:S(2)}) collective-permute-start(bf16[24,2400]{1,0:T(8,128)(2,1)S(1)} %slice.12), channel_id=1, source_target_pairs={{0,16},{16,32},{32,48},{48,64},{64,80},{80,96},{96,112},{112,0},{1... | collective-permute-start | bytes 345608 | tf_op jit(solution)/shard_map/ppermute | solution.py:300
  33.9 4.2 %collective-permute-start.9 = (bf16[16,2400]{1,0:T(8,128)(2,1)S(1)}, bf16[16,2400]{1,0:T(8,128)(2,1)S(1)}, u32[]{:S(2)}, u32[]{:S(2)}) collective-permute-start(bf16[16,2400]{1,0:T(8,128)(2,1)S(1)} %slice.13), channel_id=1, source_target_pairs={{16,0},{32,16},{48,32},{64,48},{80,64},{96,80},{112,96},{0,112},{1... | collective-permute-start | bytes 230408 | tf_op jit(solution)/shard_map/ppermute | solution.py:301
  40.7 4.3 %collective-permute-start.15 = (bf16[120,2400]{1,0:T(8,128)(2,1)S(1)}, bf16[120,2400]{1,0:T(8,128)(2,1)S(1)}, u32[]{:S(2)}, u32[]{:S(2)}) collective-permute-start(bf16[120,2400]{1,0:T(8,128)(2,1)S(1)} %pad_maximum_fusion.1.b0), channel_id=1, source_target_pairs={{0,8},{8,0},{1,9},{9,1},{2,10},{10,2},{3,11},{11,3},{4,12},{12,4},... | collective-permute-start | bytes 1728008 | tf_op jit(solution)/shard_map/ppermute | solution.py:307
  42.8 11.1 %collective-permute-start.13 = (bf16[160,2400]{1,0:T(8,128)(2,1)S(1)}, bf16[160,2400]{1,0:T(8,128)(2,1)}, u32[]{:S(2)}, u32[]{:S(2)}) collective-permute-start(bf16[160,2400]{1,0:T(8,128)(2,1)S(1)} %collective-permute-done.7.far_a), channel_id=1, source_target_pairs={{0,8},{8,0},{1,9},{9,1},{2,10},{10,2},{3,11},{11,3},{4,12},{12,4},... | collective-permute-start | bytes 2304008 | tf_op jit(solution)/shard_map/ppermute | solution.py:309
  42.9 11.0 %collective-permute-start.14 = (bf16[160,2400]{1,0:T(8,128)(2,1)S(1)}, bf16[160,2400]{1,0:T(8,128)(2,1)}, u32[]{:S(2)}, u32[]{:S(2)}) collective-permute-start(bf16[160,2400]{1,0:T(8,128)(2,1)S(1)} %pad_maximum_fusion.far_b), channel_id=1, source_target_pairs={{0,8},{8,0},{1,9},{9,1},{2,10},{10,2},{3,11},{11,3},{4,12},{12,4},... | collective-permute-start | bytes 2304008 | tf_op jit(solution)/shard_map/ppermute | solution.py:309
  47.0 6.0 %collective-permute-start.16 = (f32[200,128]{1,0:T(8,128)S(1)}, f32[200,128]{1,0:T(8,128)S(1)}, u32[]{:S(2)}, u32[]{:S(2)}) collective-permute-start(f32[200,128]{1,0:T(8,128)S(1)} %last_terms.1.t), channel_id=1, source_target_pairs={{0,128},{128,0},{1,129},{129,1},{2,130},{130,2},{3,131},{131,3},{4... | collective-permute-start | bytes 307208 | tf_op jit(solution)/shard_map/ppermute | solution.py:321
  50.0 3.9 %collective-permute-start.17 = (f32[200,128]{1,0:T(8,128)S(1)}, f32[200,128]{1,0:T(8,128)S(1)}, u32[]{:S(2)}, u32[]{:S(2)}) collective-permute-start(f32[200,128]{1,0:T(8,128)S(1)} %last_terms.1.t), channel_id=1, source_target_pairs={{0,8},{8,0},{1,9},{9,1},{2,10},{10,2},{3,11},{11,3},{4,12},{12,4},... | collective-permute-start | bytes 307208 | tf_op jit(solution)/shard_map/ppermute | solution.py:322
  53.0 1.8 %collective-permute-start.18 = (f32[200,128]{1,0:T(8,128)S(1)}, f32[200,128]{1,0:T(8,128)S(1)}, u32[]{:S(2)}, u32[]{:S(2)}) collective-permute-start(f32[200,128]{1,0:T(8,128)S(1)} %collective-permute-done.16.t_yh), channel_id=1, source_target_pairs={{0,8},{8,0},{1,9},{9,1},{2,10},{10,2},{3,11},{11,3},{4,12},{12,4},... | collective-permute-start | bytes 307208 | tf_op jit(solution)/shard_map/ppermute | solution.py:323
  53.9 10.1 %copy-start.6 = (s32[2,30]{1,0:T(2,128)S(1)}, s32[2,30]{1,0:T(2,128)}, u32[]{:S(2)}) copy-start(s32[2,30]{1,0:T(2,128)} %param.11) | copy-start | bytes 724
  59.1 12.3 %all-to-all-start = ((s16[8,48,128]{2,1,0:T(8,128)(2,1)}), s16[8,48,128]{2,1,0:T(8,128)(2,1)S(1)}, u32[]{:S(2)}, u32[]{:S(2)}) async-start(s16[8,48,128]{2,1,0:T(8,128)(2,1)} %bitcast.2), calls=%async_computation | async-start | bytes 196608 | tf_op jit(solution)/shard_map/all_to_all | solution.py:345

commit v11 on v10

--- a/solution.py
+++ b/solution.py
@@ -63,10 +63,16 @@
     return jnp.where(real, up, -down) if sign > 0 else jnp.where(real, -up, down)
 
 
+def overlaps(b, part):
+    return lax.dot_general(b, part[...], (((1,), (1,)), ((), ())), preferred_element_type=F32)
+
+
 def part_of_t(b, real, imag, w, g, width):
-    contract = (((1,), (1,)), ((), ()))
-    m = lax.dot_general(b, real[...], contract, preferred_element_type=F32)
-    m = m + turned(lax.dot_general(b, imag[...], contract, preferred_element_type=F32), width, 1)
+    return t_of(overlaps(b, real), overlaps(b, imag), w, g, width)
+
+
+def t_of(real, imag, w, g, width):
+    m = real + turned(imag, width, 1)
     t = jnp.dot(g, (w * m).astype(BF16), preferred_element_type=F32)
     half = t.shape[0] // 2
     return t[:half] + t[half:]
@@ -100,13 +106,22 @@
     t_ref[...] = part_of_t(b, own.at[0], own.at[1], w[0, : b.shape[0], :], g[...], width)
 
 
-def far_kernel(width, far_a, far_b, b0, b1, w, g, t_ref, b_ref):
+def half_kernel(far_a, b0, b1, out, b_ref):
+    out[...] = overlaps(gathered(b_ref, b0, b1), far_a)
+
+
+def far_kernel(width, part_a, far_b, b0, b1, w, g, t_ref, b_ref):
     b = gathered(b_ref, b0, b1)
-
-    def run(real, imag):
-        t_ref[...] = part_of_t(b, real, imag, w[1, : b.shape[0], :], g[...], width)
-
-    either_way(far_a, far_b, run)
+    part_b = overlaps(b, far_b)
+    odd = odd_x()
+
+    @pl.when(odd == 0)
+    def _():
+        t_ref[...] = t_of(part_a[...], part_b, w[1, : b.shape[0], :], g[...], width)
+
+    @pl.when(odd != 0)
+    def _():
+        t_ref[...] = t_of(part_b, part_a[...], w[1, : b.shape[0], :], g[...], width)
 
 
 def last_kernel(width, own, far_a, far_b, b0, b1, w, g, t_own, t_far, t_ref, b_ref):
@@ -139,17 +154,18 @@
 
 
 def coded(piece, lanes):
-    largest = jnp.maximum(jnp.max(jnp.abs(piece), axis=1, keepdims=True), 1e-30)
+    rows, columns = piece.shape
+    piece = jnp.concatenate([piece, jnp.zeros((rows, lanes - columns), F32)], 1)
+    largest = jnp.maximum(jnp.max(jnp.abs(piece), axis=0, keepdims=True), 1e-30)
     exponent = jnp.floor(jnp.log2(largest)) + 1.0
     values = jnp.floor(piece * jnp.exp2(14.0 - exponent) + 0.5)
-    rows, columns = piece.shape
-    tail = jnp.broadcast_to(exponent, (rows, lanes - columns))
-    return jnp.concatenate([values, tail], 1).astype(jnp.int32).astype(jnp.int16)
+    return jnp.concatenate([values, jnp.broadcast_to(exponent, (8, lanes))], 0)
 
 
 def decoded(value):
     value = value.astype(jnp.int32).astype(F32)
-    return value * jnp.exp2(value[:, 125:126] - 14.0)
+    rows = value.shape[0] - 8
+    return value[:rows] * jnp.exp2(value[rows : rows + 1] - 14.0)
 
 
 def packed(u, at, columns):
@@ -206,8 +222,8 @@
             @pl.when((yh == row) & (core == parity))
             def _():
                 starts = [(2 * chip + parity) * columns + row * shift for chip in range(chips)]
-                pieces = [packed(u_ref[...], at, columns) for at in starts]
-                out[...] = coded(jnp.concatenate(pieces, 0), lanes)
+                pieces = [coded(packed(u_ref[...], at, columns), lanes) for at in starts]
+                out[...] = jnp.concatenate(pieces, 0).astype(jnp.int32).astype(jnp.int16)
 
 
 def final_kernel(arrived, mask, out):
@@ -217,10 +233,10 @@
     cells, width, parts, columns = out.shape
     value = unpacked(total, columns)
     for f in range(cells):
+        kept = value[f * parts * width : (f + 1) * parts * width] * mask[pl.ds(f, 1), :]
         for part in range(parts):
             for j in range(width):
-                row = (f * parts + part) * width + j
-                out[f, j, pl.ds(part, 1), :] = value[row : row + 1] * mask[pl.ds(f, 1), :]
+                out[f, j, pl.ds(part, 1), :] = kept[part * width + j : part * width + j + 1]
 
 
 def call(kernel, name, shapes, specs, scratch=(), mib=8, flops=0):
@@ -299,8 +315,10 @@
     cut = 24
     blocks.append(lax.ppermute(from_below[:cut], "z", up))
     blocks.append(lax.ppermute(from_above[cut:], "z", down))
-    held = (blocks[-2], blocks[-1], from_left, from_right, t_own)
-    blocks[-2], blocks[-1], from_left, from_right, t_own = lax.optimization_barrier(held)
+    part = jax.ShapeDtypeStruct((early, occupied), F32)
+    part_a = call(half_kernel, "far_half", part, [vmem] * 3, scratch, flops=10**9)(far_a, first, first_near)
+    held = (blocks[-2], blocks[-1], from_left, from_right, t_own, part_a)
+    blocks[-2], blocks[-1], from_left, from_right, t_own, part_a = lax.optimization_barrier(held)
     last = jnp.concatenate(blocks[split:], 0)
     far_b = jnp.concatenate([from_left, from_right], 0)
     last, far_b = lax.optimization_barrier((last, far_b))
@@ -308,7 +326,7 @@
     later_a, _ = lax.optimization_barrier((far_a, far_b))
     diag_a, diag_b = (lax.ppermute(half, "core", swap) for half in (later_a, far_b))
     kernel = functools.partial(far_kernel, width)
-    t_far = call(kernel, "far_first", one, [vmem] * 6, scratch, flops=10**9)(far_a, far_b, *b_first)
+    t_far = call(kernel, "far_first", one, [vmem] * 6, scratch, flops=10**9)(part_a, far_b, *b_first)
     t = call(
         functools.partial(last_kernel, width),
         "last_terms",
@@ -324,7 +342,7 @@
     chips = PARTS[1]
     columns = functions // kpoint_count
     span = 2 * chips * columns
-    rows = 4 * width * 3 // 5
+    rows = 4 * width * 3 // 5 + 8
     pieces = call(
         functools.partial(cluster_kernel, width, columns),
         "cluster_terms",

time: 73.3 us -> 74.2 us (1.012)
  local copies, waits for them, and re-layouts: 2.48 us -> 4.82 us
  waiting for transfers between devices: 23 us -> 20.9 us
    unnamed x18 -> x22, local copies, waits for them, and re-layouts: 0.12 us -> 2.46 us
    ppermute x1, waiting for transfers between devices: 2.47 us -> 1.55 us  [shards(): from_left = lax.ppermute(far_a[:mid], 'x', right)]
    ppermute x3, waiting for transfers between devices: 5.18 us -> 4.25 us  [shards(): from_below = lax.ppermute(from_below, 'z', up)]
  transfers between devices with their start and end apart: 20 -> 20, of which waited for: 7 -> 8; matrix products, arithmetic and copies ran while one was open for 4% -> 5% of each run, Pallas kernels for 9% -> 9%
where the time goes in v11:
time: 74.2 us; the launch traced here: 73.2 us
  starting transfers between devices  35.7 us (48%)
  waiting for transfers between devices  20.9 us (28%)
  Pallas kernels  11.3 us (15%)
  local copies, waits for them, and re-layouts  4.82 us (6%)
    ppermute x3, starting transfers between devices, shards(): from_above = lax.ppermute(from_above, 'z', down)  9.25 us
    all_to_all x1, waiting for transfers between devices, shards(): arrived = lax.all_to_all(pieces, 'z', 0, 0, tiled=True)  7.55 us
    all_to_all x1, starting transfers between devices, shards(): arrived = lax.all_to_all(pieces, 'z', 0, 0, tiled=True)  4.89 us
    ppermute x1, waiting for transfers between devices, shards(): lax.ppermute(lax.dynamic_index_in_dim(own, odd_x(), 0, keepdims=False), '...  4.37 us
    ppermute x3, waiting for transfers between devices, shards(): from_below = lax.ppermute(from_below, 'z', up)  4.25 us
    pallas_call x1, Pallas kernels, shards(): call(functools.partial(cluster_kernel, width, columns), 'cluster_terms',...  4.15 us
    ppermute x1, starting transfers between devices, shards(): near = lax.ppermute(own, 'core', swap)  3.24 us
    ppermute x1, starting transfers between devices, shards(): lax.ppermute(lax.dynamic_index_in_dim(own, odd_x(), 0, keepdims=False), '...  3 us
  transfers between devices with their start and end apart: 20, of which 8 were waited for; matrix products, arithmetic and copies ran while one was open for 5% of the time, Pallas kernels for 9%

profile of v11, /device:TPU:1, one launch (start us, length us, event | category | flops | bytes accessed | tf_op | source)
XLA Modules:
  0.0 73.2 jit_solution(6490110498644254491)
XLA Ops:
  0.0 3.2 %collective-permute-start.4 = (bf16[2,160,2400]{2,1,0:T(8,128)(2,1)}, bf16[2,160,2400]{2,1,0:T(8,128)(2,1)S(1)}, u32[]{:S(2)}, u32[]{:S(2)}) collective-permute-start(bf16[2,160,2400]{2,1,0:T(8,128)(2,1)} %bitcast.7), channel_id=1, source_target_pairs={{0,8},{8,0},{1,9},{9,1},{2,10},{10,2},{3,11},{11,3},{4,12},{12,4},... | collective-permute-start | bytes 4608008 | tf_op jit(solution)/shard_map/ppermute | solution.py:272
  3.2 1.0 %constant_dynamic-slice_fusion = bf16[1,2,20,2400]{3,2,1,0:T(8,128)(2,1)S(1)} fusion(bf16[1,2,160,2400]{3,2,1,0:T(8,128)(2,1)} %param.7, s32[]{:T(128)S(6)} %select_n.16), kind=kLoop, calls=%fused_computation.13 | loop fusion | bytes 384004 | tf_op jit(solution)/shard_map/dynamic_slice | solution.py:273
  4.4 3.9 %collective-permute-start.2 = (bf16[40,2400]{1,0:T(8,128)(2,1)S(1)}, bf16[40,2400]{1,0:T(8,128)(2,1)}, u32[]{:S(2)}, u32[]{:S(2)}) collective-permute-start(bf16[40,2400]{1,0:T(8,128)(2,1)S(1)} %reshape.22), channel_id=1, source_target_pairs={{16,0},{32,16},{48,32},{64,48},{80,64},{96,80},{112,96},{0,112},{1... | collective-permute-start | bytes 576008 | tf_op jit(solution)/shard_map/ppermute | solution.py:279
  8.3 1.2 %dynamic-slice_bitcast_fusion = bf16[160,2400]{1,0:T(8,128)(2,1)S(1)} fusion(bf16[1,2,160,2400]{3,2,1,0:T(8,128)(2,1)} %param.7, s32[]{:T(128)S(6)} %select_n.17), kind=kLoop, calls=%fused_computation.2 | loop fusion | bytes 1536004 | tf_op jit(solution)/shard_map/jit(dynamic_index_in_dim)/squeeze | solution.py:271
  9.5 3.0 %collective-permute-start.7 = (bf16[160,2400]{1,0:T(8,128)(2,1)S(1)}, bf16[160,2400]{1,0:T(8,128)(2,1)S(1)}, u32[]{:S(2)}, u32[]{:S(2)}) collective-permute-start(bf16[160,2400]{1,0:T(8,128)(2,1)S(1)} %dynamic-slice_bitcast_fusion), channel_id=1, source_target_pairs={{0,128},{128,0},{1,129},{129,1},{2,130},{130,2},{3,131},{131,3},{4... | collective-permute-start | bytes 2304008 | tf_op jit(solution)/shard_map/ppermute | solution.py:271
  12.6 0.9 %collective-permute-done = bf16[40,2400]{1,0:T(8,128)(2,1)S(1)} collective-permute-done((bf16[40,2400]{1,0:T(8,128)(2,1)S(1)}, bf16[40,2400]{1,0:T(8,128)(2,1)S(1)}, u32[]{:S(2)}, u32[]{:S(2)}) %collective-permute-start) | collective-permute-done | bytes 192032 | tf_op jit(solution)/shard_map/ppermute | solution.py:278
  13.5 2.7 %collective-permute-start.3 = (bf16[40,2400]{1,0:T(8,128)(2,1)}, bf16[40,2400]{1,0:T(8,128)(2,1)S(1)}, u32[]{:S(2)}, u32[]{:S(2)}) collective-permute-start(bf16[40,2400]{1,0:T(8,128)(2,1)} %collective-permute-done.2), channel_id=1, source_target_pairs={{16,0},{32,16},{48,32},{64,48},{80,64},{96,80},{112,96},{0,112},{1... | collective-permute-start | bytes 576008 | tf_op jit(solution)/shard_map/ppermute | solution.py:279
  16.2 1.0 %constant_dynamic-update-slice_fusion.2 = bf16[200,2400]{1,0:T(8,128)(2,1)S(1)} fusion(bf16[200,2400]{1,0:T(8,128)(2,1)S(1)} %constant_dynamic-update-slice_fusion.3, bf16[40,2400]{1,0:T(8,128)(2,1)} %collective-permute-done.2), kind=kLoop, calls=%fused_computation.7 | loop fusion | bytes 386560
  17.1 3.4 %collective-permute-done.1 = bf16[40,2400]{1,0:T(8,128)(2,1)S(1)} collective-permute-done((bf16[40,2400]{1,0:T(8,128)(2,1)S(1)}, bf16[40,2400]{1,0:T(8,128)(2,1)S(1)}, u32[]{:S(2)}, u32[]{:S(2)}) %collective-permute-start.1) | collective-permute-done | bytes 192032 | tf_op jit(solution)/shard_map/ppermute | solution.py:278
  20.6 2.7 %collective-permute-start.6 = (bf16[40,2400]{1,0:T(8,128)(2,1)S(1)}, bf16[40,2400]{1,0:T(8,128)(2,1)S(1)}, u32[]{:S(2)}, u32[]{:S(2)}) collective-permute-start(bf16[40,2400]{1,0:T(8,128)(2,1)S(1)} %collective-permute-done.3), channel_id=1, source_target_pairs={{16,0},{32,16},{48,32},{64,48},{80,64},{96,80},{112,96},{0,112},{1... | collective-permute-start | bytes 576008 | tf_op jit(solution)/shard_map/ppermute | solution.py:279
  23.3 2.1 %collective-permute-start.12 = (bf16[200,2400]{1,0:T(8,128)(2,1)S(1)}, bf16[200,2400]{1,0:T(8,128)(2,1)S(1)}, u32[]{:S(2)}, u32[]{:S(2)}) collective-permute-start(bf16[200,2400]{1,0:T(8,128)(2,1)S(1)} %constant_dynamic-update-slice_fusion.b0), channel_id=1, source_target_pairs={{0,8},{8,0},{1,9},{9,1},{2,10},{10,2},{3,11},{11,3},{4,12},{12,4},... | collective-permute-start | bytes 2880008 | tf_op jit(solution)/shard_map/ppermute | solution.py:290
  25.4 4.4 %collective-permute-done.7.far_a = bf16[160,2400]{1,0:T(8,128)(2,1)S(1)} collective-permute-done((bf16[160,2400]{1,0:T(8,128)(2,1)S(1)}, bf16[160,2400]{1,0:T(8,128)(2,1)S(1)}, u32[]{:S(2)}, u32[]{:S(2)}) %collective-permute-start.7) | collective-permute-done | bytes 768032 | tf_op jit(solution)/shard_map/ppermute | solution.py:271
  29.9 1.3 %collective-permute-start.10 = (bf16[80,2400]{1,0:T(8,128)(2,1)S(1)}, bf16[80,2400]{1,0:T(8,128)(2,1)S(1)}, u32[]{:S(2)}, u32[]{:S(2)}) collective-permute-start(bf16[80,2400]{1,0:T(8,128)(2,1)S(1)} %get-tuple-element.44), channel_id=1, source_target_pairs={{0,1},{1,2},{2,3},{3,0},{4,5},{5,6},{6,7},{7,4},{8,9},{9,10},{10,1... | collective-permute-start | bytes 1152008 | tf_op jit(solution)/shard_map/ppermute | solution.py:286
  31.2 1.5 %collective-permute-start.11 = (bf16[80,2400]{1,0:T(8,128)(2,1)S(1)}, bf16[80,2400]{1,0:T(8,128)(2,1)S(1)}, u32[]{:S(2)}, u32[]{:S(2)}) collective-permute-start(bf16[80,2400]{1,0:T(8,128)(2,1)S(1)} %get-tuple-element.43), channel_id=1, source_target_pairs={{1,0},{2,1},{3,2},{0,3},{5,4},{6,5},{7,6},{4,7},{9,8},{10,9},{11,1... | collective-permute-start | bytes 1152008 | tf_op jit(solution)/shard_map/ppermute | solution.py:287
  32.6 1.1 %phases.1 = (f32[2,640,1]{2,1,0:T(8,128)S(1)}, bf16[160,400]{1,0:T(8,128)(2,1)S(1)}, bf16[160,240]{1,0:T(8,128)(2,1)S(1)}) custom-call(s32[2]{0:T(128)S(1)} %copy-done.4, s32[32,32]{1,0:T(8,128)S(1)} %copy-done.3, f32[32]{0:T(128)S(1)} %copy-done.5, f32[32]{0:T(128)S(1)} %copy-done.6, f32[32]{0:T(128)S(1)} %copy-done.7), custom_call_target="tpu_custom_call" | custom-call | bytes 1048576 | tf_op jit(solution)/shard_map/phases/pallas_call | solution.py:299
  33.9 2.7 %collective-permute-start.9 = (bf16[16,2400]{1,0:T(8,128)(2,1)S(1)}, bf16[16,2400]{1,0:T(8,128)(2,1)S(1)}, u32[]{:S(2)}, u32[]{:S(2)}) collective-permute-start(bf16[16,2400]{1,0:T(8,128)(2,1)S(1)} %slice.13), channel_id=1, source_target_pairs={{16,0},{32,16},{48,32},{64,48},{80,64},{96,80},{112,96},{0,112},{1... | collective-permute-start | bytes 230408 | tf_op jit(solution)/shard_map/ppermute | solution.py:317
  36.6 0.7 far_half.1.part_a
  37.4 1.4 %own_first.1.t_own = f32[80,160]{1,0:T(8,128)S(1)} custom-call(bf16[2,160,2400]{2,1,0:T(8,128)(2,1)S(1)} %bitcast.8, bf16[200,2400]{1,0:T(8,128)(2,1)S(1)} %constant_dynamic-update-slice_fusion.b0, bf16[200,2400]{1,0:T(8,128)(2,1)S(1)} %collective-permute-done.12.b1, f32[2,640,1]{2,1,0:T(8,128)S(1)} %get-tuple-element.30.w, ...), custom_call_target="tpu_custom_call" | custom-call | flops 1000000000 | bytes 1048576 | tf_op jit(solution)/shard_map/own_first/pallas_call | solution.py:314
  39.0 1.5 %collective-permute-done.10 = bf16[80,2400]{1,0:T(8,128)(2,1)S(1)} collective-permute-done((bf16[80,2400]{1,0:T(8,128)(2,1)S(1)}, bf16[80,2400]{1,0:T(8,128)(2,1)S(1)}, u32[]{:S(2)}, u32[]{:S(2)}) %collective-permute-start.10) | collective-permute-done | bytes 384032 | tf_op jit(solution)/shard_map/ppermute | solution.py:286
  40.7 2.1 %collective-permute-start.15 = (bf16[120,2400]{1,0:T(8,128)(2,1)S(1)}, bf16[120,2400]{1,0:T(8,128)(2,1)S(1)}, u32[]{:S(2)}, u32[]{:S(2)}) collective-permute-start(bf16[120,2400]{1,0:T(8,128)(2,1)S(1)} %pad_maximum_fusion.1.b0), channel_id=1, source_target_pairs={{0,8},{8,0},{1,9},{9,1},{2,10},{10,2},{3,11},{11,3},{4,12},{12,4},... | collective-permute-start | bytes 1728008 | tf_op jit(solution)/shard_map/ppermute | solution.py:325
  43.3 1.1 %far_first.1.t_far = f32[80,160]{1,0:T(8,128)S(1)} custom-call(f32[400,160]{1,0:T(8,128)S(1)} %far_half.1.part_a, bf16[160,2400]{1,0:T(8,128)(2,1)S(1)} %pad_maximum_fusion.far_b, bf16[200,2400]{1,0:T(8,128)(2,1)S(1)} %constant_dynamic-update-slice_fusion.b0, bf16[200,2400]{1,0:T(8,128)(2,1)S(1)} %collective-permute-done.12.b1, ...), custom_call_target="tpu_custom_call" | custom-call | flops 1000000000 | bytes 1048576 | tf_op jit(solution)/shard_map/far_first/pallas_call | solution.py:329
  44.4 2.0 %last_terms.1.t = f32[200,128]{1,0:T(8,128)S(1)} custom-call(bf16[2,160,2400]{2,1,0:T(8,128)(2,1)S(1)} %bitcast.9, bf16[160,2400]{1,0:T(8,128)(2,1)S(1)} %collective-permute-done.7.far_a, bf16[160,2400]{1,0:T(8,128)(2,1)S(1)} %pad_maximum_fusion.far_b, bf16[120,2400]{1,0:T(8,128)(2,1)S(1)} %pad_maximum_fusion.1.b0, ...), custom_call_target="tpu_custom_call" | custom-call | flops 1000000000 | bytes 1048576 | tf_op jit(solution)/shard_map/last_terms/pallas_call | solution.py:330
  46.4 3.0 %collective-permute-start.16 = (f32[200,128]{1,0:T(8,128)S(1)}, f32[200,128]{1,0:T(8,128)S(1)}, u32[]{:S(2)}, u32[]{:S(2)}) collective-permute-start(f32[200,128]{1,0:T(8,128)S(1)} %last_terms.1.t), channel_id=1, source_target_pairs={{0,128},{128,0},{1,129},{129,1},{2,130},{130,2},{3,131},{131,3},{4... | collective-permute-start | bytes 307208 | tf_op jit(solution)/shard_map/ppermute | solution.py:339
  49.4 0.7 collective-permute-start.17
  50.1 2.0 %collective-permute-done.16.t_yh = f32[200,128]{1,0:T(8,128)S(1)} collective-permute-done((f32[200,128]{1,0:T(8,128)S(1)}, f32[200,128]{1,0:T(8,128)S(1)}, u32[]{:S(2)}, u32[]{:S(2)}) %collective-permute-start.16) | collective-permute-done | bytes 102432 | tf_op jit(solution)/shard_map/ppermute | solution.py:339
  52.1 1.2 %collective-permute-start.18 = (f32[200,128]{1,0:T(8,128)S(1)}, f32[200,128]{1,0:T(8,128)S(1)}, u32[]{:S(2)}, u32[]{:S(2)}) collective-permute-start(f32[200,128]{1,0:T(8,128)S(1)} %collective-permute-done.16.t_yh), channel_id=1, source_target_pairs={{0,8},{8,0},{1,9},{9,1},{2,10},{10,2},{3,11},{11,3},{4,12},{12,4},... | collective-permute-start | bytes 307208 | tf_op jit(solution)/shard_map/ppermute | solution.py:341
  53.3 0.9 %collective-permute-done.18.t_diag = f32[200,128]{1,0:T(8,128)S(1)} collective-permute-done((f32[200,128]{1,0:T(8,128)S(1)}, f32[200,128]{1,0:T(8,128)S(1)}, u32[]{:S(2)}, u32[]{:S(2)}) %collective-permute-start.18) | collective-permute-done | bytes 102432 | tf_op jit(solution)/shard_map/ppermute | solution.py:341
  54.2 1.4 %copy-done.2 = bf16[2,160,2400]{2,1,0:T(8,128)(2,1)S(1)} copy-done((bf16[2,160,2400]{2,1,0:T(8,128)(2,1)S(1)}, bf16[2,160,2400]{2,1,0:T(8,128)(2,1)}, u32[]{:S(2)}) %copy-start.2) | copy-done | bytes 1536024
  55.6 4.2 %cluster_terms.1 = s16[448,128]{1,0:T(8,128)(2,1)} custom-call(bf16[2,160,2400]{2,1,0:T(8,128)(2,1)S(1)} %bitcast.10, bf16[160,2400]{1,0:T(8,128)(2,1)S(1)} %collective-permute-done.7.far_a, bf16[160,2400]{1,0:T(8,128)(2,1)S(1)} %pad_maximum_fusion.far_b, bf16[2,160,2400]{2,1,0:T(8,128)(2,1)S(1)} %copy-done.2, ...), custom_call_target="tpu_custom_call" | custom-call | flops 1000000000 | bytes 1048576 | tf_op jit(solution)/shard_map/cluster_terms/pallas_call | solution.py:346
  59.8 4.9 %all-to-all-start = ((s16[8,56,128]{2,1,0:T(8,128)(2,1)}), s16[8,56,128]{2,1,0:T(8,128)(2,1)S(1)}, u32[]{:S(2)}, u32[]{:S(2)}) async-start(s16[8,56,128]{2,1,0:T(8,128)(2,1)} %bitcast.2), calls=%async_computation | async-start | bytes 229376 | tf_op jit(solution)/shard_map/all_to_all | solution.py:363
  64.8 7.5 %all-to-all-done.arrived = s16[8,56,128]{2,1,0:T(8,128)(2,1)S(1)} async-done(((s16[8,56,128]{2,1,0:T(8,128)(2,1)}), s16[8,56,128]{2,1,0:T(8,128)(2,1)S(1)}, u32[]{:S(2)}, u32[]{:S(2)}) %all-to-all-start) | async-done | bytes 114720 | tf_op jit(solution)/shard_map/all_to_all | solution.py:363
  72.4 0.8 %sum_and_mask.1 = f32[2,20,2,75]{3,2,1,0:T(2,128)} custom-call(s16[8,56,128]{2,1,0:T(8,128)(2,1)S(1)} %all-to-all-done.arrived, f32[2,75]{1,0:T(2,128)S(1)} %convolution_bitcast_fusion.mask), custom_call_target="tpu_custom_call" | custom-call | bytes 1048576 | tf_op jit(solution)/shard_map/sum_and_mask/pallas_call | solution.py:370
  (48 shorter events, 1.5 us)
Async XLA Ops:
  0.0 20.5 %collective-permute-start.4 = (bf16[2,160,2400]{2,1,0:T(8,128)(2,1)}, bf16[2,160,2400]{2,1,0:T(8,128)(2,1)S(1)}, u32[]{:S(2)}, u32[]{:S(2)}) collective-permute-start(bf16[2,160,2400]{2,1,0:T(8,128)(2,1)} %bitcast.7), channel_id=1, source_target_pairs={{0,8},{8,0},{1,9},{9,1},{2,10},{10,2},{3,11},{11,3},{4,12},{12,4},... | collective-permute-start | bytes 4608008 | tf_op jit(solution)/shard_map/ppermute | solution.py:272
  4.3 9.1 %collective-permute-start = (bf16[40,2400]{1,0:T(8,128)(2,1)S(1)}, bf16[40,2400]{1,0:T(8,128)(2,1)S(1)}, u32[]{:S(2)}, u32[]{:S(2)}) collective-permute-start(bf16[40,2400]{1,0:T(8,128)(2,1)S(1)} %reshape.22), channel_id=1, source_target_pairs={{0,16},{16,32},{32,48},{48,64},{64,80},{80,96},{96,112},{112,0},{1... | collective-permute-start | bytes 576008 | tf_op jit(solution)/shard_map/ppermute | solution.py:278
  4.4 9.1 %collective-permute-start.2 = (bf16[40,2400]{1,0:T(8,128)(2,1)S(1)}, bf16[40,2400]{1,0:T(8,128)(2,1)}, u32[]{:S(2)}, u32[]{:S(2)}) collective-permute-start(bf16[40,2400]{1,0:T(8,128)(2,1)S(1)} %reshape.22), channel_id=1, source_target_pairs={{16,0},{32,16},{48,32},{64,48},{80,64},{96,80},{112,96},{0,112},{1... | collective-permute-start | bytes 576008 | tf_op jit(solution)/shard_map/ppermute | solution.py:279
  9.5 20.3 %collective-permute-start.7 = (bf16[160,2400]{1,0:T(8,128)(2,1)S(1)}, bf16[160,2400]{1,0:T(8,128)(2,1)S(1)}, u32[]{:S(2)}, u32[]{:S(2)}) collective-permute-start(bf16[160,2400]{1,0:T(8,128)(2,1)S(1)} %dynamic-slice_bitcast_fusion), channel_id=1, source_target_pairs={{0,128},{128,0},{1,129},{129,1},{2,130},{130,2},{3,131},{131,3},{4... | collective-permute-start | bytes 2304008 | tf_op jit(solution)/shard_map/ppermute | solution.py:271
  12.5 20.1 %copy-start.3 = (s32[32,32]{1,0:T(8,128)S(1)}, s32[32,32]{1,0:T(8,128)}, u32[]{:S(2)}) copy-start(s32[32,32]{1,0:T(8,128)} %diff_class.1) | copy-start | bytes 12292
  12.6 20.1 %copy-start.4 = (s32[2]{0:T(128)S(1)}, s32[2]{0:T(128)}, u32[]{:S(2)}) copy-start(s32[2]{0:T(128)} %cells) | copy-start | bytes 28
  12.6 20.1 %copy-start.5 = (f32[32]{0:T(128)S(1)}, f32[32]{0:T(128)}, u32[]{:S(2)}) copy-start(f32[32]{0:T(128)} %class_weight.1) | copy-start | bytes 388
  12.6 20.0 %copy-start.6 = (f32[32]{0:T(128)S(1)}, f32[32]{0:T(128)}, u32[]{:S(2)}) copy-start(f32[32]{0:T(128)} %constant.55.clone.cos_table) | copy-start | bytes 388
  12.6 20.0 %copy-start.7 = (f32[32]{0:T(128)S(1)}, f32[32]{0:T(128)}, u32[]{:S(2)}) copy-start(f32[32]{0:T(128)} %constant.56.clone.sin_table) | copy-start | bytes 388
  13.5 7.0 %collective-permute-start.1 = (bf16[40,2400]{1,0:T(8,128)(2,1)S(1)}, bf16[40,2400]{1,0:T(8,128)(2,1)S(1)}, u32[]{:S(2)}, u32[]{:S(2)}) collective-permute-start(bf16[40,2400]{1,0:T(8,128)(2,1)S(1)} %collective-permute-done), channel_id=1, source_target_pairs={{0,16},{16,32},{32,48},{48,64},{64,80},{80,96},{96,112},{112,0},{1... | collective-permute-start | bytes 576008 | tf_op jit(solution)/shard_map/ppermute | solution.py:278
  13.5 7.0 %collective-permute-start.3 = (bf16[40,2400]{1,0:T(8,128)(2,1)}, bf16[40,2400]{1,0:T(8,128)(2,1)S(1)}, u32[]{:S(2)}, u32[]{:S(2)}) collective-permute-start(bf16[40,2400]{1,0:T(8,128)(2,1)} %collective-permute-done.2), channel_id=1, source_target_pairs={{16,0},{32,16},{48,32},{64,48},{80,64},{96,80},{112,96},{0,112},{1... | collective-permute-start | bytes 576008 | tf_op jit(solution)/shard_map/ppermute | solution.py:279
  20.5 13.3 %copy-start.1 = (bf16[2,160,2400]{2,1,0:T(8,128)(2,1)}, bf16[2,160,2400]{2,1,0:T(8,128)(2,1)S(1)}, u32[]{:S(2)}) copy-start(bf16[2,160,2400]{2,1,0:T(8,128)(2,1)S(1)} %collective-permute-done.4.near_hbm) | copy-start | bytes 4608004
  20.5 9.3 %collective-permute-start.5 = (bf16[40,2400]{1,0:T(8,128)(2,1)S(1)}, bf16[40,2400]{1,0:T(8,128)(2,1)S(1)}, u32[]{:S(2)}, u32[]{:S(2)}) collective-permute-start(bf16[40,2400]{1,0:T(8,128)(2,1)S(1)} %collective-permute-done.1), channel_id=1, source_target_pairs={{0,16},{16,32},{32,48},{48,64},{64,80},{80,96},{96,112},{112,0},{1... | collective-permute-start | bytes 576008 | tf_op jit(solution)/shard_map/ppermute | solution.py:278
  20.6 9.2 %collective-permute-start.6 = (bf16[40,2400]{1,0:T(8,128)(2,1)S(1)}, bf16[40,2400]{1,0:T(8,128)(2,1)S(1)}, u32[]{:S(2)}, u32[]{:S(2)}) collective-permute-start(bf16[40,2400]{1,0:T(8,128)(2,1)S(1)} %collective-permute-done.3), channel_id=1, source_target_pairs={{16,0},{32,16},{48,32},{64,48},{80,64},{96,80},{112,96},{0,112},{1... | collective-permute-start | bytes 576008 | tf_op jit(solution)/shard_map/ppermute | solution.py:279
  23.3 13.3 %collective-permute-start.12 = (bf16[200,2400]{1,0:T(8,128)(2,1)S(1)}, bf16[200,2400]{1,0:T(8,128)(2,1)S(1)}, u32[]{:S(2)}, u32[]{:S(2)}) collective-permute-start(bf16[200,2400]{1,0:T(8,128)(2,1)S(1)} %constant_dynamic-update-slice_fusion.b0), channel_id=1, source_target_pairs={{0,8},{8,0},{1,9},{9,1},{2,10},{10,2},{3,11},{11,3},{4,12},{12,4},... | collective-permute-start | bytes 2880008 | tf_op jit(solution)/shard_map/ppermute | solution.py:290
  29.9 10.7 %collective-permute-start.10 = (bf16[80,2400]{1,0:T(8,128)(2,1)S(1)}, bf16[80,2400]{1,0:T(8,128)(2,1)S(1)}, u32[]{:S(2)}, u32[]{:S(2)}) collective-permute-start(bf16[80,2400]{1,0:T(8,128)(2,1)S(1)} %get-tuple-element.44), channel_id=1, source_target_pairs={{0,1},{1,2},{2,3},{3,0},{4,5},{5,6},{6,7},{7,4},{8,9},{9,10},{10,1... | collective-permute-start | bytes 1152008 | tf_op jit(solution)/shard_map/ppermute | solution.py:286
  31.2 9.4 %collective-permute-start.11 = (bf16[80,2400]{1,0:T(8,128)(2,1)S(1)}, bf16[80,2400]{1,0:T(8,128)(2,1)S(1)}, u32[]{:S(2)}, u32[]{:S(2)}) collective-permute-start(bf16[80,2400]{1,0:T(8,128)(2,1)S(1)} %get-tuple-element.43), channel_id=1, source_target_pairs={{1,0},{2,1},{3,2},{0,3},{5,4},{6,5},{7,6},{4,7},{9,8},{10,9},{11,1... | collective-permute-start | bytes 1152008 | tf_op jit(solution)/shard_map/ppermute | solution.py:287
  33.8 5.2 %collective-permute-start.8 = (bf16[24,2400]{1,0:T(8,128)(2,1)S(1)}, bf16[24,2400]{1,0:T(8,128)(2,1)S(1)}, u32[]{:S(2)}, u32[]{:S(2)}) collective-permute-start(bf16[24,2400]{1,0:T(8,128)(2,1)S(1)} %slice.12), channel_id=1, source_target_pairs={{0,16},{16,32},{32,48},{48,64},{64,80},{80,96},{96,112},{112,0},{1... | collective-permute-start | bytes 345608 | tf_op jit(solution)/shard_map/ppermute | solution.py:316
  33.9 3.5 %copy-start = (bf16[1,2,160,2400]{3,2,1,0:T(8,128)(2,1)S(1)}, bf16[1,2,160,2400]{3,2,1,0:T(8,128)(2,1)}, u32[]{:S(2)}) copy-start(bf16[1,2,160,2400]{3,2,1,0:T(8,128)(2,1)} %param.7) | copy-start | bytes 4608004
  33.9 4.9 %collective-permute-start.9 = (bf16[16,2400]{1,0:T(8,128)(2,1)S(1)}, bf16[16,2400]{1,0:T(8,128)(2,1)S(1)}, u32[]{:S(2)}, u32[]{:S(2)}) collective-permute-start(bf16[16,2400]{1,0:T(8,128)(2,1)S(1)} %slice.13), channel_id=1, source_target_pairs={{16,0},{32,16},{48,32},{64,48},{80,64},{96,80},{112,96},{0,112},{1... | collective-permute-start | bytes 230408 | tf_op jit(solution)/shard_map/ppermute | solution.py:317
  40.7 3.7 %collective-permute-start.15 = (bf16[120,2400]{1,0:T(8,128)(2,1)S(1)}, bf16[120,2400]{1,0:T(8,128)(2,1)S(1)}, u32[]{:S(2)}, u32[]{:S(2)}) collective-permute-start(bf16[120,2400]{1,0:T(8,128)(2,1)S(1)} %pad_maximum_fusion.1.b0), channel_id=1, source_target_pairs={{0,8},{8,0},{1,9},{9,1},{2,10},{10,2},{3,11},{11,3},{4,12},{12,4},... | collective-permute-start | bytes 1728008 | tf_op jit(solution)/shard_map/ppermute | solution.py:325
  42.8 10.5 %collective-permute-start.13 = (bf16[160,2400]{1,0:T(8,128)(2,1)S(1)}, bf16[160,2400]{1,0:T(8,128)(2,1)}, u32[]{:S(2)}, u32[]{:S(2)}) collective-permute-start(bf16[160,2400]{1,0:T(8,128)(2,1)S(1)} %collective-permute-done.7.far_a), channel_id=1, source_target_pairs={{0,8},{8,0},{1,9},{9,1},{2,10},{10,2},{3,11},{11,3},{4,12},{12,4},... | collective-permute-start | bytes 2304008 | tf_op jit(solution)/shard_map/ppermute | solution.py:327
  43.1 10.2 %collective-permute-start.14 = (bf16[160,2400]{1,0:T(8,128)(2,1)S(1)}, bf16[160,2400]{1,0:T(8,128)(2,1)}, u32[]{:S(2)}, u32[]{:S(2)}) collective-permute-start(bf16[160,2400]{1,0:T(8,128)(2,1)S(1)} %pad_maximum_fusion.far_b), channel_id=1, source_target_pairs={{0,8},{8,0},{1,9},{9,1},{2,10},{10,2},{3,11},{11,3},{4,12},{12,4},... | collective-permute-start | bytes 2304008 | tf_op jit(solution)/shard_map/ppermute | solution.py:327
  46.4 5.7 %collective-permute-start.16 = (f32[200,128]{1,0:T(8,128)S(1)}, f32[200,128]{1,0:T(8,128)S(1)}, u32[]{:S(2)}, u32[]{:S(2)}) collective-permute-start(f32[200,128]{1,0:T(8,128)S(1)} %last_terms.1.t), channel_id=1, source_target_pairs={{0,128},{128,0},{1,129},{129,1},{2,130},{130,2},{3,131},{131,3},{4... | collective-permute-start | bytes 307208 | tf_op jit(solution)/shard_map/ppermute | solution.py:339
  49.4 3.9 %collective-permute-start.17 = (f32[200,128]{1,0:T(8,128)S(1)}, f32[200,128]{1,0:T(8,128)S(1)}, u32[]{:S(2)}, u32[]{:S(2)}) collective-permute-start(f32[200,128]{1,0:T(8,128)S(1)} %last_terms.1.t), channel_id=1, source_target_pairs={{0,8},{8,0},{1,9},{9,1},{2,10},{10,2},{3,11},{11,3},{4,12},{12,4},... | collective-permute-start | bytes 307208 | tf_op jit(solution)/shard_map/ppermute | solution.py:340
  52.1 2.2 %collective-permute-start.18 = (f32[200,128]{1,0:T(8,128)S(1)}, f32[200,128]{1,0:T(8,128)S(1)}, u32[]{:S(2)}, u32[]{:S(2)}) collective-permute-start(f32[200,128]{1,0:T(8,128)S(1)} %collective-permute-done.16.t_yh), channel_id=1, source_target_pairs={{0,8},{8,0},{1,9},{9,1},{2,10},{10,2},{3,11},{11,3},{4,12},{12,4},... | collective-permute-start | bytes 307208 | tf_op jit(solution)/shard_map/ppermute | solution.py:341
  53.3 11.4 %copy-start.8 = (s32[2,30]{1,0:T(2,128)S(1)}, s32[2,30]{1,0:T(2,128)}, u32[]{:S(2)}) copy-start(s32[2,30]{1,0:T(2,128)} %param.11) | copy-start | bytes 724
  54.2 1.4 %copy-start.2 = (bf16[2,160,2400]{2,1,0:T(8,128)(2,1)S(1)}, bf16[2,160,2400]{2,1,0:T(8,128)(2,1)}, u32[]{:S(2)}) copy-start(bf16[2,160,2400]{2,1,0:T(8,128)(2,1)} %copy-done.1) | copy-start | bytes 4608004
  59.8 12.6 %all-to-all-start = ((s16[8,56,128]{2,1,0:T(8,128)(2,1)}), s16[8,56,128]{2,1,0:T(8,128)(2,1)S(1)}, u32[]{:S(2)}, u32[]{:S(2)}) async-start(s16[8,56,128]{2,1,0:T(8,128)(2,1)} %bitcast.2), calls=%async_computation | async-start | bytes 229376 | tf_op jit(solution)/shard_map/all_to_all | solution.py:363

commit v12 on v11

--- a/solution.py
+++ b/solution.py
@@ -153,13 +153,18 @@
     return pairs
 
 
-def coded(piece, lanes):
-    rows, columns = piece.shape
-    piece = jnp.concatenate([piece, jnp.zeros((rows, lanes - columns), F32)], 1)
-    largest = jnp.maximum(jnp.max(jnp.abs(piece), axis=0, keepdims=True), 1e-30)
-    exponent = jnp.floor(jnp.log2(largest)) + 1.0
-    values = jnp.floor(piece * jnp.exp2(14.0 - exponent) + 0.5)
-    return jnp.concatenate([values, jnp.broadcast_to(exponent, (8, lanes))], 0)
+def coded(pieces, lanes):
+    rows, columns = pieces[0].shape
+    spare = jnp.zeros((rows, lanes - columns), F32)
+    pieces = [jnp.concatenate([piece, spare], 1) for piece in pieces]
+    largest = jnp.concatenate([jnp.max(jnp.abs(piece), axis=0, keepdims=True) for piece in pieces], 0)
+    exponents = jnp.floor(jnp.log2(jnp.maximum(largest, 1e-30))) + 1.0
+    scales = jnp.exp2(14.0 - exponents)
+    out = []
+    for at, piece in enumerate(pieces):
+        out.append(jnp.floor(piece * scales[at : at + 1] + 0.5))
+        out.append(jnp.broadcast_to(exponents[at : at + 1], (8, lanes)))
+    return jnp.concatenate(out, 0).astype(jnp.int32).astype(jnp.int16)
 
 
 def decoded(value):
@@ -222,8 +227,7 @@
             @pl.when((yh == row) & (core == parity))
             def _():
                 starts = [(2 * chip + parity) * columns + row * shift for chip in range(chips)]
-                pieces = [coded(packed(u_ref[...], at, columns), lanes) for at in starts]
-                out[...] = jnp.concatenate(pieces, 0).astype(jnp.int32).astype(jnp.int16)
+                out[...] = coded([packed(u_ref[...], at, columns) for at in starts], lanes)
 
 
 def final_kernel(arrived, mask, out):
@@ -324,7 +328,7 @@
     last, far_b = lax.optimization_barrier((last, far_b))
     last_near = lax.ppermute(last, "core", swap)
     later_a, _ = lax.optimization_barrier((far_a, far_b))
-    diag_a, diag_b = (lax.ppermute(half, "core", swap) for half in (later_a, far_b))
+    diag_a, diag_b = (lax.ppermute(value, "core", swap) for value in (later_a, far_b))
     kernel = functools.partial(far_kernel, width)
     t_far = call(kernel, "far_first", one, [vmem] * 6, scratch, flops=10**9)(part_a, far_b, *b_first)
     t = call(
@@ -347,7 +351,7 @@
         functools.partial(cluster_kernel, width, columns),
         "cluster_terms",
         jax.ShapeDtypeStruct((chips * rows, 128), jnp.int16),
-        [vmem] * 3 + [pl.ANY] * 3 + [vmem] * 4,
+        [vmem] * 3 + [pltpu.HBM] * 3 + [vmem] * 4,
         [
             pltpu.VMEM((4 * width, span + span % 128), F32),
             pltpu.VMEM(own.shape, BF16),

time: 74.2 us -> 74.2 us (level)
  no operation moved by 1% of the time
where the time goes in v12:
time: 74.2 us; the launch traced here: 73.2 us
  starting transfers between devices  35.7 us (48%)
  waiting for transfers between devices  20.9 us (28%)
  Pallas kernels  11.3 us (15%)
  local copies, waits for them, and re-layouts  4.82 us (6%)
    ppermute x3, starting transfers between devices, shards(): from_above = lax.ppermute(from_above, 'z', down)  9.25 us
    all_to_all x1, waiting for transfers between devices, shards(): arrived = lax.all_to_all(pieces, 'z', 0, 0, tiled=True)  7.51 us
    all_to_all x1, starting transfers between devices, shards(): arrived = lax.all_to_all(pieces, 'z', 0, 0, tiled=True)  4.89 us
    ppermute x1, waiting for transfers between devices, shards(): lax.ppermute(lax.dynamic_index_in_dim(own, odd_x(), 0, keepdims=False), '...  4.37 us
    ppermute x3, waiting for transfers between devices, shards(): from_below = lax.ppermute(from_below, 'z', up)  4.25 us
    pallas_call x1, Pallas kernels, shards(): call(functools.partial(cluster_kernel, width, columns), 'cluster_terms',...  4.18 us
    ppermute x1, starting transfers between devices, shards(): near = lax.ppermute(own, 'core', swap)  3.24 us
    ppermute x1, starting transfers between devices, shards(): lax.ppermute(lax.dynamic_index_in_dim(own, odd_x(), 0, keepdims=False), '...  3 us
  transfers between devices with their start and end apart: 20, of which 8 were waited for; matrix products, arithmetic and copies ran while one was open for 5% of the time, Pallas kernels for 9%

profile of v12, /device:TPU:1, one launch (start us, length us, event | category | flops | bytes accessed | tf_op | source)
XLA Modules:
  0.0 73.2 jit_solution(8803348381530147293)
XLA Ops:
  0.0 3.2 %collective-permute-start.4 = (bf16[2,160,2400]{2,1,0:T(8,128)(2,1)}, bf16[2,160,2400]{2,1,0:T(8,128)(2,1)S(1)}, u32[]{:S(2)}, u32[]{:S(2)}) collective-permute-start(bf16[2,160,2400]{2,1,0:T(8,128)(2,1)} %bitcast.7), channel_id=1, source_target_pairs={{0,8},{8,0},{1,9},{9,1},{2,10},{10,2},{3,11},{11,3},{4,12},{12,4},... | collective-permute-start | bytes 4608008 | tf_op jit(solution)/shard_map/ppermute | solution.py:276
  3.2 1.0 %constant_dynamic-slice_fusion = bf16[1,2,20,2400]{3,2,1,0:T(8,128)(2,1)S(1)} fusion(bf16[1,2,160,2400]{3,2,1,0:T(8,128)(2,1)} %param.7, s32[]{:T(128)S(6)} %select_n.16), kind=kLoop, calls=%fused_computation.13 | loop fusion | bytes 384004 | tf_op jit(solution)/shard_map/dynamic_slice | solution.py:277
  4.4 3.9 %collective-permute-start.2 = (bf16[40,2400]{1,0:T(8,128)(2,1)S(1)}, bf16[40,2400]{1,0:T(8,128)(2,1)}, u32[]{:S(2)}, u32[]{:S(2)}) collective-permute-start(bf16[40,2400]{1,0:T(8,128)(2,1)S(1)} %reshape.22), channel_id=1, source_target_pairs={{16,0},{32,16},{48,32},{64,48},{80,64},{96,80},{112,96},{0,112},{1... | collective-permute-start | bytes 576008 | tf_op jit(solution)/shard_map/ppermute | solution.py:283
  8.3 1.2 %dynamic-slice_bitcast_fusion = bf16[160,2400]{1,0:T(8,128)(2,1)S(1)} fusion(bf16[1,2,160,2400]{3,2,1,0:T(8,128)(2,1)} %param.7, s32[]{:T(128)S(6)} %select_n.17), kind=kLoop, calls=%fused_computation.2 | loop fusion | bytes 1536004 | tf_op jit(solution)/shard_map/jit(dynamic_index_in_dim)/squeeze | solution.py:275
  9.5 3.0 %collective-permute-start.7 = (bf16[160,2400]{1,0:T(8,128)(2,1)S(1)}, bf16[160,2400]{1,0:T(8,128)(2,1)S(1)}, u32[]{:S(2)}, u32[]{:S(2)}) collective-permute-start(bf16[160,2400]{1,0:T(8,128)(2,1)S(1)} %dynamic-slice_bitcast_fusion), channel_id=1, source_target_pairs={{0,128},{128,0},{1,129},{129,1},{2,130},{130,2},{3,131},{131,3},{4... | collective-permute-start | bytes 2304008 | tf_op jit(solution)/shard_map/ppermute | solution.py:275
  12.6 0.9 %collective-permute-done = bf16[40,2400]{1,0:T(8,128)(2,1)S(1)} collective-permute-done((bf16[40,2400]{1,0:T(8,128)(2,1)S(1)}, bf16[40,2400]{1,0:T(8,128)(2,1)S(1)}, u32[]{:S(2)}, u32[]{:S(2)}) %collective-permute-start) | collective-permute-done | bytes 192032 | tf_op jit(solution)/shard_map/ppermute | solution.py:282
  13.5 2.7 %collective-permute-start.3 = (bf16[40,2400]{1,0:T(8,128)(2,1)}, bf16[40,2400]{1,0:T(8,128)(2,1)S(1)}, u32[]{:S(2)}, u32[]{:S(2)}) collective-permute-start(bf16[40,2400]{1,0:T(8,128)(2,1)} %collective-permute-done.2), channel_id=1, source_target_pairs={{16,0},{32,16},{48,32},{64,48},{80,64},{96,80},{112,96},{0,112},{1... | collective-permute-start | bytes 576008 | tf_op jit(solution)/shard_map/ppermute | solution.py:283
  16.2 1.0 %constant_dynamic-update-slice_fusion.2 = bf16[200,2400]{1,0:T(8,128)(2,1)S(1)} fusion(bf16[200,2400]{1,0:T(8,128)(2,1)S(1)} %constant_dynamic-update-slice_fusion.3, bf16[40,2400]{1,0:T(8,128)(2,1)} %collective-permute-done.2), kind=kLoop, calls=%fused_computation.7 | loop fusion | bytes 386560
  17.1 3.4 %collective-permute-done.1 = bf16[40,2400]{1,0:T(8,128)(2,1)S(1)} collective-permute-done((bf16[40,2400]{1,0:T(8,128)(2,1)S(1)}, bf16[40,2400]{1,0:T(8,128)(2,1)S(1)}, u32[]{:S(2)}, u32[]{:S(2)}) %collective-permute-start.1) | collective-permute-done | bytes 192032 | tf_op jit(solution)/shard_map/ppermute | solution.py:282
  20.6 2.7 %collective-permute-start.6 = (bf16[40,2400]{1,0:T(8,128)(2,1)S(1)}, bf16[40,2400]{1,0:T(8,128)(2,1)S(1)}, u32[]{:S(2)}, u32[]{:S(2)}) collective-permute-start(bf16[40,2400]{1,0:T(8,128)(2,1)S(1)} %collective-permute-done.3), channel_id=1, source_target_pairs={{16,0},{32,16},{48,32},{64,48},{80,64},{96,80},{112,96},{0,112},{1... | collective-permute-start | bytes 576008 | tf_op jit(solution)/shard_map/ppermute | solution.py:283
  23.3 2.1 %collective-permute-start.12 = (bf16[200,2400]{1,0:T(8,128)(2,1)S(1)}, bf16[200,2400]{1,0:T(8,128)(2,1)S(1)}, u32[]{:S(2)}, u32[]{:S(2)}) collective-permute-start(bf16[200,2400]{1,0:T(8,128)(2,1)S(1)} %constant_dynamic-update-slice_fusion.b0), channel_id=1, source_target_pairs={{0,8},{8,0},{1,9},{9,1},{2,10},{10,2},{3,11},{11,3},{4,12},{12,4},... | collective-permute-start | bytes 2880008 | tf_op jit(solution)/shard_map/ppermute | solution.py:294
  25.4 4.4 %collective-permute-done.7.far_a = bf16[160,2400]{1,0:T(8,128)(2,1)S(1)} collective-permute-done((bf16[160,2400]{1,0:T(8,128)(2,1)S(1)}, bf16[160,2400]{1,0:T(8,128)(2,1)S(1)}, u32[]{:S(2)}, u32[]{:S(2)}) %collective-permute-start.7) | collective-permute-done | bytes 768032 | tf_op jit(solution)/shard_map/ppermute | solution.py:275
  29.9 1.3 %collective-permute-start.10 = (bf16[80,2400]{1,0:T(8,128)(2,1)S(1)}, bf16[80,2400]{1,0:T(8,128)(2,1)S(1)}, u32[]{:S(2)}, u32[]{:S(2)}) collective-permute-start(bf16[80,2400]{1,0:T(8,128)(2,1)S(1)} %get-tuple-element.44), channel_id=1, source_target_pairs={{0,1},{1,2},{2,3},{3,0},{4,5},{5,6},{6,7},{7,4},{8,9},{9,10},{10,1... | collective-permute-start | bytes 1152008 | tf_op jit(solution)/shard_map/ppermute | solution.py:290
  31.2 1.5 %collective-permute-start.11 = (bf16[80,2400]{1,0:T(8,128)(2,1)S(1)}, bf16[80,2400]{1,0:T(8,128)(2,1)S(1)}, u32[]{:S(2)}, u32[]{:S(2)}) collective-permute-start(bf16[80,2400]{1,0:T(8,128)(2,1)S(1)} %get-tuple-element.43), channel_id=1, source_target_pairs={{1,0},{2,1},{3,2},{0,3},{5,4},{6,5},{7,6},{4,7},{9,8},{10,9},{11,1... | collective-permute-start | bytes 1152008 | tf_op jit(solution)/shard_map/ppermute | solution.py:291
  32.6 1.1 %phases.1 = (f32[2,640,1]{2,1,0:T(8,128)S(1)}, bf16[160,400]{1,0:T(8,128)(2,1)S(1)}, bf16[160,240]{1,0:T(8,128)(2,1)S(1)}) custom-call(s32[2]{0:T(128)S(1)} %copy-done.4, s32[32,32]{1,0:T(8,128)S(1)} %copy-done.3, f32[32]{0:T(128)S(1)} %copy-done.5, f32[32]{0:T(128)S(1)} %copy-done.6, f32[32]{0:T(128)S(1)} %copy-done.7), custom_call_target="tpu_custom_call" | custom-call | bytes 1048576 | tf_op jit(solution)/shard_map/phases/pallas_call | solution.py:303
  33.9 2.7 %collective-permute-start.9 = (bf16[16,2400]{1,0:T(8,128)(2,1)S(1)}, bf16[16,2400]{1,0:T(8,128)(2,1)S(1)}, u32[]{:S(2)}, u32[]{:S(2)}) collective-permute-start(bf16[16,2400]{1,0:T(8,128)(2,1)S(1)} %slice.13), channel_id=1, source_target_pairs={{16,0},{32,16},{48,32},{64,48},{80,64},{96,80},{112,96},{0,112},{1... | collective-permute-start | bytes 230408 | tf_op jit(solution)/shard_map/ppermute | solution.py:321
  36.6 0.7 far_half.1.part_a
  37.4 1.4 %own_first.1.t_own = f32[80,160]{1,0:T(8,128)S(1)} custom-call(bf16[2,160,2400]{2,1,0:T(8,128)(2,1)S(1)} %bitcast.8, bf16[200,2400]{1,0:T(8,128)(2,1)S(1)} %constant_dynamic-update-slice_fusion.b0, bf16[200,2400]{1,0:T(8,128)(2,1)S(1)} %collective-permute-done.12.b1, f32[2,640,1]{2,1,0:T(8,128)S(1)} %get-tuple-element.30.w, ...), custom_call_target="tpu_custom_call" | custom-call | flops 1000000000 | bytes 1048576 | tf_op jit(solution)/shard_map/own_first/pallas_call | solution.py:318
  39.0 1.5 %collective-permute-done.10 = bf16[80,2400]{1,0:T(8,128)(2,1)S(1)} collective-permute-done((bf16[80,2400]{1,0:T(8,128)(2,1)S(1)}, bf16[80,2400]{1,0:T(8,128)(2,1)S(1)}, u32[]{:S(2)}, u32[]{:S(2)}) %collective-permute-start.10) | collective-permute-done | bytes 384032 | tf_op jit(solution)/shard_map/ppermute | solution.py:290
  40.7 2.1 %collective-permute-start.15 = (bf16[120,2400]{1,0:T(8,128)(2,1)S(1)}, bf16[120,2400]{1,0:T(8,128)(2,1)S(1)}, u32[]{:S(2)}, u32[]{:S(2)}) collective-permute-start(bf16[120,2400]{1,0:T(8,128)(2,1)S(1)} %pad_maximum_fusion.1.b0), channel_id=1, source_target_pairs={{0,8},{8,0},{1,9},{9,1},{2,10},{10,2},{3,11},{11,3},{4,12},{12,4},... | collective-permute-start | bytes 1728008 | tf_op jit(solution)/shard_map/ppermute | solution.py:329
  43.3 1.1 %far_first.1.t_far = f32[80,160]{1,0:T(8,128)S(1)} custom-call(f32[400,160]{1,0:T(8,128)S(1)} %far_half.1.part_a, bf16[160,2400]{1,0:T(8,128)(2,1)S(1)} %pad_maximum_fusion.far_b, bf16[200,2400]{1,0:T(8,128)(2,1)S(1)} %constant_dynamic-update-slice_fusion.b0, bf16[200,2400]{1,0:T(8,128)(2,1)S(1)} %collective-permute-done.12.b1, ...), custom_call_target="tpu_custom_call" | custom-call | flops 1000000000 | bytes 1048576 | tf_op jit(solution)/shard_map/far_first/pallas_call | solution.py:333
  44.4 2.0 %last_terms.1.t = f32[200,128]{1,0:T(8,128)S(1)} custom-call(bf16[2,160,2400]{2,1,0:T(8,128)(2,1)S(1)} %bitcast.9, bf16[160,2400]{1,0:T(8,128)(2,1)S(1)} %collective-permute-done.7.far_a, bf16[160,2400]{1,0:T(8,128)(2,1)S(1)} %pad_maximum_fusion.far_b, bf16[120,2400]{1,0:T(8,128)(2,1)S(1)} %pad_maximum_fusion.1.b0, ...), custom_call_target="tpu_custom_call" | custom-call | flops 1000000000 | bytes 1048576 | tf_op jit(solution)/shard_map/last_terms/pallas_call | solution.py:334
  46.4 3.0 %collective-permute-start.16 = (f32[200,128]{1,0:T(8,128)S(1)}, f32[200,128]{1,0:T(8,128)S(1)}, u32[]{:S(2)}, u32[]{:S(2)}) collective-permute-start(f32[200,128]{1,0:T(8,128)S(1)} %last_terms.1.t), channel_id=1, source_target_pairs={{0,128},{128,0},{1,129},{129,1},{2,130},{130,2},{3,131},{131,3},{4... | collective-permute-start | bytes 307208 | tf_op jit(solution)/shard_map/ppermute | solution.py:343
  49.4 0.7 collective-permute-start.17
  50.1 2.0 %collective-permute-done.16.t_yh = f32[200,128]{1,0:T(8,128)S(1)} collective-permute-done((f32[200,128]{1,0:T(8,128)S(1)}, f32[200,128]{1,0:T(8,128)S(1)}, u32[]{:S(2)}, u32[]{:S(2)}) %collective-permute-start.16) | collective-permute-done | bytes 102432 | tf_op jit(solution)/shard_map/ppermute | solution.py:343
  52.1 1.2 %collective-permute-start.18 = (f32[200,128]{1,0:T(8,128)S(1)}, f32[200,128]{1,0:T(8,128)S(1)}, u32[]{:S(2)}, u32[]{:S(2)}) collective-permute-start(f32[200,128]{1,0:T(8,128)S(1)} %collective-permute-done.16.t_yh), channel_id=1, source_target_pairs={{0,8},{8,0},{1,9},{9,1},{2,10},{10,2},{3,11},{11,3},{4,12},{12,4},... | collective-permute-start | bytes 307208 | tf_op jit(solution)/shard_map/ppermute | solution.py:345
  53.3 0.9 %collective-permute-done.18.t_diag = f32[200,128]{1,0:T(8,128)S(1)} collective-permute-done((f32[200,128]{1,0:T(8,128)S(1)}, f32[200,128]{1,0:T(8,128)S(1)}, u32[]{:S(2)}, u32[]{:S(2)}) %collective-permute-start.18) | collective-permute-done | bytes 102432 | tf_op jit(solution)/shard_map/ppermute | solution.py:345
  54.2 1.4 %copy-done.2 = bf16[2,160,2400]{2,1,0:T(8,128)(2,1)S(1)} copy-done((bf16[2,160,2400]{2,1,0:T(8,128)(2,1)S(1)}, bf16[2,160,2400]{2,1,0:T(8,128)(2,1)}, u32[]{:S(2)}) %copy-start.2) | copy-done | bytes 1536024
  55.6 4.2 %cluster_terms.1 = s16[448,128]{1,0:T(8,128)(2,1)} custom-call(bf16[2,160,2400]{2,1,0:T(8,128)(2,1)S(1)} %bitcast.10, bf16[160,2400]{1,0:T(8,128)(2,1)S(1)} %collective-permute-done.7.far_a, bf16[160,2400]{1,0:T(8,128)(2,1)S(1)} %pad_maximum_fusion.far_b, bf16[2,160,2400]{2,1,0:T(8,128)(2,1)S(1)} %copy-done.2, ...), custom_call_target="tpu_custom_call" | custom-call | flops 1000000000 | bytes 1048576 | tf_op jit(solution)/shard_map/cluster_terms/pallas_call | solution.py:350
  59.8 4.9 %all-to-all-start = ((s16[8,56,128]{2,1,0:T(8,128)(2,1)}), s16[8,56,128]{2,1,0:T(8,128)(2,1)S(1)}, u32[]{:S(2)}, u32[]{:S(2)}) async-start(s16[8,56,128]{2,1,0:T(8,128)(2,1)} %bitcast.2), calls=%async_computation | async-start | bytes 229376 | tf_op jit(solution)/shard_map/all_to_all | solution.py:367
  64.9 7.5 %all-to-all-done.arrived = s16[8,56,128]{2,1,0:T(8,128)(2,1)S(1)} async-done(((s16[8,56,128]{2,1,0:T(8,128)(2,1)}), s16[8,56,128]{2,1,0:T(8,128)(2,1)S(1)}, u32[]{:S(2)}, u32[]{:S(2)}) %all-to-all-start) | async-done | bytes 114720 | tf_op jit(solution)/shard_map/all_to_all | solution.py:367
  72.4 0.8 %sum_and_mask.1 = f32[2,20,2,75]{3,2,1,0:T(2,128)} custom-call(s16[8,56,128]{2,1,0:T(8,128)(2,1)S(1)} %all-to-all-done.arrived, f32[2,75]{1,0:T(2,128)S(1)} %convolution_bitcast_fusion.mask), custom_call_target="tpu_custom_call" | custom-call | bytes 1048576 | tf_op jit(solution)/shard_map/sum_and_mask/pallas_call | solution.py:374
  (48 shorter events, 1.5 us)
Async XLA Ops:
  0.0 20.5 %collective-permute-start.4 = (bf16[2,160,2400]{2,1,0:T(8,128)(2,1)}, bf16[2,160,2400]{2,1,0:T(8,128)(2,1)S(1)}, u32[]{:S(2)}, u32[]{:S(2)}) collective-permute-start(bf16[2,160,2400]{2,1,0:T(8,128)(2,1)} %bitcast.7), channel_id=1, source_target_pairs={{0,8},{8,0},{1,9},{9,1},{2,10},{10,2},{3,11},{11,3},{4,12},{12,4},... | collective-permute-start | bytes 4608008 | tf_op jit(solution)/shard_map/ppermute | solution.py:276
  4.3 9.1 %collective-permute-start = (bf16[40,2400]{1,0:T(8,128)(2,1)S(1)}, bf16[40,2400]{1,0:T(8,128)(2,1)S(1)}, u32[]{:S(2)}, u32[]{:S(2)}) collective-permute-start(bf16[40,2400]{1,0:T(8,128)(2,1)S(1)} %reshape.22), channel_id=1, source_target_pairs={{0,16},{16,32},{32,48},{48,64},{64,80},{80,96},{96,112},{112,0},{1... | collective-permute-start | bytes 576008 | tf_op jit(solution)/shard_map/ppermute | solution.py:282
  4.4 9.1 %collective-permute-start.2 = (bf16[40,2400]{1,0:T(8,128)(2,1)S(1)}, bf16[40,2400]{1,0:T(8,128)(2,1)}, u32[]{:S(2)}, u32[]{:S(2)}) collective-permute-start(bf16[40,2400]{1,0:T(8,128)(2,1)S(1)} %reshape.22), channel_id=1, source_target_pairs={{16,0},{32,16},{48,32},{64,48},{80,64},{96,80},{112,96},{0,112},{1... | collective-permute-start | bytes 576008 | tf_op jit(solution)/shard_map/ppermute | solution.py:283
  9.5 20.3 %collective-permute-start.7 = (bf16[160,2400]{1,0:T(8,128)(2,1)S(1)}, bf16[160,2400]{1,0:T(8,128)(2,1)S(1)}, u32[]{:S(2)}, u32[]{:S(2)}) collective-permute-start(bf16[160,2400]{1,0:T(8,128)(2,1)S(1)} %dynamic-slice_bitcast_fusion), channel_id=1, source_target_pairs={{0,128},{128,0},{1,129},{129,1},{2,130},{130,2},{3,131},{131,3},{4... | collective-permute-start | bytes 2304008 | tf_op jit(solution)/shard_map/ppermute | solution.py:275
  12.5 20.1 %copy-start.3 = (s32[32,32]{1,0:T(8,128)S(1)}, s32[32,32]{1,0:T(8,128)}, u32[]{:S(2)}) copy-start(s32[32,32]{1,0:T(8,128)} %diff_class.1) | copy-start | bytes 12292
  12.6 20.1 %copy-start.4 = (s32[2]{0:T(128)S(1)}, s32[2]{0:T(128)}, u32[]{:S(2)}) copy-start(s32[2]{0:T(128)} %cells) | copy-start | bytes 28
  12.6 20.1 %copy-start.5 = (f32[32]{0:T(128)S(1)}, f32[32]{0:T(128)}, u32[]{:S(2)}) copy-start(f32[32]{0:T(128)} %class_weight.1) | copy-start | bytes 388
  12.6 20.0 %copy-start.6 = (f32[32]{0:T(128)S(1)}, f32[32]{0:T(128)}, u32[]{:S(2)}) copy-start(f32[32]{0:T(128)} %constant.55.clone.cos_table) | copy-start | bytes 388
  12.6 20.0 %copy-start.7 = (f32[32]{0:T(128)S(1)}, f32[32]{0:T(128)}, u32[]{:S(2)}) copy-start(f32[32]{0:T(128)} %constant.56.clone.sin_table) | copy-start | bytes 388
  13.5 7.0 %collective-permute-start.1 = (bf16[40,2400]{1,0:T(8,128)(2,1)S(1)}, bf16[40,2400]{1,0:T(8,128)(2,1)S(1)}, u32[]{:S(2)}, u32[]{:S(2)}) collective-permute-start(bf16[40,2400]{1,0:T(8,128)(2,1)S(1)} %collective-permute-done), channel_id=1, source_target_pairs={{0,16},{16,32},{32,48},{48,64},{64,80},{80,96},{96,112},{112,0},{1... | collective-permute-start | bytes 576008 | tf_op jit(solution)/shard_map/ppermute | solution.py:282
  13.5 7.0 %collective-permute-start.3 = (bf16[40,2400]{1,0:T(8,128)(2,1)}, bf16[40,2400]{1,0:T(8,128)(2,1)S(1)}, u32[]{:S(2)}, u32[]{:S(2)}) collective-permute-start(bf16[40,2400]{1,0:T(8,128)(2,1)} %collective-permute-done.2), channel_id=1, source_target_pairs={{16,0},{32,16},{48,32},{64,48},{80,64},{96,80},{112,96},{0,112},{1... | collective-permute-start | bytes 576008 | tf_op jit(solution)/shard_map/ppermute | solution.py:283
  20.5 13.3 %copy-start.1 = (bf16[2,160,2400]{2,1,0:T(8,128)(2,1)}, bf16[2,160,2400]{2,1,0:T(8,128)(2,1)S(1)}, u32[]{:S(2)}) copy-start(bf16[2,160,2400]{2,1,0:T(8,128)(2,1)S(1)} %collective-permute-done.4.near_hbm) | copy-start | bytes 4608004
  20.5 9.3 %collective-permute-start.5 = (bf16[40,2400]{1,0:T(8,128)(2,1)S(1)}, bf16[40,2400]{1,0:T(8,128)(2,1)S(1)}, u32[]{:S(2)}, u32[]{:S(2)}) collective-permute-start(bf16[40,2400]{1,0:T(8,128)(2,1)S(1)} %collective-permute-done.1), channel_id=1, source_target_pairs={{0,16},{16,32},{32,48},{48,64},{64,80},{80,96},{96,112},{112,0},{1... | collective-permute-start | bytes 576008 | tf_op jit(solution)/shard_map/ppermute | solution.py:282
  20.6 9.2 %collective-permute-start.6 = (bf16[40,2400]{1,0:T(8,128)(2,1)S(1)}, bf16[40,2400]{1,0:T(8,128)(2,1)S(1)}, u32[]{:S(2)}, u32[]{:S(2)}) collective-permute-start(bf16[40,2400]{1,0:T(8,128)(2,1)S(1)} %collective-permute-done.3), channel_id=1, source_target_pairs={{16,0},{32,16},{48,32},{64,48},{80,64},{96,80},{112,96},{0,112},{1... | collective-permute-start | bytes 576008 | tf_op jit(solution)/shard_map/ppermute | solution.py:283
  23.3 13.3 %collective-permute-start.12 = (bf16[200,2400]{1,0:T(8,128)(2,1)S(1)}, bf16[200,2400]{1,0:T(8,128)(2,1)S(1)}, u32[]{:S(2)}, u32[]{:S(2)}) collective-permute-start(bf16[200,2400]{1,0:T(8,128)(2,1)S(1)} %constant_dynamic-update-slice_fusion.b0), channel_id=1, source_target_pairs={{0,8},{8,0},{1,9},{9,1},{2,10},{10,2},{3,11},{11,3},{4,12},{12,4},... | collective-permute-start | bytes 2880008 | tf_op jit(solution)/shard_map/ppermute | solution.py:294
  29.9 10.7 %collective-permute-start.10 = (bf16[80,2400]{1,0:T(8,128)(2,1)S(1)}, bf16[80,2400]{1,0:T(8,128)(2,1)S(1)}, u32[]{:S(2)}, u32[]{:S(2)}) collective-permute-start(bf16[80,2400]{1,0:T(8,128)(2,1)S(1)} %get-tuple-element.44), channel_id=1, source_target_pairs={{0,1},{1,2},{2,3},{3,0},{4,5},{5,6},{6,7},{7,4},{8,9},{9,10},{10,1... | collective-permute-start | bytes 1152008 | tf_op jit(solution)/shard_map/ppermute | solution.py:290
  31.2 9.4 %collective-permute-start.11 = (bf16[80,2400]{1,0:T(8,128)(2,1)S(1)}, bf16[80,2400]{1,0:T(8,128)(2,1)S(1)}, u32[]{:S(2)}, u32[]{:S(2)}) collective-permute-start(bf16[80,2400]{1,0:T(8,128)(2,1)S(1)} %get-tuple-element.43), channel_id=1, source_target_pairs={{1,0},{2,1},{3,2},{0,3},{5,4},{6,5},{7,6},{4,7},{9,8},{10,9},{11,1... | collective-permute-start | bytes 1152008 | tf_op jit(solution)/shard_map/ppermute | solution.py:291
  33.8 5.2 %collective-permute-start.8 = (bf16[24,2400]{1,0:T(8,128)(2,1)S(1)}, bf16[24,2400]{1,0:T(8,128)(2,1)S(1)}, u32[]{:S(2)}, u32[]{:S(2)}) collective-permute-start(bf16[24,2400]{1,0:T(8,128)(2,1)S(1)} %slice.12), channel_id=1, source_target_pairs={{0,16},{16,32},{32,48},{48,64},{64,80},{80,96},{96,112},{112,0},{1... | collective-permute-start | bytes 345608 | tf_op jit(solution)/shard_map/ppermute | solution.py:320
  33.9 3.5 %copy-start = (bf16[1,2,160,2400]{3,2,1,0:T(8,128)(2,1)S(1)}, bf16[1,2,160,2400]{3,2,1,0:T(8,128)(2,1)}, u32[]{:S(2)}) copy-start(bf16[1,2,160,2400]{3,2,1,0:T(8,128)(2,1)} %param.7) | copy-start | bytes 4608004
  33.9 4.9 %collective-permute-start.9 = (bf16[16,2400]{1,0:T(8,128)(2,1)S(1)}, bf16[16,2400]{1,0:T(8,128)(2,1)S(1)}, u32[]{:S(2)}, u32[]{:S(2)}) collective-permute-start(bf16[16,2400]{1,0:T(8,128)(2,1)S(1)} %slice.13), channel_id=1, source_target_pairs={{16,0},{32,16},{48,32},{64,48},{80,64},{96,80},{112,96},{0,112},{1... | collective-permute-start | bytes 230408 | tf_op jit(solution)/shard_map/ppermute | solution.py:321
  40.7 3.7 %collective-permute-start.15 = (bf16[120,2400]{1,0:T(8,128)(2,1)S(1)}, bf16[120,2400]{1,0:T(8,128)(2,1)S(1)}, u32[]{:S(2)}, u32[]{:S(2)}) collective-permute-start(bf16[120,2400]{1,0:T(8,128)(2,1)S(1)} %pad_maximum_fusion.1.b0), channel_id=1, source_target_pairs={{0,8},{8,0},{1,9},{9,1},{2,10},{10,2},{3,11},{11,3},{4,12},{12,4},... | collective-permute-start | bytes 1728008 | tf_op jit(solution)/shard_map/ppermute | solution.py:329
  42.8 10.5 %collective-permute-start.13 = (bf16[160,2400]{1,0:T(8,128)(2,1)S(1)}, bf16[160,2400]{1,0:T(8,128)(2,1)}, u32[]{:S(2)}, u32[]{:S(2)}) collective-permute-start(bf16[160,2400]{1,0:T(8,128)(2,1)S(1)} %collective-permute-done.7.far_a), channel_id=1, source_target_pairs={{0,8},{8,0},{1,9},{9,1},{2,10},{10,2},{3,11},{11,3},{4,12},{12,4},... | collective-permute-start | bytes 2304008 | tf_op jit(solution)/shard_map/ppermute | solution.py:331
  43.1 10.2 %collective-permute-start.14 = (bf16[160,2400]{1,0:T(8,128)(2,1)S(1)}, bf16[160,2400]{1,0:T(8,128)(2,1)}, u32[]{:S(2)}, u32[]{:S(2)}) collective-permute-start(bf16[160,2400]{1,0:T(8,128)(2,1)S(1)} %pad_maximum_fusion.far_b), channel_id=1, source_target_pairs={{0,8},{8,0},{1,9},{9,1},{2,10},{10,2},{3,11},{11,3},{4,12},{12,4},... | collective-permute-start | bytes 2304008 | tf_op jit(solution)/shard_map/ppermute | solution.py:331
  46.4 5.7 %collective-permute-start.16 = (f32[200,128]{1,0:T(8,128)S(1)}, f32[200,128]{1,0:T(8,128)S(1)}, u32[]{:S(2)}, u32[]{:S(2)}) collective-permute-start(f32[200,128]{1,0:T(8,128)S(1)} %last_terms.1.t), channel_id=1, source_target_pairs={{0,128},{128,0},{1,129},{129,1},{2,130},{130,2},{3,131},{131,3},{4... | collective-permute-start | bytes 307208 | tf_op jit(solution)/shard_map/ppermute | solution.py:343
  49.4 3.9 %collective-permute-start.17 = (f32[200,128]{1,0:T(8,128)S(1)}, f32[200,128]{1,0:T(8,128)S(1)}, u32[]{:S(2)}, u32[]{:S(2)}) collective-permute-start(f32[200,128]{1,0:T(8,128)S(1)} %last_terms.1.t), channel_id=1, source_target_pairs={{0,8},{8,0},{1,9},{9,1},{2,10},{10,2},{3,11},{11,3},{4,12},{12,4},... | collective-permute-start | bytes 307208 | tf_op jit(solution)/shard_map/ppermute | solution.py:344
  52.1 2.2 %collective-permute-start.18 = (f32[200,128]{1,0:T(8,128)S(1)}, f32[200,128]{1,0:T(8,128)S(1)}, u32[]{:S(2)}, u32[]{:S(2)}) collective-permute-start(f32[200,128]{1,0:T(8,128)S(1)} %collective-permute-done.16.t_yh), channel_id=1, source_target_pairs={{0,8},{8,0},{1,9},{9,1},{2,10},{10,2},{3,11},{11,3},{4,12},{12,4},... | collective-permute-start | bytes 307208 | tf_op jit(solution)/shard_map/ppermute | solution.py:345
  53.3 11.4 %copy-start.8 = (s32[2,30]{1,0:T(2,128)S(1)}, s32[2,30]{1,0:T(2,128)}, u32[]{:S(2)}) copy-start(s32[2,30]{1,0:T(2,128)} %param.11) | copy-start | bytes 724
  54.2 1.4 %copy-start.2 = (bf16[2,160,2400]{2,1,0:T(8,128)(2,1)S(1)}, bf16[2,160,2400]{2,1,0:T(8,128)(2,1)}, u32[]{:S(2)}) copy-start(bf16[2,160,2400]{2,1,0:T(8,128)(2,1)} %copy-done.1) | copy-start | bytes 4608004
  59.8 12.5 %all-to-all-start = ((s16[8,56,128]{2,1,0:T(8,128)(2,1)}), s16[8,56,128]{2,1,0:T(8,128)(2,1)S(1)}, u32[]{:S(2)}, u32[]{:S(2)}) async-start(s16[8,56,128]{2,1,0:T(8,128)(2,1)} %bitcast.2), calls=%async_computation | async-start | bytes 229376 | tf_op jit(solution)/shard_map/all_to_all | solution.py:367

commit v13 on v10

--- a/solution.py
+++ b/solution.py
@@ -138,18 +138,24 @@
     return pairs
 
 
-def coded(piece, lanes):
-    largest = jnp.maximum(jnp.max(jnp.abs(piece), axis=1, keepdims=True), 1e-30)
-    exponent = jnp.floor(jnp.log2(largest)) + 1.0
-    values = jnp.floor(piece * jnp.exp2(14.0 - exponent) + 0.5)
-    rows, columns = piece.shape
-    tail = jnp.broadcast_to(exponent, (rows, lanes - columns))
-    return jnp.concatenate([values, tail], 1).astype(jnp.int32).astype(jnp.int16)
+def coded(pieces, lanes):
+    rows, columns = pieces[0].shape
+    spare = jnp.zeros((rows, lanes - columns), F32)
+    pieces = [jnp.concatenate([piece, spare], 1) for piece in pieces]
+    largest = jnp.concatenate([jnp.max(jnp.abs(piece), axis=0, keepdims=True) for piece in pieces], 0)
+    exponents = jnp.floor(jnp.log2(jnp.maximum(largest, 1e-30))) + 1.0
+    scales = jnp.exp2(14.0 - exponents)
+    out = []
+    for at, piece in enumerate(pieces):
+        out.append(jnp.floor(piece * scales[at : at + 1] + 0.5))
+        out.append(jnp.broadcast_to(exponents[at : at + 1], (8, lanes)))
+    return jnp.concatenate(out, 0).astype(jnp.int32).astype(jnp.int16)
 
 
 def decoded(value):
     value = value.astype(jnp.int32).astype(F32)
-    return value * jnp.exp2(value[:, 125:126] - 14.0)
+    rows = value.shape[0] - 8
+    return value[:rows] * jnp.exp2(value[rows : rows + 1] - 14.0)
 
 
 def packed(u, at, columns):
@@ -206,8 +212,7 @@
             @pl.when((yh == row) & (core == parity))
             def _():
                 starts = [(2 * chip + parity) * columns + row * shift for chip in range(chips)]
-                pieces = [packed(u_ref[...], at, columns) for at in starts]
-                out[...] = coded(jnp.concatenate(pieces, 0), lanes)
+                out[...] = coded([packed(u_ref[...], at, columns) for at in starts], lanes)
 
 
 def final_kernel(arrived, mask, out):
@@ -217,10 +222,10 @@
     cells, width, parts, columns = out.shape
     value = unpacked(total, columns)
     for f in range(cells):
+        kept = value[f * parts * width : (f + 1) * parts * width] * mask[pl.ds(f, 1), :]
         for part in range(parts):
             for j in range(width):
-                row = (f * parts + part) * width + j
-                out[f, j, pl.ds(part, 1), :] = value[row : row + 1] * mask[pl.ds(f, 1), :]
+                out[f, j, pl.ds(part, 1), :] = kept[part * width + j : part * width + j + 1]
 
 
 def call(kernel, name, shapes, specs, scratch=(), mib=8, flops=0):
@@ -252,7 +257,9 @@
     left = [(j, i) for i, j in right]
     vmem, smem = pltpu.VMEM, pltpu.SMEM
 
-    far_a = lax.ppermute(lax.dynamic_index_in_dim(own, odd_x(), 0, keepdims=False), "yh", swap)
+    half = lax.dynamic_index_in_dim(own, odd_x(), 0, keepdims=False)
+    rows_1, rows_2 = 3 * occupied // 5, 2 * occupied // 5
+    far_1 = lax.ppermute(half[:rows_1], "yh", swap)
     near = lax.ppermute(own, "core", swap)
     block = lax.dynamic_slice_in_dim(own, band * width, width, 1).reshape(group, functions)
     blocks = [block]
@@ -261,14 +268,20 @@
     for step in range(1, PARTS[1] // 2):
         from_below = lax.ppermute(from_below, "z", up)
         from_above = lax.ppermute(from_above, "z", down)
+        if step == 1:
+            half_2, _ = lax.optimization_barrier((half[rows_1:], from_below))
+            far_2 = lax.ppermute(half_2, "yh", swap)
         if step == 2:
-            from_below, from_above, near = lax.optimization_barrier((from_below, from_above, near))
+            held = (from_below, from_above, near, far_1)
+            from_below, from_above, near, far_1 = lax.optimization_barrier(held)
+            left_1 = lax.ppermute(far_1[: rows_1 // 2], "x", right)
+            right_1 = lax.ppermute(far_1[rows_1 // 2 :], "x", left)
         if step == 3:
-            from_below, from_above, far_a = lax.optimization_barrier((from_below, from_above, far_a))
+            from_below, from_above, far_2 = lax.optimization_barrier((from_below, from_above, far_2))
         blocks += [from_below, from_above]
-    mid = occupied // 2
-    from_left = lax.ppermute(far_a[:mid], "x", right)
-    from_right = lax.ppermute(far_a[mid:], "x", left)
+    left_2 = lax.ppermute(far_2[: rows_2 // 2], "x", right)
+    right_2 = lax.ppermute(far_2[rows_2 // 2 :], "x", left)
+    far_a = jnp.concatenate([far_1, far_2], 0)
     split = 5
     first = jnp.concatenate(blocks[:split], 0)
     first_near = lax.ppermute(first, "core", swap)
@@ -299,10 +312,10 @@
     cut = 24
     blocks.append(lax.ppermute(from_below[:cut], "z", up))
     blocks.append(lax.ppermute(from_above[cut:], "z", down))
-    held = (blocks[-2], blocks[-1], from_left, from_right, t_own)
-    blocks[-2], blocks[-1], from_left, from_right, t_own = lax.optimization_barrier(held)
+    held = (blocks[-2], blocks[-1], left_1, right_1, left_2, right_2, t_own)
+    blocks[-2], blocks[-1], left_1, right_1, left_2, right_2, t_own = lax.optimization_barrier(held)
     last = jnp.concatenate(blocks[split:], 0)
-    far_b = jnp.concatenate([from_left, from_right], 0)
+    far_b = jnp.concatenate([left_1, right_1, left_2, right_2], 0)
     last, far_b = lax.optimization_barrier((last, far_b))
     last_near = lax.ppermute(last, "core", swap)
     later_a, _ = lax.optimization_barrier((far_a, far_b))
@@ -324,7 +337,7 @@
     chips = PARTS[1]
     columns = functions // kpoint_count
     span = 2 * chips * columns
-    rows = 4 * width * 3 // 5
+    rows = 4 * width * 3 // 5 + 8
     pieces = call(
         functools.partial(cluster_kernel, width, columns),
         "cluster_terms",

time: 73.3 us -> 77.9 us (1.063)
  waiting for transfers between devices: 23 us -> 15.9 us
  starting transfers between devices: 35 us -> 41.3 us
  local copies, waits for them, and re-layouts: 2.48 us -> 7.73 us
    ppermute x3 -> x6, waiting for transfers between devices: 6.93 us -> 0.99 us  [the longest x1 0.97 us: shards(): far_1 = lax.ppermute(half[:rows_1], 'yh', swap)]
    ppermute x3 -> x6, starting transfers between devices: 5.75 us -> 11.4 us  [the longest x1 3.03 us: shards(): right_2 = lax.ppermute(far_2[rows_2 // 2:], 'x', left)]
    unnamed x18 -> x23, local copies, waits for them, and re-layouts: 0.12 us -> 3.51 us
    ppermute x3, waiting for transfers between devices: 5.18 us -> 2.02 us  [shards(): from_below = lax.ppermute(from_below, 'z', up)]
    ppermute x3, starting transfers between devices: 9.26 us -> 12.2 us  [shards(): from_above = lax.ppermute(from_above, 'z', down)]
    slice x1 -> x4, local copies, waits for them, and re-layouts: 0.06 us -> 2.96 us  [the longest x1 1.83 us: shards(): far_1 = lax.ppermute(half[:rows_1], 'yh', swap)]
    ppermute x1, starting transfers between devices: 3.24 us -> 0.96 us  [shards(): near = lax.ppermute(own, 'core', swap)]
    ppermute x3, waiting for transfers between devices: 0.01 us -> 1.63 us  [shards(): from_above = lax.ppermute(from_above, 'z', down)]
  transfers between devices with their start and end apart: 20 -> 23, of which waited for: 7 -> 7; matrix products, arithmetic and copies ran while one was open for 4% -> 7% of each run, Pallas kernels for 9% -> 8%
where the time goes in v13:
time: 77.9 us; the launch traced here: 76.6 us
  starting transfers between devices  41.3 us (53%)
  waiting for transfers between devices  15.9 us (20%)
  Pallas kernels  11.2 us (14%)
  local copies, waits for them, and re-layouts  7.73 us (10%)
    ppermute x3, starting transfers between devices, shards(): from_above = lax.ppermute(from_above, 'z', down)  12.2 us
    all_to_all x1, waiting for transfers between devices, shards(): arrived = lax.all_to_all(pieces, 'z', 0, 0, tiled=True)  7.52 us
    pallas_call x1, Pallas kernels, shards(): call(functools.partial(cluster_kernel, width, columns), 'cluster_terms',...  4.18 us
    all_to_all x1, starting transfers between devices, shards(): arrived = lax.all_to_all(pieces, 'z', 0, 0, tiled=True)  3.69 us
    unnamed x23, local copies, waits for them, and re-layouts  3.51 us
    ppermute x1, starting transfers between devices, shards(): t_yh = lax.ppermute(t, 'yh', swap)  3.39 us
    ppermute x1, starting transfers between devices, shards(): right_2 = lax.ppermute(far_2[rows_2 // 2:], 'x', left)  3.03 us
    ppermute x1, starting transfers between devices, shards(): far_1 = lax.ppermute(half[:rows_1], 'yh', swap)  2.91 us
  transfers between devices with their start and end apart: 23, of which 7 were waited for; matrix products, arithmetic and copies ran while one was open for 7% of the time, Pallas kernels for 8%

profile of v13, /device:TPU:1, one launch (start us, length us, event | category | flops | bytes accessed | tf_op | source)
XLA Modules:
  0.0 76.6 jit_solution(9520428434130389824)
XLA Ops:
  0.0 1.1 %constant_dynamic-slice_fusion = bf16[1,2,20,2400]{3,2,1,0:T(8,128)(2,1)S(1)} fusion(bf16[1,2,160,2400]{3,2,1,0:T(8,128)(2,1)} %param.7, s32[]{:T(128)S(6)} %select_n.16), kind=kLoop, calls=%fused_computation.16 | loop fusion | bytes 384004 | tf_op jit(solution)/shard_map/dynamic_slice | solution.py:264
  1.2 6.5 %collective-permute-start.2 = (bf16[40,2400]{1,0:T(8,128)(2,1)S(1)}, bf16[40,2400]{1,0:T(8,128)(2,1)S(1)}, u32[]{:S(2)}, u32[]{:S(2)}) collective-permute-start(bf16[40,2400]{1,0:T(8,128)(2,1)S(1)} %reshape.24), channel_id=1, source_target_pairs={{16,0},{32,16},{48,32},{64,48},{80,64},{96,80},{112,96},{0,112},{1... | collective-permute-start | bytes 576008 | tf_op jit(solution)/shard_map/ppermute | solution.py:270
  7.7 1.0 %collective-permute-start.4 = (bf16[2,160,2400]{2,1,0:T(8,128)(2,1)}, bf16[2,160,2400]{2,1,0:T(8,128)(2,1)S(1)}, u32[]{:S(2)}, u32[]{:S(2)}) collective-permute-start(bf16[2,160,2400]{2,1,0:T(8,128)(2,1)} %bitcast.9), channel_id=1, source_target_pairs={{0,8},{8,0},{1,9},{9,1},{2,10},{10,2},{3,11},{11,3},{4,12},{12,4},... | collective-permute-start | bytes 4608008 | tf_op jit(solution)/shard_map/ppermute | solution.py:263
  8.7 1.8 %dynamic-slice_bitcast_fusion = bf16[96,2400]{1,0:T(8,128)(2,1)} fusion(bf16[1,2,160,2400]{3,2,1,0:T(8,128)(2,1)} %param.7, s32[]{:T(128)S(6)} %select_n.17), kind=kLoop, calls=%fused_computation.3 | loop fusion | bytes 921604 | tf_op jit(solution)/shard_map/slice | solution.py:262
  10.5 2.9 %collective-permute-start.5 = (bf16[96,2400]{1,0:T(8,128)(2,1)}, bf16[96,2400]{1,0:T(8,128)(2,1)}, u32[]{:S(2)}, u32[]{:S(2)}) collective-permute-start(bf16[96,2400]{1,0:T(8,128)(2,1)} %dynamic-slice_bitcast_fusion), channel_id=1, source_target_pairs={{0,128},{128,0},{1,129},{129,1},{2,130},{130,2},{3,131},{131,3},{4... | collective-permute-start | bytes 1382408 | tf_op jit(solution)/shard_map/ppermute | solution.py:262
  13.4 1.0 %collective-permute-done = bf16[40,2400]{1,0:T(8,128)(2,1)} collective-permute-done((bf16[40,2400]{1,0:T(8,128)(2,1)S(1)}, bf16[40,2400]{1,0:T(8,128)(2,1)}, u32[]{:S(2)}, u32[]{:S(2)}) %collective-permute-start) | collective-permute-done | bytes 192032 | tf_op jit(solution)/shard_map/ppermute | solution.py:269
  14.4 2.9 %collective-permute-start.8 = (bf16[64,2400]{1,0:T(8,128)(2,1)S(1)}, bf16[64,2400]{1,0:T(8,128)(2,1)S(1)}, u32[]{:S(2)}, u32[]{:S(2)}) collective-permute-start(bf16[64,2400]{1,0:T(8,128)(2,1)S(1)} %dynamic-slice_bitcast_fusion.1), channel_id=1, source_target_pairs={{0,128},{128,0},{1,129},{129,1},{2,130},{130,2},{3,131},{131,3},{4... | collective-permute-start | bytes 921608 | tf_op jit(solution)/shard_map/ppermute | solution.py:273
  17.3 2.7 %collective-permute-start.3 = (bf16[40,2400]{1,0:T(8,128)(2,1)S(1)}, bf16[40,2400]{1,0:T(8,128)(2,1)S(1)}, u32[]{:S(2)}, u32[]{:S(2)}) collective-permute-start(bf16[40,2400]{1,0:T(8,128)(2,1)S(1)} %collective-permute-done.2), channel_id=1, source_target_pairs={{16,0},{32,16},{48,32},{64,48},{80,64},{96,80},{112,96},{0,112},{1... | collective-permute-start | bytes 576008 | tf_op jit(solution)/shard_map/ppermute | solution.py:270
  20.0 0.9 %constant_dynamic-update-slice_fusion.5 = bf16[200,2400]{1,0:T(8,128)(2,1)S(1)} fusion(bf16[200,2400]{1,0:T(8,128)(2,1)S(1)} %constant_dynamic-update-slice_fusion.6, bf16[40,2400]{1,0:T(8,128)(2,1)} %collective-permute-done), kind=kLoop, calls=%fused_computation.10 | loop fusion | bytes 386560
  21.0 1.6 %collective-permute-done.3 = bf16[40,2400]{1,0:T(8,128)(2,1)S(1)} collective-permute-done((bf16[40,2400]{1,0:T(8,128)(2,1)S(1)}, bf16[40,2400]{1,0:T(8,128)(2,1)S(1)}, u32[]{:S(2)}, u32[]{:S(2)}) %collective-permute-start.3) | collective-permute-done | bytes 192032 | tf_op jit(solution)/shard_map/ppermute | solution.py:270
  22.6 1.0 %collective-permute-done.1 = bf16[40,2400]{1,0:T(8,128)(2,1)S(1)} collective-permute-done((bf16[40,2400]{1,0:T(8,128)(2,1)}, bf16[40,2400]{1,0:T(8,128)(2,1)S(1)}, u32[]{:S(2)}, u32[]{:S(2)}) %collective-permute-start.1) | collective-permute-done | bytes 192032 | tf_op jit(solution)/shard_map/ppermute | solution.py:269
  23.7 1.0 %collective-permute-done.5 = bf16[96,2400]{1,0:T(8,128)(2,1)} collective-permute-done((bf16[96,2400]{1,0:T(8,128)(2,1)}, bf16[96,2400]{1,0:T(8,128)(2,1)}, u32[]{:S(2)}, u32[]{:S(2)}) %collective-permute-start.5) | collective-permute-done | bytes 460832 | tf_op jit(solution)/shard_map/ppermute | solution.py:262
  24.7 3.0 %collective-permute-start.7 = (bf16[40,2400]{1,0:T(8,128)(2,1)S(1)}, bf16[40,2400]{1,0:T(8,128)(2,1)S(1)}, u32[]{:S(2)}, u32[]{:S(2)}) collective-permute-start(bf16[40,2400]{1,0:T(8,128)(2,1)S(1)} %collective-permute-done.3), channel_id=1, source_target_pairs={{16,0},{32,16},{48,32},{64,48},{80,64},{96,80},{112,96},{0,112},{1... | collective-permute-start | bytes 576008 | tf_op jit(solution)/shard_map/ppermute | solution.py:270
  27.8 1.1 %fusion.2 = (bf16[48,2400]{1,0:T(8,128)(2,1)S(1)}, bf16[48,2400]{1,0:T(8,128)(2,1)S(1)}) fusion(bf16[96,2400]{1,0:T(8,128)(2,1)} %collective-permute-done.5), kind=kLoop, calls=%fused_computation.17 | loop fusion | bytes 921600 | tf_op jit(solution)/shard_map/slice | solution.py:278
  28.8 2.6 %collective-permute-start.12 = (bf16[48,2400]{1,0:T(8,128)(2,1)S(1)}, bf16[48,2400]{1,0:T(8,128)(2,1)S(1)}, u32[]{:S(2)}, u32[]{:S(2)}) collective-permute-start(bf16[48,2400]{1,0:T(8,128)(2,1)S(1)} %get-tuple-element.49), channel_id=1, source_target_pairs={{1,0},{2,1},{3,2},{0,3},{5,4},{6,5},{7,6},{4,7},{9,8},{10,9},{11,1... | collective-permute-start | bytes 691208 | tf_op jit(solution)/shard_map/ppermute | solution.py:278
  31.4 2.6 %collective-permute-start.15 = (bf16[200,2400]{1,0:T(8,128)(2,1)S(1)}, bf16[200,2400]{1,0:T(8,128)(2,1)S(1)}, u32[]{:S(2)}, u32[]{:S(2)}) collective-permute-start(bf16[200,2400]{1,0:T(8,128)(2,1)S(1)} %constant_dynamic-update-slice_fusion.2.b0), channel_id=1, source_target_pairs={{0,8},{8,0},{1,9},{9,1},{2,10},{10,2},{3,11},{11,3},{4,12},{12,4},... | collective-permute-start | bytes 2880008 | tf_op jit(solution)/shard_map/ppermute | solution.py:287
  34.2 3.0 %collective-permute-start.14 = (bf16[32,2400]{1,0:T(8,128)(2,1)S(1)}, bf16[32,2400]{1,0:T(8,128)(2,1)S(1)}, u32[]{:S(2)}, u32[]{:S(2)}) collective-permute-start(bf16[32,2400]{1,0:T(8,128)(2,1)S(1)} %get-tuple-element.51), channel_id=1, source_target_pairs={{1,0},{2,1},{3,2},{0,3},{5,4},{6,5},{7,6},{4,7},{9,8},{10,9},{11,1... | collective-permute-start | bytes 460808 | tf_op jit(solution)/shard_map/ppermute | solution.py:283
  37.3 1.1 %constant_dynamic-update-slice_fusion.1 = bf16[160,2400]{1,0:T(8,128)(2,1)S(1)} fusion(bf16[96,2400]{1,0:T(8,128)(2,1)} %collective-permute-done.5), kind=kLoop, calls=%fused_computation.6 | loop fusion | bytes 927744
  38.4 1.1 %phases.1 = (f32[2,640,1]{2,1,0:T(8,128)S(1)}, bf16[160,400]{1,0:T(8,128)(2,1)S(1)}, bf16[160,240]{1,0:T(8,128)(2,1)S(1)}) custom-call(s32[2]{0:T(128)S(1)} %copy-done.4, s32[32,32]{1,0:T(8,128)S(1)} %copy-done.3, f32[32]{0:T(128)S(1)} %copy-done.5, f32[32]{0:T(128)S(1)} %copy-done.7, f32[32]{0:T(128)S(1)} %copy-done.6), custom_call_target="tpu_custom_call" | custom-call | bytes 1048576 | tf_op jit(solution)/shard_map/phases/pallas_call | solution.py:296
  39.5 2.9 %collective-permute-start.10 = (bf16[16,2400]{1,0:T(8,128)(2,1)S(1)}, bf16[16,2400]{1,0:T(8,128)(2,1)S(1)}, u32[]{:S(2)}, u32[]{:S(2)}) collective-permute-start(bf16[16,2400]{1,0:T(8,128)(2,1)S(1)} %slice.35), channel_id=1, source_target_pairs={{16,0},{32,16},{48,32},{64,48},{80,64},{96,80},{112,96},{0,112},{1... | collective-permute-start | bytes 230408 | tf_op jit(solution)/shard_map/ppermute | solution.py:314
  42.4 1.4 %own_first.1.t_own = f32[80,160]{1,0:T(8,128)S(1)} custom-call(bf16[2,160,2400]{2,1,0:T(8,128)(2,1)S(1)} %bitcast.10, bf16[200,2400]{1,0:T(8,128)(2,1)S(1)} %constant_dynamic-update-slice_fusion.2.b0, bf16[200,2400]{1,0:T(8,128)(2,1)S(1)} %collective-permute-done.15.b1, f32[2,640,1]{2,1,0:T(8,128)S(1)} %get-tuple-element.35.w, ...), custom_call_target="tpu_custom_call" | custom-call | flops 1000000000 | bytes 1048576 | tf_op jit(solution)/shard_map/own_first/pallas_call | solution.py:311
  44.1 2.4 %collective-permute-start.18 = (bf16[120,2400]{1,0:T(8,128)(2,1)S(1)}, bf16[120,2400]{1,0:T(8,128)(2,1)S(1)}, u32[]{:S(2)}, u32[]{:S(2)}) collective-permute-start(bf16[120,2400]{1,0:T(8,128)(2,1)S(1)} %pad_maximum_fusion.1.b0), channel_id=1, source_target_pairs={{0,8},{8,0},{1,9},{9,1},{2,10},{10,2},{3,11},{11,3},{4,12},{12,4},... | collective-permute-start | bytes 1728008 | tf_op jit(solution)/shard_map/ppermute | solution.py:320
  47.0 1.6 %far_first.1.t_far = f32[80,160]{1,0:T(8,128)S(1)} custom-call(bf16[160,2400]{1,0:T(8,128)(2,1)S(1)} %constant_dynamic-update-slice_fusion.far_a, bf16[160,2400]{1,0:T(8,128)(2,1)S(1)} %pad_maximum_fusion.far_b, bf16[200,2400]{1,0:T(8,128)(2,1)S(1)} %constant_dynamic-update-slice_fusion.2.b0, bf16[200,2400]{1,0:T(8,128)(2,1)S(1)} %collective-permute-done.15.b1, ...), custom_call_target="tpu_custom_call" | custom-call | flops 1000000000 | bytes 1048576 | tf_op jit(solution)/shard_map/far_first/pallas_call | solution.py:324
  48.7 2.0 %last_terms.1.t = f32[200,128]{1,0:T(8,128)S(1)} custom-call(bf16[2,160,2400]{2,1,0:T(8,128)(2,1)S(1)} %bitcast.11, bf16[160,2400]{1,0:T(8,128)(2,1)S(1)} %constant_dynamic-update-slice_fusion.far_a, bf16[160,2400]{1,0:T(8,128)(2,1)S(1)} %pad_maximum_fusion.far_b, bf16[120,2400]{1,0:T(8,128)(2,1)S(1)} %pad_maximum_fusion.1.b0, ...), custom_call_target="tpu_custom_call" | custom-call | flops 1000000000 | bytes 1048576 | tf_op jit(solution)/shard_map/last_terms/pallas_call | solution.py:325
  50.7 3.4 %collective-permute-start.19 = (f32[200,128]{1,0:T(8,128)S(1)}, f32[200,128]{1,0:T(8,128)S(1)}, u32[]{:S(2)}, u32[]{:S(2)}) collective-permute-start(f32[200,128]{1,0:T(8,128)S(1)} %last_terms.1.t), channel_id=1, source_target_pairs={{0,128},{128,0},{1,129},{129,1},{2,130},{130,2},{3,131},{131,3},{4... | collective-permute-start | bytes 307208 | tf_op jit(solution)/shard_map/ppermute | solution.py:334
  54.4 2.8 %collective-permute-done.19.t_yh = f32[200,128]{1,0:T(8,128)S(1)} collective-permute-done((f32[200,128]{1,0:T(8,128)S(1)}, f32[200,128]{1,0:T(8,128)S(1)}, u32[]{:S(2)}, u32[]{:S(2)}) %collective-permute-start.19) | collective-permute-done | bytes 102432 | tf_op jit(solution)/shard_map/ppermute | solution.py:334
  57.9 0.9 %collective-permute-done.21.t_diag = f32[200,128]{1,0:T(8,128)S(1)} collective-permute-done((f32[200,128]{1,0:T(8,128)S(1)}, f32[200,128]{1,0:T(8,128)S(1)}, u32[]{:S(2)}, u32[]{:S(2)}) %collective-permute-start.21) | collective-permute-done | bytes 102432 | tf_op jit(solution)/shard_map/ppermute | solution.py:336
  58.8 1.4 %copy-done.2 = bf16[2,160,2400]{2,1,0:T(8,128)(2,1)S(1)} copy-done((bf16[2,160,2400]{2,1,0:T(8,128)(2,1)S(1)}, bf16[2,160,2400]{2,1,0:T(8,128)(2,1)}, u32[]{:S(2)}) %copy-start.2) | copy-done | bytes 1536024
  60.2 4.2 %cluster_terms.1 = s16[448,128]{1,0:T(8,128)(2,1)} custom-call(bf16[2,160,2400]{2,1,0:T(8,128)(2,1)S(1)} %bitcast.12, bf16[160,2400]{1,0:T(8,128)(2,1)S(1)} %constant_dynamic-update-slice_fusion.far_a, bf16[160,2400]{1,0:T(8,128)(2,1)S(1)} %pad_maximum_fusion.far_b, bf16[2,160,2400]{2,1,0:T(8,128)(2,1)S(1)} %copy-done.2, ...), custom_call_target="tpu_custom_call" | custom-call | flops 1000000000 | bytes 1048576 | tf_op jit(solution)/shard_map/cluster_terms/pallas_call | solution.py:341
  64.4 3.7 %all-to-all-start = ((s16[8,56,128]{2,1,0:T(8,128)(2,1)}), s16[8,56,128]{2,1,0:T(8,128)(2,1)S(1)}, u32[]{:S(2)}, u32[]{:S(2)}) async-start(s16[8,56,128]{2,1,0:T(8,128)(2,1)} %bitcast.3), calls=%async_computation | async-start | bytes 229376 | tf_op jit(solution)/shard_map/all_to_all | solution.py:358
  68.2 7.5 %all-to-all-done.arrived = s16[8,56,128]{2,1,0:T(8,128)(2,1)S(1)} async-done(((s16[8,56,128]{2,1,0:T(8,128)(2,1)}), s16[8,56,128]{2,1,0:T(8,128)(2,1)S(1)}, u32[]{:S(2)}, u32[]{:S(2)}) %all-to-all-start) | async-done | bytes 114720 | tf_op jit(solution)/shard_map/all_to_all | solution.py:358
  75.8 0.8 %sum_and_mask.1 = f32[2,20,2,75]{3,2,1,0:T(2,128)} custom-call(s16[8,56,128]{2,1,0:T(8,128)(2,1)S(1)} %all-to-all-done.arrived, f32[2,75]{1,0:T(2,128)S(1)} %convolution_bitcast_fusion.mask), custom_call_target="tpu_custom_call" | custom-call | bytes 1048576 | tf_op jit(solution)/shard_map/sum_and_mask/pallas_call | solution.py:365
  (57 shorter events, 2.3 us)
Async XLA Ops:
  0.0 13.4 %copy-start = (bf16[1,2,160,2400]{3,2,1,0:T(8,128)(2,1)S(1)}, bf16[1,2,160,2400]{3,2,1,0:T(8,128)(2,1)}, u32[]{:S(2)}) copy-start(bf16[1,2,160,2400]{3,2,1,0:T(8,128)(2,1)} %param.7) | copy-start | bytes 4608004
  1.2 16.1 %collective-permute-start.2 = (bf16[40,2400]{1,0:T(8,128)(2,1)S(1)}, bf16[40,2400]{1,0:T(8,128)(2,1)S(1)}, u32[]{:S(2)}, u32[]{:S(2)}) collective-permute-start(bf16[40,2400]{1,0:T(8,128)(2,1)S(1)} %reshape.24), channel_id=1, source_target_pairs={{16,0},{32,16},{48,32},{64,48},{80,64},{96,80},{112,96},{0,112},{1... | collective-permute-start | bytes 576008 | tf_op jit(solution)/shard_map/ppermute | solution.py:270
  7.7 6.7 %collective-permute-start = (bf16[40,2400]{1,0:T(8,128)(2,1)S(1)}, bf16[40,2400]{1,0:T(8,128)(2,1)}, u32[]{:S(2)}, u32[]{:S(2)}) collective-permute-start(bf16[40,2400]{1,0:T(8,128)(2,1)S(1)} %reshape.24), channel_id=1, source_target_pairs={{0,16},{16,32},{32,48},{48,64},{64,80},{80,96},{96,112},{112,0},{1... | collective-permute-start | bytes 576008 | tf_op jit(solution)/shard_map/ppermute | solution.py:269
  7.7 16.9 %collective-permute-start.4 = (bf16[2,160,2400]{2,1,0:T(8,128)(2,1)}, bf16[2,160,2400]{2,1,0:T(8,128)(2,1)S(1)}, u32[]{:S(2)}, u32[]{:S(2)}) collective-permute-start(bf16[2,160,2400]{2,1,0:T(8,128)(2,1)} %bitcast.9), channel_id=1, source_target_pairs={{0,8},{8,0},{1,9},{9,1},{2,10},{10,2},{3,11},{11,3},{4,12},{12,4},... | collective-permute-start | bytes 4608008 | tf_op jit(solution)/shard_map/ppermute | solution.py:263
  10.5 14.1 %collective-permute-start.5 = (bf16[96,2400]{1,0:T(8,128)(2,1)}, bf16[96,2400]{1,0:T(8,128)(2,1)}, u32[]{:S(2)}, u32[]{:S(2)}) collective-permute-start(bf16[96,2400]{1,0:T(8,128)(2,1)} %dynamic-slice_bitcast_fusion), channel_id=1, source_target_pairs={{0,128},{128,0},{1,129},{129,1},{2,130},{130,2},{3,131},{131,3},{4... | collective-permute-start | bytes 1382408 | tf_op jit(solution)/shard_map/ppermute | solution.py:262
  14.4 17.0 %collective-permute-start.8 = (bf16[64,2400]{1,0:T(8,128)(2,1)S(1)}, bf16[64,2400]{1,0:T(8,128)(2,1)S(1)}, u32[]{:S(2)}, u32[]{:S(2)}) collective-permute-start(bf16[64,2400]{1,0:T(8,128)(2,1)S(1)} %dynamic-slice_bitcast_fusion.1), channel_id=1, source_target_pairs={{0,128},{128,0},{1,129},{129,1},{2,130},{130,2},{3,131},{131,3},{4... | collective-permute-start | bytes 921608 | tf_op jit(solution)/shard_map/ppermute | solution.py:273
  17.3 6.3 %collective-permute-start.1 = (bf16[40,2400]{1,0:T(8,128)(2,1)}, bf16[40,2400]{1,0:T(8,128)(2,1)S(1)}, u32[]{:S(2)}, u32[]{:S(2)}) collective-permute-start(bf16[40,2400]{1,0:T(8,128)(2,1)} %collective-permute-done), channel_id=1, source_target_pairs={{0,16},{16,32},{32,48},{48,64},{64,80},{80,96},{96,112},{112,0},{1... | collective-permute-start | bytes 576008 | tf_op jit(solution)/shard_map/ppermute | solution.py:269
  17.3 5.3 %collective-permute-start.3 = (bf16[40,2400]{1,0:T(8,128)(2,1)S(1)}, bf16[40,2400]{1,0:T(8,128)(2,1)S(1)}, u32[]{:S(2)}, u32[]{:S(2)}) collective-permute-start(bf16[40,2400]{1,0:T(8,128)(2,1)S(1)} %collective-permute-done.2), channel_id=1, source_target_pairs={{16,0},{32,16},{48,32},{64,48},{80,64},{96,80},{112,96},{0,112},{1... | collective-permute-start | bytes 576008 | tf_op jit(solution)/shard_map/ppermute | solution.py:270
  24.6 12.6 %copy-start.1 = (bf16[2,160,2400]{2,1,0:T(8,128)(2,1)}, bf16[2,160,2400]{2,1,0:T(8,128)(2,1)S(1)}, u32[]{:S(2)}) copy-start(bf16[2,160,2400]{2,1,0:T(8,128)(2,1)S(1)} %collective-permute-done.4.near_hbm) | copy-start | bytes 4608004
  24.6 9.4 %collective-permute-start.6 = (bf16[40,2400]{1,0:T(8,128)(2,1)S(1)}, bf16[40,2400]{1,0:T(8,128)(2,1)S(1)}, u32[]{:S(2)}, u32[]{:S(2)}) collective-permute-start(bf16[40,2400]{1,0:T(8,128)(2,1)S(1)} %collective-permute-done.1), channel_id=1, source_target_pairs={{0,16},{16,32},{32,48},{48,64},{64,80},{80,96},{96,112},{112,0},{1... | collective-permute-start | bytes 576008 | tf_op jit(solution)/shard_map/ppermute | solution.py:269
  24.7 13.7 %copy-start.3 = (s32[32,32]{1,0:T(8,128)S(1)}, s32[32,32]{1,0:T(8,128)}, u32[]{:S(2)}) copy-start(s32[32,32]{1,0:T(8,128)} %diff_class.1) | copy-start | bytes 12292
  24.7 13.7 %copy-start.4 = (s32[2]{0:T(128)S(1)}, s32[2]{0:T(128)}, u32[]{:S(2)}) copy-start(s32[2]{0:T(128)} %cells) | copy-start | bytes 28
  24.7 13.7 %copy-start.5 = (f32[32]{0:T(128)S(1)}, f32[32]{0:T(128)}, u32[]{:S(2)}) copy-start(f32[32]{0:T(128)} %class_weight.1) | copy-start | bytes 388
  24.7 13.7 %copy-start.6 = (f32[32]{0:T(128)S(1)}, f32[32]{0:T(128)}, u32[]{:S(2)}) copy-start(f32[32]{0:T(128)} %constant.56.clone.sin_table) | copy-start | bytes 388
  24.7 13.7 %copy-start.7 = (f32[32]{0:T(128)S(1)}, f32[32]{0:T(128)}, u32[]{:S(2)}) copy-start(f32[32]{0:T(128)} %constant.55.clone.cos_table) | copy-start | bytes 388
  24.7 9.4 %collective-permute-start.7 = (bf16[40,2400]{1,0:T(8,128)(2,1)S(1)}, bf16[40,2400]{1,0:T(8,128)(2,1)S(1)}, u32[]{:S(2)}, u32[]{:S(2)}) collective-permute-start(bf16[40,2400]{1,0:T(8,128)(2,1)S(1)} %collective-permute-done.3), channel_id=1, source_target_pairs={{16,0},{32,16},{48,32},{64,48},{80,64},{96,80},{112,96},{0,112},{1... | collective-permute-start | bytes 576008 | tf_op jit(solution)/shard_map/ppermute | solution.py:270
  28.8 8.4 %collective-permute-start.12 = (bf16[48,2400]{1,0:T(8,128)(2,1)S(1)}, bf16[48,2400]{1,0:T(8,128)(2,1)S(1)}, u32[]{:S(2)}, u32[]{:S(2)}) collective-permute-start(bf16[48,2400]{1,0:T(8,128)(2,1)S(1)} %get-tuple-element.49), channel_id=1, source_target_pairs={{1,0},{2,1},{3,2},{0,3},{5,4},{6,5},{7,6},{4,7},{9,8},{10,9},{11,1... | collective-permute-start | bytes 691208 | tf_op jit(solution)/shard_map/ppermute | solution.py:278
  31.4 12.5 %collective-permute-start.11 = (bf16[48,2400]{1,0:T(8,128)(2,1)S(1)}, bf16[48,2400]{1,0:T(8,128)(2,1)S(1)}, u32[]{:S(2)}, u32[]{:S(2)}) collective-permute-start(bf16[48,2400]{1,0:T(8,128)(2,1)S(1)} %get-tuple-element.50), channel_id=1, source_target_pairs={{0,1},{1,2},{2,3},{3,0},{4,5},{5,6},{6,7},{7,4},{8,9},{9,10},{10,1... | collective-permute-start | bytes 691208 | tf_op jit(solution)/shard_map/ppermute | solution.py:277
  31.4 8.1 %collective-permute-start.15 = (bf16[200,2400]{1,0:T(8,128)(2,1)S(1)}, bf16[200,2400]{1,0:T(8,128)(2,1)S(1)}, u32[]{:S(2)}, u32[]{:S(2)}) collective-permute-start(bf16[200,2400]{1,0:T(8,128)(2,1)S(1)} %constant_dynamic-update-slice_fusion.2.b0), channel_id=1, source_target_pairs={{0,8},{8,0},{1,9},{9,1},{2,10},{10,2},{3,11},{11,3},{4,12},{12,4},... | collective-permute-start | bytes 2880008 | tf_op jit(solution)/shard_map/ppermute | solution.py:287
  34.1 9.8 %collective-permute-start.9 = (bf16[24,2400]{1,0:T(8,128)(2,1)S(1)}, bf16[24,2400]{1,0:T(8,128)(2,1)S(1)}, u32[]{:S(2)}, u32[]{:S(2)}) collective-permute-start(bf16[24,2400]{1,0:T(8,128)(2,1)S(1)} %slice.34), channel_id=1, source_target_pairs={{0,16},{16,32},{32,48},{48,64},{64,80},{80,96},{96,112},{112,0},{1... | collective-permute-start | bytes 345608 | tf_op jit(solution)/shard_map/ppermute | solution.py:313
  34.2 9.7 %collective-permute-start.14 = (bf16[32,2400]{1,0:T(8,128)(2,1)S(1)}, bf16[32,2400]{1,0:T(8,128)(2,1)S(1)}, u32[]{:S(2)}, u32[]{:S(2)}) collective-permute-start(bf16[32,2400]{1,0:T(8,128)(2,1)S(1)} %get-tuple-element.51), channel_id=1, source_target_pairs={{1,0},{2,1},{3,2},{0,3},{5,4},{6,5},{7,6},{4,7},{9,8},{10,9},{11,1... | collective-permute-start | bytes 460808 | tf_op jit(solution)/shard_map/ppermute | solution.py:283
  37.3 6.7 %collective-permute-start.13 = (bf16[32,2400]{1,0:T(8,128)(2,1)S(1)}, bf16[32,2400]{1,0:T(8,128)(2,1)S(1)}, u32[]{:S(2)}, u32[]{:S(2)}) collective-permute-start(bf16[32,2400]{1,0:T(8,128)(2,1)S(1)} %get-tuple-element.52), channel_id=1, source_target_pairs={{0,1},{1,2},{2,3},{3,0},{4,5},{5,6},{6,7},{7,4},{8,9},{9,10},{10,1... | collective-permute-start | bytes 460808 | tf_op jit(solution)/shard_map/ppermute | solution.py:282
  39.5 4.4 %collective-permute-start.10 = (bf16[16,2400]{1,0:T(8,128)(2,1)S(1)}, bf16[16,2400]{1,0:T(8,128)(2,1)S(1)}, u32[]{:S(2)}, u32[]{:S(2)}) collective-permute-start(bf16[16,2400]{1,0:T(8,128)(2,1)S(1)} %slice.35), channel_id=1, source_target_pairs={{16,0},{32,16},{48,32},{64,48},{80,64},{96,80},{112,96},{0,112},{1... | collective-permute-start | bytes 230408 | tf_op jit(solution)/shard_map/ppermute | solution.py:314
  44.1 4.6 %collective-permute-start.18 = (bf16[120,2400]{1,0:T(8,128)(2,1)S(1)}, bf16[120,2400]{1,0:T(8,128)(2,1)S(1)}, u32[]{:S(2)}, u32[]{:S(2)}) collective-permute-start(bf16[120,2400]{1,0:T(8,128)(2,1)S(1)} %pad_maximum_fusion.1.b0), channel_id=1, source_target_pairs={{0,8},{8,0},{1,9},{9,1},{2,10},{10,2},{3,11},{11,3},{4,12},{12,4},... | collective-permute-start | bytes 1728008 | tf_op jit(solution)/shard_map/ppermute | solution.py:320
  46.4 11.5 %collective-permute-start.16 = (bf16[160,2400]{1,0:T(8,128)(2,1)S(1)}, bf16[160,2400]{1,0:T(8,128)(2,1)}, u32[]{:S(2)}, u32[]{:S(2)}) collective-permute-start(bf16[160,2400]{1,0:T(8,128)(2,1)S(1)} %constant_dynamic-update-slice_fusion.far_a), channel_id=1, source_target_pairs={{0,8},{8,0},{1,9},{9,1},{2,10},{10,2},{3,11},{11,3},{4,12},{12,4},... | collective-permute-start | bytes 2304008 | tf_op jit(solution)/shard_map/ppermute | solution.py:322
  46.5 11.4 %collective-permute-start.17 = (bf16[160,2400]{1,0:T(8,128)(2,1)S(1)}, bf16[160,2400]{1,0:T(8,128)(2,1)}, u32[]{:S(2)}, u32[]{:S(2)}) collective-permute-start(bf16[160,2400]{1,0:T(8,128)(2,1)S(1)} %pad_maximum_fusion.far_b), channel_id=1, source_target_pairs={{0,8},{8,0},{1,9},{9,1},{2,10},{10,2},{3,11},{11,3},{4,12},{12,4},... | collective-permute-start | bytes 2304008 | tf_op jit(solution)/shard_map/ppermute | solution.py:322
  50.7 6.5 %collective-permute-start.19 = (f32[200,128]{1,0:T(8,128)S(1)}, f32[200,128]{1,0:T(8,128)S(1)}, u32[]{:S(2)}, u32[]{:S(2)}) collective-permute-start(f32[200,128]{1,0:T(8,128)S(1)} %last_terms.1.t), channel_id=1, source_target_pairs={{0,128},{128,0},{1,129},{129,1},{2,130},{130,2},{3,131},{131,3},{4... | collective-permute-start | bytes 307208 | tf_op jit(solution)/shard_map/ppermute | solution.py:334
  54.1 3.8 %collective-permute-start.20 = (f32[200,128]{1,0:T(8,128)S(1)}, f32[200,128]{1,0:T(8,128)S(1)}, u32[]{:S(2)}, u32[]{:S(2)}) collective-permute-start(f32[200,128]{1,0:T(8,128)S(1)} %last_terms.1.t), channel_id=1, source_target_pairs={{0,8},{8,0},{1,9},{9,1},{2,10},{10,2},{3,11},{11,3},{4,12},{12,4},... | collective-permute-start | bytes 307208 | tf_op jit(solution)/shard_map/ppermute | solution.py:335
  57.2 1.6 %collective-permute-start.21 = (f32[200,128]{1,0:T(8,128)S(1)}, f32[200,128]{1,0:T(8,128)S(1)}, u32[]{:S(2)}, u32[]{:S(2)}) collective-permute-start(f32[200,128]{1,0:T(8,128)S(1)} %collective-permute-done.19.t_yh), channel_id=1, source_target_pairs={{0,8},{8,0},{1,9},{9,1},{2,10},{10,2},{3,11},{11,3},{4,12},{12,4},... | collective-permute-start | bytes 307208 | tf_op jit(solution)/shard_map/ppermute | solution.py:336
  57.9 10.2 %copy-start.8 = (s32[2,30]{1,0:T(2,128)S(1)}, s32[2,30]{1,0:T(2,128)}, u32[]{:S(2)}) copy-start(s32[2,30]{1,0:T(2,128)} %param.11) | copy-start | bytes 724
  58.8 1.4 %copy-start.2 = (bf16[2,160,2400]{2,1,0:T(8,128)(2,1)S(1)}, bf16[2,160,2400]{2,1,0:T(8,128)(2,1)}, u32[]{:S(2)}) copy-start(bf16[2,160,2400]{2,1,0:T(8,128)(2,1)} %copy-done.1) | copy-start | bytes 4608004
  64.4 11.3 %all-to-all-start = ((s16[8,56,128]{2,1,0:T(8,128)(2,1)}), s16[8,56,128]{2,1,0:T(8,128)(2,1)S(1)}, u32[]{:S(2)}, u32[]{:S(2)}) async-start(s16[8,56,128]{2,1,0:T(8,128)(2,1)} %bitcast.3), calls=%async_computation | async-start | bytes 229376 | tf_op jit(solution)/shard_map/all_to_all | solution.py:358

commit v14 on v13

--- a/solution.py
+++ b/solution.py
@@ -257,9 +257,7 @@
     left = [(j, i) for i, j in right]
     vmem, smem = pltpu.VMEM, pltpu.SMEM
 
-    half = lax.dynamic_index_in_dim(own, odd_x(), 0, keepdims=False)
-    rows_1, rows_2 = 3 * occupied // 5, 2 * occupied // 5
-    far_1 = lax.ppermute(half[:rows_1], "yh", swap)
+    far_a = lax.ppermute(lax.dynamic_index_in_dim(own, odd_x(), 0, keepdims=False), "yh", swap)
     near = lax.ppermute(own, "core", swap)
     block = lax.dynamic_slice_in_dim(own, band * width, width, 1).reshape(group, functions)
     blocks = [block]
@@ -268,20 +266,14 @@
     for step in range(1, PARTS[1] // 2):
         from_below = lax.ppermute(from_below, "z", up)
         from_above = lax.ppermute(from_above, "z", down)
-        if step == 1:
-            half_2, _ = lax.optimization_barrier((half[rows_1:], from_below))
-            far_2 = lax.ppermute(half_2, "yh", swap)
         if step == 2:
-            held = (from_below, from_above, near, far_1)
-            from_below, from_above, near, far_1 = lax.optimization_barrier(held)
-            left_1 = lax.ppermute(far_1[: rows_1 // 2], "x", right)
-            right_1 = lax.ppermute(far_1[rows_1 // 2 :], "x", left)
+            from_below, from_above, near = lax.optimization_barrier((from_below, from_above, near))
         if step == 3:
-            from_below, from_above, far_2 = lax.optimization_barrier((from_below, from_above, far_2))
+            from_below, from_above, far_a = lax.optimization_barrier((from_below, from_above, far_a))
         blocks += [from_below, from_above]
-    left_2 = lax.ppermute(far_2[: rows_2 // 2], "x", right)
-    right_2 = lax.ppermute(far_2[rows_2 // 2 :], "x", left)
-    far_a = jnp.concatenate([far_1, far_2], 0)
+    mid = occupied // 2
+    from_left = lax.ppermute(far_a[:mid], "x", right)
+    from_right = lax.ppermute(far_a[mid:], "x", left)
     split = 5
     first = jnp.concatenate(blocks[:split], 0)
     first_near = lax.ppermute(first, "core", swap)
@@ -312,10 +304,10 @@
     cut = 24
     blocks.append(lax.ppermute(from_below[:cut], "z", up))
     blocks.append(lax.ppermute(from_above[cut:], "z", down))
-    held = (blocks[-2], blocks[-1], left_1, right_1, left_2, right_2, t_own)
-    blocks[-2], blocks[-1], left_1, right_1, left_2, right_2, t_own = lax.optimization_barrier(held)
+    held = (blocks[-2], blocks[-1], from_left, from_right, t_own)
+    blocks[-2], blocks[-1], from_left, from_right, t_own = lax.optimization_barrier(held)
     last = jnp.concatenate(blocks[split:], 0)
-    far_b = jnp.concatenate([left_1, right_1, left_2, right_2], 0)
+    far_b = jnp.concatenate([from_left, from_right], 0)
     last, far_b = lax.optimization_barrier((last, far_b))
     last_near = lax.ppermute(last, "core", swap)
     later_a, _ = lax.optimization_barrier((far_a, far_b))

time: 77.9 us -> 73.3 us (0.941)
  waiting for transfers between devices: 15.9 us -> 23.2 us
  starting transfers between devices: 41.3 us -> 35 us
  local copies, waits for them, and re-layouts: 7.73 us -> 2.48 us
    ppermute x6 -> x3, waiting for transfers between devices: 0.99 us -> 6.93 us  [the longest x1 4.45 us: shards(): lax.ppermute(lax.dynamic_index_in_dim(own, odd_x(), 0, keepdims=False), '...]
    ppermute x6 -> x3, starting transfers between devices: 11.4 us -> 5.75 us  [the longest x1 3 us: shards(): lax.ppermute(lax.dynamic_index_in_dim(own, odd_x(), 0, keepdims=False), '...]
    unnamed x23 -> x18, local copies, waits for them, and re-layouts: 3.51 us -> 0.12 us
    ppermute x3, waiting for transfers between devices: 2.02 us -> 5.18 us  [shards(): from_below = lax.ppermute(from_below, 'z', up)]
    ppermute x3, starting transfers between devices: 12.2 us -> 9.26 us  [shards(): from_above = lax.ppermute(from_above, 'z', down)]
    slice x4 -> x1, local copies, waits for them, and re-layouts: 2.96 us -> 0.06 us  [shards(): from_right = lax.ppermute(far_a[mid:], 'x', left)]
    ppermute x1, starting transfers between devices: 0.96 us -> 3.24 us  [shards(): near = lax.ppermute(own, 'core', swap)]
    ppermute x3, waiting for transfers between devices: 1.63 us -> 0.01 us  [shards(): from_above = lax.ppermute(from_above, 'z', down)]
  transfers between devices with their start and end apart: 23 -> 20, of which waited for: 7 -> 7; matrix products, arithmetic and copies ran while one was open for 7% -> 4% of each run, Pallas kernels for 8% -> 9%
where the time goes in v14:
time: 73.3 us; the launch traced here: 72.4 us
  starting transfers between devices  35 us (48%)
  waiting for transfers between devices  23.2 us (32%)
  Pallas kernels  11.2 us (15%)
  local copies, waits for them, and re-layouts  2.48 us (3%)
    ppermute x3, starting transfers between devices, shards(): from_above = lax.ppermute(from_above, 'z', down)  9.26 us
    all_to_all x1, waiting for transfers between devices, shards(): arrived = lax.all_to_all(pieces, 'z', 0, 0, tiled=True)  7.51 us
    ppermute x3, waiting for transfers between devices, shards(): from_below = lax.ppermute(from_below, 'z', up)  5.18 us
    all_to_all x1, starting transfers between devices, shards(): arrived = lax.all_to_all(pieces, 'z', 0, 0, tiled=True)  4.9 us
    ppermute x1, waiting for transfers between devices, shards(): lax.ppermute(lax.dynamic_index_in_dim(own, odd_x(), 0, keepdims=False), '...  4.45 us
    pallas_call x1, Pallas kernels, shards(): call(functools.partial(cluster_kernel, width, columns), 'cluster_terms',...  4.19 us
    ppermute x1, starting transfers between devices, shards(): near = lax.ppermute(own, 'core', swap)  3.24 us
    ppermute x1, starting transfers between devices, shards(): t_yh = lax.ppermute(t, 'yh', swap)  3.02 us
  transfers between devices with their start and end apart: 20, of which 7 were waited for; matrix products, arithmetic and copies ran while one was open for 4% of the time, Pallas kernels for 9%

profile of v14, /device:TPU:1, one launch (start us, length us, event | category | flops | bytes accessed | tf_op | source)
XLA Modules:
  0.0 72.4 jit_solution(16644459776901139171)
XLA Ops:
  0.0 3.2 %collective-permute-start.4 = (bf16[2,160,2400]{2,1,0:T(8,128)(2,1)}, bf16[2,160,2400]{2,1,0:T(8,128)(2,1)}, u32[]{:S(2)}, u32[]{:S(2)}) collective-permute-start(bf16[2,160,2400]{2,1,0:T(8,128)(2,1)} %bitcast.7), channel_id=1, source_target_pairs={{0,8},{8,0},{1,9},{9,1},{2,10},{10,2},{3,11},{11,3},{4,12},{12,4},... | collective-permute-start | bytes 4608008 | tf_op jit(solution)/shard_map/ppermute | solution.py:261
  3.2 1.0 %constant_dynamic-slice_fusion = bf16[1,2,20,2400]{3,2,1,0:T(8,128)(2,1)S(1)} fusion(bf16[1,2,160,2400]{3,2,1,0:T(8,128)(2,1)} %param.7, s32[]{:T(128)S(6)} %select_n.16), kind=kLoop, calls=%fused_computation.13 | loop fusion | bytes 384004 | tf_op jit(solution)/shard_map/dynamic_slice | solution.py:262
  4.4 3.9 %collective-permute-start.2 = (bf16[40,2400]{1,0:T(8,128)(2,1)S(1)}, bf16[40,2400]{1,0:T(8,128)(2,1)S(1)}, u32[]{:S(2)}, u32[]{:S(2)}) collective-permute-start(bf16[40,2400]{1,0:T(8,128)(2,1)S(1)} %reshape.22), channel_id=1, source_target_pairs={{16,0},{32,16},{48,32},{64,48},{80,64},{96,80},{112,96},{0,112},{1... | collective-permute-start | bytes 576008 | tf_op jit(solution)/shard_map/ppermute | solution.py:268
  8.3 1.2 %dynamic-slice_bitcast_fusion = bf16[160,2400]{1,0:T(8,128)(2,1)S(1)} fusion(bf16[1,2,160,2400]{3,2,1,0:T(8,128)(2,1)} %param.7, s32[]{:T(128)S(6)} %select_n.17), kind=kLoop, calls=%fused_computation.2 | loop fusion | bytes 1536004 | tf_op jit(solution)/shard_map/jit(dynamic_index_in_dim)/squeeze | solution.py:260
  9.5 3.0 %collective-permute-start.7 = (bf16[160,2400]{1,0:T(8,128)(2,1)S(1)}, bf16[160,2400]{1,0:T(8,128)(2,1)S(1)}, u32[]{:S(2)}, u32[]{:S(2)}) collective-permute-start(bf16[160,2400]{1,0:T(8,128)(2,1)S(1)} %dynamic-slice_bitcast_fusion), channel_id=1, source_target_pairs={{0,128},{128,0},{1,129},{129,1},{2,130},{130,2},{3,131},{131,3},{4... | collective-permute-start | bytes 2304008 | tf_op jit(solution)/shard_map/ppermute | solution.py:260
  12.5 0.9 %collective-permute-done = bf16[40,2400]{1,0:T(8,128)(2,1)S(1)} collective-permute-done((bf16[40,2400]{1,0:T(8,128)(2,1)S(1)}, bf16[40,2400]{1,0:T(8,128)(2,1)S(1)}, u32[]{:S(2)}, u32[]{:S(2)}) %collective-permute-start) | collective-permute-done | bytes 192032 | tf_op jit(solution)/shard_map/ppermute | solution.py:267
  13.5 2.7 %collective-permute-start.3 = (bf16[40,2400]{1,0:T(8,128)(2,1)S(1)}, bf16[40,2400]{1,0:T(8,128)(2,1)S(1)}, u32[]{:S(2)}, u32[]{:S(2)}) collective-permute-start(bf16[40,2400]{1,0:T(8,128)(2,1)S(1)} %collective-permute-done.2), channel_id=1, source_target_pairs={{16,0},{32,16},{48,32},{64,48},{80,64},{96,80},{112,96},{0,112},{1... | collective-permute-start | bytes 576008 | tf_op jit(solution)/shard_map/ppermute | solution.py:268
  16.3 4.2 %collective-permute-done.1 = bf16[40,2400]{1,0:T(8,128)(2,1)S(1)} collective-permute-done((bf16[40,2400]{1,0:T(8,128)(2,1)S(1)}, bf16[40,2400]{1,0:T(8,128)(2,1)S(1)}, u32[]{:S(2)}, u32[]{:S(2)}) %collective-permute-start.1) | collective-permute-done | bytes 192032 | tf_op jit(solution)/shard_map/ppermute | solution.py:267
  20.5 2.7 %collective-permute-start.6 = (bf16[40,2400]{1,0:T(8,128)(2,1)S(1)}, bf16[40,2400]{1,0:T(8,128)(2,1)S(1)}, u32[]{:S(2)}, u32[]{:S(2)}) collective-permute-start(bf16[40,2400]{1,0:T(8,128)(2,1)S(1)} %collective-permute-done.3), channel_id=1, source_target_pairs={{16,0},{32,16},{48,32},{64,48},{80,64},{96,80},{112,96},{0,112},{1... | collective-permute-start | bytes 576008 | tf_op jit(solution)/shard_map/ppermute | solution.py:268
  23.3 2.1 %collective-permute-start.12 = (bf16[200,2400]{1,0:T(8,128)(2,1)S(1)}, bf16[200,2400]{1,0:T(8,128)(2,1)S(1)}, u32[]{:S(2)}, u32[]{:S(2)}) collective-permute-start(bf16[200,2400]{1,0:T(8,128)(2,1)S(1)} %constant_dynamic-update-slice_fusion.b0), channel_id=1, source_target_pairs={{0,8},{8,0},{1,9},{9,1},{2,10},{10,2},{3,11},{11,3},{4,12},{12,4},... | collective-permute-start | bytes 2880008 | tf_op jit(solution)/shard_map/ppermute | solution.py:279
  25.3 4.5 %collective-permute-done.7.far_a = bf16[160,2400]{1,0:T(8,128)(2,1)S(1)} collective-permute-done((bf16[160,2400]{1,0:T(8,128)(2,1)S(1)}, bf16[160,2400]{1,0:T(8,128)(2,1)S(1)}, u32[]{:S(2)}, u32[]{:S(2)}) %collective-permute-start.7) | collective-permute-done | bytes 768032 | tf_op jit(solution)/shard_map/ppermute | solution.py:260
  29.9 1.3 %collective-permute-start.10 = (bf16[80,2400]{1,0:T(8,128)(2,1)S(1)}, bf16[80,2400]{1,0:T(8,128)(2,1)S(1)}, u32[]{:S(2)}, u32[]{:S(2)}) collective-permute-start(bf16[80,2400]{1,0:T(8,128)(2,1)S(1)} %get-tuple-element.42), channel_id=1, source_target_pairs={{0,1},{1,2},{2,3},{3,0},{4,5},{5,6},{6,7},{7,4},{8,9},{9,10},{10,1... | collective-permute-start | bytes 1152008 | tf_op jit(solution)/shard_map/ppermute | solution.py:275
  31.2 1.5 %collective-permute-start.11 = (bf16[80,2400]{1,0:T(8,128)(2,1)S(1)}, bf16[80,2400]{1,0:T(8,128)(2,1)S(1)}, u32[]{:S(2)}, u32[]{:S(2)}) collective-permute-start(bf16[80,2400]{1,0:T(8,128)(2,1)S(1)} %get-tuple-element.41), channel_id=1, source_target_pairs={{1,0},{2,1},{3,2},{0,3},{5,4},{6,5},{7,6},{4,7},{9,8},{10,9},{11,1... | collective-permute-start | bytes 1152008 | tf_op jit(solution)/shard_map/ppermute | solution.py:276
  32.8 1.1 %phases.1 = (f32[2,640,1]{2,1,0:T(8,128)S(1)}, bf16[160,400]{1,0:T(8,128)(2,1)S(1)}, bf16[160,240]{1,0:T(8,128)(2,1)S(1)}) custom-call(s32[2]{0:T(128)S(1)} %copy-done.2, s32[32,32]{1,0:T(8,128)S(1)} %copy-done.1, f32[32]{0:T(128)S(1)} %copy-done.3, f32[32]{0:T(128)S(1)} %copy-done.4, f32[32]{0:T(128)S(1)} %copy-done.5), custom_call_target="tpu_custom_call" | custom-call | bytes 1048576 | tf_op jit(solution)/shard_map/phases/pallas_call | solution.py:288
  33.9 2.7 %collective-permute-start.9 = (bf16[16,2400]{1,0:T(8,128)(2,1)S(1)}, bf16[16,2400]{1,0:T(8,128)(2,1)S(1)}, u32[]{:S(2)}, u32[]{:S(2)}) collective-permute-start(bf16[16,2400]{1,0:T(8,128)(2,1)S(1)} %slice.13), channel_id=1, source_target_pairs={{16,0},{32,16},{48,32},{64,48},{80,64},{96,80},{112,96},{0,112},{1... | collective-permute-start | bytes 230408 | tf_op jit(solution)/shard_map/ppermute | solution.py:306
  36.6 1.4 %own_first.1.t_own = f32[80,160]{1,0:T(8,128)S(1)} custom-call(bf16[2,160,2400]{2,1,0:T(8,128)(2,1)S(1)} %bitcast.8, bf16[200,2400]{1,0:T(8,128)(2,1)S(1)} %constant_dynamic-update-slice_fusion.b0, bf16[200,2400]{1,0:T(8,128)(2,1)S(1)} %collective-permute-done.12.b1, f32[2,640,1]{2,1,0:T(8,128)S(1)} %get-tuple-element.29.w, ...), custom_call_target="tpu_custom_call" | custom-call | flops 1000000000 | bytes 1048576 | tf_op jit(solution)/shard_map/own_first/pallas_call | solution.py:303
  38.1 2.5 %collective-permute-done.10 = bf16[80,2400]{1,0:T(8,128)(2,1)S(1)} collective-permute-done((bf16[80,2400]{1,0:T(8,128)(2,1)S(1)}, bf16[80,2400]{1,0:T(8,128)(2,1)S(1)}, u32[]{:S(2)}, u32[]{:S(2)}) %collective-permute-start.10) | collective-permute-done | bytes 384032 | tf_op jit(solution)/shard_map/ppermute | solution.py:275
  40.7 2.1 %collective-permute-start.15 = (bf16[120,2400]{1,0:T(8,128)(2,1)S(1)}, bf16[120,2400]{1,0:T(8,128)(2,1)S(1)}, u32[]{:S(2)}, u32[]{:S(2)}) collective-permute-start(bf16[120,2400]{1,0:T(8,128)(2,1)S(1)} %pad_maximum_fusion.1.b0), channel_id=1, source_target_pairs={{0,8},{8,0},{1,9},{9,1},{2,10},{10,2},{3,11},{11,3},{4,12},{12,4},... | collective-permute-start | bytes 1728008 | tf_op jit(solution)/shard_map/ppermute | solution.py:312
  42.8 0.1 collective-permute-start.13
  42.9 0.4 collective-permute-start.14
  43.3 1.6 %far_first.1.t_far = f32[80,160]{1,0:T(8,128)S(1)} custom-call(bf16[160,2400]{1,0:T(8,128)(2,1)S(1)} %collective-permute-done.7.far_a, bf16[160,2400]{1,0:T(8,128)(2,1)S(1)} %pad_maximum_fusion.far_b, bf16[200,2400]{1,0:T(8,128)(2,1)S(1)} %constant_dynamic-update-slice_fusion.b0, bf16[200,2400]{1,0:T(8,128)(2,1)S(1)} %collective-permute-done.12.b1, ...), custom_call_target="tpu_custom_call" | custom-call | flops 1000000000 | bytes 1048576 | tf_op jit(solution)/shard_map/far_first/pallas_call | solution.py:316
  45.0 2.0 %last_terms.1.t = f32[200,128]{1,0:T(8,128)S(1)} custom-call(bf16[2,160,2400]{2,1,0:T(8,128)(2,1)S(1)} %bitcast.9, bf16[160,2400]{1,0:T(8,128)(2,1)S(1)} %collective-permute-done.7.far_a, bf16[160,2400]{1,0:T(8,128)(2,1)S(1)} %pad_maximum_fusion.far_b, bf16[120,2400]{1,0:T(8,128)(2,1)S(1)} %pad_maximum_fusion.1.b0, ...), custom_call_target="tpu_custom_call" | custom-call | flops 1000000000 | bytes 1048576 | tf_op jit(solution)/shard_map/last_terms/pallas_call | solution.py:317
  47.0 3.0 %collective-permute-start.16 = (f32[200,128]{1,0:T(8,128)S(1)}, f32[200,128]{1,0:T(8,128)S(1)}, u32[]{:S(2)}, u32[]{:S(2)}) collective-permute-start(f32[200,128]{1,0:T(8,128)S(1)} %last_terms.1.t), channel_id=1, source_target_pairs={{0,128},{128,0},{1,129},{129,1},{2,130},{130,2},{3,131},{131,3},{4... | collective-permute-start | bytes 307208 | tf_op jit(solution)/shard_map/ppermute | solution.py:326
  50.0 0.4 collective-permute-start.17
  50.3 2.7 %collective-permute-done.16.t_yh = f32[200,128]{1,0:T(8,128)S(1)} collective-permute-done((f32[200,128]{1,0:T(8,128)S(1)}, f32[200,128]{1,0:T(8,128)S(1)}, u32[]{:S(2)}, u32[]{:S(2)}) %collective-permute-start.16) | collective-permute-done | bytes 102432 | tf_op jit(solution)/shard_map/ppermute | solution.py:326
  53.0 0.9 %collective-permute-start.18 = (f32[200,128]{1,0:T(8,128)S(1)}, f32[200,128]{1,0:T(8,128)S(1)}, u32[]{:S(2)}, u32[]{:S(2)}) collective-permute-start(f32[200,128]{1,0:T(8,128)S(1)} %collective-permute-done.16.t_yh), channel_id=1, source_target_pairs={{0,8},{8,0},{1,9},{9,1},{2,10},{10,2},{3,11},{11,3},{4,12},{12,4},... | collective-permute-start | bytes 307208 | tf_op jit(solution)/shard_map/ppermute | solution.py:328
  53.9 0.9 %collective-permute-done.18.t_diag = f32[200,128]{1,0:T(8,128)S(1)} collective-permute-done((f32[200,128]{1,0:T(8,128)S(1)}, f32[200,128]{1,0:T(8,128)S(1)}, u32[]{:S(2)}, u32[]{:S(2)}) %collective-permute-start.18) | collective-permute-done | bytes 102432 | tf_op jit(solution)/shard_map/ppermute | solution.py:328
  54.8 4.2 %cluster_terms.1 = s16[448,128]{1,0:T(8,128)(2,1)} custom-call(bf16[2,160,2400]{2,1,0:T(8,128)(2,1)S(1)} %bitcast.10, bf16[160,2400]{1,0:T(8,128)(2,1)S(1)} %collective-permute-done.7.far_a, bf16[160,2400]{1,0:T(8,128)(2,1)S(1)} %pad_maximum_fusion.far_b, bf16[2,160,2400]{2,1,0:T(8,128)(2,1)} %collective-permute-done.4.near_hbm, ...), custom_call_target="tpu_custom_call" | custom-call | flops 1000000000 | bytes 1048576 | tf_op jit(solution)/shard_map/cluster_terms/pallas_call | solution.py:333
  59.0 4.9 %all-to-all-start = ((s16[8,56,128]{2,1,0:T(8,128)(2,1)}), s16[8,56,128]{2,1,0:T(8,128)(2,1)S(1)}, u32[]{:S(2)}, u32[]{:S(2)}) async-start(s16[8,56,128]{2,1,0:T(8,128)(2,1)} %bitcast.2), calls=%async_computation | async-start | bytes 229376 | tf_op jit(solution)/shard_map/all_to_all | solution.py:350
  63.9 0.1 convolution_bitcast_fusion.mask
  64.0 7.5 %all-to-all-done.arrived = s16[8,56,128]{2,1,0:T(8,128)(2,1)S(1)} async-done(((s16[8,56,128]{2,1,0:T(8,128)(2,1)}), s16[8,56,128]{2,1,0:T(8,128)(2,1)S(1)}, u32[]{:S(2)}, u32[]{:S(2)}) %all-to-all-start) | async-done | bytes 114720 | tf_op jit(solution)/shard_map/all_to_all | solution.py:350
  71.5 0.8 %sum_and_mask.1 = f32[2,20,2,75]{3,2,1,0:T(2,128)} custom-call(s16[8,56,128]{2,1,0:T(8,128)(2,1)S(1)} %all-to-all-done.arrived, f32[2,75]{1,0:T(2,128)S(1)} %convolution_bitcast_fusion.mask), custom_call_target="tpu_custom_call" | custom-call | bytes 1048576 | tf_op jit(solution)/shard_map/sum_and_mask/pallas_call | solution.py:357
  (43 shorter events, 0.6 us)
Async XLA Ops:
  0.0 20.5 %collective-permute-start.4 = (bf16[2,160,2400]{2,1,0:T(8,128)(2,1)}, bf16[2,160,2400]{2,1,0:T(8,128)(2,1)}, u32[]{:S(2)}, u32[]{:S(2)}) collective-permute-start(bf16[2,160,2400]{2,1,0:T(8,128)(2,1)} %bitcast.7), channel_id=1, source_target_pairs={{0,8},{8,0},{1,9},{9,1},{2,10},{10,2},{3,11},{11,3},{4,12},{12,4},... | collective-permute-start | bytes 4608008 | tf_op jit(solution)/shard_map/ppermute | solution.py:261
  4.3 9.1 %collective-permute-start = (bf16[40,2400]{1,0:T(8,128)(2,1)S(1)}, bf16[40,2400]{1,0:T(8,128)(2,1)S(1)}, u32[]{:S(2)}, u32[]{:S(2)}) collective-permute-start(bf16[40,2400]{1,0:T(8,128)(2,1)S(1)} %reshape.22), channel_id=1, source_target_pairs={{0,16},{16,32},{32,48},{48,64},{64,80},{80,96},{96,112},{112,0},{1... | collective-permute-start | bytes 576008 | tf_op jit(solution)/shard_map/ppermute | solution.py:267
  4.4 9.1 %collective-permute-start.2 = (bf16[40,2400]{1,0:T(8,128)(2,1)S(1)}, bf16[40,2400]{1,0:T(8,128)(2,1)S(1)}, u32[]{:S(2)}, u32[]{:S(2)}) collective-permute-start(bf16[40,2400]{1,0:T(8,128)(2,1)S(1)} %reshape.22), channel_id=1, source_target_pairs={{16,0},{32,16},{48,32},{64,48},{80,64},{96,80},{112,96},{0,112},{1... | collective-permute-start | bytes 576008 | tf_op jit(solution)/shard_map/ppermute | solution.py:268
  9.5 20.3 %collective-permute-start.7 = (bf16[160,2400]{1,0:T(8,128)(2,1)S(1)}, bf16[160,2400]{1,0:T(8,128)(2,1)S(1)}, u32[]{:S(2)}, u32[]{:S(2)}) collective-permute-start(bf16[160,2400]{1,0:T(8,128)(2,1)S(1)} %dynamic-slice_bitcast_fusion), channel_id=1, source_target_pairs={{0,128},{128,0},{1,129},{129,1},{2,130},{130,2},{3,131},{131,3},{4... | collective-permute-start | bytes 2304008 | tf_op jit(solution)/shard_map/ppermute | solution.py:260
  13.5 7.0 %collective-permute-start.1 = (bf16[40,2400]{1,0:T(8,128)(2,1)S(1)}, bf16[40,2400]{1,0:T(8,128)(2,1)S(1)}, u32[]{:S(2)}, u32[]{:S(2)}) collective-permute-start(bf16[40,2400]{1,0:T(8,128)(2,1)S(1)} %collective-permute-done), channel_id=1, source_target_pairs={{0,16},{16,32},{32,48},{48,64},{64,80},{80,96},{96,112},{112,0},{1... | collective-permute-start | bytes 576008 | tf_op jit(solution)/shard_map/ppermute | solution.py:267
  13.5 7.0 %collective-permute-start.3 = (bf16[40,2400]{1,0:T(8,128)(2,1)S(1)}, bf16[40,2400]{1,0:T(8,128)(2,1)S(1)}, u32[]{:S(2)}, u32[]{:S(2)}) collective-permute-start(bf16[40,2400]{1,0:T(8,128)(2,1)S(1)} %collective-permute-done.2), channel_id=1, source_target_pairs={{16,0},{32,16},{48,32},{64,48},{80,64},{96,80},{112,96},{0,112},{1... | collective-permute-start | bytes 576008 | tf_op jit(solution)/shard_map/ppermute | solution.py:268
  16.2 16.5 %copy-start.1 = (s32[32,32]{1,0:T(8,128)S(1)}, s32[32,32]{1,0:T(8,128)}, u32[]{:S(2)}) copy-start(s32[32,32]{1,0:T(8,128)} %diff_class.1) | copy-start | bytes 12292
  16.2 16.5 %copy-start.2 = (s32[2]{0:T(128)S(1)}, s32[2]{0:T(128)}, u32[]{:S(2)}) copy-start(s32[2]{0:T(128)} %cells) | copy-start | bytes 28
  16.2 16.5 %copy-start.3 = (f32[32]{0:T(128)S(1)}, f32[32]{0:T(128)}, u32[]{:S(2)}) copy-start(f32[32]{0:T(128)} %class_weight.1) | copy-start | bytes 388
  16.2 16.5 %copy-start.4 = (f32[32]{0:T(128)S(1)}, f32[32]{0:T(128)}, u32[]{:S(2)}) copy-start(f32[32]{0:T(128)} %constant.55.clone.cos_table) | copy-start | bytes 388
  16.2 16.5 %copy-start.5 = (f32[32]{0:T(128)S(1)}, f32[32]{0:T(128)}, u32[]{:S(2)}) copy-start(f32[32]{0:T(128)} %constant.56.clone.sin_table) | copy-start | bytes 388
  16.2 20.4 %copy-start = (bf16[1,2,160,2400]{3,2,1,0:T(8,128)(2,1)S(1)}, bf16[1,2,160,2400]{3,2,1,0:T(8,128)(2,1)}, u32[]{:S(2)}) copy-start(bf16[1,2,160,2400]{3,2,1,0:T(8,128)(2,1)} %param.7) | copy-start | bytes 4608004
  20.5 9.3 %collective-permute-start.5 = (bf16[40,2400]{1,0:T(8,128)(2,1)S(1)}, bf16[40,2400]{1,0:T(8,128)(2,1)S(1)}, u32[]{:S(2)}, u32[]{:S(2)}) collective-permute-start(bf16[40,2400]{1,0:T(8,128)(2,1)S(1)} %collective-permute-done.1), channel_id=1, source_target_pairs={{0,16},{16,32},{32,48},{48,64},{64,80},{80,96},{96,112},{112,0},{1... | collective-permute-start | bytes 576008 | tf_op jit(solution)/shard_map/ppermute | solution.py:267
  20.5 9.3 %collective-permute-start.6 = (bf16[40,2400]{1,0:T(8,128)(2,1)S(1)}, bf16[40,2400]{1,0:T(8,128)(2,1)S(1)}, u32[]{:S(2)}, u32[]{:S(2)}) collective-permute-start(bf16[40,2400]{1,0:T(8,128)(2,1)S(1)} %collective-permute-done.3), channel_id=1, source_target_pairs={{16,0},{32,16},{48,32},{64,48},{80,64},{96,80},{112,96},{0,112},{1... | collective-permute-start | bytes 576008 | tf_op jit(solution)/shard_map/ppermute | solution.py:268
  23.3 13.4 %collective-permute-start.12 = (bf16[200,2400]{1,0:T(8,128)(2,1)S(1)}, bf16[200,2400]{1,0:T(8,128)(2,1)S(1)}, u32[]{:S(2)}, u32[]{:S(2)}) collective-permute-start(bf16[200,2400]{1,0:T(8,128)(2,1)S(1)} %constant_dynamic-update-slice_fusion.b0), channel_id=1, source_target_pairs={{0,8},{8,0},{1,9},{9,1},{2,10},{10,2},{3,11},{11,3},{4,12},{12,4},... | collective-permute-start | bytes 2880008 | tf_op jit(solution)/shard_map/ppermute | solution.py:279
  29.9 10.7 %collective-permute-start.10 = (bf16[80,2400]{1,0:T(8,128)(2,1)S(1)}, bf16[80,2400]{1,0:T(8,128)(2,1)S(1)}, u32[]{:S(2)}, u32[]{:S(2)}) collective-permute-start(bf16[80,2400]{1,0:T(8,128)(2,1)S(1)} %get-tuple-element.42), channel_id=1, source_target_pairs={{0,1},{1,2},{2,3},{3,0},{4,5},{5,6},{6,7},{7,4},{8,9},{9,10},{10,1... | collective-permute-start | bytes 1152008 | tf_op jit(solution)/shard_map/ppermute | solution.py:275
  31.2 9.4 %collective-permute-start.11 = (bf16[80,2400]{1,0:T(8,128)(2,1)S(1)}, bf16[80,2400]{1,0:T(8,128)(2,1)S(1)}, u32[]{:S(2)}, u32[]{:S(2)}) collective-permute-start(bf16[80,2400]{1,0:T(8,128)(2,1)S(1)} %get-tuple-element.41), channel_id=1, source_target_pairs={{1,0},{2,1},{3,2},{0,3},{5,4},{6,5},{7,6},{4,7},{9,8},{10,9},{11,1... | collective-permute-start | bytes 1152008 | tf_op jit(solution)/shard_map/ppermute | solution.py:276
  32.6 5.5 %collective-permute-start.8 = (bf16[24,2400]{1,0:T(8,128)(2,1)S(1)}, bf16[24,2400]{1,0:T(8,128)(2,1)S(1)}, u32[]{:S(2)}, u32[]{:S(2)}) collective-permute-start(bf16[24,2400]{1,0:T(8,128)(2,1)S(1)} %slice.12), channel_id=1, source_target_pairs={{0,16},{16,32},{32,48},{48,64},{64,80},{80,96},{96,112},{112,0},{1... | collective-permute-start | bytes 345608 | tf_op jit(solution)/shard_map/ppermute | solution.py:305
  33.9 4.2 %collective-permute-start.9 = (bf16[16,2400]{1,0:T(8,128)(2,1)S(1)}, bf16[16,2400]{1,0:T(8,128)(2,1)S(1)}, u32[]{:S(2)}, u32[]{:S(2)}) collective-permute-start(bf16[16,2400]{1,0:T(8,128)(2,1)S(1)} %slice.13), channel_id=1, source_target_pairs={{16,0},{32,16},{48,32},{64,48},{80,64},{96,80},{112,96},{0,112},{1... | collective-permute-start | bytes 230408 | tf_op jit(solution)/shard_map/ppermute | solution.py:306
  40.7 4.3 %collective-permute-start.15 = (bf16[120,2400]{1,0:T(8,128)(2,1)S(1)}, bf16[120,2400]{1,0:T(8,128)(2,1)S(1)}, u32[]{:S(2)}, u32[]{:S(2)}) collective-permute-start(bf16[120,2400]{1,0:T(8,128)(2,1)S(1)} %pad_maximum_fusion.1.b0), channel_id=1, source_target_pairs={{0,8},{8,0},{1,9},{9,1},{2,10},{10,2},{3,11},{11,3},{4,12},{12,4},... | collective-permute-start | bytes 1728008 | tf_op jit(solution)/shard_map/ppermute | solution.py:312
  42.8 11.1 %collective-permute-start.13 = (bf16[160,2400]{1,0:T(8,128)(2,1)S(1)}, bf16[160,2400]{1,0:T(8,128)(2,1)}, u32[]{:S(2)}, u32[]{:S(2)}) collective-permute-start(bf16[160,2400]{1,0:T(8,128)(2,1)S(1)} %collective-permute-done.7.far_a), channel_id=1, source_target_pairs={{0,8},{8,0},{1,9},{9,1},{2,10},{10,2},{3,11},{11,3},{4,12},{12,4},... | collective-permute-start | bytes 2304008 | tf_op jit(solution)/shard_map/ppermute | solution.py:314
  42.9 11.0 %collective-permute-start.14 = (bf16[160,2400]{1,0:T(8,128)(2,1)S(1)}, bf16[160,2400]{1,0:T(8,128)(2,1)}, u32[]{:S(2)}, u32[]{:S(2)}) collective-permute-start(bf16[160,2400]{1,0:T(8,128)(2,1)S(1)} %pad_maximum_fusion.far_b), channel_id=1, source_target_pairs={{0,8},{8,0},{1,9},{9,1},{2,10},{10,2},{3,11},{11,3},{4,12},{12,4},... | collective-permute-start | bytes 2304008 | tf_op jit(solution)/shard_map/ppermute | solution.py:314
  47.0 6.0 %collective-permute-start.16 = (f32[200,128]{1,0:T(8,128)S(1)}, f32[200,128]{1,0:T(8,128)S(1)}, u32[]{:S(2)}, u32[]{:S(2)}) collective-permute-start(f32[200,128]{1,0:T(8,128)S(1)} %last_terms.1.t), channel_id=1, source_target_pairs={{0,128},{128,0},{1,129},{129,1},{2,130},{130,2},{3,131},{131,3},{4... | collective-permute-start | bytes 307208 | tf_op jit(solution)/shard_map/ppermute | solution.py:326
  50.0 3.9 %collective-permute-start.17 = (f32[200,128]{1,0:T(8,128)S(1)}, f32[200,128]{1,0:T(8,128)S(1)}, u32[]{:S(2)}, u32[]{:S(2)}) collective-permute-start(f32[200,128]{1,0:T(8,128)S(1)} %last_terms.1.t), channel_id=1, source_target_pairs={{0,8},{8,0},{1,9},{9,1},{2,10},{10,2},{3,11},{11,3},{4,12},{12,4},... | collective-permute-start | bytes 307208 | tf_op jit(solution)/shard_map/ppermute | solution.py:327
  53.0 1.8 %collective-permute-start.18 = (f32[200,128]{1,0:T(8,128)S(1)}, f32[200,128]{1,0:T(8,128)S(1)}, u32[]{:S(2)}, u32[]{:S(2)}) collective-permute-start(f32[200,128]{1,0:T(8,128)S(1)} %collective-permute-done.16.t_yh), channel_id=1, source_target_pairs={{0,8},{8,0},{1,9},{9,1},{2,10},{10,2},{3,11},{11,3},{4,12},{12,4},... | collective-permute-start | bytes 307208 | tf_op jit(solution)/shard_map/ppermute | solution.py:328
  53.9 10.0 %copy-start.6 = (s32[2,30]{1,0:T(2,128)S(1)}, s32[2,30]{1,0:T(2,128)}, u32[]{:S(2)}) copy-start(s32[2,30]{1,0:T(2,128)} %param.11) | copy-start | bytes 724
  59.0 12.5 %all-to-all-start = ((s16[8,56,128]{2,1,0:T(8,128)(2,1)}), s16[8,56,128]{2,1,0:T(8,128)(2,1)S(1)}, u32[]{:S(2)}, u32[]{:S(2)}) async-start(s16[8,56,128]{2,1,0:T(8,128)(2,1)} %bitcast.2), calls=%async_computation | async-start | bytes 229376 | tf_op jit(solution)/shard_map/all_to_all | solution.py:350
